TPU v7x, 256 devices: a whole 4x4x8 slice. The times are simulated.
256 devices in a mesh: alpha: 16 (over y_hi, x, core), beta: 16 (over y_lo, z).
Axes of the slice: x: 4, y: 4 (y_hi: 2, y_lo: 2; y = y_hi * 2 + y_lo), z: 8, core: 2. Of those that a mesh axis runs over, the one named last changes fastest.
Arguments:
- coeffs: float32 [8192, 8192], P('alpha', 'beta'), may hold values from -6 to 6
- diag_alpha: float32 [8192], P('alpha'), may hold values from 0.5 to 2
- diag_beta: float32 [8192], P('beta'), may hold values from 0.5 to 2
- alpha_tiles: float32 [32, 8, 256, 256], P('alpha'), may hold values from -0.375 to 0.375
- beta_hamiltonian_tiles: float32 [32, 8, 256, 256], P('beta'), may hold values from -0.375 to 0.375
- alpha_source: int32 [32, 8], replicated, may hold values from 0 to 31, as said below
- alpha_live: int32 [32, 8], replicated, may hold values from 0 to 1, as said below
- beta_source_block: int32 [32, 8], replicated, may hold values from 0 to 31, as said below
- beta_live: int32 [32, 8], replicated, may hold values from 0 to 1, as said below
Outputs:
- sigma: float32 [8192, 8192], P('alpha', 'beta')
Inputs may be any that keep to these rules, and one draw needn't show every extreme that they name: `beta_source_block`: target blocks are grouped by device: the 32 / 16 consecutive target blocks of one beta index ask, over all their slots, exactly (32 // 16 * 8) // 16 source blocks (counted with repetition) of every beta index, where beta index k holds blocks k * (32 // 16) onward. `alpha_source`: likewise for alpha: the 2 consecutive target blocks of one alpha index ask, over all their slots, exactly 2 * 8 // 16 source blocks of every alpha index. `beta_live`: in each target block the live slots come first, and slot 0 is live. `alpha_live`: in each target block the live slots come first, and slot 0 is live.
All inputs are finite; a program needn't handle non-finite values.
Results may differ from a plain program's by a relative error of at most 0.0003.
Values sent between devices are 32-bit elements; how exact they have to be, the bound alone decides.
No kernel may reach another device: no remote copies, remote signals or barrier semaphores. Data moves between devices by JAX's collectives and lax.ppermute only.
A program may use at most 128 MiB of HBM per device.

v0:
```python
import jax
import jax.numpy as jnp
from jax import lax
from jax.sharding import PartitionSpec as P


def outbound_dispatch_table(table_all, own_index, blocks_dev, capacity):
    owners = table_all // blocks_dev
    to_me = (owners == own_index).astype(jnp.int32)
    order_in = jnp.cumsum(to_me, axis=1) - 1
    slot_ids = jnp.arange(capacity)
    matched = to_me[:, :, None] * (order_in[:, :, None] == slot_ids[None, None, :]).astype(
        jnp.int32
    )
    inner_identifiers = table_all - own_index * blocks_dev
    return jnp.sum(matched * inner_identifiers[:, :, None], axis=1)


def receive_plan(sources_mine, blocks_dev, capacity):
    owners = sources_mine // blocks_dev
    requests = sources_mine.shape[0]
    same_owner = (owners[:, None] == owners[None, :]).astype(jnp.int32)
    earlier = jnp.tril(jnp.ones((requests, requests), jnp.int32), -1)
    order_in = jnp.sum(same_owner * earlier, axis=1)
    return owners * capacity + order_in


def per_device(
    coeffs,
    diag_alpha,
    diag_beta,
    alpha_tiles,
    beta_hamiltonian_tiles,
    alpha_source,
    alpha_live,
    beta_source_block,
    beta_live,
):
    rows_dev, cols_dev = coeffs.shape
    block_size = beta_hamiltonian_tiles.shape[2]
    couplings = beta_hamiltonian_tiles.shape[1]
    alpha_count = alpha_tiles.shape[0]
    beta_count = beta_hamiltonian_tiles.shape[0]
    alpha_devices = lax.axis_size("alpha")
    beta_devices = lax.axis_size("beta")
    alpha_index = lax.axis_index("alpha")
    beta_index = lax.axis_index("beta")
    beta_requests = beta_count * couplings
    beta_table = beta_source_block.reshape(beta_devices, beta_requests)
    beta_mine = lax.dynamic_index_in_dim(beta_table, beta_index, 0, keepdims=False)
    beta_flags = lax.dynamic_slice_in_dim(beta_live, beta_index * beta_count, beta_count, 0).astype(
        jnp.float32
    )
    whole = lax.all_gather(coeffs, "beta", axis=1, tiled=True)
    whole_blocks = whole.reshape(rows_dev, beta_devices * beta_count, block_size)
    beta_gathered = jnp.take(whole_blocks, beta_mine, axis=1)
    beta_masked = beta_hamiltonian_tiles * beta_flags[:, :, None, None]
    beta_grouped = beta_gathered.reshape(rows_dev, beta_count, couplings, block_size)
    beta_term = jnp.einsum(
        "ajcb,jcbd->ajd", beta_grouped, beta_masked, precision=lax.Precision.HIGHEST
    )
    beta_term = beta_term.reshape(rows_dev, cols_dev)
    alpha_requests = alpha_count * couplings
    alpha_capacity = alpha_requests // alpha_devices
    alpha_table = alpha_source.reshape(alpha_devices, alpha_requests)
    alpha_mine = lax.dynamic_index_in_dim(alpha_table, alpha_index, 0, keepdims=False)
    alpha_flags = lax.dynamic_slice_in_dim(
        alpha_live, alpha_index * alpha_count, alpha_count, 0
    ).astype(jnp.float32)
    alpha_send = outbound_dispatch_table(alpha_table, alpha_index, alpha_count, alpha_capacity)
    alpha_blocks = coeffs.reshape(alpha_count, block_size, cols_dev)
    alpha_out = jnp.take(alpha_blocks, alpha_send.reshape(-1), axis=0)
    alpha_out = alpha_out.reshape(alpha_devices, alpha_capacity, block_size, cols_dev)
    alpha_in = lax.all_to_all(alpha_out, "alpha", split_axis=0, concat_axis=0, tiled=True)
    alpha_where = receive_plan(alpha_mine, alpha_count, alpha_capacity)
    alpha_gathered = jnp.take(
        alpha_in.reshape(alpha_requests, block_size, cols_dev), alpha_where, axis=0
    )
    alpha_collated = alpha_gathered.reshape(alpha_count, couplings, block_size, cols_dev)
    alpha_filtered = alpha_tiles * alpha_flags[:, :, None, None]
    alpha_term = jnp.einsum(
        "znog,zngx->zox", alpha_filtered, alpha_collated, precision=lax.Precision.HIGHEST
    )
    alpha_term = alpha_term.reshape(rows_dev, cols_dev)
    diagonal = diag_alpha[:, None] + diag_beta[None, :]
    return diagonal * coeffs + beta_term + alpha_term


def solution(mesh):
    return jax.shard_map(
        per_device,
        mesh=mesh,
        in_specs=(
            P("alpha", "beta"),
            P("alpha"),
            P("beta"),
            P("alpha", None, None, None),
            P("beta", None, None, None),
            P(),
            P(),
            P(),
            P(),
        ),
        out_specs=P("alpha", "beta"),
        check_vma=False,
    )
```

profile of v0, /device:TPU:1, one launch (start us, length us, event | category | flops | bytes accessed | tf_op | source)
XLA Modules:
  0.0 362.6 jit_solution(11961935233513448246)
XLA Ops:
  6.5 2.6 copy.56
  9.2 0.8 copy.61
  10.0 0.1 reshape.213
  10.0 0.2 reduce_window_sum.11
  10.2 0.1 eq.46
  10.3 0.1 copy.62
  10.4 0.7 multiply_reduce_fusion
  11.1 0.1 reduce_sum.34
  11.2 0.1 reduce_sum.35
  11.3 4.3 %gather_fusion.1 = f32[16,256,512]{2,1,0:T(8,128)} fusion(f32[2,256,512]{2,1,0:T(8,128)S(1)} %bitcast.54, s32[1024]{0:T(1024)S(1)} %pad_clamp_fusion.1), kind=kCustom, calls=%fused_computation.1 | custom fusion | bytes 16777280 | tf_op jit(solution)/shard_map/jit(_take)/gather | solution.py:72
  15.6 8.1 %bitcast_select_fusion = f32[16,1,256,512]{3,2,1,0:T(8,128)} fusion(f32[16,256,512]{2,1,0:T(8,128)} %gather_fusion.1, pred[16]{0:T(512)(128)(4,1)S(1)} %compare_and_fusion), kind=kLoop, calls=%fused_computation.3 | loop fusion | flops 2097152 | bytes 16777232 | tf_op jit(solution)/shard_map/jit(_take)/select_n | solution.py:72
  23.7 8.6 %all-to-all-start = ((f32[16,1,256,512]{3,2,1,0:T(8,128)}), f32[16,1,256,512]{3,2,1,0:T(8,128)}, u32[]{:S(2)}, u32[]{:S(2)}) async-start(f32[16,1,256,512]{3,2,1,0:T(8,128)} %bitcast_select_fusion), calls=%async_computation | async-start | bytes 16777216 | tf_op jit(solution)/shard_map/all_to_all | solution.py:74
  32.3 0.1 dynamic-slice_convert_fusion
  32.4 0.1 copy.60
  32.5 0.1 dynamic-slice_convert_fusion.1
  32.6 0.1 copy.54
  32.7 0.1 copy.55
  32.7 0.1 reshape.210
  32.8 0.1 squeeze.13
  32.9 0.6 broadcast.333
  33.5 0.7 fusion.26
  34.2 0.1 squeeze.15
  34.3 0.2 select_reduce_fusion
  34.5 0.1 reduce_sum.32
  34.6 254.6 %all-to-all-done = f32[16,1,256,512]{3,2,1,0:T(8,128)} async-done(((f32[16,1,256,512]{3,2,1,0:T(8,128)}), f32[16,1,256,512]{3,2,1,0:T(8,128)}, u32[]{:S(2)}, u32[]{:S(2)}) %all-to-all-start) | async-done | bytes 8388640 | tf_op jit(solution)/shard_map/all_to_all | solution.py:74
  289.2 7.7 %gather_fusion.2 = f32[16,256,512]{2,1,0:T(8,128)} fusion(f32[16,256,512]{2,1,0:T(8,128)} %bitcast.15, s32[1024]{0:T(1024)S(1)} %pad_clamp_fusion), kind=kCustom, calls=%fused_computation.2 | custom fusion | bytes 16777280 | tf_op jit(solution)/shard_map/jit(_take)/gather | solution.py:76
  296.9 10.7 %fusion = f32[2,256,512,1]{2,1,3,0:T(8,128)S(1)} fusion(f32[2,8,256,512]{3,2,1,0:T(8,128)} %bitcast.56, f32[2,8,256,256]{3,2,1,0:T(8,128)} %param.12, pred[2,8]{1,0:T(4,128)(4,1)S(1)} %get-tuple-element.7, f32[2,8]{1,0:T(2,128)S(1)} %copy.60), kind=kOutput, calls=%fused_computation.4 | convolution fusion | flops 6445596672 | bytes 13631568 | tf_op jit(solution)/shard_map/znog,zngx->zox/dot_general | solution.py:81
  307.6 17.5 %copy.57 = f32[512,32,256]{2,0,1:T(8,128)} copy(f32[512,32,256]{0,2,1:T(8,128)} %bitcast.57) | data formatting | bytes 33554432 | tf_op jit(solution)/shard_map/reshape | solution.py:55
  325.1 10.1 %gather_fusion = f32[16,512,256]{2,1,0:T(8,128)} fusion(f32[512,32,256]{2,0,1:T(8,128)} %copy.57, s32[1024]{0:T(1024)S(1)} %pad_clamp_fusion.2), kind=kCustom, calls=%fused_computation | custom fusion | bytes 16777280 | tf_op jit(solution)/shard_map/jit(_take)/gather | solution.py:56
  335.2 16.7 %fusion.2 = f32[2,256,512,1]{2,1,3,0:T(8,128)S(1)} fusion(f32[512,2,8,256]{3,0,2,1:T(8,128)} %bitcast.55, f32[2,8,256,256]{3,2,1,0:T(8,128)} %param.13, pred[2,8]{1,0:T(4,128)(4,1)S(1)} %get-tuple-element.8, f32[2,8]{1,0:T(2,128)S(1)} %copy.54), kind=kOutput, calls=%fused_computation.6 | convolution fusion | flops 6445596672 | bytes 13631568 | tf_op jit(solution)/shard_map/ajcb,jcbd->ajd/dot_general | solution.py:59
  351.9 1.3 copy.59
  353.2 2.5 bitcast_add_fusion
  (29 shorter events, 0.2 us)
Async XLA Ops:
  6.5 4.8 %copy-start = (f32[512,512]{1,0:T(8,128)S(1)}, f32[512,512]{1,0:T(8,128)}, u32[]{:S(2)}) copy-start(f32[512,512]{1,0:T(8,128)} %param.9) | copy-start | bytes 3145732
  6.5 301.1 %all-gather.2.cloned.1.call-start = ((), (), s32[]{:S(2)}) async-start(), calls=%async_computation.1 | async-start | bytes 17825792 | tf_op jit(solution)/shard_map/all_gather | solution.py:54
  23.7 8.6 %copy-start.2 = (s32[32,8]{0,1:T(8,128)S(1)}, s32[32,8]{0,1:T(8,128)}, u32[]{:S(2)}) copy-start(s32[32,8]{0,1:T(8,128)} %param.15) | copy-start | bytes 3076
  23.7 8.8 %copy-start.3 = (s32[32,8]{0,1:T(8,128)S(1)}, s32[32,8]{0,1:T(8,128)}, u32[]{:S(2)}) copy-start(s32[32,8]{0,1:T(8,128)} %param.17) | copy-start | bytes 3076
  23.7 8.9 %copy-start.1 = (s32[32,8]{0,1:T(8,128)S(1)}, s32[32,8]{0,1:T(8,128)}, u32[]{:S(2)}) copy-start(s32[32,8]{0,1:T(8,128)} %param.16) | copy-start | bytes 3076
  23.7 265.5 %all-to-all-start = ((f32[16,1,256,512]{3,2,1,0:T(8,128)}), f32[16,1,256,512]{3,2,1,0:T(8,128)}, u32[]{:S(2)}, u32[]{:S(2)}) async-start(f32[16,1,256,512]{3,2,1,0:T(8,128)} %bitcast_select_fusion), calls=%async_computation | async-start | bytes 16777216 | tf_op jit(solution)/shard_map/all_to_all | solution.py:74
  335.2 18.0 %copy-start.4 = (f32[512]{0:T(512)S(1)}, f32[512]{0:T(512)}, u32[]{:S(2)}) copy-start(f32[512]{0:T(512)} %param.11) | copy-start | bytes 6148
  335.2 18.0 %copy-start.5 = (f32[512]{0:T(512)S(1)}, f32[512]{0:T(512)}, u32[]{:S(2)}) copy-start(f32[512]{0:T(512)} %param.10) | copy-start | bytes 6148
Sparse Core Ops, SparseCore 0:
  9.3 256.5 all-gather.1
where the time goes:
time: 363 us
  waiting for transfers between devices  255 us (70%)
  local copies, waits for them, and re-layouts  46.4 us (13%)
  matrix products  27.4 us (8%)
  between operations  13.5 us (4%)
  other arithmetic  12.1 us (3%)
  starting transfers between devices  8.58 us (2%)
    all_to_all x1, waiting for transfers between devices, per_device(): lax.all_to_all(alpha_out, 'alpha', split_axis=0, concat_axis=0, tiled=True)  255 us
    reshape x1, local copies, waits for them, and re-layouts, per_device(): whole.reshape(rows_dev, beta_devices * beta_count, block_size)  17.5 us
    dot_general x1, matrix products, per_device(): jnp.einsum('ajcb,jcbd->ajd', beta_grouped, beta_masked, precision=lax.Pre...  16.7 us
    dot_general x1, matrix products, per_device(): jnp.einsum('znog,zngx->zox', alpha_filtered, alpha_collated, precision=la...  10.7 us
    gather x1, local copies, waits for them, and re-layouts, per_device(): beta_gathered = jnp.take(whole_blocks, beta_mine, axis=1)  10.1 us
    all_to_all x1, starting transfers between devices, per_device(): lax.all_to_all(alpha_out, 'alpha', split_axis=0, concat_axis=0, tiled=True)  8.58 us
    select_n x2, other arithmetic, per_device(): alpha_out = jnp.take(alpha_blocks, alpha_send.reshape(-1), axis=0)  8.09 us
    gather x1, local copies, waits for them, and re-layouts, per_device(): jnp.take(alpha_in.reshape(alpha_requests, block_size, cols_dev), alpha_wh...  7.67 us
  transfers between devices with their start and end apart: 2, of which 1 were waited for; matrix products, arithmetic and copies ran while one was open for 10% of the time, Pallas kernels for 0%

commit v1 on v0

v1 whole, which is shorter than its diff:
```python
import functools

import jax
import jax.numpy as jnp
from jax import lax
from jax.experimental import pallas as pl
from jax.experimental.pallas import tpu as pltpu
from jax.sharding import Mesh
from jax.sharding import PartitionSpec as P

AXES = ("yhi", "x", "core", "ylo", "z")
SIZES = (2, 4, 2, 2, 8)
ALPHA = ("yhi", "x", "core")
BETA = ("ylo", "z")
BS = 256


def shift(value, axis, step):
    n = lax.axis_size(axis)
    return lax.ppermute(value, axis, [(i, (i + step) % n) for i in range(n)])


def dot3(a, b):
    a_hi = a.astype(jnp.bfloat16)
    b_hi = b.astype(jnp.bfloat16)
    a_lo = (a - a_hi.astype(jnp.float32)).astype(jnp.bfloat16)
    b_lo = (b - b_hi.astype(jnp.float32)).astype(jnp.bfloat16)
    dot = functools.partial(jnp.dot, preferred_element_type=jnp.float32)
    return dot(a_hi, b_hi) + (dot(a_hi, b_lo) + dot(a_lo, b_hi))


def alpha_kernel(
    where, source, live, u0, uf, ub, u2a, u2b, v0, vf, vb, v2a, v2b, own, sib, out, data, tiles, sem
):
    copies = []
    for y, (a, f, b, la, lb) in enumerate(((u0, uf, ub, u2a, u2b), (v0, vf, vb, v2a, v2b))):
        copies += [
            (a, data.at[y, 0]),
            (f, data.at[y, 3]),
            (b, data.at[y, 1]),
            (la, data.at[y, 2, 0]),
            (lb, data.at[y, 2, 1]),
        ]
    copies += [(own, tiles.at[0]), (sib, tiles.at[1])]
    copies = [pltpu.make_async_copy(s, d, sem.at[i]) for i, (s, d) in enumerate(copies)]
    for copy in copies:
        copy.start()
    out[...] = jnp.zeros_like(out)
    me = where[0]
    for copy in copies:
        copy.wait()
    for target in range(2):
        for block in range(2):

            def slot(c, _, target=target, block=block):
                row = 2 * (me ^ target) + block

                @pl.when(live[row, c] > 0)
                def _():
                    src = source[row, c]
                    owner = src >> 1
                    y = (owner >> 3) ^ (me >> 3)
                    x = ((owner >> 1) - (me >> 1)) & 3
                    core = (owner & 1) ^ (me & 1)
                    first = pl.multiple_of((src & 1) * BS, BS)
                    rows = data[y, x, core, pl.ds(first, BS), :]
                    out[target, block * BS : (block + 1) * BS, :] += dot3(
                        tiles[target, block, c], rows
                    )

                return 0

            lax.fori_loop(0, 8, slot, 0)


def beta_kernel(
    where, source, live, ring, p0, f1, b1, f2, b2, f3, b3, f4, b4, own, par, out, data, tiles, sem
):
    me = where[1]
    z = me & 7
    half = p0.shape[0] // 2
    copies = [(ring, data.at[0]), (p0, data.at[1, z])]
    for k, (f, b) in enumerate(((f1, b1), (f2, b2), (f3, b3)), 1):
        copies += [(f, data.at[1, (z - k) & 7]), (b, data.at[1, (z + k) & 7])]
    copies += [
        (f4, data.at[1, (z + 4) & 7, pl.ds(0, half)]),
        (b4, data.at[1, (z + 4) & 7, pl.ds(half, half)]),
        (own, tiles.at[0]),
        (par, tiles.at[1]),
    ]
    copies = [pltpu.make_async_copy(s, d, sem.at[i]) for i, (s, d) in enumerate(copies)]
    for copy in copies:
        copy.start()
    out[...] = jnp.zeros_like(out)
    for copy in copies:
        copy.wait()
    for target in range(2):
        for block in range(2):

            def slot(c, _, target=target, block=block):
                row = 2 * (me ^ (8 * target)) + block

                @pl.when(live[row, c] > 0)
                def _():
                    src = source[row, c]
                    owner = src >> 1
                    y = (owner >> 3) ^ (me >> 3)
                    first = pl.multiple_of((src & 1) * BS, BS)
                    columns = data[y, owner & 7, :, pl.ds(first, BS)]
                    out[target, :, block * BS : (block + 1) * BS] += dot3(
                        columns, tiles[target, block, c]
                    )

                return 0

            lax.fori_loop(0, 8, slot, 0)


def last_kernel(where, x, da, db, alpha, alpha_other, beta, beta_other, out):
    core = where[0] & 1
    ylo = where[1] >> 3
    out[...] = (da[...] + db[...]) * x[...]

    def columns(first, part):
        out[:, first : first + BS] += part[...]

    def rows(first, part):
        out[first : first + BS, :] += part[...]

    for side in range(2):

        @pl.when(core == side)
        def _(side=side):
            columns(side * BS, alpha)
            columns((1 - side) * BS, alpha_other)

        @pl.when(ylo == side)
        def _(side=side):
            rows(side * BS, beta)
            rows((1 - side) * BS, beta_other)


SMEM = pl.BlockSpec(memory_space=pltpu.SMEM)
ANY = pl.BlockSpec(memory_space=pl.ANY)
VMEM = pl.BlockSpec(memory_space=pltpu.VMEM)
MIB = 1 << 20


def per_device(
    coeffs,
    diag_alpha,
    diag_beta,
    alpha_tiles,
    beta_tiles,
    alpha_source,
    alpha_live,
    beta_source,
    beta_live,
):
    n = coeffs.shape[0]
    core = lax.axis_index("core")
    ylo = lax.axis_index("ylo")
    where = jnp.stack([lax.axis_index(ALPHA), lax.axis_index(BETA)]).astype(jnp.int32)

    keep = lax.dynamic_slice_in_dim(coeffs, ylo * BS, BS, 0)
    give = lax.dynamic_slice_in_dim(coeffs, (1 - ylo) * BS, BS, 0)
    ring = lax.all_gather(keep, "z")
    p0 = shift(give, "ylo", 1)
    f1, b1 = shift(p0, "z", 1), shift(p0, "z", -1)
    f2, b2 = shift(f1, "z", 1), shift(b1, "z", -1)
    f3, b3 = shift(f2, "z", 1), shift(b2, "z", -1)
    f4, b4 = shift(f3[: BS // 2], "z", 1), shift(b3[BS // 2 :], "z", -1)
    mine = lax.dynamic_index_in_dim(beta_tiles, core, 0, keepdims=False)
    got = shift(mine, "ylo", 1)
    other = shift(got, "core", 1)
    par_tiles = jnp.stack([jnp.where(core == 0, got, other), jnp.where(core == 0, other, got)])

    left = lax.dynamic_slice_in_dim(coeffs, core * BS, BS, 1)
    right = lax.dynamic_slice_in_dim(coeffs, (1 - core) * BS, BS, 1)
    u0 = jnp.stack([left, shift(right, "core", 1)])
    v0 = shift(u0, "yhi", 1)
    gathered = []
    for first in (u0, v0):
        f, b = shift(first, "x", 1), shift(first, "x", -1)
        gathered += [first, f, b, shift(f[0], "x", 1), shift(b[1], "x", -1)]
    sib_tiles = shift(alpha_tiles, "core", 1)

    flops = 2 * 32 * BS**3 * 3
    alpha = pl.pallas_call(
        alpha_kernel,
        out_shape=jax.ShapeDtypeStruct((2, n, BS), jnp.float32),
        in_specs=[SMEM] * 3 + [ANY] * 12,
        out_specs=VMEM,
        scratch_shapes=[
            pltpu.VMEM((2, 4, 2, n, BS), jnp.float32),
            pltpu.VMEM((2, 2, 8, BS, BS), jnp.float32),
            pltpu.SemaphoreType.DMA((12,)),
        ],
        compiler_params=pltpu.CompilerParams(vmem_limit_bytes=32 * MIB),
        cost_estimate=pl.CostEstimate(flops=flops, bytes_accessed=17 * MIB, transcendentals=0),
        name="alpha",
    )(where, alpha_source, alpha_live, *gathered, alpha_tiles, sib_tiles)
    alpha_other = shift(alpha[1], "core", 1)

    beta = pl.pallas_call(
        beta_kernel,
        out_shape=jax.ShapeDtypeStruct((2, BS, n), jnp.float32),
        in_specs=[SMEM] * 3 + [ANY] * 12,
        out_specs=VMEM,
        scratch_shapes=[
            pltpu.VMEM((2, 8, BS, n), jnp.float32),
            pltpu.VMEM((2, 2, 8, BS, BS), jnp.float32),
            pltpu.SemaphoreType.DMA((12,)),
        ],
        compiler_params=pltpu.CompilerParams(vmem_limit_bytes=32 * MIB),
        cost_estimate=pl.CostEstimate(flops=flops, bytes_accessed=17 * MIB, transcendentals=0),
        name="beta",
    )(where, beta_source, beta_live, ring, p0, f1, b1, f2, b2, f3, b3, f4, b4, beta_tiles, par_tiles)
    beta_other = shift(beta[1], "ylo", 1)

    return pl.pallas_call(
        last_kernel,
        out_shape=jax.ShapeDtypeStruct((n, n), jnp.float32),
        in_specs=[SMEM] + [VMEM] * 7,
        out_specs=VMEM,
        cost_estimate=pl.CostEstimate(flops=4 * n * n, bytes_accessed=5 * MIB, transcendentals=0),
        name="last",
    )(where, coeffs, diag_alpha[:, None], diag_beta[None, :], alpha[0], alpha_other, beta[0], beta_other)


def solution(mesh):
    parts = Mesh(mesh.devices.reshape(SIZES), AXES)
    return jax.shard_map(
        per_device,
        mesh=parts,
        in_specs=(
            P(ALPHA, BETA),
            P(ALPHA),
            P(BETA),
            P(ALPHA, None, None, None),
            P(BETA, None, None, None),
            P(),
            P(),
            P(),
            P(),
        ),
        out_specs=P(ALPHA, BETA),
        check_vma=False,
    )
```

time: 363 us -> 241 us (0.66)
  waiting for transfers between devices: 255 us -> 121 us
  starting transfers between devices: 8.58 us -> 44.6 us
  matrix products: 27.4 us -> 0 us
  Pallas kernels: 0 us -> 23 us
  local copies, waits for them, and re-layouts: 46.4 us -> 31.6 us
  other arithmetic: 12.1 us -> 6.34 us
    all_to_all x1 -> x0, waiting for transfers between devices: 255 us -> none  [per_device(): lax.all_to_all(alpha_out, 'alpha', split_axis=0, concat_axis=0, tiled=True)]
    ppermute x0 -> x24, waiting for transfers between devices: none -> 121 us  [shift(): return lax.ppermute(value, axis, [(i, (i + step) % n) for i in range(n)])]
    ppermute x0 -> x24, starting transfers between devices: none -> 44.6 us  [shift(): return lax.ppermute(value, axis, [(i, (i + step) % n) for i in range(n)])]
    dot_general x2 -> x0, matrix products: 27.4 us -> none  [the longest x1 16.7 us: per_device(): jnp.einsum('ajcb,jcbd->ajd', beta_grouped, beta_masked, precision=lax.Pre...]
    pallas_call x0 -> x3, Pallas kernels: none -> 23 us  [the longest x1 10.2 us: per_device(): pl.pallas_call(beta_kernel, out_shape=jax.ShapeDtypeStruct((2, BS, n), jn...]
    gather x3 -> x0, local copies, waits for them, and re-layouts: 22 us -> none  [the longest x1 10.1 us: per_device(): beta_gathered = jnp.take(whole_blocks, beta_mine, axis=1)]
    reshape x4 -> x0, local copies, waits for them, and re-layouts: 18.9 us -> none  [the longest x1 17.5 us: per_device(): whole.reshape(rows_dev, beta_devices * beta_count, block_size)]
    unnamed x15 -> x70, local copies, waits for them, and re-layouts: 3.48 us -> 19.6 us
  transfers between devices with their start and end apart: 2 -> 25, of which waited for: 1 -> 13; matrix products, arithmetic and copies ran while one was open for 10% -> 7% of each run, Pallas kernels for 0% -> 8%
where the time goes in v1:
time: 241 us; the launch traced here: 240 us
  waiting for transfers between devices  121 us (50%)
  starting transfers between devices  44.6 us (19%)
  local copies, waits for them, and re-layouts  31.6 us (13%)
  Pallas kernels  23 us (10%)
  between operations  13.6 us (6%)
  other arithmetic  6.34 us (3%)
    ppermute x24, waiting for transfers between devices, shift(): return lax.ppermute(value, axis, [(i, (i + step) % n) for i in range(n)])  121 us
    ppermute x24, starting transfers between devices, shift(): return lax.ppermute(value, axis, [(i, (i + step) % n) for i in range(n)])  44.6 us
    unnamed x70, local copies, waits for them, and re-layouts  19.6 us
    pallas_call x1, Pallas kernels, per_device(): pl.pallas_call(beta_kernel, out_shape=jax.ShapeDtypeStruct((2, BS, n), jn...  10.2 us
    pallas_call x1, Pallas kernels, per_device(): pl.pallas_call(alpha_kernel, out_shape=jax.ShapeDtypeStruct((2, n, BS), j...  9.49 us
    another operation x2, other arithmetic, per_device(): jnp.stack([jnp.where(core == 0, got, other), jnp.where(core == 0, other,...  4.97 us
  transfers between devices with their start and end apart: 25, of which 13 were waited for; matrix products, arithmetic and copies ran while one was open for 7% of the time, Pallas kernels for 8%

profile of v1, /device:TPU:1, one launch (start us, length us, event | category | flops | bytes accessed | tf_op | source)
XLA Modules:
  0.0 240.4 jit_solution(10065343429351137940)
XLA Ops:
  6.5 2.2 constant_dynamic-slice_fusion
  8.7 2.2 collective-permute-start.12
  13.0 8.3 %collective-permute-done.12.p0 = f32[256,512]{1,0:T(8,128)S(1)} collective-permute-done((f32[256,512]{1,0:T(8,128)S(1)}, f32[256,512]{1,0:T(8,128)S(1)}, u32[]{:S(2)}, u32[]{:S(2)}) %collective-permute-start.12) | collective-permute-done | bytes 524320 | tf_op jit(solution)/shard_map/ppermute | solution.py:20
  21.3 2.7 %collective-permute-start.13 = (f32[256,512]{1,0:T(8,128)S(1)}, f32[256,512]{1,0:T(8,128)S(1)}, u32[]{:S(2)}, u32[]{:S(2)}) collective-permute-start(f32[256,512]{1,0:T(8,128)S(1)} %collective-permute-done.12.p0), channel_id=1, source_target_pairs={{0,1},{1,2},{2,3},{3,4},{4,5},{5,6},{6,7},{7,0},{8,9},{9,10},{10,1... | collective-permute-start | bytes 1572872 | tf_op jit(solution)/shard_map/ppermute | solution.py:20
  25.9 3.7 %collective-permute-start.14 = (f32[256,512]{1,0:T(8,128)S(1)}, f32[256,512]{1,0:T(8,128)S(1)}, u32[]{:S(2)}, u32[]{:S(2)}) collective-permute-start(f32[256,512]{1,0:T(8,128)S(1)} %collective-permute-done.12.p0), channel_id=1, source_target_pairs={{0,7},{1,0},{2,1},{3,2},{4,3},{5,4},{6,5},{7,6},{8,15},{9,8},{10,9... | collective-permute-start | bytes 1572872 | tf_op jit(solution)/shard_map/ppermute | solution.py:20
  32.7 18.1 %collective-permute-done.13.f1 = f32[256,512]{1,0:T(8,128)S(1)} collective-permute-done((f32[256,512]{1,0:T(8,128)S(1)}, f32[256,512]{1,0:T(8,128)S(1)}, u32[]{:S(2)}, u32[]{:S(2)}) %collective-permute-start.13) | collective-permute-done | bytes 524320 | tf_op jit(solution)/shard_map/ppermute | solution.py:20
  52.2 3.1 %collective-permute-start.5 = (f32[2,512,256]{2,1,0:T(8,128)S(1)}, f32[2,512,256]{2,1,0:T(8,128)S(1)}, u32[]{:S(2)}, u32[]{:S(2)}) collective-permute-start(f32[2,512,256]{2,1,0:T(8,128)S(1)} %pad_maximum_fusion.1.u0), channel_id=1, source_target_pairs={{0,128},{128,0},{1,129},{129,1},{2,130},{130,2},{3,131},{131,3},{4... | collective-permute-start | bytes 3145736 | tf_op jit(solution)/shard_map/ppermute | solution.py:20
  56.5 19.9 %collective-permute-done.15.f2 = f32[256,512]{1,0:T(8,128)S(1)} collective-permute-done((f32[256,512]{1,0:T(8,128)S(1)}, f32[256,512]{1,0:T(8,128)S(1)}, u32[]{:S(2)}, u32[]{:S(2)}) %collective-permute-start.15) | collective-permute-done | bytes 524320 | tf_op jit(solution)/shard_map/ppermute | solution.py:20
  77.5 17.9 %collective-permute-done.16.b2 = f32[256,512]{1,0:T(8,128)S(1)} collective-permute-done((f32[256,512]{1,0:T(8,128)S(1)}, f32[256,512]{1,0:T(8,128)S(1)}, u32[]{:S(2)}, u32[]{:S(2)}) %collective-permute-start.16) | collective-permute-done | bytes 524320 | tf_op jit(solution)/shard_map/ppermute | solution.py:20
  95.4 2.6 %collective-permute-start.2 = (f32[2,512,256]{2,1,0:T(8,128)S(1)}, f32[2,512,256]{2,1,0:T(8,128)S(1)}, u32[]{:S(2)}, u32[]{:S(2)}) collective-permute-start(f32[2,512,256]{2,1,0:T(8,128)S(1)} %pad_maximum_fusion.1.u0), channel_id=1, source_target_pairs={{0,96},{32,0},{64,32},{96,64},{1,97},{33,1},{65,33},{97,65},{2,98}... | collective-permute-start | bytes 3145736 | tf_op jit(solution)/shard_map/ppermute | solution.py:20
  97.9 5.3 %collective-permute-done.5.v0 = f32[2,512,256]{2,1,0:T(8,128)S(1)} collective-permute-done((f32[2,512,256]{2,1,0:T(8,128)S(1)}, f32[2,512,256]{2,1,0:T(8,128)S(1)}, u32[]{:S(2)}, u32[]{:S(2)}) %collective-permute-start.5) | collective-permute-done | bytes 1048608 | tf_op jit(solution)/shard_map/ppermute | solution.py:20
  107.7 11.0 %collective-permute-done.2.ub = f32[2,512,256]{2,1,0:T(8,128)S(1)} collective-permute-done((f32[2,512,256]{2,1,0:T(8,128)S(1)}, f32[2,512,256]{2,1,0:T(8,128)S(1)}, u32[]{:S(2)}, u32[]{:S(2)}) %collective-permute-start.2) | collective-permute-done | bytes 1048608 | tf_op jit(solution)/shard_map/ppermute | solution.py:20
  119.4 8.6 %collective-permute-done.6.vf = f32[2,512,256]{2,1,0:T(8,128)S(1)} collective-permute-done((f32[2,512,256]{2,1,0:T(8,128)S(1)}, f32[2,512,256]{2,1,0:T(8,128)S(1)}, u32[]{:S(2)}, u32[]{:S(2)}) %collective-permute-start.6) | collective-permute-done | bytes 1048608 | tf_op jit(solution)/shard_map/ppermute | solution.py:20
  128.8 12.3 %collective-permute-done.7.vb = f32[2,512,256]{2,1,0:T(8,128)S(1)} collective-permute-done((f32[2,512,256]{2,1,0:T(8,128)S(1)}, f32[2,512,256]{2,1,0:T(8,128)S(1)}, u32[]{:S(2)}, u32[]{:S(2)}) %collective-permute-start.7) | collective-permute-done | bytes 1048608 | tf_op jit(solution)/shard_map/ppermute | solution.py:20
  141.1 2.6 %collective-permute-start.18 = (f32[256,512]{1,0:T(8,128)S(1)}, f32[256,512]{1,0:T(8,128)}, u32[]{:S(2)}, u32[]{:S(2)}) collective-permute-start(f32[256,512]{1,0:T(8,128)S(1)} %collective-permute-done.16.b2), channel_id=1, source_target_pairs={{0,7},{1,0},{2,1},{3,2},{4,3},{5,4},{6,5},{7,6},{8,15},{9,8},{10,9... | collective-permute-start | bytes 1572872 | tf_op jit(solution)/shard_map/ppermute | solution.py:20
  147.1 3.3 %collective-permute-start.4 = (f32[512,256]{1,0:T(8,128)}, f32[512,256]{1,0:T(8,128)}, u32[]{:S(2)}, u32[]{:S(2)}) collective-permute-start(f32[512,256]{1,0:T(8,128)} %slice_bitcast_fusion.6), channel_id=1, source_target_pairs={{0,96},{32,0},{64,32},{96,64},{1,97},{33,1},{65,33},{97,65},{2,98}... | collective-permute-start | bytes 1572872 | tf_op jit(solution)/shard_map/ppermute | solution.py:20
  150.3 1.8 collective-permute-done.18.b3
  154.0 2.2 collective-permute-start.9
  160.2 4.1 %collective-permute-done.8.v2a = f32[512,256]{1,0:T(8,128)} collective-permute-done((f32[512,256]{1,0:T(8,128)}, f32[512,256]{1,0:T(8,128)}, u32[]{:S(2)}, u32[]{:S(2)}) %collective-permute-start.8) | collective-permute-done | bytes 524320 | tf_op jit(solution)/shard_map/ppermute | solution.py:20
  164.3 3.3 %collective-permute-start.20 = (f32[128,512]{1,0:T(8,128)S(1)}, f32[128,512]{1,0:T(8,128)S(1)}, u32[]{:S(2)}, u32[]{:S(2)}) collective-permute-start(f32[128,512]{1,0:T(8,128)S(1)} %slice.47), channel_id=1, source_target_pairs={{0,7},{1,0},{2,1},{3,2},{4,3},{5,4},{6,5},{7,6},{8,15},{9,8},{10,9... | collective-permute-start | bytes 786440 | tf_op jit(solution)/shard_map/ppermute | solution.py:20
  167.5 2.4 collective-permute-done.9.v2b
  169.9 2.2 copy-done.2
  176.8 9.5 %alpha.1 = f32[2,512,256]{2,1,0:T(8,128)S(1)} custom-call(s32[2]{0:T(128)S(1)} %pad_add_fusion.where, s32[32,8]{1,0:T(8,128)S(1)} %copy.14.source, s32[32,8]{1,0:T(8,128)S(1)} %copy.15.live, f32[2,512,256]{2,1,0:T(8,128)S(1)} %pad_maximum_fusion.1.u0, f32[2,512,256]{2,1,0:T(8,128)S(1)} %collective-permute-done.1.uf, ...), custom_call_target="tpu_custom_call" | custom-call | flops 3221225472 | bytes 17825792 | tf_op jit(solution)/shard_map/alpha/pallas_call | solution.py:189
  187.4 4.1 %collective-permute-start.11 = (f32[512,256]{1,0:T(8,128)}, f32[512,256]{1,0:T(8,128)S(1)}, u32[]{:S(2)}, u32[]{:S(2)}) collective-permute-start(f32[512,256]{1,0:T(8,128)} %get-tuple-element.11), channel_id=1, source_target_pairs={{0,16},{16,0},{1,17},{17,1},{2,18},{18,2},{3,19},{19,3},{4,20},{20... | collective-permute-start | bytes 1572872 | tf_op jit(solution)/shard_map/ppermute | solution.py:20
  191.5 2.6 %select_bitcast_fusion.1 = (f32[1,8,256,256]{3,2,1,0:T(8,128)S(1)}, f32[1,8,256,256]{3,2,1,0:T(8,128)S(1)}) fusion(f32[8,256,256]{2,1,0:T(8,128)} %collective-permute-done.21, f32[8,256,256]{2,1,0:T(8,128)} %collective-permute-done.22, pred[]{:T(512)S(6)} %eq.4), kind=kLoop, calls=%fused_computation.2 | loop fusion | flops 1048576 | bytes 8388609 | tf_op jit(solution)/shard_map/stack | solution.py:176
  194.1 2.4 pad_maximum_fusion.par
  197.3 2.2 copy-done
  199.4 2.2 copy-done.1
  201.6 2.2 copy-done.3
  204.8 10.2 %beta.1 = f32[2,256,512]{2,1,0:T(8,128)S(1)} custom-call(s32[2]{0:T(128)S(1)} %pad_add_fusion.where, s32[32,8]{1,0:T(8,128)S(1)} %copy.16.source, s32[32,8]{1,0:T(8,128)S(1)} %copy.17.live, f32[8,256,512]{2,1,0:T(8,128)S(1)} %bitcast.30, f32[256,512]{1,0:T(8,128)S(1)} %copy-done.11, f32[256,512]{1,0:T(8,128)S(1)} %copy-done.13, f32[256,512]{1,0:T(8,128)S(1)} %copy-done.15, ...), custom_call_target="tpu_custom_call" | custom-call | flops 3221225472 | bytes 17825792 | tf_op jit(solution)/shard_map/beta/pallas_call | solution.py:205
  218.1 11.4 %collective-permute-done.23.beta_other = f32[256,512]{1,0:T(8,128)S(1)} collective-permute-done((f32[256,512]{1,0:T(8,128)S(1)}, f32[256,512]{1,0:T(8,128)S(1)}, u32[]{:S(2)}, u32[]{:S(2)}) %collective-permute-start.23) | collective-permute-done | bytes 524320 | tf_op jit(solution)/shard_map/ppermute | solution.py:20
  230.2 3.3 %last.1 = f32[512,512]{1,0:T(8,128)} custom-call(s32[2]{0:T(128)} %copy-done.24, f32[512,512]{1,0:T(8,128)} %x.1, f32[512,1]{1,0:T(8,128)} %copy.18.da, f32[1,512]{1,0:T(1,128)} %bitcast.32, f32[512,256]{1,0:T(8,128)} %get-tuple-element.12.alpha, f32[512,256]{1,0:T(8,128)} %copy-done.26, f32[256,512]{1,0:T(8,128)} %get-tuple-element.8.beta, ...), custom_call_target="tpu_custom_call" | custom-call | flops 1048576 | bytes 5242880 | tf_op jit(solution)/shard_map/last/pallas_call | solution.py:221
  (108 shorter events, 37.1 us)
Async XLA Ops:
  6.5 190.7 %all-gather.3.cloned.1.call-start = ((), (), s32[]{:S(2)}) async-start(), calls=%async_computation | async-start | bytes 4718592 | tf_op jit(solution)/shard_map/all_gather | solution.py:167
  8.7 12.6 %collective-permute-start.12 = (f32[256,512]{1,0:T(8,128)S(1)}, f32[256,512]{1,0:T(8,128)S(1)}, u32[]{:S(2)}, u32[]{:S(2)}) collective-permute-start(f32[256,512]{1,0:T(8,128)S(1)} %get-tuple-element.9), channel_id=1, source_target_pairs={{0,8},{8,0},{1,9},{9,1},{2,10},{10,2},{3,11},{11,3},{4,12},{12,4},... | collective-permute-start | bytes 1572872 | tf_op jit(solution)/shard_map/ppermute | solution.py:20
  10.9 159.0 %collective-permute-start.10 = (f32[2,8,256,256]{3,2,1,0:T(8,128)}, f32[2,8,256,256]{3,2,1,0:T(8,128)}, u32[]{:S(2)}, u32[]{:S(2)}) collective-permute-start(f32[2,8,256,256]{3,2,1,0:T(8,128)} %own.2), channel_id=1, source_target_pairs={{0,16},{16,0},{1,17},{17,1},{2,18},{18,2},{3,19},{19,3},{4,20},{20... | collective-permute-start | bytes 12582920 | tf_op jit(solution)/shard_map/ppermute | solution.py:20
  21.3 29.5 %collective-permute-start.13 = (f32[256,512]{1,0:T(8,128)S(1)}, f32[256,512]{1,0:T(8,128)S(1)}, u32[]{:S(2)}, u32[]{:S(2)}) collective-permute-start(f32[256,512]{1,0:T(8,128)S(1)} %collective-permute-done.12.p0), channel_id=1, source_target_pairs={{0,1},{1,2},{2,3},{3,4},{4,5},{5,6},{6,7},{7,0},{8,9},{9,10},{10,1... | collective-permute-start | bytes 1572872 | tf_op jit(solution)/shard_map/ppermute | solution.py:20
  24.1 26.8 %collective-permute-start = (f32[512,256]{1,0:T(8,128)}, f32[512,256]{1,0:T(8,128)}, u32[]{:S(2)}, u32[]{:S(2)}) collective-permute-start(f32[512,256]{1,0:T(8,128)} %get-tuple-element.14), channel_id=1, source_target_pairs={{0,16},{16,0},{1,17},{17,1},{2,18},{18,2},{3,19},{19,3},{4,20},{20... | collective-permute-start | bytes 1572872 | tf_op jit(solution)/shard_map/ppermute | solution.py:20
  25.9 29.4 %collective-permute-start.14 = (f32[256,512]{1,0:T(8,128)S(1)}, f32[256,512]{1,0:T(8,128)S(1)}, u32[]{:S(2)}, u32[]{:S(2)}) collective-permute-start(f32[256,512]{1,0:T(8,128)S(1)} %collective-permute-done.12.p0), channel_id=1, source_target_pairs={{0,7},{1,0},{2,1},{3,2},{4,3},{5,4},{6,5},{7,6},{8,15},{9,8},{10,9... | collective-permute-start | bytes 1572872 | tf_op jit(solution)/shard_map/ppermute | solution.py:20
  31.3 74.6 %collective-permute-start.21 = (f32[8,256,256]{2,1,0:T(8,128)S(1)}, f32[8,256,256]{2,1,0:T(8,128)}, u32[]{:S(2)}, u32[]{:S(2)}) collective-permute-start(f32[8,256,256]{2,1,0:T(8,128)S(1)} %dynamic-slice_bitcast_fusion), channel_id=1, source_target_pairs={{0,8},{8,0},{1,9},{9,1},{2,10},{10,2},{3,11},{11,3},{4,12},{12,4},... | collective-permute-start | bytes 6291464 | tf_op jit(solution)/shard_map/ppermute | solution.py:20
  50.9 25.8 %copy-start.12 = (f32[256,512]{1,0:T(8,128)}, f32[256,512]{1,0:T(8,128)S(1)}, u32[]{:S(2)}) copy-start(f32[256,512]{1,0:T(8,128)S(1)} %collective-permute-done.13.f1) | copy-start | bytes 1572868
  50.9 25.6 %collective-permute-start.15 = (f32[256,512]{1,0:T(8,128)S(1)}, f32[256,512]{1,0:T(8,128)S(1)}, u32[]{:S(2)}, u32[]{:S(2)}) collective-permute-start(f32[256,512]{1,0:T(8,128)S(1)} %collective-permute-done.13.f1), channel_id=1, source_target_pairs={{0,1},{1,2},{2,3},{3,4},{4,5},{5,6},{6,7},{7,0},{8,9},{9,10},{10,1... | collective-permute-start | bytes 1572872 | tf_op jit(solution)/shard_map/ppermute | solution.py:20
  52.2 104.1 %copy-start.28 = (s32[32,8]{0,1:T(8,128)S(1)}, s32[32,8]{0,1:T(8,128)}, u32[]{:S(2)}) copy-start(s32[32,8]{0,1:T(8,128)} %param.16) | copy-start | bytes 3076
  52.2 104.1 %copy-start.29 = (s32[32,8]{0,1:T(8,128)S(1)}, s32[32,8]{0,1:T(8,128)}, u32[]{:S(2)}) copy-start(s32[32,8]{0,1:T(8,128)} %param.17) | copy-start | bytes 3076
  52.2 104.2 %copy-start.30 = (s32[32,8]{0,1:T(8,128)S(1)}, s32[32,8]{0,1:T(8,128)}, u32[]{:S(2)}) copy-start(s32[32,8]{0,1:T(8,128)} %param.14) | copy-start | bytes 3076
  52.2 104.3 %copy-start.31 = (s32[32,8]{0,1:T(8,128)S(1)}, s32[32,8]{0,1:T(8,128)}, u32[]{:S(2)}) copy-start(s32[32,8]{0,1:T(8,128)} %param.15) | copy-start | bytes 3076
  52.2 51.0 %collective-permute-start.5 = (f32[2,512,256]{2,1,0:T(8,128)S(1)}, f32[2,512,256]{2,1,0:T(8,128)S(1)}, u32[]{:S(2)}, u32[]{:S(2)}) collective-permute-start(f32[2,512,256]{2,1,0:T(8,128)S(1)} %pad_maximum_fusion.1.u0), channel_id=1, source_target_pairs={{0,128},{128,0},{1,129},{129,1},{2,130},{130,2},{3,131},{131,3},{4... | collective-permute-start | bytes 3145736 | tf_op jit(solution)/shard_map/ppermute | solution.py:20
  55.3 49.1 %collective-permute-start.1 = (f32[2,512,256]{2,1,0:T(8,128)S(1)}, f32[2,512,256]{2,1,0:T(8,128)S(1)}, u32[]{:S(2)}, u32[]{:S(2)}) collective-permute-start(f32[2,512,256]{2,1,0:T(8,128)S(1)} %pad_maximum_fusion.1.u0), channel_id=1, source_target_pairs={{0,32},{32,64},{64,96},{96,0},{1,33},{33,65},{65,97},{97,1},{2,34}... | collective-permute-start | bytes 3145736 | tf_op jit(solution)/shard_map/ppermute | solution.py:20
  76.4 18.9 %collective-permute-start.16 = (f32[256,512]{1,0:T(8,128)S(1)}, f32[256,512]{1,0:T(8,128)S(1)}, u32[]{:S(2)}, u32[]{:S(2)}) collective-permute-start(f32[256,512]{1,0:T(8,128)S(1)} %collective-permute-done.14.b1), channel_id=1, source_target_pairs={{0,7},{1,0},{2,1},{3,2},{4,3},{5,4},{6,5},{7,6},{8,15},{9,8},{10,9... | collective-permute-start | bytes 1572872 | tf_op jit(solution)/shard_map/ppermute | solution.py:20
  95.4 23.3 %collective-permute-start.2 = (f32[2,512,256]{2,1,0:T(8,128)S(1)}, f32[2,512,256]{2,1,0:T(8,128)S(1)}, u32[]{:S(2)}, u32[]{:S(2)}) collective-permute-start(f32[2,512,256]{2,1,0:T(8,128)S(1)} %pad_maximum_fusion.1.u0), channel_id=1, source_target_pairs={{0,96},{32,0},{64,32},{96,64},{1,97},{33,1},{65,33},{97,65},{2,98}... | collective-permute-start | bytes 3145736 | tf_op jit(solution)/shard_map/ppermute | solution.py:20
  103.3 43.8 %copy-start.8 = (f32[2,512,256]{2,1,0:T(8,128)}, f32[2,512,256]{2,1,0:T(8,128)S(1)}, u32[]{:S(2)}) copy-start(f32[2,512,256]{2,1,0:T(8,128)S(1)} %collective-permute-done.5.v0) | copy-start | bytes 3145732
  103.3 24.7 %collective-permute-start.6 = (f32[2,512,256]{2,1,0:T(8,128)S(1)}, f32[2,512,256]{2,1,0:T(8,128)S(1)}, u32[]{:S(2)}, u32[]{:S(2)}) collective-permute-start(f32[2,512,256]{2,1,0:T(8,128)S(1)} %collective-permute-done.5.v0), channel_id=1, source_target_pairs={{0,32},{32,64},{64,96},{96,0},{1,33},{33,65},{65,97},{97,1},{2,34}... | collective-permute-start | bytes 3145736 | tf_op jit(solution)/shard_map/ppermute | solution.py:20
  104.5 36.7 %collective-permute-start.7 = (f32[2,512,256]{2,1,0:T(8,128)S(1)}, f32[2,512,256]{2,1,0:T(8,128)S(1)}, u32[]{:S(2)}, u32[]{:S(2)}) collective-permute-start(f32[2,512,256]{2,1,0:T(8,128)S(1)} %collective-permute-done.5.v0), channel_id=1, source_target_pairs={{0,96},{32,0},{64,32},{96,64},{1,97},{33,1},{65,33},{97,65},{2,98}... | collective-permute-start | bytes 3145736 | tf_op jit(solution)/shard_map/ppermute | solution.py:20
  105.9 85.5 %collective-permute-start.22 = (f32[8,256,256]{2,1,0:T(8,128)}, f32[8,256,256]{2,1,0:T(8,128)}, u32[]{:S(2)}, u32[]{:S(2)}) collective-permute-start(f32[8,256,256]{2,1,0:T(8,128)} %collective-permute-done.21), channel_id=1, source_target_pairs={{0,16},{16,0},{1,17},{17,1},{2,18},{18,2},{3,19},{19,3},{4,20},{20... | collective-permute-start | bytes 6291464 | tf_op jit(solution)/shard_map/ppermute | solution.py:20
  118.7 34.5 %collective-permute-start.3 = (f32[512,256]{1,0:T(8,128)S(1)}, f32[512,256]{1,0:T(8,128)S(1)}, u32[]{:S(2)}, u32[]{:S(2)}) collective-permute-start(f32[512,256]{1,0:T(8,128)S(1)} %slice_bitcast_fusion.7), channel_id=1, source_target_pairs={{0,32},{32,64},{64,96},{96,0},{1,33},{33,65},{65,97},{97,1},{2,34}... | collective-permute-start | bytes 1572872 | tf_op jit(solution)/shard_map/ppermute | solution.py:20
  128.0 19.1 %collective-permute-start.17 = (f32[256,512]{1,0:T(8,128)S(1)}, f32[256,512]{1,0:T(8,128)}, u32[]{:S(2)}, u32[]{:S(2)}) collective-permute-start(f32[256,512]{1,0:T(8,128)S(1)} %collective-permute-done.15.f2), channel_id=1, source_target_pairs={{0,1},{1,2},{2,3},{3,4},{4,5},{5,6},{6,7},{7,0},{8,9},{9,10},{10,1... | collective-permute-start | bytes 1572872 | tf_op jit(solution)/shard_map/ppermute | solution.py:20
  141.1 11.0 %collective-permute-start.18 = (f32[256,512]{1,0:T(8,128)S(1)}, f32[256,512]{1,0:T(8,128)}, u32[]{:S(2)}, u32[]{:S(2)}) collective-permute-start(f32[256,512]{1,0:T(8,128)S(1)} %collective-permute-done.16.b2), channel_id=1, source_target_pairs={{0,7},{1,0},{2,1},{3,2},{4,3},{5,4},{6,5},{7,6},{8,15},{9,8},{10,9... | collective-permute-start | bytes 1572872 | tf_op jit(solution)/shard_map/ppermute | solution.py:20
  147.1 11.6 %collective-permute-start.4 = (f32[512,256]{1,0:T(8,128)}, f32[512,256]{1,0:T(8,128)}, u32[]{:S(2)}, u32[]{:S(2)}) collective-permute-start(f32[512,256]{1,0:T(8,128)} %slice_bitcast_fusion.6), channel_id=1, source_target_pairs={{0,96},{32,0},{64,32},{96,64},{1,97},{33,1},{65,33},{97,65},{2,98}... | collective-permute-start | bytes 1572872 | tf_op jit(solution)/shard_map/ppermute | solution.py:20
  152.2 12.1 %collective-permute-start.8 = (f32[512,256]{1,0:T(8,128)}, f32[512,256]{1,0:T(8,128)}, u32[]{:S(2)}, u32[]{:S(2)}) collective-permute-start(f32[512,256]{1,0:T(8,128)} %slice_bitcast_fusion.5), channel_id=1, source_target_pairs={{0,32},{32,64},{64,96},{96,0},{1,33},{33,65},{65,97},{97,1},{2,34}... | collective-permute-start | bytes 1572872 | tf_op jit(solution)/shard_map/ppermute | solution.py:20
  154.0 15.9 %collective-permute-start.9 = (f32[512,256]{1,0:T(8,128)}, f32[512,256]{1,0:T(8,128)}, u32[]{:S(2)}, u32[]{:S(2)}) collective-permute-start(f32[512,256]{1,0:T(8,128)} %slice_bitcast_fusion.4), channel_id=1, source_target_pairs={{0,96},{32,0},{64,32},{96,64},{1,97},{33,1},{65,33},{97,65},{2,98}... | collective-permute-start | bytes 1572872 | tf_op jit(solution)/shard_map/ppermute | solution.py:20
  156.7 40.5 %copy-start.24 = (s32[2]{0:T(128)}, s32[2]{0:T(128)S(1)}, u32[]{:S(2)}) copy-start(s32[2]{0:T(128)S(1)} %pad_add_fusion.where) | copy-start | bytes 28
  158.7 37.8 %collective-permute-start.19 = (f32[128,512]{1,0:T(8,128)S(1)}, f32[128,512]{1,0:T(8,128)S(1)}, u32[]{:S(2)}, u32[]{:S(2)}) collective-permute-start(f32[128,512]{1,0:T(8,128)S(1)} %slice.46), channel_id=1, source_target_pairs={{0,1},{1,2},{2,3},{3,4},{4,5},{5,6},{6,7},{7,0},{8,9},{9,10},{10,1... | collective-permute-start | bytes 786440 | tf_op jit(solution)/shard_map/ppermute | solution.py:20
  164.3 32.2 %collective-permute-start.20 = (f32[128,512]{1,0:T(8,128)S(1)}, f32[128,512]{1,0:T(8,128)S(1)}, u32[]{:S(2)}, u32[]{:S(2)}) collective-permute-start(f32[128,512]{1,0:T(8,128)S(1)} %slice.47), channel_id=1, source_target_pairs={{0,7},{1,0},{2,1},{3,2},{4,3},{5,4},{6,5},{7,6},{8,15},{9,8},{10,9... | collective-permute-start | bytes 786440 | tf_op jit(solution)/shard_map/ppermute | solution.py:20
  187.4 30.7 %collective-permute-start.11 = (f32[512,256]{1,0:T(8,128)}, f32[512,256]{1,0:T(8,128)S(1)}, u32[]{:S(2)}, u32[]{:S(2)}) collective-permute-start(f32[512,256]{1,0:T(8,128)} %get-tuple-element.11), channel_id=1, source_target_pairs={{0,16},{16,0},{1,17},{17,1},{2,18},{18,2},{3,19},{19,3},{4,20},{20... | collective-permute-start | bytes 1572872 | tf_op jit(solution)/shard_map/ppermute | solution.py:20
  215.9 13.6 %collective-permute-start.23 = (f32[256,512]{1,0:T(8,128)S(1)}, f32[256,512]{1,0:T(8,128)S(1)}, u32[]{:S(2)}, u32[]{:S(2)}) collective-permute-start(f32[256,512]{1,0:T(8,128)S(1)} %get-tuple-element.7), channel_id=1, source_target_pairs={{0,8},{8,0},{1,9},{9,1},{2,10},{10,2},{3,11},{11,3},{4,12},{12,4},... | collective-permute-start | bytes 1572872 | tf_op jit(solution)/shard_map/ppermute | solution.py:20
  (26 other events, 86.6 us)
Sparse Core Ops, SparseCore 0:
  9.1 83.1 all-gather.2

commit v2 on v0

v2 whole, which is shorter than its diff:
```python
import functools

import jax
import jax.numpy as jnp
from jax import lax
from jax.experimental import pallas as pl
from jax.experimental.pallas import tpu as pltpu
from jax.sharding import Mesh
from jax.sharding import PartitionSpec as P

AXES = ("yhi", "x", "core", "ylo", "z")
SIZES = (2, 4, 2, 2, 8)
ALPHA = ("yhi", "x", "core")
BETA = ("ylo", "z")
BS = 256
SLOTS = 8
MIB = 1 << 20

SMEM = pl.BlockSpec(memory_space=pltpu.SMEM)
HBM = pl.BlockSpec(memory_space=pltpu.HBM)
VMEM = pl.BlockSpec(memory_space=pltpu.VMEM)


def swap(value, axis):
    return lax.ppermute(value, axis, [(0, 1), (1, 0)])


def step(value, axis):
    n = lax.axis_size(axis)
    if axis == "z":
        pairs = [(i, (i + 1) % n) for i in range(n)]
        pairs += [(n + i, n + (i - 1) % n) for i in range(n)]
        return lax.ppermute(value, ("core", axis), pairs)
    pairs = [(2 * i, 2 * ((i + 1) % n)) for i in range(n)]
    pairs += [(2 * i + 1, 2 * ((i - 1) % n) + 1) for i in range(n)]
    return lax.ppermute(value, (axis, "core"), pairs)


def after(value, *earlier):
    return lax.optimization_barrier((value, *earlier))[0]


def dot3(a, b):
    a_hi = a.astype(jnp.bfloat16)
    b_hi = b.astype(jnp.bfloat16)
    a_lo = (a - a_hi.astype(jnp.float32)).astype(jnp.bfloat16)
    b_lo = (b - b_hi.astype(jnp.float32)).astype(jnp.bfloat16)
    dot = functools.partial(jnp.dot, preferred_element_type=jnp.float32)
    return dot(a_hi, b_hi) + (dot(a_hi, b_lo) + dot(a_lo, b_hi))


def each_slot(body):
    for target in range(2):
        for block in range(2):
            lax.fori_loop(
                0, SLOTS, lambda c, _, t=target, b=block: (body(t, b, c), 0)[1], 0
            )


def alpha_kernel(side, where, source, live, *refs):
    arrived, (own, sib), refs = refs[:4], refs[4:6], refs[6:]
    before, refs = (refs[:2], refs[2:]) if side else ((), refs)
    outs, (data, tiles, data_sem, tile_sem, out_sem) = refs[:2], refs[2:]
    me = where[0]

    def copy_of(d):
        return pltpu.make_async_copy(arrived[d], data.at[d], data_sem.at[d])

    def tile_of(target, block, c):
        index = (target * 2 + block) * SLOTS + c
        return pltpu.make_async_copy(
            (own, sib)[target].at[block, c], tiles.at[index], tile_sem.at[index]
        )

    def when_mine(target, block, c, body):
        row = 2 * (me ^ target) + block
        src = source[row, c]
        owner = src >> 1
        mine = (live[row, c] > 0) & (((owner >> 3) ^ (me >> 3)) == side)
        pl.when(mine)(lambda: body(src))

    for d in range(4):
        copy_of(d).start()
    each_slot(
        lambda t, b, c: when_mine(t, b, c, lambda src: tile_of(t, b, c).start())
    )
    for i, out in enumerate(outs):
        if side:
            pltpu.make_async_copy(before[i], out, out_sem.at[i]).start()
        else:
            out[...] = jnp.zeros_like(out)
    for i, out in enumerate(outs):
        if side:
            pltpu.make_async_copy(before[i], out, out_sem.at[i]).wait()
    for d in range(4):
        copy_of(d).wait()

    def product(target, block, c):
        def body(src):
            owner = src >> 1
            ahead = (me >> 1) - (owner >> 1)
            d = jnp.where((me & 1) == 0, ahead, -ahead) & 3
            core = (owner & 1) ^ (me & 1)
            first = pl.multiple_of((src & 1) * BS, BS)
            tile_of(target, block, c).wait()
            rows = data[d, core, pl.ds(first, BS), :]
            tile = tiles[(target * 2 + block) * SLOTS + c]
            outs[target][block * BS : (block + 1) * BS, :] += dot3(tile, rows)

        when_mine(target, block, c, body)

    each_slot(product)


def alpha_call(side, where, source, live, arrived, own, sib, before=()):
    n = own.shape[0] * BS
    return pl.pallas_call(
        functools.partial(alpha_kernel, side),
        out_shape=[jax.ShapeDtypeStruct((n, BS), jnp.float32)] * 2,
        in_specs=[SMEM] * 3 + [HBM] * (6 + len(before)),
        out_specs=[VMEM] * 2,
        scratch_shapes=[
            pltpu.VMEM((4, 2, n, BS), jnp.float32),
            pltpu.VMEM((4 * SLOTS, BS, BS), jnp.float32),
            pltpu.SemaphoreType.DMA((4,)),
            pltpu.SemaphoreType.DMA((4 * SLOTS,)),
            pltpu.SemaphoreType.DMA((2,)),
        ],
        compiler_params=pltpu.CompilerParams(vmem_limit_bytes=20 * MIB),
        cost_estimate=pl.CostEstimate(
            flops=16 * 6 * BS**3, bytes_accessed=8 * MIB, transcendentals=0
        ),
        name=f"alpha{side}",
    )(where, source, live, *arrived, own, sib, *before)


def beta_kernel(steps, done, late, where, source, live, *refs):
    count = steps[0] + steps[1] + 2
    arrived, refs = refs[:count], refs[count:]
    arrived = (arrived[: steps[0] + 1], arrived[steps[0] + 1 :])
    own, refs = refs[0], refs[1:]
    par, refs = refs[: 4 if late else 2], refs[4 if late else 2 :]
    before, refs = (refs[:2], refs[2:]) if done else ((), refs)
    outs, (data, tiles, need, data_sem, tile_sem, out_sem) = refs[:2], refs[2:]
    me, core = where[1], where[0] & 1

    def origin(src):
        owner = src >> 1
        y = (owner >> 3) ^ (me >> 3)
        ahead = me - owner
        return y, jnp.where(core == 0, ahead, -ahead) & 7

    def here(hops, has_late, y, d, target, c):
        if hops is None:
            return False
        ready = jnp.where(y == 0, d <= hops[0], d <= hops[1])
        if target == 1 and not has_late:
            ready = ready & (c < SLOTS // 2)
        return ready

    def when_mine(target, block, c, body):
        row = 2 * (me ^ (8 * target)) + block
        src = source[row, c]
        y, d = origin(src)
        mine = (live[row, c] > 0) & here(steps, late, y, d, target, c)
        if done:
            mine = mine & jnp.logical_not(here(done, False, y, d, target, c))
        pl.when(mine)(lambda: body(src, y, d))

    def copy_of(y, d):
        return pltpu.make_async_copy(arrived[y][d], data.at[y * 8 + d], data_sem.at[y * 8 + d])

    def tile_at(ref, index):
        return pltpu.make_async_copy(ref, tiles.at[index], tile_sem.at[index])

    for i, out in enumerate(outs):
        if done:
            pltpu.make_async_copy(before[i], out, out_sem.at[i]).start()
    for i in range(16):
        need[i] = 0

    def fetch(target, block, c):
        index = (target * 2 + block) * SLOTS + c

        def body(src, y, d):
            need[y * 8 + d] = 1
            if target == 0:
                tile_at(own.at[block, c], index).start()
                return
            for half in range(len(par) // 2):
                for held in range(2):
                    ok = ((core ^ block) == held) & ((c >> 2) == half)

                    @pl.when(ok)
                    def _(half=half, held=held):
                        tile_at(par[2 * half + held].at[c & 3], index).start()

        when_mine(target, block, c, body)

    each_slot(fetch)
    for y in range(2):
        for d in range(steps[y] + 1):
            pl.when(need[y * 8 + d] == 1)(lambda y=y, d=d: copy_of(y, d).start())
    for i, out in enumerate(outs):
        if done:
            pltpu.make_async_copy(before[i], out, out_sem.at[i]).wait()
        else:
            out[...] = jnp.zeros_like(out)

    def product(target, block, c):
        index = (target * 2 + block) * SLOTS + c

        def body(src, y, d):
            place = y * 8 + d

            @pl.when(need[place] == 1)
            def _():
                pltpu.make_async_copy(arrived[0][0], data.at[place], data_sem.at[place]).wait()
                need[place] = 2

            tile_at(own.at[0, 0], index).wait()
            first = pl.multiple_of((src & 1) * BS, BS)
            columns = data[place, :, pl.ds(first, BS)]
            outs[target][:, block * BS : (block + 1) * BS] += dot3(columns, tiles[index])

        when_mine(target, block, c, body)

    each_slot(product)


def beta_call(steps, done, late, where, source, live, chains, own, par, before=()):
    rows, n = chains[0][0].shape
    arrived = chains[0][: steps[0] + 1] + chains[1][: steps[1] + 1]
    return pl.pallas_call(
        functools.partial(beta_kernel, steps, done, late),
        out_shape=[jax.ShapeDtypeStruct((rows, n), jnp.float32)] * 2,
        in_specs=[SMEM] * 3 + [HBM] * (len(arrived) + 1 + len(par) + len(before)),
        out_specs=[VMEM] * 2,
        scratch_shapes=[
            pltpu.VMEM((16, rows, n), jnp.float32),
            pltpu.VMEM((4 * SLOTS, BS, BS), jnp.float32),
            pltpu.SMEM((16,), jnp.int32),
            pltpu.SemaphoreType.DMA((16,)),
            pltpu.SemaphoreType.DMA((4 * SLOTS,)),
            pltpu.SemaphoreType.DMA((2,)),
        ],
        compiler_params=pltpu.CompilerParams(vmem_limit_bytes=24 * MIB),
        cost_estimate=pl.CostEstimate(
            flops=16 * 6 * BS**3, bytes_accessed=8 * MIB, transcendentals=0
        ),
        name=f"beta{len(before) // 2}",
    )(where, source, live, *arrived, own, *par, *before)


def join_kernel(where, x, da, db, alpha, alpha_other, beta, out):
    core = where[0] & 1
    ylo = where[1] >> 3
    out[...] = (da[...] + db[...]) * x[...]
    for side in range(2):

        @pl.when(core == side)
        def _(side=side):
            out[:, side * BS : (side + 1) * BS] += alpha[...]
            out[:, (1 - side) * BS : (2 - side) * BS] += alpha_other[...]

        @pl.when(ylo == side)
        def _(side=side):
            out[side * BS : (side + 1) * BS, :] += beta[...]


def last_kernel(where, joined, beta_other, out, total, part, sems):
    first = pl.multiple_of((1 - (where[1] >> 3)) * BS, BS)
    rows = out.at[pl.ds(first, BS)]
    copies = [
        pltpu.make_async_copy(joined.at[pl.ds(first, BS)], total, sems.at[0]),
        pltpu.make_async_copy(beta_other, part, sems.at[1]),
    ]
    for copy in copies:
        copy.start()
    for copy in copies:
        copy.wait()
    total[...] += part[...]
    back = pltpu.make_async_copy(total, rows, sems.at[2])
    back.start()
    back.wait()


def per_device(
    coeffs,
    diag_alpha,
    diag_beta,
    alpha_tiles,
    beta_tiles,
    alpha_source,
    alpha_live,
    beta_source,
    beta_live,
):
    n = coeffs.shape[0]
    core = lax.axis_index("core")
    ylo = lax.axis_index("ylo")
    where = jnp.stack([lax.axis_index(ALPHA), lax.axis_index(BETA)]).astype(jnp.int32)

    a = [lax.dynamic_slice_in_dim(coeffs, ylo * BS, BS, 0)]
    give = lax.dynamic_slice_in_dim(coeffs, (1 - ylo) * BS, BS, 0)
    b = [swap(give, "ylo")]
    a.append(step(a[0], "z"))
    whole = after(coeffs, a[0], give)
    left = lax.dynamic_slice_in_dim(whole, core * BS, BS, 1)
    right = lax.dynamic_slice_in_dim(whole, (1 - core) * BS, BS, 1)
    u = [jnp.stack([left, swap(right, "core")])]
    v = [swap(u[0], "yhi")]
    sib_tiles = swap(after(alpha_tiles, u[0]), "core")
    mine = lax.dynamic_index_in_dim(beta_tiles, core, 0, keepdims=False)

    u.append(step(u[0], "x"))
    b.append(step(b[0], "z"))
    a.append(step(after(a[1], b[0]), "z"))
    u.append(step(after(u[1], b[0], a[1]), "x"))
    b.append(step(b[1], "z"))
    a.append(step(after(a[2], b[1], u[1], sib_tiles), "z"))
    u.append(step(after(u[2], b[1], a[2]), "x"))
    b.append(step(b[2], "z"))
    a.append(step(after(a[3], b[2], u[2], v[0]), "z"))
    got0 = swap(after(mine[: SLOTS // 2], v[0]), "ylo")
    v.append(step(after(v[0], u[3], b[2], a[3]), "x"))
    b.append(step(b[3], "z"))
    a.append(step(after(a[4], b[3], u[3]), "z"))
    alpha = alpha_call(
        0, where, alpha_source, alpha_live, [after(u[0], a[4]), *u[1:]], alpha_tiles, sib_tiles
    )
    v.append(step(v[1], "x"))
    b.append(step(b[4], "z"))
    a.append(step(after(a[5], b[4], v[1]), "z"))
    oth0 = swap(got0, "core")
    got1 = swap(after(mine[SLOTS // 2 :], got0), "ylo")
    v.append(step(v[2], "x"))
    b.append(step(b[5], "z"))
    a.append(step(after(a[6], b[5], v[2], oth0), "z"))
    own = after(beta_tiles, a[6])
    beta = beta_call(
        (5, 4), None, False, where, beta_source, beta_live, (a, b), own, [got0, oth0]
    )
    oth1 = swap(got1, "core")
    b.append(step(b[6], "z"))
    alpha = alpha_call(
        1, where, alpha_source, alpha_live, [after(v[0], a[7]), *v[1:]], alpha_tiles, sib_tiles, alpha
    )
    alpha_other = swap(alpha[1], "core")
    beta = beta_call(
        (7, 7),
        (5, 4),
        True,
        where,
        beta_source,
        beta_live,
        (a, b),
        own,
        [got0, oth0, got1, oth1],
        beta,
    )
    beta_other = swap(beta[1], "ylo")

    joined = pl.pallas_call(
        join_kernel,
        out_shape=jax.ShapeDtypeStruct((n, n), jnp.float32),
        in_specs=[SMEM] + [VMEM] * 6,
        out_specs=VMEM,
        cost_estimate=pl.CostEstimate(flops=4 * n * n, bytes_accessed=5 * MIB, transcendentals=0),
        name="join",
    )(where, coeffs, diag_alpha[:, None], diag_beta[None, :], alpha[0], alpha_other, beta[0])
    return pl.pallas_call(
        last_kernel,
        out_shape=jax.ShapeDtypeStruct((n, n), jnp.float32),
        in_specs=[SMEM, HBM, HBM],
        out_specs=HBM,
        scratch_shapes=[
            pltpu.VMEM((BS, n), jnp.float32),
            pltpu.VMEM((BS, n), jnp.float32),
            pltpu.SemaphoreType.DMA((3,)),
        ],
        input_output_aliases={1: 0},
        cost_estimate=pl.CostEstimate(flops=n * BS, bytes_accessed=2 * MIB, transcendentals=0),
        name="last",
    )(where, joined, beta_other)


def solution(mesh):
    parts = Mesh(mesh.devices.reshape(SIZES), AXES)
    return jax.shard_map(
        per_device,
        mesh=parts,
        in_specs=(
            P(ALPHA, BETA),
            P(ALPHA),
            P(BETA),
            P(ALPHA, None, None, None),
            P(BETA, None, None, None),
            P(),
            P(),
            P(),
            P(),
        ),
        out_specs=P(ALPHA, BETA),
        check_vma=False,
    )
```

time: 363 us -> 172 us (0.47)
  waiting for transfers between devices: 255 us -> 46.9 us
  starting transfers between devices: 8.58 us -> 63.7 us
  Pallas kernels: 0 us -> 34.7 us
  matrix products: 27.4 us -> 0 us
  local copies, waits for them, and re-layouts: 46.4 us -> 24.6 us
  between operations: 13.5 us -> 0.51 us
  other arithmetic: 12.1 us -> 0.14 us
    all_to_all x1 -> x0, waiting for transfers between devices: 255 us -> none  [per_device(): lax.all_to_all(alpha_out, 'alpha', split_axis=0, concat_axis=0, tiled=True)]
    ppermute x0 -> x30, starting transfers between devices: none -> 63.7 us  [the longest x14 38.2 us: step(): return lax.ppermute(value, ('core', axis), pairs)]
    ppermute x0 -> x30, waiting for transfers between devices: none -> 46.9 us  [the longest x10 26.6 us: swap(): return lax.ppermute(value, axis, [(0, 1), (1, 0)])]
    pallas_call x0 -> x6, Pallas kernels: none -> 34.7 us  [the longest x2 15.5 us: alpha_call(): pl.pallas_call(functools.partial(alpha_kernel, side), out_shape=[jax.Shap...]
    dot_general x2 -> x0, matrix products: 27.4 us -> none  [the longest x1 16.7 us: per_device(): jnp.einsum('ajcb,jcbd->ajd', beta_grouped, beta_masked, precision=lax.Pre...]
    gather x3 -> x0, local copies, waits for them, and re-layouts: 22 us -> none  [the longest x1 10.1 us: per_device(): beta_gathered = jnp.take(whole_blocks, beta_mine, axis=1)]
    reshape x4 -> x0, local copies, waits for them, and re-layouts: 18.9 us -> none  [the longest x1 17.5 us: per_device(): whole.reshape(rows_dev, beta_devices * beta_count, block_size)]
    unnamed x15 -> x74, local copies, waits for them, and re-layouts: 3.48 us -> 19.4 us
  transfers between devices with their start and end apart: 2 -> 30, of which waited for: 1 -> 13; matrix products, arithmetic and copies ran while one was open for 10% -> 2% of each run, Pallas kernels for 0% -> 19%
where the time goes in v2:
time: 172 us; the launch traced here: 171 us
  starting transfers between devices  63.7 us (37%)
  waiting for transfers between devices  46.9 us (27%)
  Pallas kernels  34.7 us (20%)
  local copies, waits for them, and re-layouts  24.6 us (14%)
    ppermute x14, starting transfers between devices, step(): return lax.ppermute(value, ('core', axis), pairs)  38.2 us
    ppermute x10, waiting for transfers between devices, swap(): return lax.ppermute(value, axis, [(0, 1), (1, 0)])  26.6 us
    ppermute x10, starting transfers between devices, swap(): return lax.ppermute(value, axis, [(0, 1), (1, 0)])  19.4 us
    unnamed x74, local copies, waits for them, and re-layouts  19.4 us
    pallas_call x2, Pallas kernels, alpha_call(): pl.pallas_call(functools.partial(alpha_kernel, side), out_shape=[jax.Shap...  15.5 us
    pallas_call x2, Pallas kernels, beta_call(): pl.pallas_call(functools.partial(beta_kernel, steps, done, late), out_sha...  13.4 us
    ppermute x14, waiting for transfers between devices, step(): return lax.ppermute(value, ('core', axis), pairs)  11.6 us
    ppermute x6, waiting for transfers between devices, step(): return lax.ppermute(value, (axis, 'core'), pairs)  8.79 us
  transfers between devices with their start and end apart: 30, of which 13 were waited for; matrix products, arithmetic and copies ran while one was open for 2% of the time, Pallas kernels for 19%

profile of v2, /device:TPU:1, one launch (start us, length us, event | category | flops | bytes accessed | tf_op | source)
XLA Modules:
  0.0 170.6 jit_solution(15679962440980183737)
XLA Ops:
  2.8 3.3 %collective-permute-start = (f32[512,256]{1,0:T(8,128)S(1)}, f32[512,256]{1,0:T(8,128)S(1)}, u32[]{:S(2)}, u32[]{:S(2)}) collective-permute-start(f32[512,256]{1,0:T(8,128)S(1)} %get-tuple-element.56), channel_id=1, source_target_pairs={{0,16},{16,0},{1,17},{17,1},{2,18},{18,2},{3,19},{19,3},{4,20},{20... | collective-permute-start | bytes 1572872 | tf_op jit(solution)/shard_map/ppermute | solution.py:25
  10.2 5.6 %collective-permute-start.2 = (f32[256,512]{1,0:T(8,128)S(1)}, f32[256,512]{1,0:T(8,128)S(1)}, u32[]{:S(2)}, u32[]{:S(2)}) collective-permute-start(f32[256,512]{1,0:T(8,128)S(1)} %get-tuple-element.58.refs_0_), channel_id=1, source_target_pairs={{0,1},{1,2},{2,3},{3,4},{4,5},{5,6},{6,7},{7,0},{16,23},{17,16},{1... | collective-permute-start | bytes 1572872 | tf_op jit(solution)/shard_map/ppermute | solution.py:33
  15.8 7.0 %collective-permute-done.3.refs_6_.refs_8_ = f32[256,512]{1,0:T(8,128)S(1)} collective-permute-done((f32[256,512]{1,0:T(8,128)S(1)}, f32[256,512]{1,0:T(8,128)S(1)}, u32[]{:S(2)}, u32[]{:S(2)}) %collective-permute-start.3) | collective-permute-done | bytes 524320 | tf_op jit(solution)/shard_map/ppermute | solution.py:25
  24.8 5.6 %collective-permute-start.5 = (f32[256,512]{1,0:T(8,128)S(1)}, f32[256,512]{1,0:T(8,128)S(1)}, u32[]{:S(2)}, u32[]{:S(2)}) collective-permute-start(f32[256,512]{1,0:T(8,128)S(1)} %collective-permute-done.3.refs_6_.refs_8_), channel_id=1, source_target_pairs={{0,1},{1,2},{2,3},{3,4},{4,5},{5,6},{6,7},{7,0},{16,23},{17,16},{1... | collective-permute-start | bytes 1572872 | tf_op jit(solution)/shard_map/ppermute | solution.py:33
  31.9 2.9 %collective-permute-start.1 = (f32[2,512,256]{2,1,0:T(8,128)S(1)}, f32[2,512,256]{2,1,0:T(8,128)}, u32[]{:S(2)}, u32[]{:S(2)}) collective-permute-start(f32[2,512,256]{2,1,0:T(8,128)S(1)} %pad_maximum_fusion.refs_0_), channel_id=1, source_target_pairs={{0,128},{128,0},{1,129},{129,1},{2,130},{130,2},{3,131},{131,3},{4... | collective-permute-start | bytes 3145736 | tf_op jit(solution)/shard_map/ppermute | solution.py:25
  36.5 5.6 %collective-permute-done.4.refs_2_ = f32[256,512]{1,0:T(8,128)} collective-permute-done((f32[256,512]{1,0:T(8,128)S(1)}, f32[256,512]{1,0:T(8,128)}, u32[]{:S(2)}, u32[]{:S(2)}) %collective-permute-start.4) | collective-permute-done | bytes 524320 | tf_op jit(solution)/shard_map/ppermute | solution.py:33
  42.1 3.5 %collective-permute-start.9 = (f32[256,512]{1,0:T(8,128)S(1)}, f32[256,512]{1,0:T(8,128)S(1)}, u32[]{:S(2)}, u32[]{:S(2)}) collective-permute-start(f32[256,512]{1,0:T(8,128)S(1)} %collective-permute-done.5.refs_7_.refs_9_), channel_id=1, source_target_pairs={{0,1},{1,2},{2,3},{3,4},{4,5},{5,6},{6,7},{7,0},{16,23},{17,16},{1... | collective-permute-start | bytes 1572872 | tf_op jit(solution)/shard_map/ppermute | solution.py:33
  46.4 2.0 %copy-done.4 = f32[2,8,256,256]{3,2,1,0:T(8,128)} copy-done((f32[2,8,256,256]{3,2,1,0:T(8,128)}, f32[2,8,256,256]{3,2,1,0:T(8,128)S(1)}, u32[]{:S(2)}) %copy-start.4) | copy-done | bytes 4194328
  48.4 3.3 %collective-permute-done.9.refs_8_.refs_10_ = f32[256,512]{1,0:T(8,128)S(1)} collective-permute-done((f32[256,512]{1,0:T(8,128)S(1)}, f32[256,512]{1,0:T(8,128)S(1)}, u32[]{:S(2)}, u32[]{:S(2)}) %collective-permute-start.9) | collective-permute-done | bytes 524320 | tf_op jit(solution)/shard_map/ppermute | solution.py:33
  51.7 3.7 %collective-permute-done.1.refs_0_ = f32[2,512,256]{2,1,0:T(8,128)} collective-permute-done((f32[2,512,256]{2,1,0:T(8,128)S(1)}, f32[2,512,256]{2,1,0:T(8,128)}, u32[]{:S(2)}, u32[]{:S(2)}) %collective-permute-start.1) | collective-permute-done | bytes 1048608 | tf_op jit(solution)/shard_map/ppermute | solution.py:25
  58.2 1.7 dynamic-slice_bitcast_fusion
  61.5 2.2 %collective-permute-start.12 = (f32[256,512]{1,0:T(8,128)S(1)}, f32[256,512]{1,0:T(8,128)S(1)}, u32[]{:S(2)}, u32[]{:S(2)}) collective-permute-start(f32[256,512]{1,0:T(8,128)S(1)} %collective-permute-done.9.refs_8_.refs_10_), channel_id=1, source_target_pairs={{0,1},{1,2},{2,3},{3,4},{4,5},{5,6},{6,7},{7,0},{16,23},{17,16},{1... | collective-permute-start | bytes 1572872 | tf_op jit(solution)/shard_map/ppermute | solution.py:33
  63.7 7.9 %collective-permute-done.16.refs_1_ = f32[2,512,256]{2,1,0:T(8,128)S(1)} collective-permute-done((f32[2,512,256]{2,1,0:T(8,128)}, f32[2,512,256]{2,1,0:T(8,128)S(1)}, u32[]{:S(2)}, u32[]{:S(2)}) %collective-permute-start.16) | collective-permute-done | bytes 1048608 | tf_op jit(solution)/shard_map/ppermute | solution.py:36
  71.6 1.9 %collective-permute-start.19 = (f32[2,512,256]{2,1,0:T(8,128)S(1)}, f32[2,512,256]{2,1,0:T(8,128)}, u32[]{:S(2)}, u32[]{:S(2)}) collective-permute-start(f32[2,512,256]{2,1,0:T(8,128)S(1)} %collective-permute-done.16.refs_1_), channel_id=1, source_target_pairs={{0,32},{32,64},{64,96},{96,0},{16,112},{48,16},{80,48},{112,80},{1... | collective-permute-start | bytes 3145736 | tf_op jit(solution)/shard_map/ppermute | solution.py:36
  74.5 2.3 %collective-permute-start.15 = (f32[256,512]{1,0:T(8,128)S(1)}, f32[256,512]{1,0:T(8,128)S(1)}, u32[]{:S(2)}, u32[]{:S(2)}) collective-permute-start(f32[256,512]{1,0:T(8,128)S(1)} %collective-permute-done.12.refs_9_.refs_11_), channel_id=1, source_target_pairs={{0,1},{1,2},{2,3},{3,4},{4,5},{5,6},{6,7},{7,0},{16,23},{17,16},{1... | collective-permute-start | bytes 1572872 | tf_op jit(solution)/shard_map/ppermute | solution.py:33
  77.6 4.0 %collective-permute-done.20.refs_12_.refs_17_ = f32[4,256,256]{2,1,0:T(8,128)S(1)} collective-permute-done((f32[4,256,256]{2,1,0:T(8,128)S(1)}, f32[4,256,256]{2,1,0:T(8,128)S(1)}, u32[]{:S(2)}, u32[]{:S(2)}) %collective-permute-start.20) | collective-permute-done | bytes 1048608 | tf_op jit(solution)/shard_map/ppermute | solution.py:25
  83.3 3.9 %collective-permute-start.14 = (f32[256,512]{1,0:T(8,128)S(1)}, f32[256,512]{1,0:T(8,128)S(1)}, u32[]{:S(2)}, u32[]{:S(2)}) collective-permute-start(f32[256,512]{1,0:T(8,128)S(1)} %collective-permute-done.11.refs_4_), channel_id=1, source_target_pairs={{0,1},{1,2},{2,3},{3,4},{4,5},{5,6},{6,7},{7,0},{16,23},{17,16},{1... | collective-permute-start | bytes 1572872 | tf_op jit(solution)/shard_map/ppermute | solution.py:33
  88.8 2.9 %collective-permute-start.18 = (f32[256,512]{1,0:T(8,128)S(1)}, f32[256,512]{1,0:T(8,128)}, u32[]{:S(2)}, u32[]{:S(2)}) collective-permute-start(f32[256,512]{1,0:T(8,128)S(1)} %collective-permute-done.15.refs_10_.refs_12_), channel_id=1, source_target_pairs={{0,1},{1,2},{2,3},{3,4},{4,5},{5,6},{6,7},{7,0},{16,23},{17,16},{1... | collective-permute-start | bytes 1572872 | tf_op jit(solution)/shard_map/ppermute | solution.py:33
  93.3 3.1 %collective-permute-start.17 = (f32[256,512]{1,0:T(8,128)S(1)}, f32[256,512]{1,0:T(8,128)}, u32[]{:S(2)}, u32[]{:S(2)}) collective-permute-start(f32[256,512]{1,0:T(8,128)S(1)} %collective-permute-done.14.refs_5_), channel_id=1, source_target_pairs={{0,1},{1,2},{2,3},{3,4},{4,5},{5,6},{6,7},{7,0},{16,23},{17,16},{1... | collective-permute-start | bytes 1572872 | tf_op jit(solution)/shard_map/ppermute | solution.py:33
  97.2 1.7 %collective-permute-start.23 = (f32[2,512,256]{2,1,0:T(8,128)}, f32[2,512,256]{2,1,0:T(8,128)}, u32[]{:S(2)}, u32[]{:S(2)}) collective-permute-start(f32[2,512,256]{2,1,0:T(8,128)} %collective-permute-done.19.refs_2_), channel_id=1, source_target_pairs={{0,32},{32,64},{64,96},{96,0},{16,112},{48,16},{80,48},{112,80},{1... | collective-permute-start | bytes 3145736 | tf_op jit(solution)/shard_map/ppermute | solution.py:36
  98.9 3.2 %collective-permute-start.25 = (f32[256,512]{1,0:T(8,128)}, f32[256,512]{1,0:T(8,128)}, u32[]{:S(2)}, u32[]{:S(2)}) collective-permute-start(f32[256,512]{1,0:T(8,128)} %collective-permute-done.18.refs_13_), channel_id=1, source_target_pairs={{0,1},{1,2},{2,3},{3,4},{4,5},{5,6},{6,7},{7,0},{16,23},{17,16},{1... | collective-permute-start | bytes 1572872 | tf_op jit(solution)/shard_map/ppermute | solution.py:33
  103.5 4.6 %collective-permute-start.28 = (f32[4,256,256]{2,1,0:T(8,128)}, f32[4,256,256]{2,1,0:T(8,128)}, u32[]{:S(2)}, u32[]{:S(2)}) collective-permute-start(f32[4,256,256]{2,1,0:T(8,128)} %collective-permute-done.27.refs_19_), channel_id=1, source_target_pairs={{0,16},{16,0},{1,17},{17,1},{2,18},{18,2},{3,19},{19,3},{4,20},{20... | collective-permute-start | bytes 3145736 | tf_op jit(solution)/shard_map/ppermute | solution.py:25
  108.2 3.7 %collective-permute-start.22 = (f32[256,512]{1,0:T(8,128)}, f32[256,512]{1,0:T(8,128)}, u32[]{:S(2)}, u32[]{:S(2)}) collective-permute-start(f32[256,512]{1,0:T(8,128)} %collective-permute-done.17.refs_6_), channel_id=1, source_target_pairs={{0,1},{1,2},{2,3},{3,4},{4,5},{5,6},{6,7},{7,0},{16,23},{17,16},{1... | collective-permute-start | bytes 1572872 | tf_op jit(solution)/shard_map/ppermute | solution.py:33
  113.7 2.2 %copy-done.2 = f32[2,8,256,256]{3,2,1,0:T(8,128)S(1)} copy-done((f32[2,8,256,256]{3,2,1,0:T(8,128)S(1)}, f32[2,8,256,256]{3,2,1,0:T(8,128)}, u32[]{:S(2)}) %copy-start.2) | copy-done | bytes 4194328
  115.9 2.2 %copy-done.5 = f32[2,8,256,256]{3,2,1,0:T(8,128)S(1)} copy-done((f32[2,8,256,256]{3,2,1,0:T(8,128)S(1)}, f32[2,8,256,256]{3,2,1,0:T(8,128)}, u32[]{:S(2)}) %copy-start.5) | copy-done | bytes 4194328
  120.6 7.2 %alpha0.1 = (f32[512,256]{1,0:T(8,128)S(1)}, f32[512,256]{1,0:T(8,128)S(1)}) custom-call(s32[2]{0:T(128)S(1)} %pad_add_fusion.where, s32[32,8]{1,0:T(8,128)S(1)} %copy.21.source, s32[32,8]{1,0:T(8,128)S(1)} %copy.22.live, f32[2,512,256]{2,1,0:T(8,128)S(1)} %copy-done.7, f32[2,512,256]{2,1,0:T(8,128)S(1)} %copy-done.23, ...), custom_call_target="tpu_custom_call" | custom-call | flops 1610612736 | bytes 8388608 | tf_op jit(solution)/shard_map/alpha0/pallas_call | solution.py:117
  128.0 6.7 %beta0.1 = (f32[256,512]{1,0:T(8,128)S(1)}, f32[256,512]{1,0:T(8,128)S(1)}) custom-call(s32[2]{0:T(128)S(1)} %pad_add_fusion.where, s32[32,8]{1,0:T(8,128)S(1)} %copy.25.source, s32[32,8]{1,0:T(8,128)S(1)} %copy.26.live, f32[256,512]{1,0:T(8,128)S(1)} %get-tuple-element.58.refs_0_, f32[256,512]{1,0:T(8,128)S(1)} %copy-done.9, ...), custom_call_target="tpu_custom_call" | custom-call | flops 1610612736 | bytes 8388608 | tf_op jit(solution)/shard_map/beta0/pallas_call | solution.py:234
  134.7 8.2 %alpha1.1 = (f32[512,256]{1,0:T(8,128)S(1)}, f32[512,256]{1,0:T(8,128)}) custom-call(s32[2]{0:T(128)S(1)} %pad_add_fusion.where, s32[32,8]{1,0:T(8,128)S(1)} %copy.21.source, s32[32,8]{1,0:T(8,128)S(1)} %copy.22.live, f32[2,512,256]{2,1,0:T(8,128)} %collective-permute-done.1.refs_0_, f32[2,512,256]{2,1,0:T(8,128)S(1)} %copy-done.25, ...), custom_call_target="tpu_custom_call" | custom-call | flops 1610612736 | bytes 8388608 | tf_op jit(solution)/shard_map/alpha1/pallas_call | solution.py:117
  145.4 6.7 %beta1.1 = (f32[256,512]{1,0:T(8,128)S(1)}, f32[256,512]{1,0:T(8,128)}) custom-call(s32[2]{0:T(128)S(1)} %pad_add_fusion.where, s32[32,8]{1,0:T(8,128)S(1)} %copy.25.source, s32[32,8]{1,0:T(8,128)S(1)} %copy.26.live, f32[256,512]{1,0:T(8,128)S(1)} %get-tuple-element.58.refs_0_, f32[256,512]{1,0:T(8,128)S(1)} %copy-done.9, ...), custom_call_target="tpu_custom_call" | custom-call | flops 1610612736 | bytes 8388608 | tf_op jit(solution)/shard_map/beta1/pallas_call | solution.py:234
  154.9 3.1 %join.1.joined = f32[512,512]{1,0:T(8,128)} custom-call(s32[2]{0:T(128)} %copy-done.28, f32[512,512]{1,0:T(8,128)} %x.1, f32[512,1]{1,0:T(8,128)} %copy.27.da, f32[1,512]{1,0:T(1,128)} %bitcast.13, f32[512,256]{1,0:T(8,128)} %copy-done.26, f32[512,256]{1,0:T(8,128)} %collective-permute-done.24.alpha_other, f32[256,512]{1,0:T(8,128)} %copy-done.27), custom_call_target="tpu_custom_call" | custom-call | flops 1048576 | bytes 5242880 | tf_op jit(solution)/shard_map/join/pallas_call | solution.py:364
  157.9 8.9 %collective-permute-done.29.beta_other = f32[256,512]{1,0:T(8,128)S(1)} collective-permute-done((f32[256,512]{1,0:T(8,128)}, f32[256,512]{1,0:T(8,128)S(1)}, u32[]{:S(2)}, u32[]{:S(2)}) %collective-permute-start.29) | collective-permute-done | bytes 524320 | tf_op jit(solution)/shard_map/ppermute | solution.py:25
  167.6 2.7 %last.1 = f32[512,512]{1,0:T(8,128)} custom-call(s32[2]{0:T(128)} %copy-done.28, f32[512,512]{1,0:T(8,128)} %join.1.joined, f32[256,512]{1,0:T(8,128)} %copy-done.29), custom_call_target="tpu_custom_call", output_to_operand_aliasing={{}: (1, {})} | custom-call | flops 131072 | bytes 2097152 | tf_op jit(solution)/shard_map/last/pallas_call | solution.py:372
  (114 shorter events, 36.4 us)
Async XLA Ops:
  1.3 110.7 %copy-start.32 = (s32[32,8]{0,1:T(8,128)S(1)}, s32[32,8]{0,1:T(8,128)}, u32[]{:S(2)}) copy-start(s32[32,8]{0,1:T(8,128)} %param.16) | copy-start | bytes 3076
  1.3 110.8 %copy-start.33 = (s32[32,8]{0,1:T(8,128)S(1)}, s32[32,8]{0,1:T(8,128)}, u32[]{:S(2)}) copy-start(s32[32,8]{0,1:T(8,128)} %param.17) | copy-start | bytes 3076
  2.8 4.9 %collective-permute-start = (f32[512,256]{1,0:T(8,128)S(1)}, f32[512,256]{1,0:T(8,128)S(1)}, u32[]{:S(2)}, u32[]{:S(2)}) collective-permute-start(f32[512,256]{1,0:T(8,128)S(1)} %get-tuple-element.56), channel_id=1, source_target_pairs={{0,16},{16,0},{1,17},{17,1},{2,18},{18,2},{3,19},{19,3},{4,20},{20... | collective-permute-start | bytes 1572872 | tf_op jit(solution)/shard_map/ppermute | solution.py:25
  7.7 38.7 %collective-permute-start.7 = (f32[2,8,256,256]{3,2,1,0:T(8,128)S(1)}, f32[2,8,256,256]{3,2,1,0:T(8,128)S(1)}, u32[]{:S(2)}, u32[]{:S(2)}) collective-permute-start(f32[2,8,256,256]{3,2,1,0:T(8,128)S(1)} %copy-done.1), channel_id=1, source_target_pairs={{0,16},{16,0},{1,17},{17,1},{2,18},{18,2},{3,19},{19,3},{4,20},{20... | collective-permute-start | bytes 12582920 | tf_op jit(solution)/shard_map/ppermute | solution.py:25
  8.2 14.6 %collective-permute-start.6 = (f32[2,512,256]{2,1,0:T(8,128)S(1)}, f32[2,512,256]{2,1,0:T(8,128)S(1)}, u32[]{:S(2)}, u32[]{:S(2)}) collective-permute-start(f32[2,512,256]{2,1,0:T(8,128)S(1)} %pad_maximum_fusion.refs_0_), channel_id=1, source_target_pairs={{0,32},{32,64},{64,96},{96,0},{16,112},{48,16},{80,48},{112,80},{1... | collective-permute-start | bytes 3145736 | tf_op jit(solution)/shard_map/ppermute | solution.py:36
  8.9 13.9 %collective-permute-start.3 = (f32[256,512]{1,0:T(8,128)S(1)}, f32[256,512]{1,0:T(8,128)S(1)}, u32[]{:S(2)}, u32[]{:S(2)}) collective-permute-start(f32[256,512]{1,0:T(8,128)S(1)} %get-tuple-element.57), channel_id=1, source_target_pairs={{0,8},{8,0},{1,9},{9,1},{2,10},{10,2},{3,11},{11,3},{4,12},{12,4},... | collective-permute-start | bytes 1572872 | tf_op jit(solution)/shard_map/ppermute | solution.py:25
  10.2 12.6 %collective-permute-start.2 = (f32[256,512]{1,0:T(8,128)S(1)}, f32[256,512]{1,0:T(8,128)S(1)}, u32[]{:S(2)}, u32[]{:S(2)}) collective-permute-start(f32[256,512]{1,0:T(8,128)S(1)} %get-tuple-element.58.refs_0_), channel_id=1, source_target_pairs={{0,1},{1,2},{2,3},{3,4},{4,5},{5,6},{6,7},{7,0},{16,23},{17,16},{1... | collective-permute-start | bytes 1572872 | tf_op jit(solution)/shard_map/ppermute | solution.py:33
  22.8 19.3 %collective-permute-start.10 = (f32[2,512,256]{2,1,0:T(8,128)S(1)}, f32[2,512,256]{2,1,0:T(8,128)}, u32[]{:S(2)}, u32[]{:S(2)}) collective-permute-start(f32[2,512,256]{2,1,0:T(8,128)S(1)} %collective-permute-done.6.refs_1_), channel_id=1, source_target_pairs={{0,32},{32,64},{64,96},{96,0},{16,112},{48,16},{80,48},{112,80},{1... | collective-permute-start | bytes 3145736 | tf_op jit(solution)/shard_map/ppermute | solution.py:36
  24.8 11.7 %collective-permute-start.5 = (f32[256,512]{1,0:T(8,128)S(1)}, f32[256,512]{1,0:T(8,128)S(1)}, u32[]{:S(2)}, u32[]{:S(2)}) collective-permute-start(f32[256,512]{1,0:T(8,128)S(1)} %collective-permute-done.3.refs_6_.refs_8_), channel_id=1, source_target_pairs={{0,1},{1,2},{2,3},{3,4},{4,5},{5,6},{6,7},{7,0},{16,23},{17,16},{1... | collective-permute-start | bytes 1572872 | tf_op jit(solution)/shard_map/ppermute | solution.py:33
  30.3 11.7 %collective-permute-start.4 = (f32[256,512]{1,0:T(8,128)S(1)}, f32[256,512]{1,0:T(8,128)}, u32[]{:S(2)}, u32[]{:S(2)}) collective-permute-start(f32[256,512]{1,0:T(8,128)S(1)} %collective-permute-done.2.refs_1_), channel_id=1, source_target_pairs={{0,1},{1,2},{2,3},{3,4},{4,5},{5,6},{6,7},{7,0},{16,23},{17,16},{1... | collective-permute-start | bytes 1572872 | tf_op jit(solution)/shard_map/ppermute | solution.py:33
  31.9 23.6 %collective-permute-start.1 = (f32[2,512,256]{2,1,0:T(8,128)S(1)}, f32[2,512,256]{2,1,0:T(8,128)}, u32[]{:S(2)}, u32[]{:S(2)}) collective-permute-start(f32[2,512,256]{2,1,0:T(8,128)S(1)} %pad_maximum_fusion.refs_0_), channel_id=1, source_target_pairs={{0,128},{128,0},{1,129},{129,1},{2,130},{130,2},{3,131},{131,3},{4... | collective-permute-start | bytes 3145736 | tf_op jit(solution)/shard_map/ppermute | solution.py:25
  42.1 14.3 %collective-permute-start.13 = (f32[2,512,256]{2,1,0:T(8,128)}, f32[2,512,256]{2,1,0:T(8,128)}, u32[]{:S(2)}, u32[]{:S(2)}) collective-permute-start(f32[2,512,256]{2,1,0:T(8,128)} %collective-permute-done.10.refs_2_), channel_id=1, source_target_pairs={{0,32},{32,64},{64,96},{96,0},{16,112},{48,16},{80,48},{112,80},{1... | collective-permute-start | bytes 3145736 | tf_op jit(solution)/shard_map/ppermute | solution.py:36
  42.1 9.6 %collective-permute-start.9 = (f32[256,512]{1,0:T(8,128)S(1)}, f32[256,512]{1,0:T(8,128)S(1)}, u32[]{:S(2)}, u32[]{:S(2)}) collective-permute-start(f32[256,512]{1,0:T(8,128)S(1)} %collective-permute-done.5.refs_7_.refs_9_), channel_id=1, source_target_pairs={{0,1},{1,2},{2,3},{3,4},{4,5},{5,6},{6,7},{7,0},{16,23},{17,16},{1... | collective-permute-start | bytes 1572872 | tf_op jit(solution)/shard_map/ppermute | solution.py:33
  48.4 9.1 %collective-permute-start.8 = (f32[256,512]{1,0:T(8,128)}, f32[256,512]{1,0:T(8,128)}, u32[]{:S(2)}, u32[]{:S(2)}) collective-permute-start(f32[256,512]{1,0:T(8,128)} %collective-permute-done.4.refs_2_), channel_id=1, source_target_pairs={{0,1},{1,2},{2,3},{3,4},{4,5},{5,6},{6,7},{7,0},{16,23},{17,16},{1... | collective-permute-start | bytes 1572872 | tf_op jit(solution)/shard_map/ppermute | solution.py:33
  57.5 14.2 %collective-permute-start.16 = (f32[2,512,256]{2,1,0:T(8,128)}, f32[2,512,256]{2,1,0:T(8,128)S(1)}, u32[]{:S(2)}, u32[]{:S(2)}) collective-permute-start(f32[2,512,256]{2,1,0:T(8,128)} %collective-permute-done.1.refs_0_), channel_id=1, source_target_pairs={{0,32},{32,64},{64,96},{96,0},{16,112},{48,16},{80,48},{112,80},{1... | collective-permute-start | bytes 3145736 | tf_op jit(solution)/shard_map/ppermute | solution.py:36
  59.9 21.8 %collective-permute-start.20 = (f32[4,256,256]{2,1,0:T(8,128)S(1)}, f32[4,256,256]{2,1,0:T(8,128)S(1)}, u32[]{:S(2)}, u32[]{:S(2)}) collective-permute-start(f32[4,256,256]{2,1,0:T(8,128)S(1)} %get-tuple-element.39), channel_id=1, source_target_pairs={{0,8},{8,0},{1,9},{9,1},{2,10},{10,2},{3,11},{11,3},{4,12},{12,4},... | collective-permute-start | bytes 3145736 | tf_op jit(solution)/shard_map/ppermute | solution.py:25
  61.5 13.0 %collective-permute-start.12 = (f32[256,512]{1,0:T(8,128)S(1)}, f32[256,512]{1,0:T(8,128)S(1)}, u32[]{:S(2)}, u32[]{:S(2)}) collective-permute-start(f32[256,512]{1,0:T(8,128)S(1)} %collective-permute-done.9.refs_8_.refs_10_), channel_id=1, source_target_pairs={{0,1},{1,2},{2,3},{3,4},{4,5},{5,6},{6,7},{7,0},{16,23},{17,16},{1... | collective-permute-start | bytes 1572872 | tf_op jit(solution)/shard_map/ppermute | solution.py:33
  63.7 19.6 %collective-permute-start.11 = (f32[256,512]{1,0:T(8,128)}, f32[256,512]{1,0:T(8,128)S(1)}, u32[]{:S(2)}, u32[]{:S(2)}) collective-permute-start(f32[256,512]{1,0:T(8,128)} %collective-permute-done.8.refs_3_), channel_id=1, source_target_pairs={{0,1},{1,2},{2,3},{3,4},{4,5},{5,6},{6,7},{7,0},{16,23},{17,16},{1... | collective-permute-start | bytes 1572872 | tf_op jit(solution)/shard_map/ppermute | solution.py:33
  71.6 25.6 %collective-permute-start.19 = (f32[2,512,256]{2,1,0:T(8,128)S(1)}, f32[2,512,256]{2,1,0:T(8,128)}, u32[]{:S(2)}, u32[]{:S(2)}) collective-permute-start(f32[2,512,256]{2,1,0:T(8,128)S(1)} %collective-permute-done.16.refs_1_), channel_id=1, source_target_pairs={{0,32},{32,64},{64,96},{96,0},{16,112},{48,16},{80,48},{112,80},{1... | collective-permute-start | bytes 3145736 | tf_op jit(solution)/shard_map/ppermute | solution.py:36
  74.5 14.3 %collective-permute-start.15 = (f32[256,512]{1,0:T(8,128)S(1)}, f32[256,512]{1,0:T(8,128)S(1)}, u32[]{:S(2)}, u32[]{:S(2)}) collective-permute-start(f32[256,512]{1,0:T(8,128)S(1)} %collective-permute-done.12.refs_9_.refs_11_), channel_id=1, source_target_pairs={{0,1},{1,2},{2,3},{3,4},{4,5},{5,6},{6,7},{7,0},{16,23},{17,16},{1... | collective-permute-start | bytes 1572872 | tf_op jit(solution)/shard_map/ppermute | solution.py:33
  81.7 21.9 %collective-permute-start.27 = (f32[4,256,256]{2,1,0:T(8,128)S(1)}, f32[4,256,256]{2,1,0:T(8,128)}, u32[]{:S(2)}, u32[]{:S(2)}) collective-permute-start(f32[4,256,256]{2,1,0:T(8,128)S(1)} %get-tuple-element.48), channel_id=1, source_target_pairs={{0,8},{8,0},{1,9},{9,1},{2,10},{10,2},{3,11},{11,3},{4,12},{12,4},... | collective-permute-start | bytes 3145736 | tf_op jit(solution)/shard_map/ppermute | solution.py:25
  83.3 10.0 %collective-permute-start.14 = (f32[256,512]{1,0:T(8,128)S(1)}, f32[256,512]{1,0:T(8,128)S(1)}, u32[]{:S(2)}, u32[]{:S(2)}) collective-permute-start(f32[256,512]{1,0:T(8,128)S(1)} %collective-permute-done.11.refs_4_), channel_id=1, source_target_pairs={{0,1},{1,2},{2,3},{3,4},{4,5},{5,6},{6,7},{7,0},{16,23},{17,16},{1... | collective-permute-start | bytes 1572872 | tf_op jit(solution)/shard_map/ppermute | solution.py:33
  87.9 20.2 %collective-permute-start.21 = (f32[4,256,256]{2,1,0:T(8,128)S(1)}, f32[4,256,256]{2,1,0:T(8,128)S(1)}, u32[]{:S(2)}, u32[]{:S(2)}) collective-permute-start(f32[4,256,256]{2,1,0:T(8,128)S(1)} %collective-permute-done.20.refs_12_.refs_17_), channel_id=1, source_target_pairs={{0,16},{16,0},{1,17},{17,1},{2,18},{18,2},{3,19},{19,3},{4,20},{20... | collective-permute-start | bytes 3145736 | tf_op jit(solution)/shard_map/ppermute | solution.py:25
  88.8 10.1 %collective-permute-start.18 = (f32[256,512]{1,0:T(8,128)S(1)}, f32[256,512]{1,0:T(8,128)}, u32[]{:S(2)}, u32[]{:S(2)}) collective-permute-start(f32[256,512]{1,0:T(8,128)S(1)} %collective-permute-done.15.refs_10_.refs_12_), channel_id=1, source_target_pairs={{0,1},{1,2},{2,3},{3,4},{4,5},{5,6},{6,7},{7,0},{16,23},{17,16},{1... | collective-permute-start | bytes 1572872 | tf_op jit(solution)/shard_map/ppermute | solution.py:33
  93.3 14.9 %collective-permute-start.17 = (f32[256,512]{1,0:T(8,128)S(1)}, f32[256,512]{1,0:T(8,128)}, u32[]{:S(2)}, u32[]{:S(2)}) collective-permute-start(f32[256,512]{1,0:T(8,128)S(1)} %collective-permute-done.14.refs_5_), channel_id=1, source_target_pairs={{0,1},{1,2},{2,3},{3,4},{4,5},{5,6},{6,7},{7,0},{16,23},{17,16},{1... | collective-permute-start | bytes 1572872 | tf_op jit(solution)/shard_map/ppermute | solution.py:33
  97.2 37.5 %collective-permute-start.23 = (f32[2,512,256]{2,1,0:T(8,128)}, f32[2,512,256]{2,1,0:T(8,128)}, u32[]{:S(2)}, u32[]{:S(2)}) collective-permute-start(f32[2,512,256]{2,1,0:T(8,128)} %collective-permute-done.19.refs_2_), channel_id=1, source_target_pairs={{0,32},{32,64},{64,96},{96,0},{16,112},{48,16},{80,48},{112,80},{1... | collective-permute-start | bytes 3145736 | tf_op jit(solution)/shard_map/ppermute | solution.py:36
  98.9 13.2 %collective-permute-start.25 = (f32[256,512]{1,0:T(8,128)}, f32[256,512]{1,0:T(8,128)}, u32[]{:S(2)}, u32[]{:S(2)}) collective-permute-start(f32[256,512]{1,0:T(8,128)} %collective-permute-done.18.refs_13_), channel_id=1, source_target_pairs={{0,1},{1,2},{2,3},{3,4},{4,5},{5,6},{6,7},{7,0},{16,23},{17,16},{1... | collective-permute-start | bytes 1572872 | tf_op jit(solution)/shard_map/ppermute | solution.py:33
  103.5 41.9 %collective-permute-start.28 = (f32[4,256,256]{2,1,0:T(8,128)}, f32[4,256,256]{2,1,0:T(8,128)}, u32[]{:S(2)}, u32[]{:S(2)}) collective-permute-start(f32[4,256,256]{2,1,0:T(8,128)} %collective-permute-done.27.refs_19_), channel_id=1, source_target_pairs={{0,16},{16,0},{1,17},{17,1},{2,18},{18,2},{3,19},{19,3},{4,20},{20... | collective-permute-start | bytes 3145736 | tf_op jit(solution)/shard_map/ppermute | solution.py:25
  108.2 26.5 %collective-permute-start.22 = (f32[256,512]{1,0:T(8,128)}, f32[256,512]{1,0:T(8,128)}, u32[]{:S(2)}, u32[]{:S(2)}) collective-permute-start(f32[256,512]{1,0:T(8,128)} %collective-permute-done.17.refs_6_), channel_id=1, source_target_pairs={{0,1},{1,2},{2,3},{3,4},{4,5},{5,6},{6,7},{7,0},{16,23},{17,16},{1... | collective-permute-start | bytes 1572872 | tf_op jit(solution)/shard_map/ppermute | solution.py:33
  112.2 33.2 %collective-permute-start.26 = (f32[256,512]{1,0:T(8,128)}, f32[256,512]{1,0:T(8,128)S(1)}, u32[]{:S(2)}, u32[]{:S(2)}) collective-permute-start(f32[256,512]{1,0:T(8,128)} %collective-permute-done.25.refs_14_), channel_id=1, source_target_pairs={{0,1},{1,2},{2,3},{3,4},{4,5},{5,6},{6,7},{7,0},{16,23},{17,16},{1... | collective-permute-start | bytes 1572872 | tf_op jit(solution)/shard_map/ppermute | solution.py:33
  143.8 11.1 %collective-permute-start.24 = (f32[512,256]{1,0:T(8,128)}, f32[512,256]{1,0:T(8,128)}, u32[]{:S(2)}, u32[]{:S(2)}) collective-permute-start(f32[512,256]{1,0:T(8,128)} %get-tuple-element.46), channel_id=1, source_target_pairs={{0,16},{16,0},{1,17},{17,1},{2,18},{18,2},{3,19},{19,3},{4,20},{20... | collective-permute-start | bytes 1572872 | tf_op jit(solution)/shard_map/ppermute | solution.py:25
  153.0 13.9 %collective-permute-start.29 = (f32[256,512]{1,0:T(8,128)}, f32[256,512]{1,0:T(8,128)S(1)}, u32[]{:S(2)}, u32[]{:S(2)}) collective-permute-start(f32[256,512]{1,0:T(8,128)} %get-tuple-element.52), channel_id=1, source_target_pairs={{0,8},{8,0},{1,9},{9,1},{2,10},{10,2},{3,11},{11,3},{4,12},{12,4},... | collective-permute-start | bytes 1572872 | tf_op jit(solution)/shard_map/ppermute | solution.py:25
  (33 other events, 383.8 us)

commit v3 on v0

v3 whole, which is shorter than its diff:
```python
import functools

import jax
import jax.numpy as jnp
from jax import lax
from jax.experimental import pallas as pl
from jax.experimental.pallas import tpu as pltpu
from jax.sharding import Mesh
from jax.sharding import PartitionSpec as P

AXES = ("yhi", "x", "core", "ylo", "z")
SIZES = (2, 4, 2, 2, 8)
ALPHA = ("yhi", "x", "core")
BETA = ("ylo", "z")
BS = 256
SLOTS = 8
MIB = 1 << 20

SMEM = pl.BlockSpec(memory_space=pltpu.SMEM)
HBM = pl.BlockSpec(memory_space=pltpu.HBM)
ANY = pl.BlockSpec(memory_space=pl.ANY)
VMEM = pl.BlockSpec(memory_space=pltpu.VMEM)


def swap(value, axis):
    return lax.ppermute(value, axis, [(0, 1), (1, 0)])


def step(value, axis):
    n = lax.axis_size(axis)
    if axis == "z":
        pairs = [(i, (i + 1) % n) for i in range(n)]
        pairs += [(n + i, n + (i - 1) % n) for i in range(n)]
        return lax.ppermute(value, ("core", axis), pairs)
    pairs = [(2 * i, 2 * ((i + 1) % n)) for i in range(n)]
    pairs += [(2 * i + 1, 2 * ((i - 1) % n) + 1) for i in range(n)]
    return lax.ppermute(value, (axis, "core"), pairs)


def in_hbm(*values):
    return [pltpu.with_memory_space_constraint(value, pltpu.HBM) for value in values]


def after(value, *earlier):
    return lax.optimization_barrier((value, *earlier))[0]


def dot3(a, b):
    a_hi = a.astype(jnp.bfloat16)
    b_hi = b.astype(jnp.bfloat16)
    a_lo = (a - a_hi.astype(jnp.float32)).astype(jnp.bfloat16)
    b_lo = (b - b_hi.astype(jnp.float32)).astype(jnp.bfloat16)
    dot = functools.partial(jnp.dot, preferred_element_type=jnp.float32)
    return dot(a_hi, b_hi) + (dot(a_hi, b_lo) + dot(a_lo, b_hi))


HOPS = ((5, 4), (7, 7))


def plan_kernel(where, alpha_source, alpha_live, beta_source, beta_live, alpha_plan, beta_plan):
    me, mb = where[0], where[1]
    up = (me & 1) == 0
    for row in range(2):
        alpha_plan[row, 0] = 0
    for row in range(4):
        beta_plan[row, 0] = 0

    def put(plan, row, word):
        count = plan[row, 0] + 1
        plan[row, 0] = count
        plan[row, count] = word

    def alpha(slot, _):
        row, c = 2 * me + (slot >> 3), slot & 7

        @pl.when(alpha_live[row, c] > 0)
        def _():
            src = alpha_source[row, c]
            owner = src >> 1
            ahead = (me >> 1) - (owner >> 1)
            hops = jnp.where((owner & 1) == 0, ahead, -ahead) & 3
            piece = 2 * hops + ((owner ^ me) & 1)
            put(alpha_plan, (owner >> 3) ^ (me >> 3), piece * 64 + (src & 1) * 32 + slot)

        return 0

    def beta(target, slot, _):
        row, c = 2 * (mb ^ (8 * target)) + (slot >> 3), slot & 7

        @pl.when(beta_live[row, c] > 0)
        def _():
            src = beta_source[row, c]
            owner = src >> 1
            y = (owner >> 3) ^ (mb >> 3)
            ahead = mb - owner
            d = jnp.where(up, ahead, -ahead) & 7
            early = d <= jnp.where(y == 0, HOPS[0][0], HOPS[0][1])
            if target:
                early = early & (c < SLOTS // 2)
            call = jnp.where(early, 0, 1)
            put(beta_plan, 2 * call + target, (y * 8 + d) * 64 + (src & 1) * 32 + slot)

        return 0

    lax.fori_loop(0, 2 * SLOTS, alpha, 0)
    for target in range(2):
        lax.fori_loop(0, 2 * SLOTS, functools.partial(beta, target), 0)


def start_one_of(pieces, piece, make):
    for i, ref in enumerate(pieces):
        pl.when(piece == i)(lambda ref=ref: make(ref).start())


def alpha_kernel(side, plan, *refs):
    pieces, own, refs = refs[:8], refs[8], refs[9:]
    before, refs = (refs[:1], refs[1:]) if side else ((), refs)
    out, data, tiles, data_sem, tile_sem, out_sem = refs
    count = plan[side, 0]
    if side:
        first = pltpu.make_async_copy(before[0], out, out_sem)
        first.start()

    def tile_of(k, slot):
        return pltpu.make_async_copy(own.at[slot >> 3, slot & 7], tiles.at[k], tile_sem.at[k])

    def rows_of(k, ref, block):
        first = pl.multiple_of(block * BS, BS)
        return pltpu.make_async_copy(ref.at[pl.ds(first, BS)], data.at[k], data_sem.at[k])

    def fetch(k, _):
        word = plan[side, k + 1]
        tile_of(k, word & 31).start()
        start_one_of(pieces, word >> 6, lambda ref: rows_of(k, ref, (word >> 5) & 1))
        return 0

    lax.fori_loop(0, count, fetch, 0)
    if side:
        first.wait()
    else:
        out[...] = jnp.zeros_like(out)

    def product(k, _):
        slot = plan[side, k + 1] & 31
        tile_of(k, slot).wait()
        rows_of(k, pieces[0], 0).wait()
        rows = pl.multiple_of((slot >> 3) * BS, BS)
        out[pl.ds(rows, BS), :] += dot3(tiles[k], data[k])
        return 0

    lax.fori_loop(0, count, product, 0)


def alpha_call(side, plan, pieces, own, before=()):
    n = own.shape[0] * BS
    return pl.pallas_call(
        functools.partial(alpha_kernel, side),
        out_shape=jax.ShapeDtypeStruct((n, n), jnp.float32),
        in_specs=[SMEM] + [HBM] * 9 + [ANY] * len(before),
        out_specs=VMEM,
        scratch_shapes=[
            pltpu.VMEM((SLOTS, BS, n), jnp.float32),
            pltpu.VMEM((SLOTS, BS, BS), jnp.float32),
            pltpu.SemaphoreType.DMA((SLOTS,)),
            pltpu.SemaphoreType.DMA((SLOTS,)),
            pltpu.SemaphoreType.DMA,
        ],
        compiler_params=pltpu.CompilerParams(vmem_limit_bytes=16 * MIB),
        cost_estimate=pl.CostEstimate(
            flops=8 * 12 * BS**3, bytes_accessed=8 * MIB, transcendentals=0
        ),
        name=f"alpha{side}",
    )(plan, *in_hbm(*pieces, own), *before)


def beta_kernel(call, targets, where, plan, *refs):
    hops = HOPS[call]
    numbers = [d for d in range(hops[0] + 1)] + [8 + d for d in range(hops[1] + 1)]
    pieces, refs = dict(zip(numbers, refs)), refs[len(numbers) :]
    own, refs = refs[0], refs[1:]
    par, refs = refs[: 2 * call + 2], refs[2 * call + 2 :]
    before, refs = (refs[: len(targets)], refs[len(targets) :]) if call else ((), refs)
    outs, (data, tiles, data_sem, tile_sem, out_sem) = refs[: len(targets)], refs[len(targets) :]
    core = where[0] & 1
    firsts = [
        pltpu.make_async_copy(b, out, out_sem.at[i]) for i, (b, out) in enumerate(zip(before, outs))
    ]
    for first in firsts:
        first.start()

    def columns_of(k, ref, block):
        first = pl.multiple_of(block * BS, BS)
        return pltpu.make_async_copy(ref.at[:, pl.ds(first, BS)], data.at[k], data_sem.at[k])

    def tile_from(k, ref):
        return pltpu.make_async_copy(ref, tiles.at[k], tile_sem.at[k])

    base = 0
    for target in targets:
        row = 2 * call + target

        def fetch(j, _, target=target, row=row, base=base):
            word = plan[row, j + 1]
            k = base + j
            slot = word & 31
            for number, ref in pieces.items():
                pl.when((word >> 6) == number)(
                    lambda ref=ref: columns_of(k, ref, (word >> 5) & 1).start()
                )
            if target == 0:
                tile_from(k, own.at[slot >> 3, slot & 7]).start()
            else:
                which = (core ^ (slot >> 3)) + 2 * ((slot >> 2) & 1)
                start_one_of(par, which, lambda ref: tile_from(k, ref.at[slot & 3]))
            return 0

        lax.fori_loop(0, plan[row, 0], fetch, 0)
        base = base + plan[row, 0]
    for out in outs:
        if not call:
            out[...] = jnp.zeros_like(out)
    for first in firsts:
        first.wait()
    base = 0
    for target, out in zip(targets, outs):
        row = 2 * call + target

        def product(j, _, out=out, row=row, base=base):
            k = base + j
            slot = plan[row, j + 1] & 31
            columns_of(k, pieces[0], 0).wait()
            tile_from(k, own.at[0, 0]).wait()
            columns = pl.multiple_of((slot >> 3) * BS, BS)
            out[:, pl.ds(columns, BS)] += dot3(data[k], tiles[k])
            return 0

        lax.fori_loop(0, plan[row, 0], product, 0)
        base = base + plan[row, 0]


def beta_call(call, targets, where, plan, chains, own, par, before=()):
    rows, n = chains[0][0].shape
    pieces = chains[0][: HOPS[call][0] + 1] + chains[1][: HOPS[call][1] + 1]
    most = 2 * SLOTS * len(targets)
    return pl.pallas_call(
        functools.partial(beta_kernel, call, targets),
        out_shape=[jax.ShapeDtypeStruct((rows, n), jnp.float32)] * len(targets),
        in_specs=[SMEM] * 2 + [HBM] * (len(pieces) + 1 + len(par)) + [ANY] * len(before),
        out_specs=[VMEM] * len(targets),
        scratch_shapes=[
            pltpu.VMEM((most, rows, BS), jnp.float32),
            pltpu.VMEM((most, BS, BS), jnp.float32),
            pltpu.SemaphoreType.DMA((most,)),
            pltpu.SemaphoreType.DMA((most,)),
            pltpu.SemaphoreType.DMA((2,)),
        ],
        compiler_params=pltpu.CompilerParams(vmem_limit_bytes=24 * MIB),
        cost_estimate=pl.CostEstimate(
            flops=8 * 6 * BS**3 * len(targets), bytes_accessed=6 * MIB, transcendentals=0
        ),
        name=f"beta{call}{len(targets)}",
    )(where, plan, *in_hbm(*pieces, own, *par), *before)


def join_kernel(where, x, da, db, alpha, beta, out):
    ylo = where[1] >> 3
    out[...] = (da[...] + db[...]) * x[...] + alpha[...]
    rows = pl.ds(pl.multiple_of(ylo * BS, BS), BS)
    out[rows, :] += beta[...]


def last_kernel(where, joined, beta_other, out, total, part, sems):
    first = pl.multiple_of((1 - (where[1] >> 3)) * BS, BS)
    rows = out.at[pl.ds(first, BS)]
    copies = [
        pltpu.make_async_copy(joined.at[pl.ds(first, BS)], total, sems.at[0]),
        pltpu.make_async_copy(beta_other, part, sems.at[1]),
    ]
    for copy in copies:
        copy.start()
    for copy in copies:
        copy.wait()
    total[...] += part[...]
    back = pltpu.make_async_copy(total, rows, sems.at[2])
    back.start()
    back.wait()


def per_device(
    coeffs,
    diag_alpha,
    diag_beta,
    alpha_tiles,
    beta_tiles,
    alpha_source,
    alpha_live,
    beta_source,
    beta_live,
):
    n = coeffs.shape[0]
    core = lax.axis_index("core")
    ylo = lax.axis_index("ylo")
    where = jnp.stack([lax.axis_index(ALPHA), lax.axis_index(BETA)]).astype(jnp.int32)
    alpha_plan, beta_plan = pl.pallas_call(
        plan_kernel,
        out_shape=[
            jax.ShapeDtypeStruct((2, 16), jnp.int32),
            jax.ShapeDtypeStruct((4, 32), jnp.int32),
        ],
        in_specs=[SMEM] * 5,
        out_specs=[SMEM] * 2,
        name="plan",
    )(where, alpha_source, alpha_live, beta_source, beta_live)

    a = [lax.dynamic_slice_in_dim(coeffs, ylo * BS, BS, 0)]
    give = lax.dynamic_slice_in_dim(coeffs, (1 - ylo) * BS, BS, 0)
    b = [swap(give, "ylo")]
    a.append(step(a[0], "z"))
    u = [coeffs, step(coeffs, "x")]
    v = [swap(after(coeffs, b[0]), "yhi")]
    us = [swap(coeffs, "core")]
    mine = lax.dynamic_index_in_dim(beta_tiles, core, 0, keepdims=False)

    b.append(step(b[0], "z"))
    a.append(step(after(a[1], b[0], us[0], alpha_plan), "z"))
    u.append(step(after(u[1], b[0], a[1]), "x"))
    us.append(swap(u[1], "core"))
    b.append(step(b[1], "z"))
    a.append(step(after(a[2], b[1], u[1]), "z"))
    u.append(step(after(u[2], b[1], a[2], us[1]), "x"))
    us.append(swap(u[2], "core"))
    b.append(step(b[2], "z"))
    a.append(step(after(a[3], b[2], u[2], us[1]), "z"))
    got0 = swap(after(mine[: SLOTS // 2], v[0]), "ylo")
    v.append(step(after(v[0], u[3], b[2], a[3], us[2]), "x"))
    us.append(swap(u[3], "core"))
    b.append(step(b[3], "z"))
    a.append(step(after(a[4], b[3], u[3], v[0], us[2]), "z"))
    alpha = alpha_call(
        0,
        alpha_plan,
        [p for pair in zip([after(u[0], a[4]), *u[1:]], us) for p in pair],
        alpha_tiles,
    )
    vs = [swap(v[0], "core")]
    v.append(step(v[1], "x"))
    vs.append(swap(v[1], "core"))
    b.append(step(b[4], "z"))
    a.append(step(after(a[5], b[4], v[1], alpha, vs[0]), "z"))
    oth0 = swap(got0, "core")
    got1 = swap(after(mine[SLOTS // 2 :], got0), "ylo")
    v.append(step(v[2], "x"))
    vs.append(swap(v[2], "core"))
    b.append(step(b[5], "z"))
    a.append(step(after(a[6], b[5], v[2], oth0, vs[1]), "z"))
    beta_own, beta_par = beta_call(
        0, (0, 1), where, beta_plan, (a, b), after(beta_tiles, b[5]), [got0, oth0]
    )
    oth1 = swap(got1, "core")
    vs.append(swap(v[3], "core"))
    b.append(step(after(b[6], beta_own, vs[2]), "z"))
    alpha = alpha_call(
        1, alpha_plan, [p for pair in zip(v, vs) for p in pair], alpha_tiles, [alpha]
    )
    par = [got0, oth0, got1, oth1]
    (beta_par,) = beta_call(
        1, (1,), where, beta_plan, (a, b), after(beta_tiles, alpha), par, [beta_par]
    )
    beta_other = swap(beta_par, "ylo")
    (beta_own,) = beta_call(
        1, (0,), where, beta_plan, (a, b), after(beta_tiles, beta_par), par, [beta_own]
    )

    joined = pl.pallas_call(
        join_kernel,
        out_shape=jax.ShapeDtypeStruct((n, n), jnp.float32),
        in_specs=[SMEM] + [VMEM] * 5,
        out_specs=VMEM,
        cost_estimate=pl.CostEstimate(flops=4 * n * n, bytes_accessed=5 * MIB, transcendentals=0),
        name="join",
    )(where, coeffs, diag_alpha[:, None], diag_beta[None, :], alpha, beta_own)
    return pl.pallas_call(
        last_kernel,
        out_shape=jax.ShapeDtypeStruct((n, n), jnp.float32),
        in_specs=[SMEM, ANY, ANY],
        out_specs=ANY,
        scratch_shapes=[
            pltpu.VMEM((BS, n), jnp.float32),
            pltpu.VMEM((BS, n), jnp.float32),
            pltpu.SemaphoreType.DMA((3,)),
        ],
        input_output_aliases={1: 0},
        cost_estimate=pl.CostEstimate(flops=n * BS, bytes_accessed=2 * MIB, transcendentals=0),
        name="last",
    )(where, joined, beta_other)


def solution(mesh):
    parts = Mesh(mesh.devices.reshape(SIZES), AXES)
    return jax.shard_map(
        per_device,
        mesh=parts,
        in_specs=(
            P(ALPHA, BETA),
            P(ALPHA),
            P(BETA),
            P(ALPHA, None, None, None),
            P(BETA, None, None, None),
            P(),
            P(),
            P(),
            P(),
        ),
        out_specs=P(ALPHA, BETA),
        check_vma=False,
    )
```

time: 363 us -> 175 us (0.48)
  waiting for transfers between devices: 255 us -> 61.2 us
  starting transfers between devices: 8.58 us -> 68.1 us
  local copies, waits for them, and re-layouts: 46.4 us -> 13.7 us
  Pallas kernels: 0 us -> 27.9 us
  matrix products: 27.4 us -> 0 us
  between operations: 13.5 us -> 0.53 us
  other arithmetic: 12.1 us -> 0.65 us
    all_to_all x1 -> x0, waiting for transfers between devices: 255 us -> none  [per_device(): lax.all_to_all(alpha_out, 'alpha', split_axis=0, concat_axis=0, tiled=True)]
    ppermute x0 -> x35, starting transfers between devices: none -> 68.1 us  [the longest x14 35.9 us: step(): return lax.ppermute(value, ('core', axis), pairs)]
    ppermute x0 -> x35, waiting for transfers between devices: none -> 61.2 us  [the longest x14 27.2 us: step(): return lax.ppermute(value, ('core', axis), pairs)]
    pallas_call x0 -> x8, Pallas kernels: none -> 27.9 us  [the longest x3 11.8 us: beta_call(): pl.pallas_call(functools.partial(beta_kernel, call, targets), out_shape=[...]
    dot_general x2 -> x0, matrix products: 27.4 us -> none  [the longest x1 16.7 us: per_device(): jnp.einsum('ajcb,jcbd->ajd', beta_grouped, beta_masked, precision=lax.Pre...]
    gather x3 -> x0, local copies, waits for them, and re-layouts: 22 us -> none  [the longest x1 10.1 us: per_device(): beta_gathered = jnp.take(whole_blocks, beta_mine, axis=1)]
    reshape x4 -> x0, local copies, waits for them, and re-layouts: 18.9 us -> none  [the longest x1 17.5 us: per_device(): whole.reshape(rows_dev, beta_devices * beta_count, block_size)]
    all_to_all x1 -> x0, starting transfers between devices: 8.58 us -> none  [per_device(): lax.all_to_all(alpha_out, 'alpha', split_axis=0, concat_axis=0, tiled=True)]
  transfers between devices with their start and end apart: 2 -> 35, of which waited for: 1 -> 12; matrix products, arithmetic and copies ran while one was open for 10% -> 6% of each run, Pallas kernels for 0% -> 13%
where the time goes in v3:
time: 175 us; the launch traced here: 172 us
  starting transfers between devices  68.1 us (39%)
  waiting for transfers between devices  61.2 us (35%)
  Pallas kernels  27.9 us (16%)
  local copies, waits for them, and re-layouts  13.7 us (8%)
    ppermute x14, starting transfers between devices, step(): return lax.ppermute(value, ('core', axis), pairs)  35.9 us
    ppermute x14, waiting for transfers between devices, step(): return lax.ppermute(value, ('core', axis), pairs)  27.2 us
    ppermute x15, waiting for transfers between devices, swap(): return lax.ppermute(value, axis, [(0, 1), (1, 0)])  26.7 us
    ppermute x15, starting transfers between devices, swap(): return lax.ppermute(value, axis, [(0, 1), (1, 0)])  17.3 us
    ppermute x6, starting transfers between devices, step(): return lax.ppermute(value, (axis, 'core'), pairs)  14.8 us
    pallas_call x3, Pallas kernels, beta_call(): pl.pallas_call(functools.partial(beta_kernel, call, targets), out_shape=[...  11.8 us
    unnamed x74, local copies, waits for them, and re-layouts  9.93 us
    ppermute x6, waiting for transfers between devices, step(): return lax.ppermute(value, (axis, 'core'), pairs)  7.34 us
  transfers between devices with their start and end apart: 35, of which 12 were waited for; matrix products, arithmetic and copies ran while one was open for 6% of the time, Pallas kernels for 13%

profile of v3, /device:TPU:1, one launch (start us, length us, event | category | flops | bytes accessed | tf_op | source)
XLA Modules:
  0.0 172.1 jit_solution(9513001405631481887)
XLA Ops:
  0.0 3.3 %collective-permute-start.3 = (f32[512,512]{1,0:T(8,128)}, f32[512,512]{1,0:T(8,128)S(1)}, u32[]{:S(2)}, u32[]{:S(2)}) collective-permute-start(f32[512,512]{1,0:T(8,128)} %x.1), channel_id=1, source_target_pairs={{0,32},{32,64},{64,96},{96,0},{16,112},{48,16},{80,48},{112,80},{1... | collective-permute-start | bytes 3145736 | tf_op jit(solution)/shard_map/ppermute | solution.py:37
  6.0 5.6 %collective-permute-start.4 = (f32[256,512]{1,0:T(8,128)S(1)}, f32[256,512]{1,0:T(8,128)S(1)}, u32[]{:S(2)}, u32[]{:S(2)}) collective-permute-start(f32[256,512]{1,0:T(8,128)S(1)} %get-tuple-element.49.refs_0_), channel_id=1, source_target_pairs={{0,1},{1,2},{2,3},{3,4},{4,5},{5,6},{6,7},{7,0},{16,23},{17,16},{1... | collective-permute-start | bytes 1572872 | tf_op jit(solution)/shard_map/ppermute | solution.py:34
  11.6 6.1 %collective-permute-done.refs_6_.refs_8_ = f32[256,512]{1,0:T(8,128)S(1)} collective-permute-done((f32[256,512]{1,0:T(8,128)S(1)}, f32[256,512]{1,0:T(8,128)S(1)}, u32[]{:S(2)}, u32[]{:S(2)}) %collective-permute-start) | collective-permute-done | bytes 524320 | tf_op jit(solution)/shard_map/ppermute | solution.py:26
  17.7 3.5 %collective-permute-start.5 = (f32[512,512]{1,0:T(8,128)S(1)}, f32[512,512]{1,0:T(8,128)}, u32[]{:S(2)}, u32[]{:S(2)}) collective-permute-start(f32[512,512]{1,0:T(8,128)S(1)} %collective-permute-done.3.refs_2_), channel_id=1, source_target_pairs={{0,32},{32,64},{64,96},{96,0},{16,112},{48,16},{80,48},{112,80},{1... | collective-permute-start | bytes 3145736 | tf_op jit(solution)/shard_map/ppermute | solution.py:37
  27.3 3.6 %plan.1 = (s32[2,16]{1,0:T(2,128)}, s32[4,32]{1,0:T(4,128)}) custom-call(s32[2]{0:T(128)} %pad_add_fusion.where, s32[32,8]{1,0:T(8,128)} %copy.15.alpha_source, s32[32,8]{1,0:T(8,128)} %copy.16.alpha_live, s32[32,8]{1,0:T(8,128)} %copy.17.beta_source, s32[32,8]{1,0:T(8,128)} %copy.18.beta_live), custom_call_target="tpu_custom_call" | custom-call | tf_op jit(solution)/shard_map/plan/pallas_call | solution.py:304
  30.9 4.7 %collective-permute-start.6 = (f32[256,512]{1,0:T(8,128)S(1)}, f32[256,512]{1,0:T(8,128)S(1)}, u32[]{:S(2)}, u32[]{:S(2)}) collective-permute-start(f32[256,512]{1,0:T(8,128)S(1)} %collective-permute-done.refs_6_.refs_8_), channel_id=1, source_target_pairs={{0,1},{1,2},{2,3},{3,4},{4,5},{5,6},{6,7},{7,0},{16,23},{17,16},{1... | collective-permute-start | bytes 1572872 | tf_op jit(solution)/shard_map/ppermute | solution.py:34
  36.4 2.9 %collective-permute-start.1 = (f32[512,512]{1,0:T(8,128)}, f32[512,512]{1,0:T(8,128)}, u32[]{:S(2)}, u32[]{:S(2)}) collective-permute-start(f32[512,512]{1,0:T(8,128)} %x.1), channel_id=1, source_target_pairs={{0,128},{128,0},{1,129},{129,1},{2,130},{130,2},{3,131},{131,3},{4... | collective-permute-start | bytes 3145736 | tf_op jit(solution)/shard_map/ppermute | solution.py:26
  39.3 2.5 %collective-permute-done.6.refs_7_.refs_9_ = f32[256,512]{1,0:T(8,128)S(1)} collective-permute-done((f32[256,512]{1,0:T(8,128)S(1)}, f32[256,512]{1,0:T(8,128)S(1)}, u32[]{:S(2)}, u32[]{:S(2)}) %collective-permute-start.6) | collective-permute-done | bytes 524320 | tf_op jit(solution)/shard_map/ppermute | solution.py:34
  41.8 5.6 %collective-permute-done.8.refs_2_ = f32[256,512]{1,0:T(8,128)S(1)} collective-permute-done((f32[256,512]{1,0:T(8,128)S(1)}, f32[256,512]{1,0:T(8,128)S(1)}, u32[]{:S(2)}, u32[]{:S(2)}) %collective-permute-start.8) | collective-permute-done | bytes 524320 | tf_op jit(solution)/shard_map/ppermute | solution.py:34
  50.0 2.9 %collective-permute-start.11 = (f32[256,512]{1,0:T(8,128)S(1)}, f32[256,512]{1,0:T(8,128)S(1)}, u32[]{:S(2)}, u32[]{:S(2)}) collective-permute-start(f32[256,512]{1,0:T(8,128)S(1)} %collective-permute-done.6.refs_7_.refs_9_), channel_id=1, source_target_pairs={{0,1},{1,2},{2,3},{3,4},{4,5},{5,6},{6,7},{7,0},{16,23},{17,16},{1... | collective-permute-start | bytes 1572872 | tf_op jit(solution)/shard_map/ppermute | solution.py:34
  53.0 8.1 %collective-permute-done.1.refs_0_ = f32[512,512]{1,0:T(8,128)} collective-permute-done((f32[512,512]{1,0:T(8,128)}, f32[512,512]{1,0:T(8,128)}, u32[]{:S(2)}, u32[]{:S(2)}) %collective-permute-start.1) | collective-permute-done | bytes 1048608 | tf_op jit(solution)/shard_map/ppermute | solution.py:26
  61.1 3.5 %collective-permute-done.12.refs_3_ = f32[256,512]{1,0:T(8,128)S(1)} collective-permute-done((f32[256,512]{1,0:T(8,128)S(1)}, f32[256,512]{1,0:T(8,128)S(1)}, u32[]{:S(2)}, u32[]{:S(2)}) %collective-permute-start.12) | collective-permute-done | bytes 524320 | tf_op jit(solution)/shard_map/ppermute | solution.py:34
  71.6 7.3 %collective-permute-done.14.refs_2_ = f32[512,512]{1,0:T(8,128)} collective-permute-done((f32[512,512]{1,0:T(8,128)}, f32[512,512]{1,0:T(8,128)}, u32[]{:S(2)}, u32[]{:S(2)}) %collective-permute-start.14) | collective-permute-done | bytes 1048608 | tf_op jit(solution)/shard_map/ppermute | solution.py:37
  81.2 2.5 %collective-permute-start.20 = (f32[256,512]{1,0:T(8,128)S(1)}, f32[256,512]{1,0:T(8,128)S(1)}, u32[]{:S(2)}, u32[]{:S(2)}) collective-permute-start(f32[256,512]{1,0:T(8,128)S(1)} %collective-permute-done.12.refs_3_), channel_id=1, source_target_pairs={{0,1},{1,2},{2,3},{3,4},{4,5},{5,6},{6,7},{7,0},{16,23},{17,16},{1... | collective-permute-start | bytes 1572872 | tf_op jit(solution)/shard_map/ppermute | solution.py:34
  83.7 6.1 %collective-permute-done.20.refs_4_ = f32[256,512]{1,0:T(8,128)S(1)} collective-permute-done((f32[256,512]{1,0:T(8,128)S(1)}, f32[256,512]{1,0:T(8,128)S(1)}, u32[]{:S(2)}, u32[]{:S(2)}) %collective-permute-start.20) | collective-permute-done | bytes 524320 | tf_op jit(solution)/shard_map/ppermute | solution.py:34
  89.8 3.4 %collective-permute-start.24 = (f32[256,512]{1,0:T(8,128)S(1)}, f32[256,512]{1,0:T(8,128)S(1)}, u32[]{:S(2)}, u32[]{:S(2)}) collective-permute-start(f32[256,512]{1,0:T(8,128)S(1)} %collective-permute-done.22.refs_9_.refs_11_), channel_id=1, source_target_pairs={{0,1},{1,2},{2,3},{3,4},{4,5},{5,6},{6,7},{7,0},{16,23},{17,16},{1... | collective-permute-start | bytes 1572872 | tf_op jit(solution)/shard_map/ppermute | solution.py:34
  94.1 2.7 %collective-permute-start.18 = (f32[512,512]{1,0:T(8,128)S(1)}, f32[512,512]{1,0:T(8,128)S(1)}, u32[]{:S(2)}, u32[]{:S(2)}) collective-permute-start(f32[512,512]{1,0:T(8,128)S(1)} %collective-permute-done.16.refs_4_), channel_id=1, source_target_pairs={{0,32},{32,64},{64,96},{96,0},{16,112},{48,16},{80,48},{112,80},{1... | collective-permute-start | bytes 3145736 | tf_op jit(solution)/shard_map/ppermute | solution.py:37
  96.8 2.5 %collective-permute-done.24.refs_10_.refs_12_ = f32[256,512]{1,0:T(8,128)S(1)} collective-permute-done((f32[256,512]{1,0:T(8,128)S(1)}, f32[256,512]{1,0:T(8,128)S(1)}, u32[]{:S(2)}, u32[]{:S(2)}) %collective-permute-start.24) | collective-permute-done | bytes 524320 | tf_op jit(solution)/shard_map/ppermute | solution.py:34
  99.3 3.1 %collective-permute-start.26 = (f32[256,512]{1,0:T(8,128)S(1)}, f32[256,512]{1,0:T(8,128)S(1)}, u32[]{:S(2)}, u32[]{:S(2)}) collective-permute-start(f32[256,512]{1,0:T(8,128)S(1)} %collective-permute-done.24.refs_10_.refs_12_), channel_id=1, source_target_pairs={{0,1},{1,2},{2,3},{3,4},{4,5},{5,6},{6,7},{7,0},{16,23},{17,16},{1... | collective-permute-start | bytes 1572872 | tf_op jit(solution)/shard_map/ppermute | solution.py:34
  102.4 2.5 %collective-permute-done.23.refs_5_ = f32[256,512]{1,0:T(8,128)S(1)} collective-permute-done((f32[256,512]{1,0:T(8,128)S(1)}, f32[256,512]{1,0:T(8,128)S(1)}, u32[]{:S(2)}, u32[]{:S(2)}) %collective-permute-start.23) | collective-permute-done | bytes 524320 | tf_op jit(solution)/shard_map/ppermute | solution.py:34
  106.2 4.4 %collective-permute-start.15 = (f32[512,512]{1,0:T(8,128)}, f32[512,512]{1,0:T(8,128)S(1)}, u32[]{:S(2)}, u32[]{:S(2)}) collective-permute-start(f32[512,512]{1,0:T(8,128)} %collective-permute-done.14.refs_2_), channel_id=1, source_target_pairs={{0,16},{16,0},{1,17},{17,1},{2,18},{18,2},{3,19},{19,3},{4,20},{20... | collective-permute-start | bytes 3145736 | tf_op jit(solution)/shard_map/ppermute | solution.py:26
  110.6 2.6 %alpha0.1.refs_9_ = f32[512,512]{1,0:T(8,128)S(1)} custom-call(s32[2,16]{1,0:T(2,128)S(1)} %copy-done.4, f32[512,512]{1,0:T(8,128)} %x.1, f32[512,512]{1,0:T(8,128)} %collective-permute-done.7.refs_1_, f32[512,512]{1,0:T(8,128)} %copy-done.25, f32[512,512]{1,0:T(8,128)} %collective-permute-done.9.refs_3_, f32[512,512]{1,0:T(8,128)} %collective-permute-done.5.refs_4_, ...), custom_call_target="tpu_custom_call" | custom-call | flops 1610612736 | bytes 8388608 | tf_op jit(solution)/shard_map/alpha0/pallas_call | solution.py:156
  115.4 9.9 %collective-permute-done.32.refs_19_ = f32[4,256,256]{2,1,0:T(8,128)S(1)} collective-permute-done((f32[4,256,256]{2,1,0:T(8,128)S(1)}, f32[4,256,256]{2,1,0:T(8,128)S(1)}, u32[]{:S(2)}, u32[]{:S(2)}) %collective-permute-start.32) | collective-permute-done | bytes 1048608 | tf_op jit(solution)/shard_map/ppermute | solution.py:26
  125.3 7.6 %collective-permute-start.30 = (f32[256,512]{1,0:T(8,128)S(1)}, f32[256,512]{1,0:T(8,128)S(1)}, u32[]{:S(2)}, u32[]{:S(2)}) collective-permute-start(f32[256,512]{1,0:T(8,128)S(1)} %collective-permute-done.26.refs_13_), channel_id=1, source_target_pairs={{0,1},{1,2},{2,3},{3,4},{4,5},{5,6},{6,7},{7,0},{16,23},{17,16},{1... | collective-permute-start | bytes 1572872 | tf_op jit(solution)/shard_map/ppermute | solution.py:34
  133.0 5.9 %beta02.1 = (f32[256,512]{1,0:T(8,128)S(1)}, f32[256,512]{1,0:T(8,128)S(1)}) custom-call(s32[2]{0:T(128)S(1)} %copy-done.2, s32[4,32]{1,0:T(4,128)S(1)} %copy-done.3, f32[256,512]{1,0:T(8,128)} %copy-done.7, f32[256,512]{1,0:T(8,128)} %copy-done.9, f32[256,512]{1,0:T(8,128)} %copy-done.11, f32[256,512]{1,0:T(8,128)} %copy-done.13, f32[256,512]{1,0:T(8,128)} %copy-done.15, ...), custom_call_target="tpu_custom_call" | custom-call | flops 1610612736 | bytes 6291456 | tf_op jit(solution)/shard_map/beta02/pallas_call | solution.py:245
  143.2 4.2 %alpha1.1.alpha = f32[512,512]{1,0:T(8,128)S(1)} custom-call(s32[2,16]{1,0:T(2,128)S(1)} %copy-done.4, f32[512,512]{1,0:T(8,128)} %collective-permute-done.1.refs_0_, f32[512,512]{1,0:T(8,128)} %copy-done.26, f32[512,512]{1,0:T(8,128)} %collective-permute-done.14.refs_2_, f32[512,512]{1,0:T(8,128)} %copy-done.29, f32[512,512]{1,0:T(8,128)} %copy-done.27, ...), custom_call_target="tpu_custom_call" | custom-call | flops 1610612736 | bytes 8388608 | tf_op jit(solution)/shard_map/alpha1/pallas_call | solution.py:156
  148.5 4.4 %collective-permute-done.31.refs_15_ = f32[256,512]{1,0:T(8,128)S(1)} collective-permute-done((f32[256,512]{1,0:T(8,128)S(1)}, f32[256,512]{1,0:T(8,128)S(1)}, u32[]{:S(2)}, u32[]{:S(2)}) %collective-permute-start.31) | collective-permute-done | bytes 524320 | tf_op jit(solution)/shard_map/ppermute | solution.py:34
  153.7 3.1 %beta11.2 = f32[256,512]{1,0:T(8,128)S(1)} custom-call(s32[2]{0:T(128)S(1)} %copy-done.2, s32[4,32]{1,0:T(4,128)S(1)} %copy-done.3, f32[256,512]{1,0:T(8,128)} %copy-done.7, f32[256,512]{1,0:T(8,128)} %copy-done.9, f32[256,512]{1,0:T(8,128)} %copy-done.11, f32[256,512]{1,0:T(8,128)} %copy-done.13, f32[256,512]{1,0:T(8,128)} %copy-done.15, ...), custom_call_target="tpu_custom_call" | custom-call | flops 805306368 | bytes 6291456 | tf_op jit(solution)/shard_map/beta11/pallas_call | solution.py:245
  159.2 2.8 %beta11.3.beta = f32[256,512]{1,0:T(8,128)S(1)} custom-call(s32[2]{0:T(128)S(1)} %copy-done.2, s32[4,32]{1,0:T(4,128)S(1)} %copy-done.3, f32[256,512]{1,0:T(8,128)} %copy-done.7, f32[256,512]{1,0:T(8,128)} %copy-done.9, f32[256,512]{1,0:T(8,128)} %copy-done.11, f32[256,512]{1,0:T(8,128)} %copy-done.13, f32[256,512]{1,0:T(8,128)} %copy-done.15, ...), custom_call_target="tpu_custom_call" | custom-call | flops 805306368 | bytes 6291456 | tf_op jit(solution)/shard_map/beta11/pallas_call | solution.py:245
  162.9 3.0 %join.1.joined = f32[512,512]{1,0:T(8,128)} custom-call(s32[2]{0:T(128)} %pad_add_fusion.where, f32[512,512]{1,0:T(8,128)} %x.1, f32[512,1]{1,0:T(8,128)} %copy.19.da, f32[1,512]{1,0:T(1,128)} %bitcast.9, f32[512,512]{1,0:T(8,128)} %copy-done, f32[256,512]{1,0:T(8,128)} %copy-done.1), custom_call_target="tpu_custom_call" | custom-call | flops 1048576 | bytes 5242880 | tf_op jit(solution)/shard_map/join/pallas_call | solution.py:374
  165.8 2.5 %collective-permute-done.34.beta_other = f32[256,512]{1,0:T(8,128)S(1)} collective-permute-done((f32[256,512]{1,0:T(8,128)S(1)}, f32[256,512]{1,0:T(8,128)S(1)}, u32[]{:S(2)}, u32[]{:S(2)}) %collective-permute-start.34) | collective-permute-done | bytes 524320 | tf_op jit(solution)/shard_map/ppermute | solution.py:26
  169.2 2.7 %last.1 = f32[512,512]{1,0:T(8,128)} custom-call(s32[2]{0:T(128)} %pad_add_fusion.where, f32[512,512]{1,0:T(8,128)} %join.1.joined, f32[256,512]{1,0:T(8,128)} %copy-done.33), custom_call_target="tpu_custom_call", output_to_operand_aliasing={{}: (1, {})} | custom-call | flops 131072 | bytes 2097152 | tf_op jit(solution)/shard_map/last/pallas_call | solution.py:382
  (124 shorter events, 35.9 us)
Async XLA Ops:
  0.0 17.7 %collective-permute-start.3 = (f32[512,512]{1,0:T(8,128)}, f32[512,512]{1,0:T(8,128)S(1)}, u32[]{:S(2)}, u32[]{:S(2)}) collective-permute-start(f32[512,512]{1,0:T(8,128)} %x.1), channel_id=1, source_target_pairs={{0,32},{32,64},{64,96},{96,0},{16,112},{48,16},{80,48},{112,80},{1... | collective-permute-start | bytes 3145736 | tf_op jit(solution)/shard_map/ppermute | solution.py:37
  3.3 32.4 %collective-permute-start.7 = (f32[512,512]{1,0:T(8,128)}, f32[512,512]{1,0:T(8,128)}, u32[]{:S(2)}, u32[]{:S(2)}) collective-permute-start(f32[512,512]{1,0:T(8,128)} %x.1), channel_id=1, source_target_pairs={{0,16},{16,0},{1,17},{17,1},{2,18},{18,2},{3,19},{19,3},{4,20},{20... | collective-permute-start | bytes 3145736 | tf_op jit(solution)/shard_map/ppermute | solution.py:26
  4.6 13.1 %collective-permute-start = (f32[256,512]{1,0:T(8,128)S(1)}, f32[256,512]{1,0:T(8,128)S(1)}, u32[]{:S(2)}, u32[]{:S(2)}) collective-permute-start(f32[256,512]{1,0:T(8,128)S(1)} %get-tuple-element.50), channel_id=1, source_target_pairs={{0,8},{8,0},{1,9},{9,1},{2,10},{10,2},{3,11},{11,3},{4,12},{12,4},... | collective-permute-start | bytes 1572872 | tf_op jit(solution)/shard_map/ppermute | solution.py:26
  6.0 11.7 %collective-permute-start.4 = (f32[256,512]{1,0:T(8,128)S(1)}, f32[256,512]{1,0:T(8,128)S(1)}, u32[]{:S(2)}, u32[]{:S(2)}) collective-permute-start(f32[256,512]{1,0:T(8,128)S(1)} %get-tuple-element.49.refs_0_), channel_id=1, source_target_pairs={{0,1},{1,2},{2,3},{3,4},{4,5},{5,6},{6,7},{7,0},{16,23},{17,16},{1... | collective-permute-start | bytes 1572872 | tf_op jit(solution)/shard_map/ppermute | solution.py:34
  17.7 29.7 %collective-permute-start.5 = (f32[512,512]{1,0:T(8,128)S(1)}, f32[512,512]{1,0:T(8,128)}, u32[]{:S(2)}, u32[]{:S(2)}) collective-permute-start(f32[512,512]{1,0:T(8,128)S(1)} %collective-permute-done.3.refs_2_), channel_id=1, source_target_pairs={{0,32},{32,64},{64,96},{96,0},{16,112},{48,16},{80,48},{112,80},{1... | collective-permute-start | bytes 3145736 | tf_op jit(solution)/shard_map/ppermute | solution.py:37
  21.2 26.2 %collective-permute-start.9 = (f32[512,512]{1,0:T(8,128)S(1)}, f32[512,512]{1,0:T(8,128)}, u32[]{:S(2)}, u32[]{:S(2)}) collective-permute-start(f32[512,512]{1,0:T(8,128)S(1)} %collective-permute-done.3.refs_2_), channel_id=1, source_target_pairs={{0,16},{16,0},{1,17},{17,1},{2,18},{18,2},{3,19},{19,3},{4,20},{20... | collective-permute-start | bytes 3145736 | tf_op jit(solution)/shard_map/ppermute | solution.py:26
  30.9 10.8 %collective-permute-start.6 = (f32[256,512]{1,0:T(8,128)S(1)}, f32[256,512]{1,0:T(8,128)S(1)}, u32[]{:S(2)}, u32[]{:S(2)}) collective-permute-start(f32[256,512]{1,0:T(8,128)S(1)} %collective-permute-done.refs_6_.refs_8_), channel_id=1, source_target_pairs={{0,1},{1,2},{2,3},{3,4},{4,5},{5,6},{6,7},{7,0},{16,23},{17,16},{1... | collective-permute-start | bytes 1572872 | tf_op jit(solution)/shard_map/ppermute | solution.py:34
  35.7 11.7 %collective-permute-start.8 = (f32[256,512]{1,0:T(8,128)S(1)}, f32[256,512]{1,0:T(8,128)S(1)}, u32[]{:S(2)}, u32[]{:S(2)}) collective-permute-start(f32[256,512]{1,0:T(8,128)S(1)} %collective-permute-done.4.refs_1_), channel_id=1, source_target_pairs={{0,1},{1,2},{2,3},{3,4},{4,5},{5,6},{6,7},{7,0},{16,23},{17,16},{1... | collective-permute-start | bytes 1572872 | tf_op jit(solution)/shard_map/ppermute | solution.py:34
  36.4 24.7 %collective-permute-start.1 = (f32[512,512]{1,0:T(8,128)}, f32[512,512]{1,0:T(8,128)}, u32[]{:S(2)}, u32[]{:S(2)}) collective-permute-start(f32[512,512]{1,0:T(8,128)} %x.1), channel_id=1, source_target_pairs={{0,128},{128,0},{1,129},{129,1},{2,130},{130,2},{3,131},{131,3},{4... | collective-permute-start | bytes 3145736 | tf_op jit(solution)/shard_map/ppermute | solution.py:26
  47.4 17.2 %collective-permute-start.10 = (f32[512,512]{1,0:T(8,128)}, f32[512,512]{1,0:T(8,128)}, u32[]{:S(2)}, u32[]{:S(2)}) collective-permute-start(f32[512,512]{1,0:T(8,128)} %collective-permute-done.5.refs_4_), channel_id=1, source_target_pairs={{0,32},{32,64},{64,96},{96,0},{16,112},{48,16},{80,48},{112,80},{1... | collective-permute-start | bytes 3145736 | tf_op jit(solution)/shard_map/ppermute | solution.py:37
  49.3 15.4 %collective-permute-start.13 = (f32[512,512]{1,0:T(8,128)}, f32[512,512]{1,0:T(8,128)}, u32[]{:S(2)}, u32[]{:S(2)}) collective-permute-start(f32[512,512]{1,0:T(8,128)} %collective-permute-done.5.refs_4_), channel_id=1, source_target_pairs={{0,16},{16,0},{1,17},{17,1},{2,18},{18,2},{3,19},{19,3},{4,20},{20... | collective-permute-start | bytes 3145736 | tf_op jit(solution)/shard_map/ppermute | solution.py:26
  50.0 11.1 %collective-permute-start.11 = (f32[256,512]{1,0:T(8,128)S(1)}, f32[256,512]{1,0:T(8,128)S(1)}, u32[]{:S(2)}, u32[]{:S(2)}) collective-permute-start(f32[256,512]{1,0:T(8,128)S(1)} %collective-permute-done.6.refs_7_.refs_9_), channel_id=1, source_target_pairs={{0,1},{1,2},{2,3},{3,4},{4,5},{5,6},{6,7},{7,0},{16,23},{17,16},{1... | collective-permute-start | bytes 1572872 | tf_op jit(solution)/shard_map/ppermute | solution.py:34
  52.9 11.7 %collective-permute-start.12 = (f32[256,512]{1,0:T(8,128)S(1)}, f32[256,512]{1,0:T(8,128)S(1)}, u32[]{:S(2)}, u32[]{:S(2)}) collective-permute-start(f32[256,512]{1,0:T(8,128)S(1)} %collective-permute-done.8.refs_2_), channel_id=1, source_target_pairs={{0,1},{1,2},{2,3},{3,4},{4,5},{5,6},{6,7},{7,0},{16,23},{17,16},{1... | collective-permute-start | bytes 1572872 | tf_op jit(solution)/shard_map/ppermute | solution.py:34
  64.6 14.3 %collective-permute-start.14 = (f32[512,512]{1,0:T(8,128)}, f32[512,512]{1,0:T(8,128)}, u32[]{:S(2)}, u32[]{:S(2)}) collective-permute-start(f32[512,512]{1,0:T(8,128)} %collective-permute-done.1.refs_0_), channel_id=1, source_target_pairs={{0,32},{32,64},{64,96},{96,0},{16,112},{48,16},{80,48},{112,80},{1... | collective-permute-start | bytes 3145736 | tf_op jit(solution)/shard_map/ppermute | solution.py:37
  67.5 25.7 %collective-permute-start.2 = (f32[512,512]{1,0:T(8,128)}, f32[512,512]{1,0:T(8,128)S(1)}, u32[]{:S(2)}, u32[]{:S(2)}) collective-permute-start(f32[512,512]{1,0:T(8,128)} %collective-permute-done.1.refs_0_), channel_id=1, source_target_pairs={{0,16},{16,0},{1,17},{17,1},{2,18},{18,2},{3,19},{19,3},{4,20},{20... | collective-permute-start | bytes 3145736 | tf_op jit(solution)/shard_map/ppermute | solution.py:26
  68.5 24.8 %collective-permute-start.27 = (f32[4,256,256]{2,1,0:T(8,128)S(1)}, f32[4,256,256]{2,1,0:T(8,128)S(1)}, u32[]{:S(2)}, u32[]{:S(2)}) collective-permute-start(f32[4,256,256]{2,1,0:T(8,128)S(1)} %get-tuple-element.38), channel_id=1, source_target_pairs={{0,8},{8,0},{1,9},{9,1},{2,10},{10,2},{3,11},{11,3},{4,12},{12,4},... | collective-permute-start | bytes 3145736 | tf_op jit(solution)/shard_map/ppermute | solution.py:26
  69.8 13.9 %collective-permute-start.22 = (f32[256,512]{1,0:T(8,128)S(1)}, f32[256,512]{1,0:T(8,128)S(1)}, u32[]{:S(2)}, u32[]{:S(2)}) collective-permute-start(f32[256,512]{1,0:T(8,128)S(1)} %collective-permute-done.11.refs_8_.refs_10_), channel_id=1, source_target_pairs={{0,1},{1,2},{2,3},{3,4},{4,5},{5,6},{6,7},{7,0},{16,23},{17,16},{1... | collective-permute-start | bytes 1572872 | tf_op jit(solution)/shard_map/ppermute | solution.py:34
  79.0 15.1 %collective-permute-start.16 = (f32[512,512]{1,0:T(8,128)}, f32[512,512]{1,0:T(8,128)S(1)}, u32[]{:S(2)}, u32[]{:S(2)}) collective-permute-start(f32[512,512]{1,0:T(8,128)} %collective-permute-done.14.refs_2_), channel_id=1, source_target_pairs={{0,32},{32,64},{64,96},{96,0},{16,112},{48,16},{80,48},{112,80},{1... | collective-permute-start | bytes 3145736 | tf_op jit(solution)/shard_map/ppermute | solution.py:37
  83.6 22.6 %collective-permute-start.21 = (f32[512,512]{1,0:T(8,128)}, f32[512,512]{1,0:T(8,128)S(1)}, u32[]{:S(2)}, u32[]{:S(2)}) collective-permute-start(f32[512,512]{1,0:T(8,128)} %collective-permute-done.10.refs_6_), channel_id=1, source_target_pairs={{0,16},{16,0},{1,17},{17,1},{2,18},{18,2},{3,19},{19,3},{4,20},{20... | collective-permute-start | bytes 3145736 | tf_op jit(solution)/shard_map/ppermute | solution.py:26
  93.2 11.7 %collective-permute-start.23 = (f32[256,512]{1,0:T(8,128)S(1)}, f32[256,512]{1,0:T(8,128)S(1)}, u32[]{:S(2)}, u32[]{:S(2)}) collective-permute-start(f32[256,512]{1,0:T(8,128)S(1)} %collective-permute-done.20.refs_4_), channel_id=1, source_target_pairs={{0,1},{1,2},{2,3},{3,4},{4,5},{5,6},{6,7},{7,0},{16,23},{17,16},{1... | collective-permute-start | bytes 1572872 | tf_op jit(solution)/shard_map/ppermute | solution.py:34
  93.3 21.9 %collective-permute-start.28 = (f32[4,256,256]{2,1,0:T(8,128)S(1)}, f32[4,256,256]{2,1,0:T(8,128)S(1)}, u32[]{:S(2)}, u32[]{:S(2)}) collective-permute-start(f32[4,256,256]{2,1,0:T(8,128)S(1)} %collective-permute-done.27.refs_12_.refs_17_), channel_id=1, source_target_pairs={{0,16},{16,0},{1,17},{17,1},{2,18},{18,2},{3,19},{19,3},{4,20},{20... | collective-permute-start | bytes 3145736 | tf_op jit(solution)/shard_map/ppermute | solution.py:26
  94.1 21.2 %collective-permute-start.18 = (f32[512,512]{1,0:T(8,128)S(1)}, f32[512,512]{1,0:T(8,128)S(1)}, u32[]{:S(2)}, u32[]{:S(2)}) collective-permute-start(f32[512,512]{1,0:T(8,128)S(1)} %collective-permute-done.16.refs_4_), channel_id=1, source_target_pairs={{0,32},{32,64},{64,96},{96,0},{16,112},{48,16},{80,48},{112,80},{1... | collective-permute-start | bytes 3145736 | tf_op jit(solution)/shard_map/ppermute | solution.py:37
  99.3 14.0 %collective-permute-start.26 = (f32[256,512]{1,0:T(8,128)S(1)}, f32[256,512]{1,0:T(8,128)S(1)}, u32[]{:S(2)}, u32[]{:S(2)}) collective-permute-start(f32[256,512]{1,0:T(8,128)S(1)} %collective-permute-done.24.refs_10_.refs_12_), channel_id=1, source_target_pairs={{0,1},{1,2},{2,3},{3,4},{4,5},{5,6},{6,7},{7,0},{16,23},{17,16},{1... | collective-permute-start | bytes 1572872 | tf_op jit(solution)/shard_map/ppermute | solution.py:34
  104.9 20.4 %collective-permute-start.32 = (f32[4,256,256]{2,1,0:T(8,128)S(1)}, f32[4,256,256]{2,1,0:T(8,128)S(1)}, u32[]{:S(2)}, u32[]{:S(2)}) collective-permute-start(f32[4,256,256]{2,1,0:T(8,128)S(1)} %get-tuple-element.44), channel_id=1, source_target_pairs={{0,8},{8,0},{1,9},{9,1},{2,10},{10,2},{3,11},{11,3},{4,12},{12,4},... | collective-permute-start | bytes 3145736 | tf_op jit(solution)/shard_map/ppermute | solution.py:26
  106.2 32.6 %collective-permute-start.15 = (f32[512,512]{1,0:T(8,128)}, f32[512,512]{1,0:T(8,128)S(1)}, u32[]{:S(2)}, u32[]{:S(2)}) collective-permute-start(f32[512,512]{1,0:T(8,128)} %collective-permute-done.14.refs_2_), channel_id=1, source_target_pairs={{0,16},{16,0},{1,17},{17,1},{2,18},{18,2},{3,19},{19,3},{4,20},{20... | collective-permute-start | bytes 3145736 | tf_op jit(solution)/shard_map/ppermute | solution.py:26
  113.3 26.7 %collective-permute-start.17 = (f32[512,512]{1,0:T(8,128)S(1)}, f32[512,512]{1,0:T(8,128)S(1)}, u32[]{:S(2)}, u32[]{:S(2)}) collective-permute-start(f32[512,512]{1,0:T(8,128)S(1)} %collective-permute-done.16.refs_4_), channel_id=1, source_target_pairs={{0,16},{16,0},{1,17},{17,1},{2,18},{18,2},{3,19},{19,3},{4,20},{20... | collective-permute-start | bytes 3145736 | tf_op jit(solution)/shard_map/ppermute | solution.py:26
  115.2 17.8 %collective-permute-start.25 = (f32[256,512]{1,0:T(8,128)S(1)}, f32[256,512]{1,0:T(8,128)S(1)}, u32[]{:S(2)}, u32[]{:S(2)}) collective-permute-start(f32[256,512]{1,0:T(8,128)S(1)} %collective-permute-done.23.refs_5_), channel_id=1, source_target_pairs={{0,1},{1,2},{2,3},{3,4},{4,5},{5,6},{6,7},{7,0},{16,23},{17,16},{1... | collective-permute-start | bytes 1572872 | tf_op jit(solution)/shard_map/ppermute | solution.py:34
  115.3 27.0 %collective-permute-start.19 = (f32[512,512]{1,0:T(8,128)S(1)}, f32[512,512]{1,0:T(8,128)S(1)}, u32[]{:S(2)}, u32[]{:S(2)}) collective-permute-start(f32[512,512]{1,0:T(8,128)S(1)} %collective-permute-done.18.refs_6_), channel_id=1, source_target_pairs={{0,16},{16,0},{1,17},{17,1},{2,18},{18,2},{3,19},{19,3},{4,20},{20... | collective-permute-start | bytes 3145736 | tf_op jit(solution)/shard_map/ppermute | solution.py:26
  125.3 14.7 %collective-permute-start.30 = (f32[256,512]{1,0:T(8,128)S(1)}, f32[256,512]{1,0:T(8,128)S(1)}, u32[]{:S(2)}, u32[]{:S(2)}) collective-permute-start(f32[256,512]{1,0:T(8,128)S(1)} %collective-permute-done.26.refs_13_), channel_id=1, source_target_pairs={{0,1},{1,2},{2,3},{3,4},{4,5},{5,6},{6,7},{7,0},{16,23},{17,16},{1... | collective-permute-start | bytes 1572872 | tf_op jit(solution)/shard_map/ppermute | solution.py:34
  132.9 15.5 %collective-permute-start.33 = (f32[4,256,256]{2,1,0:T(8,128)S(1)}, f32[4,256,256]{2,1,0:T(8,128)S(1)}, u32[]{:S(2)}, u32[]{:S(2)}) collective-permute-start(f32[4,256,256]{2,1,0:T(8,128)S(1)} %collective-permute-done.32.refs_19_), channel_id=1, source_target_pairs={{0,16},{16,0},{1,17},{17,1},{2,18},{18,2},{3,19},{19,3},{4,20},{20... | collective-permute-start | bytes 3145736 | tf_op jit(solution)/shard_map/ppermute | solution.py:26
  140.1 12.9 %collective-permute-start.31 = (f32[256,512]{1,0:T(8,128)S(1)}, f32[256,512]{1,0:T(8,128)S(1)}, u32[]{:S(2)}, u32[]{:S(2)}) collective-permute-start(f32[256,512]{1,0:T(8,128)S(1)} %collective-permute-done.30.refs_14_), channel_id=1, source_target_pairs={{0,1},{1,2},{2,3},{3,4},{4,5},{5,6},{6,7},{7,0},{16,23},{17,16},{1... | collective-permute-start | bytes 1572872 | tf_op jit(solution)/shard_map/ppermute | solution.py:34
  156.8 11.5 %collective-permute-start.34 = (f32[256,512]{1,0:T(8,128)S(1)}, f32[256,512]{1,0:T(8,128)S(1)}, u32[]{:S(2)}, u32[]{:S(2)}) collective-permute-start(f32[256,512]{1,0:T(8,128)S(1)} %beta11.2), channel_id=1, source_target_pairs={{0,8},{8,0},{1,9},{9,1},{2,10},{10,2},{3,11},{11,3},{4,12},{12,4},... | collective-permute-start | bytes 1572872 | tf_op jit(solution)/shard_map/ppermute | solution.py:26
  (38 other events, 799.5 us)

commit v4 on v3

--- a/solution.py
+++ b/solution.py
@@ -26,14 +26,14 @@
     return lax.ppermute(value, axis, [(0, 1), (1, 0)])
 
 
-def step(value, axis):
+def step(value, axis, way=1):
     n = lax.axis_size(axis)
     if axis == "z":
-        pairs = [(i, (i + 1) % n) for i in range(n)]
-        pairs += [(n + i, n + (i - 1) % n) for i in range(n)]
+        pairs = [(i, (i + way) % n) for i in range(n)]
+        pairs += [(n + i, n + (i - way) % n) for i in range(n)]
         return lax.ppermute(value, ("core", axis), pairs)
-    pairs = [(2 * i, 2 * ((i + 1) % n)) for i in range(n)]
-    pairs += [(2 * i + 1, 2 * ((i - 1) % n) + 1) for i in range(n)]
+    pairs = [(2 * i, 2 * ((i + way) % n)) for i in range(n)]
+    pairs += [(2 * i + 1, 2 * ((i - way) % n) + 1) for i in range(n)]
     return lax.ppermute(value, (axis, "core"), pairs)
 
 
@@ -54,10 +54,10 @@
     return dot(a_hi, b_hi) + (dot(a_hi, b_lo) + dot(a_lo, b_hi))
 
 
-HOPS = ((5, 4), (7, 7))
-
-
-def plan_kernel(where, alpha_source, alpha_live, beta_source, beta_live, alpha_plan, beta_plan):
+EARLY = (0, 1, 2, 6, 7)
+
+
+def plan_kernel(where, alpha_source, alpha_live, beta_source, beta_live, alpha_plan, beta_plan, picks):
     me, mb = where[0], where[1]
     up = (me & 1) == 0
     for row in range(2):
@@ -79,8 +79,16 @@
             owner = src >> 1
             ahead = (me >> 1) - (owner >> 1)
             hops = jnp.where((owner & 1) == 0, ahead, -ahead) & 3
-            piece = 2 * hops + ((owner ^ me) & 1)
+            piece = hops + 4 * ((owner ^ me) & 1)
             put(alpha_plan, (owner >> 3) ^ (me >> 3), piece * 64 + (src & 1) * 32 + slot)
+
+        src = alpha_source[2 * (me ^ 1) + (slot >> 3), c]
+        owner = src >> 1
+
+        @pl.when(((owner ^ me) & 1) == 0)
+        def _():
+            ahead = (me >> 1) - (owner >> 1)
+            picks[(owner >> 3) ^ (me >> 3), jnp.where(up, ahead, -ahead) & 3] = src & 1
 
         return 0
 
@@ -94,11 +102,12 @@
             y = (owner >> 3) ^ (mb >> 3)
             ahead = mb - owner
             d = jnp.where(up, ahead, -ahead) & 7
-            early = d <= jnp.where(y == 0, HOPS[0][0], HOPS[0][1])
+            early = (y == 0) | (d <= 2) | (d >= 6)
             if target:
                 early = early & (c < SLOTS // 2)
             call = jnp.where(early, 0, 1)
-            put(beta_plan, 2 * call + target, (y * 8 + d) * 64 + (src & 1) * 32 + slot)
+            piece = jnp.where(y == 0, owner & 7, 8 + d)
+            put(beta_plan, 2 * call + target, piece * 64 + (src & 1) * 32 + slot)
 
         return 0
 
@@ -112,8 +121,35 @@
         pl.when(piece == i)(lambda ref=ref: make(ref).start())
 
 
+def pick_kernel(side, picks, *refs):
+    pieces, (out, sem) = refs[:4], refs[4:]
+    copies = [
+        pltpu.make_async_copy(
+            piece.at[pl.ds(pl.multiple_of(picks[side, d] * BS, BS), BS)], out.at[d], sem.at[d]
+        )
+        for d, piece in enumerate(pieces)
+    ]
+    for copy in copies:
+        copy.start()
+    for copy in copies:
+        copy.wait()
+
+
+def pick_call(side, picks, pieces):
+    n = pieces[0].shape[1]
+    return pl.pallas_call(
+        functools.partial(pick_kernel, side),
+        out_shape=jax.ShapeDtypeStruct((4, BS, n), jnp.float32),
+        in_specs=[SMEM] + [ANY] * 4,
+        out_specs=ANY,
+        scratch_shapes=[pltpu.SemaphoreType.DMA((4,))],
+        cost_estimate=pl.CostEstimate(flops=0, bytes_accessed=4 * MIB, transcendentals=0),
+        name=f"pick{side}",
+    )(picks, *pieces)
+
+
 def alpha_kernel(side, plan, *refs):
-    pieces, own, refs = refs[:8], refs[8], refs[9:]
+    pieces, picked, own, refs = refs[:4], refs[4], refs[5], refs[6:]
     before, refs = (refs[:1], refs[1:]) if side else ((), refs)
     out, data, tiles, data_sem, tile_sem, out_sem = refs
     count = plan[side, 0]
@@ -124,14 +160,16 @@
     def tile_of(k, slot):
         return pltpu.make_async_copy(own.at[slot >> 3, slot & 7], tiles.at[k], tile_sem.at[k])
 
-    def rows_of(k, ref, block):
-        first = pl.multiple_of(block * BS, BS)
-        return pltpu.make_async_copy(ref.at[pl.ds(first, BS)], data.at[k], data_sem.at[k])
+    def rows_of(k, ref):
+        return pltpu.make_async_copy(ref, data.at[k], data_sem.at[k])
 
     def fetch(k, _):
         word = plan[side, k + 1]
+        piece = word >> 6
         tile_of(k, word & 31).start()
-        start_one_of(pieces, word >> 6, lambda ref: rows_of(k, ref, (word >> 5) & 1))
+        rows = pl.ds(pl.multiple_of(((word >> 5) & 1) * BS, BS), BS)
+        start_one_of(pieces, piece, lambda ref: rows_of(k, ref.at[rows]))
+        pl.when(piece >= 4)(lambda: rows_of(k, picked.at[piece & 3]).start())
         return 0
 
     lax.fori_loop(0, count, fetch, 0)
@@ -143,7 +181,7 @@
     def product(k, _):
         slot = plan[side, k + 1] & 31
         tile_of(k, slot).wait()
-        rows_of(k, pieces[0], 0).wait()
+        rows_of(k, picked.at[0]).wait()
         rows = pl.multiple_of((slot >> 3) * BS, BS)
         out[pl.ds(rows, BS), :] += dot3(tiles[k], data[k])
         return 0
@@ -151,12 +189,12 @@
     lax.fori_loop(0, count, product, 0)
 
 
-def alpha_call(side, plan, pieces, own, before=()):
+def alpha_call(side, plan, pieces, picked, own, before=()):
     n = own.shape[0] * BS
     return pl.pallas_call(
         functools.partial(alpha_kernel, side),
         out_shape=jax.ShapeDtypeStruct((n, n), jnp.float32),
-        in_specs=[SMEM] + [HBM] * 9 + [ANY] * len(before),
+        in_specs=[SMEM] + [HBM] * 6 + [ANY] * len(before),
         out_specs=VMEM,
         scratch_shapes=[
             pltpu.VMEM((SLOTS, BS, n), jnp.float32),
@@ -170,12 +208,20 @@
             flops=8 * 12 * BS**3, bytes_accessed=8 * MIB, transcendentals=0
         ),
         name=f"alpha{side}",
-    )(plan, *in_hbm(*pieces, own), *before)
+    )(plan, *in_hbm(*pieces, picked, own), *before)
+
+
+def which_pieces(call, targets):
+    if not call:
+        return True, EARLY
+    if 1 in targets:
+        return True, tuple(range(8))
+    return False, (3, 4, 5)
 
 
 def beta_kernel(call, targets, where, plan, *refs):
-    hops = HOPS[call]
-    numbers = [d for d in range(hops[0] + 1)] + [8 + d for d in range(hops[1] + 1)]
+    has_ring, numbers = which_pieces(call, targets)
+    ring, refs = (refs[0], refs[1:]) if has_ring else (None, refs)
     pieces, refs = dict(zip(numbers, refs)), refs[len(numbers) :]
     own, refs = refs[0], refs[1:]
     par, refs = refs[: 2 * call + 2], refs[2 * call + 2 :]
@@ -203,8 +249,13 @@
             word = plan[row, j + 1]
             k = base + j
             slot = word & 31
+            piece = word >> 6
+            if has_ring:
+                pl.when(piece < 8)(
+                    lambda: columns_of(k, ring.at[piece & 7], (word >> 5) & 1).start()
+                )
             for number, ref in pieces.items():
-                pl.when((word >> 6) == number)(
+                pl.when(piece == 8 + number)(
                     lambda ref=ref: columns_of(k, ref, (word >> 5) & 1).start()
                 )
             if target == 0:
@@ -228,7 +279,7 @@
         def product(j, _, out=out, row=row, base=base):
             k = base + j
             slot = plan[row, j + 1] & 31
-            columns_of(k, pieces[0], 0).wait()
+            columns_of(k, pieces[3 if call else 0], 0).wait()
             tile_from(k, own.at[0, 0]).wait()
             columns = pl.multiple_of((slot >> 3) * BS, BS)
             out[:, pl.ds(columns, BS)] += dot3(data[k], tiles[k])
@@ -238,9 +289,10 @@
         base = base + plan[row, 0]
 
 
-def beta_call(call, targets, where, plan, chains, own, par, before=()):
-    rows, n = chains[0][0].shape
-    pieces = chains[0][: HOPS[call][0] + 1] + chains[1][: HOPS[call][1] + 1]
+def beta_call(call, targets, where, plan, ring, held, own, par, before=()):
+    rows, n = held[0].shape
+    has_ring, numbers = which_pieces(call, targets)
+    pieces = [ring] * has_ring + [held[i] for i in numbers]
     most = 2 * SLOTS * len(targets)
     return pl.pallas_call(
         functools.partial(beta_kernel, call, targets),
@@ -301,74 +353,56 @@
     core = lax.axis_index("core")
     ylo = lax.axis_index("ylo")
     where = jnp.stack([lax.axis_index(ALPHA), lax.axis_index(BETA)]).astype(jnp.int32)
-    alpha_plan, beta_plan = pl.pallas_call(
+    alpha_plan, beta_plan, picks = pl.pallas_call(
         plan_kernel,
         out_shape=[
             jax.ShapeDtypeStruct((2, 16), jnp.int32),
             jax.ShapeDtypeStruct((4, 32), jnp.int32),
+            jax.ShapeDtypeStruct((2, 4), jnp.int32),
         ],
         in_specs=[SMEM] * 5,
-        out_specs=[SMEM] * 2,
+        out_specs=[SMEM] * 3,
         name="plan",
     )(where, alpha_source, alpha_live, beta_source, beta_live)
 
-    a = [lax.dynamic_slice_in_dim(coeffs, ylo * BS, BS, 0)]
+    keep = lax.dynamic_slice_in_dim(coeffs, ylo * BS, BS, 0)
     give = lax.dynamic_slice_in_dim(coeffs, (1 - ylo) * BS, BS, 0)
-    b = [swap(give, "ylo")]
-    a.append(step(a[0], "z"))
-    u = [coeffs, step(coeffs, "x")]
-    v = [swap(after(coeffs, b[0]), "yhi")]
-    us = [swap(coeffs, "core")]
+    ring = lax.all_gather(keep, "z")
+    p = swap(give, "ylo")
     mine = lax.dynamic_index_in_dim(beta_tiles, core, 0, keepdims=False)
-
-    b.append(step(b[0], "z"))
-    a.append(step(after(a[1], b[0], us[0], alpha_plan), "z"))
-    u.append(step(after(u[1], b[0], a[1]), "x"))
-    us.append(swap(u[1], "core"))
-    b.append(step(b[1], "z"))
-    a.append(step(after(a[2], b[1], u[1]), "z"))
-    u.append(step(after(u[2], b[1], a[2], us[1]), "x"))
-    us.append(swap(u[2], "core"))
-    b.append(step(b[2], "z"))
-    a.append(step(after(a[3], b[2], u[2], us[1]), "z"))
-    got0 = swap(after(mine[: SLOTS // 2], v[0]), "ylo")
-    v.append(step(after(v[0], u[3], b[2], a[3], us[2]), "x"))
-    us.append(swap(u[3], "core"))
-    b.append(step(b[3], "z"))
-    a.append(step(after(a[4], b[3], u[3], v[0], us[2]), "z"))
-    alpha = alpha_call(
-        0,
-        alpha_plan,
-        [p for pair in zip([after(u[0], a[4]), *u[1:]], us) for p in pair],
-        alpha_tiles,
+    uf, ub = step(coeffs, "x"), step(coeffs, "x", -1)
+    f1, b1 = step(p, "z"), step(p, "z", -1)
+    v = swap(after(coeffs, p), "yhi")
+    f1, b1, uf, ub, v, picks = lax.optimization_barrier((f1, b1, uf, ub, v, picks))
+    f2, b2 = step(f1, "z"), step(b1, "z", -1)
+    u2 = step(uf, "x")
+    got0 = swap(after(mine[: SLOTS // 2], v), "ylo")
+    f2, b2, u2, got0 = lax.optimization_barrier((f2, b2, u2, got0))
+    f3, b3 = step(f2, "z"), step(b2, "z", -1)
+    vf, vb = step(after(v, f2), "x"), step(after(v, f2), "x", -1)
+    u_picked = swap(pick_call(0, picks, [coeffs, uf, u2, ub]), "core")
+    alpha = alpha_call(0, alpha_plan, [coeffs, uf, u2, ub], u_picked, alpha_tiles)
+    got1 = swap(after(mine[SLOTS // 2 :], got0, u_picked), "ylo")
+    f3, b3, vf, vb, alpha, got1, ring = lax.optimization_barrier(
+        (f3, b3, vf, vb, alpha, got1, ring)
     )
-    vs = [swap(v[0], "core")]
-    v.append(step(v[1], "x"))
-    vs.append(swap(v[1], "core"))
-    b.append(step(b[4], "z"))
-    a.append(step(after(a[5], b[4], v[1], alpha, vs[0]), "z"))
+    f4 = step(f3, "z")
+    v2 = step(vf, "x")
     oth0 = swap(got0, "core")
-    got1 = swap(after(mine[SLOTS // 2 :], got0), "ylo")
-    v.append(step(v[2], "x"))
-    vs.append(swap(v[2], "core"))
-    b.append(step(b[5], "z"))
-    a.append(step(after(a[6], b[5], v[2], oth0, vs[1]), "z"))
+    held = [p, f1, f2, f3, f4, b3, b2, b1]
     beta_own, beta_par = beta_call(
-        0, (0, 1), where, beta_plan, (a, b), after(beta_tiles, b[5]), [got0, oth0]
+        0, (0, 1), where, beta_plan, ring, held, after(beta_tiles, f3), [got0, oth0]
     )
+    v_picked = swap(pick_call(1, picks, [v, vf, after(v2, f4), vb]), "core")
     oth1 = swap(got1, "core")
-    vs.append(swap(v[3], "core"))
-    b.append(step(after(b[6], beta_own, vs[2]), "z"))
-    alpha = alpha_call(
-        1, alpha_plan, [p for pair in zip(v, vs) for p in pair], alpha_tiles, [alpha]
-    )
+    alpha = alpha_call(1, alpha_plan, [v, vf, v2, vb], v_picked, alpha_tiles, [alpha])
     par = [got0, oth0, got1, oth1]
     (beta_par,) = beta_call(
-        1, (1,), where, beta_plan, (a, b), after(beta_tiles, alpha), par, [beta_par]
+        1, (1,), where, beta_plan, ring, held, after(beta_tiles, alpha), par, [beta_par]
     )
     beta_other = swap(beta_par, "ylo")
     (beta_own,) = beta_call(
-        1, (0,), where, beta_plan, (a, b), after(beta_tiles, beta_par), par, [beta_own]
+        1, (0,), where, beta_plan, ring, held, after(beta_tiles, beta_par), par, [beta_own]
     )
 
     joined = pl.pallas_call(

time: 175 us -> 313 us (1.79)
  Pallas kernels: 27.9 us -> 157 us
  starting transfers between devices: 68.1 us -> 30.6 us
  waiting for transfers between devices: 61.2 us -> 91.1 us
  between operations: 0.53 us -> 13.6 us
  local copies, waits for them, and re-layouts: 13.7 us -> 18.8 us
    pallas_call x0 -> x2, Pallas kernels: none -> 131 us  [pick_call(): pl.pallas_call(functools.partial(pick_kernel, side), out_shape=jax.ShapeD...]
    ppermute x14 -> x7, waiting for transfers between devices: 27.2 us -> 57.6 us  [step(): return lax.ppermute(value, ('core', axis), pairs)]
    ppermute x14 -> x7, starting transfers between devices: 35.9 us -> 10.5 us  [step(): return lax.ppermute(value, ('core', axis), pairs)]
    ppermute x6, starting transfers between devices: 14.8 us -> 7.9 us  [step(): return lax.ppermute(value, (axis, 'core'), pairs)]
    ppermute x15 -> x9, starting transfers between devices: 17.3 us -> 12.3 us  [swap(): return lax.ppermute(value, axis, [(0, 1), (1, 0)])]
    unnamed x74 -> x42, local copies, waits for them, and re-layouts: 9.93 us -> 13.2 us
    ppermute x15 -> x9, waiting for transfers between devices: 26.7 us -> 23.5 us  [swap(): return lax.ppermute(value, axis, [(0, 1), (1, 0)])]
  transfers between devices with their start and end apart: 35 -> 23, of which waited for: 12 -> 15; matrix products, arithmetic and copies ran while one was open for 6% -> 3% of each run, Pallas kernels for 13% -> 28%
where the time goes in v4:
time: 313 us; the launch traced here: 312 us
  Pallas kernels  157 us (50%)
  waiting for transfers between devices  91.1 us (29%)
  starting transfers between devices  30.6 us (10%)
  local copies, waits for them, and re-layouts  18.8 us (6%)
  between operations  13.6 us (4%)
    pallas_call x2, Pallas kernels, pick_call(): pl.pallas_call(functools.partial(pick_kernel, side), out_shape=jax.ShapeD...  131 us
    ppermute x7, waiting for transfers between devices, step(): return lax.ppermute(value, ('core', axis), pairs)  57.6 us
    ppermute x9, waiting for transfers between devices, swap(): return lax.ppermute(value, axis, [(0, 1), (1, 0)])  23.5 us
    unnamed x42, local copies, waits for them, and re-layouts  13.2 us
    ppermute x9, starting transfers between devices, swap(): return lax.ppermute(value, axis, [(0, 1), (1, 0)])  12.3 us
    pallas_call x3, Pallas kernels, beta_call(): pl.pallas_call(functools.partial(beta_kernel, call, targets), out_shape=[...  11.1 us
    ppermute x7, starting transfers between devices, step(): return lax.ppermute(value, ('core', axis), pairs)  10.5 us
    ppermute x6, waiting for transfers between devices, step(): return lax.ppermute(value, (axis, 'core'), pairs)  10.1 us
  transfers between devices with their start and end apart: 23, of which 15 were waited for; matrix products, arithmetic and copies ran while one was open for 3% of the time, Pallas kernels for 28%

profile of v4, /device:TPU:1, one launch (start us, length us, event | category | flops | bytes accessed | tf_op | source)
XLA Modules:
  0.0 312.2 jit_solution(14479001167865033681)
XLA Ops:
  6.5 2.1 constant_dynamic-slice_fusion
  8.6 2.2 collective-permute-start
  10.9 2.5 collective-permute-start.3
  13.3 7.9 %collective-permute-done.refs_1_ = f32[256,512]{1,0:T(8,128)S(1)} collective-permute-done((f32[256,512]{1,0:T(8,128)S(1)}, f32[256,512]{1,0:T(8,128)S(1)}, u32[]{:S(2)}, u32[]{:S(2)}) %collective-permute-start) | collective-permute-done | bytes 524320 | tf_op jit(solution)/shard_map/ppermute | solution.py:26
  21.3 4.0 %collective-permute-start.5 = (f32[512,512]{1,0:T(8,128)}, f32[512,512]{1,0:T(8,128)}, u32[]{:S(2)}, u32[]{:S(2)}) collective-permute-start(f32[512,512]{1,0:T(8,128)} %x.1), channel_id=1, source_target_pairs={{0,128},{128,0},{1,129},{129,1},{2,130},{130,2},{3,131},{131,3},{4... | collective-permute-start | bytes 3145736 | tf_op jit(solution)/shard_map/ppermute | solution.py:26
  25.3 5.6 %collective-permute-start.1 = (f32[256,512]{1,0:T(8,128)S(1)}, f32[256,512]{1,0:T(8,128)S(1)}, u32[]{:S(2)}, u32[]{:S(2)}) collective-permute-start(f32[256,512]{1,0:T(8,128)S(1)} %collective-permute-done.refs_1_), channel_id=1, source_target_pairs={{0,1},{1,2},{2,3},{3,4},{4,5},{5,6},{6,7},{7,0},{16,23},{17,16},{1... | collective-permute-start | bytes 1572872 | tf_op jit(solution)/shard_map/ppermute | solution.py:34
  36.9 3.7 %plan.1 = (s32[2,16]{1,0:T(2,128)}, s32[4,32]{1,0:T(4,128)}, s32[2,4]{1,0:T(2,128)}) custom-call(s32[2]{0:T(128)} %pad_add_fusion.where, s32[32,8]{1,0:T(8,128)} %copy.15.alpha_source, s32[32,8]{1,0:T(8,128)} %copy.16.alpha_live, s32[32,8]{1,0:T(8,128)} %copy.17.beta_source, s32[32,8]{1,0:T(8,128)} %copy.18.beta_live), custom_call_target="tpu_custom_call" | custom-call | tf_op jit(solution)/shard_map/plan/pallas_call | solution.py:356
  40.7 2.7 dynamic-slice_bitcast_fusion
  43.4 9.3 %collective-permute-done.1.refs_2_ = f32[256,512]{1,0:T(8,128)S(1)} collective-permute-done((f32[256,512]{1,0:T(8,128)S(1)}, f32[256,512]{1,0:T(8,128)S(1)}, u32[]{:S(2)}, u32[]{:S(2)}) %collective-permute-start.1) | collective-permute-done | bytes 524320 | tf_op jit(solution)/shard_map/ppermute | solution.py:34
  52.8 4.3 %collective-permute-done.2.refs_5_.refs_8_ = f32[256,512]{1,0:T(8,128)} collective-permute-done((f32[256,512]{1,0:T(8,128)S(1)}, f32[256,512]{1,0:T(8,128)}, u32[]{:S(2)}, u32[]{:S(2)}) %collective-permute-start.2) | collective-permute-done | bytes 524320 | tf_op jit(solution)/shard_map/ppermute | solution.py:34
  57.1 2.6 collective-permute-start.8
  61.5 23.7 %collective-permute-done.6.refs_3_ = f32[256,512]{1,0:T(8,128)S(1)} collective-permute-done((f32[256,512]{1,0:T(8,128)S(1)}, f32[256,512]{1,0:T(8,128)S(1)}, u32[]{:S(2)}, u32[]{:S(2)}) %collective-permute-start.6) | collective-permute-done | bytes 524320 | tf_op jit(solution)/shard_map/ppermute | solution.py:34
  88.3 65.4 %pick0.1 = f32[4,256,512]{2,1,0:T(8,128)} custom-call(s32[2,4]{1,0:T(2,128)} %get-tuple-element.48.picks, f32[512,512]{1,0:T(8,128)} %x.1, f32[512,512]{1,0:T(8,128)} %copy-done.8, f32[512,512]{1,0:T(8,128)} %copy-done.10, f32[512,512]{1,0:T(8,128)} %copy-done.9), custom_call_target="tpu_custom_call" | custom-call | bytes 4194304 | tf_op jit(solution)/shard_map/pick0/pallas_call | solution.py:140
  155.5 2.6 collective-permute-done.14.refs_4_
  160.8 2.6 alpha0.1.refs_6_
  163.4 9.1 %collective-permute-done.10.refs_4_.refs_0_ = f32[256,512]{1,0:T(8,128)} collective-permute-done((f32[256,512]{1,0:T(8,128)}, f32[256,512]{1,0:T(8,128)}, u32[]{:S(2)}, u32[]{:S(2)}) %collective-permute-start.10) | collective-permute-done | bytes 524320 | tf_op jit(solution)/shard_map/ppermute | solution.py:34
  172.5 3.0 collective-permute-done.11.refs_6_.refs_2_
  175.5 2.1 collective-permute-done.12.refs_1_
  177.6 3.5 %collective-permute-done.13.refs_3_ = f32[512,512]{1,0:T(8,128)} collective-permute-done((f32[512,512]{1,0:T(8,128)}, f32[512,512]{1,0:T(8,128)}, u32[]{:S(2)}, u32[]{:S(2)}) %collective-permute-start.13) | collective-permute-done | bytes 1048608 | tf_op jit(solution)/shard_map/ppermute | solution.py:37
  181.1 1.9 collective-permute-done.15.refs_12_.refs_6_
  186.0 6.8 %collective-permute-done.17.refs_5_.refs_1_ = f32[256,512]{1,0:T(8,128)} collective-permute-done((f32[256,512]{1,0:T(8,128)}, f32[256,512]{1,0:T(8,128)}, u32[]{:S(2)}, u32[]{:S(2)}) %collective-permute-start.17) | collective-permute-done | bytes 524320 | tf_op jit(solution)/shard_map/ppermute | solution.py:34
  192.8 4.5 %collective-permute-done.16.refs_2_ = f32[512,512]{1,0:T(8,128)} collective-permute-done((f32[512,512]{1,0:T(8,128)}, f32[512,512]{1,0:T(8,128)}, u32[]{:S(2)}, u32[]{:S(2)}) %collective-permute-start.16) | collective-permute-done | bytes 1048608 | tf_op jit(solution)/shard_map/ppermute | solution.py:37
  197.3 65.4 %pick1.1 = f32[4,256,512]{2,1,0:T(8,128)} custom-call(s32[2,4]{1,0:T(2,128)} %get-tuple-element.48.picks, f32[512,512]{1,0:T(8,128)} %collective-permute-done.5.refs_0_, f32[512,512]{1,0:T(8,128)} %collective-permute-done.12.refs_1_, f32[512,512]{1,0:T(8,128)} %collective-permute-done.16.refs_2_, f32[512,512]{1,0:T(8,128)} %collective-permute-done.13.refs_3_), custom_call_target="tpu_custom_call" | custom-call | bytes 4194304 | tf_op jit(solution)/shard_map/pick1/pallas_call | solution.py:140
  262.7 3.1 collective-permute-start.18
  266.3 6.1 %collective-permute-done.19.refs_8_.refs_11_.refs_5_ = f32[4,256,256]{2,1,0:T(8,128)S(1)} collective-permute-done((f32[4,256,256]{2,1,0:T(8,128)S(1)}, f32[4,256,256]{2,1,0:T(8,128)S(1)}, u32[]{:S(2)}, u32[]{:S(2)}) %collective-permute-start.19) | collective-permute-done | bytes 1048608 | tf_op jit(solution)/shard_map/ppermute | solution.py:26
  273.4 5.6 %beta02.1 = (f32[256,512]{1,0:T(8,128)S(1)}, f32[256,512]{1,0:T(8,128)S(1)}) custom-call(s32[2]{0:T(128)S(1)} %copy-done.2, s32[4,32]{1,0:T(4,128)S(1)} %copy-done.3, f32[8,256,512]{2,1,0:T(8,128)} %bitcast.9, f32[256,512]{1,0:T(8,128)} %copy-done.12, f32[256,512]{1,0:T(8,128)} %copy-done.13, f32[256,512]{1,0:T(8,128)} %copy-done.14, f32[256,512]{1,0:T(8,128)} %copy-done.15, ...), custom_call_target="tpu_custom_call" | custom-call | flops 1610612736 | bytes 6291456 | tf_op jit(solution)/shard_map/beta02/pallas_call | solution.py:297
  280.4 3.4 %alpha1.1.alpha = f32[512,512]{1,0:T(8,128)S(1)} custom-call(s32[2,16]{1,0:T(2,128)S(1)} %copy-done.4, f32[512,512]{1,0:T(8,128)} %collective-permute-done.5.refs_0_, f32[512,512]{1,0:T(8,128)} %collective-permute-done.12.refs_1_, f32[512,512]{1,0:T(8,128)} %collective-permute-done.16.refs_2_, f32[512,512]{1,0:T(8,128)} %collective-permute-done.13.refs_3_, ...), custom_call_target="tpu_custom_call" | custom-call | flops 1610612736 | bytes 8388608 | tf_op jit(solution)/shard_map/alpha1/pallas_call | solution.py:194
  285.8 3.4 %beta11.2 = f32[256,512]{1,0:T(8,128)S(1)} custom-call(s32[2]{0:T(128)S(1)} %copy-done.2, s32[4,32]{1,0:T(4,128)S(1)} %copy-done.3, f32[8,256,512]{2,1,0:T(8,128)} %bitcast.10, f32[256,512]{1,0:T(8,128)} %copy-done.12, f32[256,512]{1,0:T(8,128)} %copy-done.13, f32[256,512]{1,0:T(8,128)} %copy-done.14, f32[256,512]{1,0:T(8,128)} %collective-permute-done.10.refs_4_.refs_0_, ...), custom_call_target="tpu_custom_call" | custom-call | flops 805306368 | bytes 6291456 | tf_op jit(solution)/shard_map/beta11/pallas_call | solution.py:297
  290.9 2.2 beta11.3.beta
  293.9 3.0 join.1.joined
  296.9 4.9 %collective-permute-done.21.beta_other = f32[256,512]{1,0:T(8,128)S(1)} collective-permute-done((f32[256,512]{1,0:T(8,128)S(1)}, f32[256,512]{1,0:T(8,128)S(1)}, u32[]{:S(2)}, u32[]{:S(2)}) %collective-permute-start.21) | collective-permute-done | bytes 524320 | tf_op jit(solution)/shard_map/ppermute | solution.py:26
  302.6 2.7 last.1
  (71 shorter events, 26.7 us)
Async XLA Ops:
  6.5 176.5 %all-gather.3.cloned.1.call-start = ((), (), s32[]{:S(2)}) async-start(), calls=%async_computation | async-start | bytes 4718592 | tf_op jit(solution)/shard_map/all_gather | solution.py:370
  8.6 12.6 %collective-permute-start = (f32[256,512]{1,0:T(8,128)S(1)}, f32[256,512]{1,0:T(8,128)S(1)}, u32[]{:S(2)}, u32[]{:S(2)}) collective-permute-start(f32[256,512]{1,0:T(8,128)S(1)} %get-tuple-element.68), channel_id=1, source_target_pairs={{0,8},{8,0},{1,9},{9,1},{2,10},{10,2},{3,11},{11,3},{4,12},{12,4},... | collective-permute-start | bytes 1572872 | tf_op jit(solution)/shard_map/ppermute | solution.py:26
  10.9 46.2 %collective-permute-start.3 = (f32[512,512]{1,0:T(8,128)}, f32[512,512]{1,0:T(8,128)S(1)}, u32[]{:S(2)}, u32[]{:S(2)}) collective-permute-start(f32[512,512]{1,0:T(8,128)} %x.1), channel_id=1, source_target_pairs={{0,32},{32,64},{64,96},{96,0},{16,112},{48,16},{80,48},{112,80},{1... | collective-permute-start | bytes 3145736 | tf_op jit(solution)/shard_map/ppermute | solution.py:37
  13.3 43.8 %collective-permute-start.4 = (f32[512,512]{1,0:T(8,128)}, f32[512,512]{1,0:T(8,128)S(1)}, u32[]{:S(2)}, u32[]{:S(2)}) collective-permute-start(f32[512,512]{1,0:T(8,128)} %x.1), channel_id=1, source_target_pairs={{0,96},{32,0},{64,32},{96,64},{16,48},{48,80},{80,112},{112,16},{1... | collective-permute-start | bytes 3145736 | tf_op jit(solution)/shard_map/ppermute | solution.py:37
  21.3 132.4 %copy-start.12 = (f32[256,512]{1,0:T(8,128)}, f32[256,512]{1,0:T(8,128)S(1)}, u32[]{:S(2)}) copy-start(f32[256,512]{1,0:T(8,128)S(1)} %collective-permute-done.refs_1_) | copy-start | bytes 1572868
  21.3 35.8 %collective-permute-start.5 = (f32[512,512]{1,0:T(8,128)}, f32[512,512]{1,0:T(8,128)}, u32[]{:S(2)}, u32[]{:S(2)}) collective-permute-start(f32[512,512]{1,0:T(8,128)} %x.1), channel_id=1, source_target_pairs={{0,128},{128,0},{1,129},{129,1},{2,130},{130,2},{3,131},{131,3},{4... | collective-permute-start | bytes 3145736 | tf_op jit(solution)/shard_map/ppermute | solution.py:26
  25.3 27.5 %collective-permute-start.1 = (f32[256,512]{1,0:T(8,128)S(1)}, f32[256,512]{1,0:T(8,128)S(1)}, u32[]{:S(2)}, u32[]{:S(2)}) collective-permute-start(f32[256,512]{1,0:T(8,128)S(1)} %collective-permute-done.refs_1_), channel_id=1, source_target_pairs={{0,1},{1,2},{2,3},{3,4},{4,5},{5,6},{6,7},{7,0},{16,23},{17,16},{1... | collective-permute-start | bytes 1572872 | tf_op jit(solution)/shard_map/ppermute | solution.py:34
  30.8 26.2 %collective-permute-start.2 = (f32[256,512]{1,0:T(8,128)S(1)}, f32[256,512]{1,0:T(8,128)}, u32[]{:S(2)}, u32[]{:S(2)}) collective-permute-start(f32[256,512]{1,0:T(8,128)S(1)} %collective-permute-done.refs_1_), channel_id=1, source_target_pairs={{0,7},{1,0},{2,1},{3,2},{4,3},{5,4},{6,5},{7,6},{16,17},{17,18},{1... | collective-permute-start | bytes 1572872 | tf_op jit(solution)/shard_map/ppermute | solution.py:34
  43.4 117.4 %copy-start.4 = (s32[2,16]{1,0:T(2,128)S(1)}, s32[2,16]{1,0:T(2,128)}, u32[]{:S(2)}) copy-start(s32[2,16]{1,0:T(2,128)} %get-tuple-element.35.plan) | copy-start | bytes 388
  52.7 219.7 %copy-start.13 = (f32[256,512]{1,0:T(8,128)}, f32[256,512]{1,0:T(8,128)S(1)}, u32[]{:S(2)}) copy-start(f32[256,512]{1,0:T(8,128)S(1)} %collective-permute-done.1.refs_2_) | copy-start | bytes 1572868
  57.1 31.2 %copy-start.8 = (f32[512,512]{1,0:T(8,128)}, f32[512,512]{1,0:T(8,128)S(1)}, u32[]{:S(2)}) copy-start(f32[512,512]{1,0:T(8,128)S(1)} %collective-permute-done.3.refs_1_) | copy-start | bytes 3145732
  57.1 29.4 %collective-permute-start.8 = (f32[512,512]{1,0:T(8,128)S(1)}, f32[512,512]{1,0:T(8,128)S(1)}, u32[]{:S(2)}, u32[]{:S(2)}) collective-permute-start(f32[512,512]{1,0:T(8,128)S(1)} %collective-permute-done.3.refs_1_), channel_id=1, source_target_pairs={{0,32},{32,64},{64,96},{96,0},{16,112},{48,16},{80,48},{112,80},{1... | collective-permute-start | bytes 3145736 | tf_op jit(solution)/shard_map/ppermute | solution.py:37
  59.7 28.6 %collective-permute-start.9 = (f32[4,256,256]{2,1,0:T(8,128)S(1)}, f32[4,256,256]{2,1,0:T(8,128)S(1)}, u32[]{:S(2)}, u32[]{:S(2)}) collective-permute-start(f32[4,256,256]{2,1,0:T(8,128)S(1)} %get-tuple-element.42), channel_id=1, source_target_pairs={{0,8},{8,0},{1,9},{9,1},{2,10},{10,2},{3,11},{11,3},{4,12},{12,4},... | collective-permute-start | bytes 3145736 | tf_op jit(solution)/shard_map/ppermute | solution.py:26
  60.1 25.1 %collective-permute-start.6 = (f32[256,512]{1,0:T(8,128)S(1)}, f32[256,512]{1,0:T(8,128)S(1)}, u32[]{:S(2)}, u32[]{:S(2)}) collective-permute-start(f32[256,512]{1,0:T(8,128)S(1)} %collective-permute-done.1.refs_2_), channel_id=1, source_target_pairs={{0,1},{1,2},{2,3},{3,4},{4,5},{5,6},{6,7},{7,0},{16,23},{17,16},{1... | collective-permute-start | bytes 1572872 | tf_op jit(solution)/shard_map/ppermute | solution.py:34
  60.1 26.4 %collective-permute-start.7 = (f32[256,512]{1,0:T(8,128)}, f32[256,512]{1,0:T(8,128)S(1)}, u32[]{:S(2)}, u32[]{:S(2)}) collective-permute-start(f32[256,512]{1,0:T(8,128)} %collective-permute-done.2.refs_5_.refs_8_), channel_id=1, source_target_pairs={{0,7},{1,0},{2,1},{3,2},{4,3},{5,4},{6,5},{7,6},{16,17},{17,18},{1... | collective-permute-start | bytes 1572872 | tf_op jit(solution)/shard_map/ppermute | solution.py:34
  88.3 177.5 %copy-start.5 = (f32[4,256,256]{2,1,0:T(8,128)}, f32[4,256,256]{2,1,0:T(8,128)S(1)}, u32[]{:S(2)}) copy-start(f32[4,256,256]{2,1,0:T(8,128)S(1)} %collective-permute-done.9.refs_7_.refs_10_.refs_4_) | copy-start | bytes 3145732
  153.7 4.5 %collective-permute-start.14 = (f32[4,256,512]{2,1,0:T(8,128)}, f32[4,256,512]{2,1,0:T(8,128)S(1)}, u32[]{:S(2)}, u32[]{:S(2)}) collective-permute-start(f32[4,256,512]{2,1,0:T(8,128)} %pick0.1), channel_id=1, source_target_pairs={{0,16},{16,0},{1,17},{17,1},{2,18},{18,2},{3,19},{19,3},{4,20},{20... | collective-permute-start | bytes 6291464 | tf_op jit(solution)/shard_map/ppermute | solution.py:26
  153.8 23.9 %collective-permute-start.12 = (f32[512,512]{1,0:T(8,128)}, f32[512,512]{1,0:T(8,128)}, u32[]{:S(2)}, u32[]{:S(2)}) collective-permute-start(f32[512,512]{1,0:T(8,128)} %collective-permute-done.5.refs_0_), channel_id=1, source_target_pairs={{0,32},{32,64},{64,96},{96,0},{16,112},{48,16},{80,48},{112,80},{1... | collective-permute-start | bytes 3145736 | tf_op jit(solution)/shard_map/ppermute | solution.py:37
  155.5 25.6 %collective-permute-start.13 = (f32[512,512]{1,0:T(8,128)}, f32[512,512]{1,0:T(8,128)}, u32[]{:S(2)}, u32[]{:S(2)}) collective-permute-start(f32[512,512]{1,0:T(8,128)} %collective-permute-done.5.refs_0_), channel_id=1, source_target_pairs={{0,96},{32,0},{64,32},{96,64},{16,48},{48,80},{80,112},{112,16},{1... | collective-permute-start | bytes 3145736 | tf_op jit(solution)/shard_map/ppermute | solution.py:37
  158.1 2.7 copy-start.16
  158.1 24.9 %collective-permute-start.15 = (f32[4,256,256]{2,1,0:T(8,128)}, f32[4,256,256]{2,1,0:T(8,128)}, u32[]{:S(2)}, u32[]{:S(2)}) collective-permute-start(f32[4,256,256]{2,1,0:T(8,128)} %get-tuple-element.50), channel_id=1, source_target_pairs={{0,8},{8,0},{1,9},{9,1},{2,10},{10,2},{3,11},{11,3},{4,12},{12,4},... | collective-permute-start | bytes 3145736 | tf_op jit(solution)/shard_map/ppermute | solution.py:26
  159.2 13.4 %collective-permute-start.10 = (f32[256,512]{1,0:T(8,128)}, f32[256,512]{1,0:T(8,128)}, u32[]{:S(2)}, u32[]{:S(2)}) collective-permute-start(f32[256,512]{1,0:T(8,128)} %copy-done.14), channel_id=1, source_target_pairs={{0,1},{1,2},{2,3},{3,4},{4,5},{5,6},{6,7},{7,0},{16,23},{17,16},{1... | collective-permute-start | bytes 1572872 | tf_op jit(solution)/shard_map/ppermute | solution.py:34
  160.8 14.7 %collective-permute-start.11 = (f32[256,512]{1,0:T(8,128)}, f32[256,512]{1,0:T(8,128)}, u32[]{:S(2)}, u32[]{:S(2)}) collective-permute-start(f32[256,512]{1,0:T(8,128)} %copy-done.15), channel_id=1, source_target_pairs={{0,7},{1,0},{2,1},{3,2},{4,3},{5,4},{6,5},{7,6},{16,17},{17,18},{1... | collective-permute-start | bytes 1572872 | tf_op jit(solution)/shard_map/ppermute | solution.py:34
  163.4 110.0 %copy-start.2 = (s32[2]{0:T(128)S(1)}, s32[2]{0:T(128)}, u32[]{:S(2)}) copy-start(s32[2]{0:T(128)} %pad_add_fusion.where) | copy-start | bytes 28
  163.4 110.0 %copy-start.3 = (s32[4,32]{1,0:T(4,128)S(1)}, s32[4,32]{1,0:T(4,128)}, u32[]{:S(2)}) copy-start(s32[4,32]{1,0:T(4,128)} %get-tuple-element.56.plan) | copy-start | bytes 1540
  183.1 14.3 %collective-permute-start.16 = (f32[512,512]{1,0:T(8,128)}, f32[512,512]{1,0:T(8,128)}, u32[]{:S(2)}, u32[]{:S(2)}) collective-permute-start(f32[512,512]{1,0:T(8,128)} %collective-permute-done.12.refs_1_), channel_id=1, source_target_pairs={{0,32},{32,64},{64,96},{96,0},{16,112},{48,16},{80,48},{112,80},{1... | collective-permute-start | bytes 3145736 | tf_op jit(solution)/shard_map/ppermute | solution.py:37
  184.2 8.6 %collective-permute-start.17 = (f32[256,512]{1,0:T(8,128)}, f32[256,512]{1,0:T(8,128)}, u32[]{:S(2)}, u32[]{:S(2)}) collective-permute-start(f32[256,512]{1,0:T(8,128)} %collective-permute-done.10.refs_4_.refs_0_), channel_id=1, source_target_pairs={{0,1},{1,2},{2,3},{3,4},{4,5},{5,6},{6,7},{7,0},{16,23},{17,16},{1... | collective-permute-start | bytes 1572872 | tf_op jit(solution)/shard_map/ppermute | solution.py:34
  262.7 16.3 %collective-permute-start.18 = (f32[4,256,512]{2,1,0:T(8,128)}, f32[4,256,512]{2,1,0:T(8,128)S(1)}, u32[]{:S(2)}, u32[]{:S(2)}) collective-permute-start(f32[4,256,512]{2,1,0:T(8,128)} %pick1.1), channel_id=1, source_target_pairs={{0,16},{16,0},{1,17},{17,1},{2,18},{18,2},{3,19},{19,3},{4,20},{20... | collective-permute-start | bytes 6291464 | tf_op jit(solution)/shard_map/ppermute | solution.py:26
  265.8 6.7 %collective-permute-start.19 = (f32[4,256,256]{2,1,0:T(8,128)S(1)}, f32[4,256,256]{2,1,0:T(8,128)S(1)}, u32[]{:S(2)}, u32[]{:S(2)}) collective-permute-start(f32[4,256,256]{2,1,0:T(8,128)S(1)} %collective-permute-done.9.refs_7_.refs_10_.refs_4_), channel_id=1, source_target_pairs={{0,16},{16,0},{1,17},{17,1},{2,18},{18,2},{3,19},{19,3},{4,20},{20... | collective-permute-start | bytes 3145736 | tf_op jit(solution)/shard_map/ppermute | solution.py:26
  265.9 18.9 %collective-permute-start.20 = (f32[4,256,256]{2,1,0:T(8,128)}, f32[4,256,256]{2,1,0:T(8,128)S(1)}, u32[]{:S(2)}, u32[]{:S(2)}) collective-permute-start(f32[4,256,256]{2,1,0:T(8,128)} %collective-permute-done.15.refs_12_.refs_6_), channel_id=1, source_target_pairs={{0,16},{16,0},{1,17},{17,1},{2,18},{18,2},{3,19},{19,3},{4,20},{20... | collective-permute-start | bytes 3145736 | tf_op jit(solution)/shard_map/ppermute | solution.py:26
  285.8 4.2 %copy-start.18 = (f32[512]{0:T(512)S(1)}, f32[512]{0:T(512)}, u32[]{:S(2)}) copy-start(f32[512]{0:T(512)} %param.10) | copy-start | bytes 6148
  289.1 12.6 %collective-permute-start.21 = (f32[256,512]{1,0:T(8,128)S(1)}, f32[256,512]{1,0:T(8,128)S(1)}, u32[]{:S(2)}, u32[]{:S(2)}) collective-permute-start(f32[256,512]{1,0:T(8,128)S(1)} %beta11.2), channel_id=1, source_target_pairs={{0,8},{8,0},{1,9},{9,1},{2,10},{10,2},{3,11},{11,3},{4,12},{12,4},... | collective-permute-start | bytes 1572872 | tf_op jit(solution)/shard_map/ppermute | solution.py:26
  (10 other events, 11.6 us)
Sparse Core Ops, SparseCore 0:
  9.1 81.0 all-gather.2

commit v5 on v4

--- a/solution.py
+++ b/solution.py
@@ -54,9 +54,6 @@
     return dot(a_hi, b_hi) + (dot(a_hi, b_lo) + dot(a_lo, b_hi))
 
 
-EARLY = (0, 1, 2, 6, 7)
-
-
 def plan_kernel(where, alpha_source, alpha_live, beta_source, beta_live, alpha_plan, beta_plan, picks):
     me, mb = where[0], where[1]
     up = (me & 1) == 0
@@ -99,15 +96,9 @@
         def _():
             src = beta_source[row, c]
             owner = src >> 1
-            y = (owner >> 3) ^ (mb >> 3)
-            ahead = mb - owner
-            d = jnp.where(up, ahead, -ahead) & 7
-            early = (y == 0) | (d <= 2) | (d >= 6)
-            if target:
-                early = early & (c < SLOTS // 2)
-            call = jnp.where(early, 0, 1)
-            piece = jnp.where(y == 0, owner & 7, 8 + d)
-            put(beta_plan, 2 * call + target, piece * 64 + (src & 1) * 32 + slot)
+            side = (owner >> 3) ^ (mb >> 3)
+            piece = owner & 7
+            put(beta_plan, 2 * side + target, piece * 64 + (src & 1) * 32 + slot)
 
         return 0
 
@@ -141,7 +132,7 @@
         functools.partial(pick_kernel, side),
         out_shape=jax.ShapeDtypeStruct((4, BS, n), jnp.float32),
         in_specs=[SMEM] + [ANY] * 4,
-        out_specs=ANY,
+        out_specs=VMEM,
         scratch_shapes=[pltpu.SemaphoreType.DMA((4,))],
         cost_estimate=pl.CostEstimate(flops=0, bytes_accessed=4 * MIB, transcendentals=0),
         name=f"pick{side}",
@@ -211,20 +202,10 @@
     )(plan, *in_hbm(*pieces, picked, own), *before)
 
 
-def which_pieces(call, targets):
-    if not call:
-        return True, EARLY
-    if 1 in targets:
-        return True, tuple(range(8))
-    return False, (3, 4, 5)
-
-
 def beta_kernel(call, targets, where, plan, *refs):
-    has_ring, numbers = which_pieces(call, targets)
-    ring, refs = (refs[0], refs[1:]) if has_ring else (None, refs)
-    pieces, refs = dict(zip(numbers, refs)), refs[len(numbers) :]
+    ring, refs = refs[0], refs[1:]
     own, refs = refs[0], refs[1:]
-    par, refs = refs[: 2 * call + 2], refs[2 * call + 2 :]
+    par, refs = refs[:2], refs[2:]
     before, refs = (refs[: len(targets)], refs[len(targets) :]) if call else ((), refs)
     outs, (data, tiles, data_sem, tile_sem, out_sem) = refs[: len(targets)], refs[len(targets) :]
     core = where[0] & 1
@@ -249,20 +230,11 @@
             word = plan[row, j + 1]
             k = base + j
             slot = word & 31
-            piece = word >> 6
-            if has_ring:
-                pl.when(piece < 8)(
-                    lambda: columns_of(k, ring.at[piece & 7], (word >> 5) & 1).start()
-                )
-            for number, ref in pieces.items():
-                pl.when(piece == 8 + number)(
-                    lambda ref=ref: columns_of(k, ref, (word >> 5) & 1).start()
-                )
+            columns_of(k, ring.at[word >> 6], (word >> 5) & 1).start()
             if target == 0:
                 tile_from(k, own.at[slot >> 3, slot & 7]).start()
             else:
-                which = (core ^ (slot >> 3)) + 2 * ((slot >> 2) & 1)
-                start_one_of(par, which, lambda ref: tile_from(k, ref.at[slot & 3]))
+                start_one_of(par, core ^ (slot >> 3), lambda ref: tile_from(k, ref.at[slot & 7]))
             return 0
 
         lax.fori_loop(0, plan[row, 0], fetch, 0)
@@ -279,7 +251,7 @@
         def product(j, _, out=out, row=row, base=base):
             k = base + j
             slot = plan[row, j + 1] & 31
-            columns_of(k, pieces[3 if call else 0], 0).wait()
+            columns_of(k, ring.at[0], 0).wait()
             tile_from(k, own.at[0, 0]).wait()
             columns = pl.multiple_of((slot >> 3) * BS, BS)
             out[:, pl.ds(columns, BS)] += dot3(data[k], tiles[k])
@@ -289,15 +261,13 @@
         base = base + plan[row, 0]
 
 
-def beta_call(call, targets, where, plan, ring, held, own, par, before=()):
-    rows, n = held[0].shape
-    has_ring, numbers = which_pieces(call, targets)
-    pieces = [ring] * has_ring + [held[i] for i in numbers]
+def beta_call(call, targets, where, plan, ring, own, par, before=()):
+    _, rows, n = ring.shape
     most = 2 * SLOTS * len(targets)
     return pl.pallas_call(
         functools.partial(beta_kernel, call, targets),
         out_shape=[jax.ShapeDtypeStruct((rows, n), jnp.float32)] * len(targets),
-        in_specs=[SMEM] * 2 + [HBM] * (len(pieces) + 1 + len(par)) + [ANY] * len(before),
+        in_specs=[SMEM] * 2 + [HBM] * (2 + len(par)) + [ANY] * len(before),
         out_specs=[VMEM] * len(targets),
         scratch_shapes=[
             pltpu.VMEM((most, rows, BS), jnp.float32),
@@ -311,7 +281,7 @@
             flops=8 * 6 * BS**3 * len(targets), bytes_accessed=6 * MIB, transcendentals=0
         ),
         name=f"beta{call}{len(targets)}",
-    )(where, plan, *in_hbm(*pieces, own, *par), *before)
+    )(where, plan, *in_hbm(ring, own, *par), *before)
 
 
 def join_kernel(where, x, da, db, alpha, beta, out):
@@ -353,6 +323,14 @@
     core = lax.axis_index("core")
     ylo = lax.axis_index("ylo")
     where = jnp.stack([lax.axis_index(ALPHA), lax.axis_index(BETA)]).astype(jnp.int32)
+    keep = lax.dynamic_slice_in_dim(coeffs, ylo * BS, BS, 0)
+    give = lax.dynamic_slice_in_dim(coeffs, (1 - ylo) * BS, BS, 0)
+    near = lax.all_gather(keep, "z")
+    p = swap(give, "ylo")
+    far = lax.all_gather(p, "z")
+    mine = lax.dynamic_index_in_dim(beta_tiles, core, 0, keepdims=False)
+    uf, ub = step(coeffs, "x"), step(coeffs, "x", -1)
+    v = swap(after(coeffs, p), "yhi")
     alpha_plan, beta_plan, picks = pl.pallas_call(
         plan_kernel,
         out_shape=[
@@ -363,46 +341,28 @@
         in_specs=[SMEM] * 5,
         out_specs=[SMEM] * 3,
         name="plan",
-    )(where, alpha_source, alpha_live, beta_source, beta_live)
-
-    keep = lax.dynamic_slice_in_dim(coeffs, ylo * BS, BS, 0)
-    give = lax.dynamic_slice_in_dim(coeffs, (1 - ylo) * BS, BS, 0)
-    ring = lax.all_gather(keep, "z")
-    p = swap(give, "ylo")
-    mine = lax.dynamic_index_in_dim(beta_tiles, core, 0, keepdims=False)
-    uf, ub = step(coeffs, "x"), step(coeffs, "x", -1)
-    f1, b1 = step(p, "z"), step(p, "z", -1)
-    v = swap(after(coeffs, p), "yhi")
-    f1, b1, uf, ub, v, picks = lax.optimization_barrier((f1, b1, uf, ub, v, picks))
-    f2, b2 = step(f1, "z"), step(b1, "z", -1)
+    )(after(where, uf), alpha_source, alpha_live, beta_source, beta_live)
+    uf, ub = lax.optimization_barrier((uf, ub))
     u2 = step(uf, "x")
-    got0 = swap(after(mine[: SLOTS // 2], v), "ylo")
-    f2, b2, u2, got0 = lax.optimization_barrier((f2, b2, u2, got0))
-    f3, b3 = step(f2, "z"), step(b2, "z", -1)
-    vf, vb = step(after(v, f2), "x"), step(after(v, f2), "x", -1)
+    got = swap(after(mine, uf), "ylo")
+    u2, v, picks = lax.optimization_barrier((u2, v, picks))
+    vf, vb = step(v, "x"), step(v, "x", -1)
     u_picked = swap(pick_call(0, picks, [coeffs, uf, u2, ub]), "core")
     alpha = alpha_call(0, alpha_plan, [coeffs, uf, u2, ub], u_picked, alpha_tiles)
-    got1 = swap(after(mine[SLOTS // 2 :], got0, u_picked), "ylo")
-    f3, b3, vf, vb, alpha, got1, ring = lax.optimization_barrier(
-        (f3, b3, vf, vb, alpha, got1, ring)
-    )
-    f4 = step(f3, "z")
+    vf, vb, alpha, near = lax.optimization_barrier((vf, vb, alpha, near))
     v2 = step(vf, "x")
-    oth0 = swap(got0, "core")
-    held = [p, f1, f2, f3, f4, b3, b2, b1]
-    beta_own, beta_par = beta_call(
-        0, (0, 1), where, beta_plan, ring, held, after(beta_tiles, f3), [got0, oth0]
-    )
-    v_picked = swap(pick_call(1, picks, [v, vf, after(v2, f4), vb]), "core")
-    oth1 = swap(got1, "core")
+    other = swap(after(got, vf), "core")
+    beta = beta_call(0, (0, 1), where, beta_plan, near, beta_tiles, [got, other])
+    v2, beta_own, beta_par = lax.optimization_barrier((v2, *beta))
+    v_picked = swap(pick_call(1, picks, [v, vf, v2, vb]), "core")
     alpha = alpha_call(1, alpha_plan, [v, vf, v2, vb], v_picked, alpha_tiles, [alpha])
-    par = [got0, oth0, got1, oth1]
+    far = after(far, alpha)
     (beta_par,) = beta_call(
-        1, (1,), where, beta_plan, ring, held, after(beta_tiles, alpha), par, [beta_par]
+        1, (1,), where, beta_plan, far, beta_tiles, [got, other], [beta_par]
     )
     beta_other = swap(beta_par, "ylo")
     (beta_own,) = beta_call(
-        1, (0,), where, beta_plan, ring, held, after(beta_tiles, beta_par), par, [beta_own]
+        1, (0,), where, beta_plan, far, after(beta_tiles, beta_par), [got, other], [beta_own]
     )
 
     joined = pl.pallas_call(

time: 313 us -> 167 us (0.53)
  Pallas kernels: 157 us -> 32.7 us
  starting transfers between devices: 30.6 us -> 18.4 us
  waiting for transfers between devices: 91.1 us -> 83.9 us
    pallas_call x2, Pallas kernels: 131 us -> 7.24 us  [pick_call(): pl.pallas_call(functools.partial(pick_kernel, side), out_shape=jax.ShapeD...]
    ppermute x7 -> x0, waiting for transfers between devices: 57.6 us -> none  [step(): return lax.ppermute(value, ('core', axis), pairs)]
    ppermute x6, waiting for transfers between devices: 10.1 us -> 39.4 us  [step(): return lax.ppermute(value, (axis, 'core'), pairs)]
    ppermute x9 -> x7, waiting for transfers between devices: 23.5 us -> 44.4 us  [swap(): return lax.ppermute(value, axis, [(0, 1), (1, 0)])]
    ppermute x7 -> x0, starting transfers between devices: 10.5 us -> none  [step(): return lax.ppermute(value, ('core', axis), pairs)]
    squeeze x0 -> x1, local copies, waits for them, and re-layouts: none -> 3.21 us  [per_device(): mine = lax.dynamic_index_in_dim(beta_tiles, core, 0, keepdims=False)]
    unnamed x42 -> x44, local copies, waits for them, and re-layouts: 13.2 us -> 10.2 us
    ppermute x9 -> x7, starting transfers between devices: 12.3 us -> 11.1 us  [swap(): return lax.ppermute(value, axis, [(0, 1), (1, 0)])]
  transfers between devices with their start and end apart: 23 -> 15, of which waited for: 15 -> 12; matrix products, arithmetic and copies ran while one was open for 3% -> 4% of each run, Pallas kernels for 28% -> 16%
where the time goes in v5:
time: 167 us; the launch traced here: 166 us
  waiting for transfers between devices  83.9 us (50%)
  Pallas kernels  32.7 us (20%)
  starting transfers between devices  18.4 us (11%)
  local copies, waits for them, and re-layouts  16.4 us (10%)
  between operations  13.6 us (8%)
    ppermute x7, waiting for transfers between devices, swap(): return lax.ppermute(value, axis, [(0, 1), (1, 0)])  44.4 us
    ppermute x6, waiting for transfers between devices, step(): return lax.ppermute(value, (axis, 'core'), pairs)  39.4 us
    ppermute x7, starting transfers between devices, swap(): return lax.ppermute(value, axis, [(0, 1), (1, 0)])  11.1 us
    pallas_call x3, Pallas kernels, beta_call(): pl.pallas_call(functools.partial(beta_kernel, call, targets), out_shape=[...  10.9 us
    unnamed x44, local copies, waits for them, and re-layouts  10.2 us
    pallas_call x2, Pallas kernels, pick_call(): pl.pallas_call(functools.partial(pick_kernel, side), out_shape=jax.ShapeD...  7.24 us
    ppermute x6, starting transfers between devices, step(): return lax.ppermute(value, (axis, 'core'), pairs)  7.15 us
    pallas_call x2, Pallas kernels, alpha_call(): pl.pallas_call(functools.partial(alpha_kernel, side), out_shape=jax.Shape...  5.24 us
  transfers between devices with their start and end apart: 15, of which 12 were waited for; matrix products, arithmetic and copies ran while one was open for 4% of the time, Pallas kernels for 16%

profile of v5, /device:TPU:1, one launch (start us, length us, event | category | flops | bytes accessed | tf_op | source)
XLA Modules:
  0.0 165.5 jit_solution(12250667576563509439)
XLA Ops:
  6.6 2.1 %constant_dynamic-slice_fusion = (f32[256,512]{1,0:T(8,128)}, f32[256,512]{1,0:T(8,128)S(1)}) fusion(f32[512,512]{1,0:T(8,128)} %x.1, s32[]{:T(128)S(6)} %select_n.11, s32[]{:T(128)S(6)} %select_n.10), kind=kLoop, calls=%fused_computation.1 | loop fusion | bytes 2097160 | tf_op jit(solution)/shard_map/dynamic_slice | solution.py:326
  8.8 3.4 %collective-permute-start = (f32[512,512]{1,0:T(8,128)S(1)}, f32[512,512]{1,0:T(8,128)S(1)}, u32[]{:S(2)}, u32[]{:S(2)}) collective-permute-start(f32[512,512]{1,0:T(8,128)S(1)} %copy-done.7), channel_id=1, source_target_pairs={{0,32},{32,64},{64,96},{96,0},{16,112},{48,16},{80,48},{112,80},{1... | collective-permute-start | bytes 3145736 | tf_op jit(solution)/shard_map/ppermute | solution.py:37
  13.5 9.6 %collective-permute-done.3 = f32[256,512]{1,0:T(8,128)S(1)} collective-permute-done((f32[256,512]{1,0:T(8,128)S(1)}, f32[256,512]{1,0:T(8,128)S(1)}, u32[]{:S(2)}, u32[]{:S(2)}) %collective-permute-start.3) | collective-permute-done | bytes 524320 | tf_op jit(solution)/shard_map/ppermute | solution.py:26
  23.9 4.1 %collective-permute-start.4 = (f32[512,512]{1,0:T(8,128)S(1)}, f32[512,512]{1,0:T(8,128)S(1)}, u32[]{:S(2)}, u32[]{:S(2)}) collective-permute-start(f32[512,512]{1,0:T(8,128)S(1)} %copy-done.7), channel_id=1, source_target_pairs={{0,128},{128,0},{1,129},{129,1},{2,130},{130,2},{3,131},{131,3},{4... | collective-permute-start | bytes 3145736 | tf_op jit(solution)/shard_map/ppermute | solution.py:26
  28.0 3.8 %collective-permute-done.refs_1_ = f32[512,512]{1,0:T(8,128)S(1)} collective-permute-done((f32[512,512]{1,0:T(8,128)S(1)}, f32[512,512]{1,0:T(8,128)S(1)}, u32[]{:S(2)}, u32[]{:S(2)}) %collective-permute-start) | collective-permute-done | bytes 1048608 | tf_op jit(solution)/shard_map/ppermute | solution.py:37
  31.8 6.6 %collective-permute-done.1.refs_3_ = f32[512,512]{1,0:T(8,128)} collective-permute-done((f32[512,512]{1,0:T(8,128)S(1)}, f32[512,512]{1,0:T(8,128)}, u32[]{:S(2)}, u32[]{:S(2)}) %collective-permute-start.1) | collective-permute-done | bytes 1048608 | tf_op jit(solution)/shard_map/ppermute | solution.py:37
  41.8 3.6 %plan.1 = (s32[2,16]{1,0:T(2,128)}, s32[4,32]{1,0:T(4,128)}, s32[2,4]{1,0:T(2,128)}) custom-call(s32[2]{0:T(128)} %pad_add_fusion.where, s32[32,8]{1,0:T(8,128)} %copy.15.alpha_source, s32[32,8]{1,0:T(8,128)} %copy.16.alpha_live, s32[32,8]{1,0:T(8,128)} %copy.17.beta_source, s32[32,8]{1,0:T(8,128)} %copy.18.beta_live), custom_call_target="tpu_custom_call" | custom-call | tf_op jit(solution)/shard_map/plan/pallas_call | solution.py:334
  45.4 3.5 %collective-permute-done.4.refs_0_ = f32[512,512]{1,0:T(8,128)S(1)} collective-permute-done((f32[512,512]{1,0:T(8,128)S(1)}, f32[512,512]{1,0:T(8,128)S(1)}, u32[]{:S(2)}, u32[]{:S(2)}) %collective-permute-start.4) | collective-permute-done | bytes 1048608 | tf_op jit(solution)/shard_map/ppermute | solution.py:26
  48.9 3.6 %collective-permute-done.2.refs_2_ = f32[512,512]{1,0:T(8,128)} collective-permute-done((f32[512,512]{1,0:T(8,128)S(1)}, f32[512,512]{1,0:T(8,128)}, u32[]{:S(2)}, u32[]{:S(2)}) %collective-permute-start.2) | collective-permute-done | bytes 1048608 | tf_op jit(solution)/shard_map/ppermute | solution.py:37
  52.5 3.6 %pick0.1 = f32[4,256,512]{2,1,0:T(8,128)} custom-call(s32[2,4]{1,0:T(2,128)} %get-tuple-element.36.picks, f32[512,512]{1,0:T(8,128)} %x.1, f32[512,512]{1,0:T(8,128)} %copy-done.10, f32[512,512]{1,0:T(8,128)} %collective-permute-done.2.refs_2_, f32[512,512]{1,0:T(8,128)} %collective-permute-done.1.refs_3_), custom_call_target="tpu_custom_call" | custom-call | bytes 4194304 | tf_op jit(solution)/shard_map/pick0/pallas_call | solution.py:131
  56.1 2.8 %collective-permute-start.7 = (f32[4,256,512]{2,1,0:T(8,128)}, f32[4,256,512]{2,1,0:T(8,128)S(1)}, u32[]{:S(2)}, u32[]{:S(2)}) collective-permute-start(f32[4,256,512]{2,1,0:T(8,128)} %pick0.1), channel_id=1, source_target_pairs={{0,16},{16,0},{1,17},{17,1},{2,18},{18,2},{3,19},{19,3},{4,20},{20... | collective-permute-start | bytes 6291464 | tf_op jit(solution)/shard_map/ppermute | solution.py:26
  58.9 3.2 %dynamic-slice_bitcast_fusion = f32[8,256,256]{2,1,0:T(8,128)} fusion(f32[2,8,256,256]{3,2,1,0:T(8,128)} %refs_1_.4, s32[]{:T(128)S(6)} %select_n.12), kind=kLoop, calls=%fused_computation | loop fusion | bytes 4194308 | tf_op jit(solution)/shard_map/jit(dynamic_index_in_dim)/squeeze | solution.py:331
  62.1 2.5 %collective-permute-start.5 = (f32[512,512]{1,0:T(8,128)S(1)}, f32[512,512]{1,0:T(8,128)}, u32[]{:S(2)}, u32[]{:S(2)}) collective-permute-start(f32[512,512]{1,0:T(8,128)S(1)} %copy-done.9), channel_id=1, source_target_pairs={{0,32},{32,64},{64,96},{96,0},{16,112},{48,16},{80,48},{112,80},{1... | collective-permute-start | bytes 3145736 | tf_op jit(solution)/shard_map/ppermute | solution.py:37
  64.7 1.4 copy-done.12
  66.1 2.2 %alpha0.1.refs_6_ = f32[512,512]{1,0:T(8,128)S(1)} custom-call(s32[2,16]{1,0:T(2,128)S(1)} %copy-done.4, f32[512,512]{1,0:T(8,128)} %x.1, f32[512,512]{1,0:T(8,128)} %copy-done.10, f32[512,512]{1,0:T(8,128)} %collective-permute-done.2.refs_2_, f32[512,512]{1,0:T(8,128)} %collective-permute-done.1.refs_3_, f32[4,256,512]{2,1,0:T(8,128)} %copy-done.12, ...), custom_call_target="tpu_custom_call" | custom-call | flops 1610612736 | bytes 8388608 | tf_op jit(solution)/shard_map/alpha0/pallas_call | solution.py:185
  68.3 18.7 %collective-permute-done.5.refs_1_ = f32[512,512]{1,0:T(8,128)} collective-permute-done((f32[512,512]{1,0:T(8,128)S(1)}, f32[512,512]{1,0:T(8,128)}, u32[]{:S(2)}, u32[]{:S(2)}) %collective-permute-start.5) | collective-permute-done | bytes 1048608 | tf_op jit(solution)/shard_map/ppermute | solution.py:37
  87.0 2.1 %collective-permute-done.6.refs_3_ = f32[512,512]{1,0:T(8,128)} collective-permute-done((f32[512,512]{1,0:T(8,128)S(1)}, f32[512,512]{1,0:T(8,128)}, u32[]{:S(2)}, u32[]{:S(2)}) %collective-permute-start.6) | collective-permute-done | bytes 1048608 | tf_op jit(solution)/shard_map/ppermute | solution.py:37
  89.1 20.6 %collective-permute-done.9.refs_2_ = f32[8,256,256]{2,1,0:T(8,128)S(1)} collective-permute-done((f32[8,256,256]{2,1,0:T(8,128)}, f32[8,256,256]{2,1,0:T(8,128)S(1)}, u32[]{:S(2)}, u32[]{:S(2)}) %collective-permute-start.9) | collective-permute-done | bytes 2097184 | tf_op jit(solution)/shard_map/ppermute | solution.py:26
  111.6 2.6 %collective-permute-done.10.refs_3_ = f32[8,256,256]{2,1,0:T(8,128)S(1)} collective-permute-done((f32[8,256,256]{2,1,0:T(8,128)S(1)}, f32[8,256,256]{2,1,0:T(8,128)S(1)}, u32[]{:S(2)}, u32[]{:S(2)}) %collective-permute-start.10) | collective-permute-done | bytes 2097184 | tf_op jit(solution)/shard_map/ppermute | solution.py:26
  114.2 1.4 copy-done.6
  115.5 4.5 %beta02.1 = (f32[256,512]{1,0:T(8,128)S(1)}, f32[256,512]{1,0:T(8,128)S(1)}) custom-call(s32[2]{0:T(128)S(1)} %copy-done.3, s32[4,32]{1,0:T(4,128)S(1)} %copy-done.2, f32[8,256,512]{2,1,0:T(8,128)} %bitcast.10, f32[2,8,256,256]{3,2,1,0:T(8,128)} %refs_1_.4, f32[8,256,256]{2,1,0:T(8,128)} %copy-done.5, f32[8,256,256]{2,1,0:T(8,128)} %copy-done.6), custom_call_target="tpu_custom_call" | custom-call | flops 1610612736 | bytes 6291456 | tf_op jit(solution)/shard_map/beta02/pallas_call | solution.py:267
  120.0 4.6 %collective-permute-done.8.refs_2_ = f32[512,512]{1,0:T(8,128)} collective-permute-done((f32[512,512]{1,0:T(8,128)}, f32[512,512]{1,0:T(8,128)}, u32[]{:S(2)}, u32[]{:S(2)}) %collective-permute-start.8) | collective-permute-done | bytes 1048608 | tf_op jit(solution)/shard_map/ppermute | solution.py:37
  124.6 3.6 %pick1.1 = f32[4,256,512]{2,1,0:T(8,128)} custom-call(s32[2,4]{1,0:T(2,128)} %get-tuple-element.36.picks, f32[512,512]{1,0:T(8,128)} %copy-done.8, f32[512,512]{1,0:T(8,128)} %collective-permute-done.5.refs_1_, f32[512,512]{1,0:T(8,128)} %collective-permute-done.8.refs_2_, f32[512,512]{1,0:T(8,128)} %collective-permute-done.6.refs_3_), custom_call_target="tpu_custom_call" | custom-call | bytes 4194304 | tf_op jit(solution)/shard_map/pick1/pallas_call | solution.py:131
  128.3 2.2 %collective-permute-start.11 = (f32[4,256,512]{2,1,0:T(8,128)}, f32[4,256,512]{2,1,0:T(8,128)S(1)}, u32[]{:S(2)}, u32[]{:S(2)}) collective-permute-start(f32[4,256,512]{2,1,0:T(8,128)} %pick1.1), channel_id=1, source_target_pairs={{0,16},{16,0},{1,17},{17,1},{2,18},{18,2},{3,19},{19,3},{4,20},{20... | collective-permute-start | bytes 6291464 | tf_op jit(solution)/shard_map/ppermute | solution.py:26
  130.4 4.0 %collective-permute-done.11.refs_4_ = f32[4,256,512]{2,1,0:T(8,128)S(1)} collective-permute-done((f32[4,256,512]{2,1,0:T(8,128)}, f32[4,256,512]{2,1,0:T(8,128)S(1)}, u32[]{:S(2)}, u32[]{:S(2)}) %collective-permute-start.11) | collective-permute-done | bytes 2097184 | tf_op jit(solution)/shard_map/ppermute | solution.py:26
  134.4 1.4 copy-done.11
  135.8 3.0 %alpha1.1.alpha = f32[512,512]{1,0:T(8,128)S(1)} custom-call(s32[2,16]{1,0:T(2,128)S(1)} %copy-done.4, f32[512,512]{1,0:T(8,128)} %copy-done.8, f32[512,512]{1,0:T(8,128)} %collective-permute-done.5.refs_1_, f32[512,512]{1,0:T(8,128)} %collective-permute-done.8.refs_2_, f32[512,512]{1,0:T(8,128)} %collective-permute-done.6.refs_3_, ...), custom_call_target="tpu_custom_call" | custom-call | flops 1610612736 | bytes 8388608 | tf_op jit(solution)/shard_map/alpha1/pallas_call | solution.py:185
  139.8 3.4 %beta11.2 = f32[256,512]{1,0:T(8,128)S(1)} custom-call(s32[2]{0:T(128)S(1)} %copy-done.3, s32[4,32]{1,0:T(4,128)S(1)} %copy-done.2, f32[8,256,512]{2,1,0:T(8,128)} %bitcast.8, f32[2,8,256,256]{3,2,1,0:T(8,128)} %refs_1_.4, f32[8,256,256]{2,1,0:T(8,128)} %copy-done.5, f32[8,256,256]{2,1,0:T(8,128)} %copy-done.6, f32[256,512]{1,0:T(8,128)S(1)} %get-tuple-element.48.refs_4_), custom_call_target="tpu_custom_call" | custom-call | flops 805306368 | bytes 6291456 | tf_op jit(solution)/shard_map/beta11/pallas_call | solution.py:267
  144.2 3.1 %beta11.3.beta = f32[256,512]{1,0:T(8,128)S(1)} custom-call(s32[2]{0:T(128)S(1)} %copy-done.3, s32[4,32]{1,0:T(4,128)S(1)} %copy-done.2, f32[8,256,512]{2,1,0:T(8,128)} %bitcast.9, f32[2,8,256,256]{3,2,1,0:T(8,128)} %refs_1_.4, f32[8,256,256]{2,1,0:T(8,128)} %copy-done.5, f32[8,256,256]{2,1,0:T(8,128)} %copy-done.6, f32[256,512]{1,0:T(8,128)S(1)} %get-tuple-element.50.refs_4_), custom_call_target="tpu_custom_call" | custom-call | flops 805306368 | bytes 6291456 | tf_op jit(solution)/shard_map/beta11/pallas_call | solution.py:267
  148.0 3.0 %join.1.joined = f32[512,512]{1,0:T(8,128)} custom-call(s32[2]{0:T(128)} %pad_add_fusion.where, f32[512,512]{1,0:T(8,128)} %x.1, f32[512,1]{1,0:T(8,128)} %copy.19.da, f32[1,512]{1,0:T(1,128)} %bitcast.12, f32[512,512]{1,0:T(8,128)} %copy-done, f32[256,512]{1,0:T(8,128)} %copy-done.1), custom_call_target="tpu_custom_call" | custom-call | flops 1048576 | bytes 5242880 | tf_op jit(solution)/shard_map/join/pallas_call | solution.py:368
  151.0 4.1 %collective-permute-done.12.beta_other = f32[256,512]{1,0:T(8,128)S(1)} collective-permute-done((f32[256,512]{1,0:T(8,128)S(1)}, f32[256,512]{1,0:T(8,128)S(1)}, u32[]{:S(2)}, u32[]{:S(2)}) %collective-permute-start.12) | collective-permute-done | bytes 524320 | tf_op jit(solution)/shard_map/ppermute | solution.py:26
  156.0 2.7 %last.1 = f32[512,512]{1,0:T(8,128)} custom-call(s32[2]{0:T(128)} %pad_add_fusion.where, f32[512,512]{1,0:T(8,128)} %join.1.joined, f32[256,512]{1,0:T(8,128)} %copy-done.14), custom_call_target="tpu_custom_call", output_to_operand_aliasing={{}: (1, {})} | custom-call | flops 131072 | bytes 2097152 | tf_op jit(solution)/shard_map/last/pallas_call | solution.py:376
  (58 shorter events, 11.0 us)
Async XLA Ops:
  6.5 2.3 %copy-start.7 = (f32[512,512]{1,0:T(8,128)S(1)}, f32[512,512]{1,0:T(8,128)}, u32[]{:S(2)}) copy-start(f32[512,512]{1,0:T(8,128)} %x.1) | copy-start | bytes 3145732
  6.5 31.9 %copy-start.15 = (s32[32,8]{0,1:T(8,128)S(1)}, s32[32,8]{0,1:T(8,128)}, u32[]{:S(2)}) copy-start(s32[32,8]{0,1:T(8,128)} %param.14) | copy-start | bytes 3076
  6.5 32.6 %copy-start.16 = (s32[32,8]{0,1:T(8,128)S(1)}, s32[32,8]{0,1:T(8,128)}, u32[]{:S(2)}) copy-start(s32[32,8]{0,1:T(8,128)} %param.15) | copy-start | bytes 3076
  6.5 33.3 %copy-start.17 = (s32[32,8]{0,1:T(8,128)S(1)}, s32[32,8]{0,1:T(8,128)}, u32[]{:S(2)}) copy-start(s32[32,8]{0,1:T(8,128)} %param.16) | copy-start | bytes 3076
  6.5 33.9 %copy-start.18 = (s32[32,8]{0,1:T(8,128)S(1)}, s32[32,8]{0,1:T(8,128)}, u32[]{:S(2)}) copy-start(s32[32,8]{0,1:T(8,128)} %param.17) | copy-start | bytes 3076
  6.5 82.5 %all-gather.5.cloned.1.call-start = ((), (), s32[]{:S(2)}) async-start(), calls=%async_computation | async-start | bytes 4718592 | tf_op jit(solution)/shard_map/all_gather | solution.py:328
  8.8 131.1 %all-gather.7.cloned.1.call-start = ((), (), s32[]{:S(2)}) async-start(), calls=%async_computation.1 | async-start | bytes 4718592 | tf_op jit(solution)/shard_map/all_gather | solution.py:330
  8.8 22.9 %collective-permute-start = (f32[512,512]{1,0:T(8,128)S(1)}, f32[512,512]{1,0:T(8,128)S(1)}, u32[]{:S(2)}, u32[]{:S(2)}) collective-permute-start(f32[512,512]{1,0:T(8,128)S(1)} %copy-done.7), channel_id=1, source_target_pairs={{0,32},{32,64},{64,96},{96,0},{16,112},{48,16},{80,48},{112,80},{1... | collective-permute-start | bytes 3145736 | tf_op jit(solution)/shard_map/ppermute | solution.py:37
  12.2 26.2 %collective-permute-start.1 = (f32[512,512]{1,0:T(8,128)S(1)}, f32[512,512]{1,0:T(8,128)}, u32[]{:S(2)}, u32[]{:S(2)}) collective-permute-start(f32[512,512]{1,0:T(8,128)S(1)} %copy-done.7), channel_id=1, source_target_pairs={{0,96},{32,0},{64,32},{96,64},{16,48},{48,80},{80,112},{112,16},{1... | collective-permute-start | bytes 3145736 | tf_op jit(solution)/shard_map/ppermute | solution.py:37
  12.2 10.9 %collective-permute-start.3 = (f32[256,512]{1,0:T(8,128)S(1)}, f32[256,512]{1,0:T(8,128)S(1)}, u32[]{:S(2)}, u32[]{:S(2)}) collective-permute-start(f32[256,512]{1,0:T(8,128)S(1)} %get-tuple-element.52), channel_id=1, source_target_pairs={{0,8},{8,0},{1,9},{9,1},{2,10},{10,2},{3,11},{11,3},{4,12},{12,4},... | collective-permute-start | bytes 1572872 | tf_op jit(solution)/shard_map/ppermute | solution.py:26
  23.9 25.0 %collective-permute-start.4 = (f32[512,512]{1,0:T(8,128)S(1)}, f32[512,512]{1,0:T(8,128)S(1)}, u32[]{:S(2)}, u32[]{:S(2)}) collective-permute-start(f32[512,512]{1,0:T(8,128)S(1)} %copy-done.7), channel_id=1, source_target_pairs={{0,128},{128,0},{1,129},{129,1},{2,130},{130,2},{3,131},{131,3},{4... | collective-permute-start | bytes 3145736 | tf_op jit(solution)/shard_map/ppermute | solution.py:26
  31.8 20.7 %copy-start.10 = (f32[512,512]{1,0:T(8,128)}, f32[512,512]{1,0:T(8,128)S(1)}, u32[]{:S(2)}) copy-start(f32[512,512]{1,0:T(8,128)S(1)} %collective-permute-done.refs_1_) | copy-start | bytes 3145732
  38.4 14.0 %collective-permute-start.2 = (f32[512,512]{1,0:T(8,128)S(1)}, f32[512,512]{1,0:T(8,128)}, u32[]{:S(2)}, u32[]{:S(2)}) collective-permute-start(f32[512,512]{1,0:T(8,128)S(1)} %collective-permute-done.refs_1_), channel_id=1, source_target_pairs={{0,32},{32,64},{64,96},{96,0},{16,112},{48,16},{80,48},{112,80},{1... | collective-permute-start | bytes 3145736 | tf_op jit(solution)/shard_map/ppermute | solution.py:37
  48.9 7.2 %copy-start.8 = (f32[512,512]{1,0:T(8,128)}, f32[512,512]{1,0:T(8,128)S(1)}, u32[]{:S(2)}) copy-start(f32[512,512]{1,0:T(8,128)S(1)} %collective-permute-done.4.refs_0_) | copy-start | bytes 3145732
  56.1 10.0 %copy-start.4 = (s32[2,16]{1,0:T(2,128)S(1)}, s32[2,16]{1,0:T(2,128)}, u32[]{:S(2)}) copy-start(s32[2,16]{1,0:T(2,128)} %get-tuple-element.29.plan) | copy-start | bytes 388
  56.1 8.6 %collective-permute-start.7 = (f32[4,256,512]{2,1,0:T(8,128)}, f32[4,256,512]{2,1,0:T(8,128)S(1)}, u32[]{:S(2)}, u32[]{:S(2)}) collective-permute-start(f32[4,256,512]{2,1,0:T(8,128)} %pick0.1), channel_id=1, source_target_pairs={{0,16},{16,0},{1,17},{17,1},{2,18},{18,2},{3,19},{19,3},{4,20},{20... | collective-permute-start | bytes 6291464 | tf_op jit(solution)/shard_map/ppermute | solution.py:26
  58.9 3.2 %copy-start.9 = (f32[512,512]{1,0:T(8,128)S(1)}, f32[512,512]{1,0:T(8,128)}, u32[]{:S(2)}) copy-start(f32[512,512]{1,0:T(8,128)} %copy-done.8) | copy-start | bytes 3145732
  62.1 47.6 %collective-permute-start.9 = (f32[8,256,256]{2,1,0:T(8,128)}, f32[8,256,256]{2,1,0:T(8,128)S(1)}, u32[]{:S(2)}, u32[]{:S(2)}) collective-permute-start(f32[8,256,256]{2,1,0:T(8,128)} %dynamic-slice_bitcast_fusion), channel_id=1, source_target_pairs={{0,8},{8,0},{1,9},{9,1},{2,10},{10,2},{3,11},{11,3},{4,12},{12,4},... | collective-permute-start | bytes 6291464 | tf_op jit(solution)/shard_map/ppermute | solution.py:26
  62.1 24.8 %collective-permute-start.5 = (f32[512,512]{1,0:T(8,128)S(1)}, f32[512,512]{1,0:T(8,128)}, u32[]{:S(2)}, u32[]{:S(2)}) collective-permute-start(f32[512,512]{1,0:T(8,128)S(1)} %copy-done.9), channel_id=1, source_target_pairs={{0,32},{32,64},{64,96},{96,0},{16,112},{48,16},{80,48},{112,80},{1... | collective-permute-start | bytes 3145736 | tf_op jit(solution)/shard_map/ppermute | solution.py:37
  64.7 24.4 %collective-permute-start.6 = (f32[512,512]{1,0:T(8,128)S(1)}, f32[512,512]{1,0:T(8,128)}, u32[]{:S(2)}, u32[]{:S(2)}) collective-permute-start(f32[512,512]{1,0:T(8,128)S(1)} %copy-done.9), channel_id=1, source_target_pairs={{0,96},{32,0},{64,32},{96,64},{16,48},{48,80},{80,112},{112,16},{1... | collective-permute-start | bytes 3145736 | tf_op jit(solution)/shard_map/ppermute | solution.py:37
  64.7 1.4 copy-start.12
  66.0 49.5 %copy-start.2 = (s32[4,32]{1,0:T(4,128)S(1)}, s32[4,32]{1,0:T(4,128)}, u32[]{:S(2)}) copy-start(s32[4,32]{1,0:T(4,128)} %get-tuple-element.38.plan) | copy-start | bytes 1540
  66.0 49.5 %copy-start.3 = (s32[2]{0:T(128)S(1)}, s32[2]{0:T(128)}, u32[]{:S(2)}) copy-start(s32[2]{0:T(128)} %pad_add_fusion.where) | copy-start | bytes 28
  109.7 4.5 %copy-start.5 = (f32[8,256,256]{2,1,0:T(8,128)}, f32[8,256,256]{2,1,0:T(8,128)S(1)}, u32[]{:S(2)}) copy-start(f32[8,256,256]{2,1,0:T(8,128)S(1)} %collective-permute-done.9.refs_2_) | copy-start | bytes 6291460
  109.7 4.5 %collective-permute-start.10 = (f32[8,256,256]{2,1,0:T(8,128)S(1)}, f32[8,256,256]{2,1,0:T(8,128)S(1)}, u32[]{:S(2)}, u32[]{:S(2)}) collective-permute-start(f32[8,256,256]{2,1,0:T(8,128)S(1)} %collective-permute-done.9.refs_2_), channel_id=1, source_target_pairs={{0,16},{16,0},{1,17},{17,1},{2,18},{18,2},{3,19},{19,3},{4,20},{20... | collective-permute-start | bytes 6291464 | tf_op jit(solution)/shard_map/ppermute | solution.py:26
  110.4 14.3 %collective-permute-start.8 = (f32[512,512]{1,0:T(8,128)}, f32[512,512]{1,0:T(8,128)}, u32[]{:S(2)}, u32[]{:S(2)}) collective-permute-start(f32[512,512]{1,0:T(8,128)} %collective-permute-done.5.refs_1_), channel_id=1, source_target_pairs={{0,32},{32,64},{64,96},{96,0},{16,112},{48,16},{80,48},{112,80},{1... | collective-permute-start | bytes 3145736 | tf_op jit(solution)/shard_map/ppermute | solution.py:37
  114.2 1.4 copy-start.6
  128.3 6.2 %collective-permute-start.11 = (f32[4,256,512]{2,1,0:T(8,128)}, f32[4,256,512]{2,1,0:T(8,128)S(1)}, u32[]{:S(2)}, u32[]{:S(2)}) collective-permute-start(f32[4,256,512]{2,1,0:T(8,128)} %pick1.1), channel_id=1, source_target_pairs={{0,16},{16,0},{1,17},{17,1},{2,18},{18,2},{3,19},{19,3},{4,20},{20... | collective-permute-start | bytes 6291464 | tf_op jit(solution)/shard_map/ppermute | solution.py:26
  134.4 1.4 copy-start.11
  138.8 1.0 copy-start
  139.8 3.5 %copy-start.19 = (f32[512]{0:T(512)S(1)}, f32[512]{0:T(512)}, u32[]{:S(2)}) copy-start(f32[512]{0:T(512)} %param.10) | copy-start | bytes 6148
  143.2 12.0 %collective-permute-start.12 = (f32[256,512]{1,0:T(8,128)S(1)}, f32[256,512]{1,0:T(8,128)S(1)}, u32[]{:S(2)}, u32[]{:S(2)}) collective-permute-start(f32[256,512]{1,0:T(8,128)S(1)} %beta11.2), channel_id=1, source_target_pairs={{0,8},{8,0},{1,9},{9,1},{2,10},{10,2},{3,11},{11,3},{4,12},{12,4},... | collective-permute-start | bytes 1572872 | tf_op jit(solution)/shard_map/ppermute | solution.py:26
  (3 other events, 2.3 us)
Sparse Core Ops, SparseCore 0:
  9.2 58.6 all-gather.4
  69.6 53.4 all-gather.6

commit v6 on v5

--- a/solution.py
+++ b/solution.py
@@ -15,6 +15,7 @@
 BS = 256
 SLOTS = 8
 MIB = 1 << 20
+SMALL = pl.CostEstimate(flops=1 << 20, bytes_accessed=1 << 18, transcendentals=0)
 
 SMEM = pl.BlockSpec(memory_space=pltpu.SMEM)
 HBM = pl.BlockSpec(memory_space=pltpu.HBM)
@@ -54,7 +55,9 @@
     return dot(a_hi, b_hi) + (dot(a_hi, b_lo) + dot(a_lo, b_hi))
 
 
-def plan_kernel(where, alpha_source, alpha_live, beta_source, beta_live, alpha_plan, beta_plan, picks):
+def plan_kernel(
+    where, alpha_source, alpha_live, beta_source, beta_live, alpha_plan, beta_plan, picks, sends
+):
     me, mb = where[0], where[1]
     up = (me & 1) == 0
     for row in range(2):
@@ -91,14 +94,25 @@
 
     def beta(target, slot, _):
         row, c = 2 * (mb ^ (8 * target)) + (slot >> 3), slot & 7
-
-        @pl.when(beta_live[row, c] > 0)
+        src = beta_source[row, c]
+        owner = src >> 1
+        near = (owner >> 3) == (mb >> 3)
+        place = owner & 7
+
+        @pl.when(near & (beta_live[row, c] > 0))
         def _():
-            src = beta_source[row, c]
-            owner = src >> 1
-            side = (owner >> 3) ^ (mb >> 3)
-            piece = owner & 7
-            put(beta_plan, 2 * side + target, piece * 64 + (src & 1) * 32 + slot)
+            ahead = mb - owner
+            d = jnp.where(up, ahead, -ahead) & 7
+            call = jnp.where((d <= 2) | (d >= 6), 0, 1)
+            tile = place if target else c
+            word = d * 64 + (src & 1) * 32 + (slot >> 3) * 16 + tile
+            put(beta_plan, 2 * call + target, word)
+
+        if not target:
+
+            @pl.when(jnp.logical_not(near))
+            def _():
+                sends[place] = slot
 
         return 0
 
@@ -134,7 +148,7 @@
         in_specs=[SMEM] + [ANY] * 4,
         out_specs=VMEM,
         scratch_shapes=[pltpu.SemaphoreType.DMA((4,))],
-        cost_estimate=pl.CostEstimate(flops=0, bytes_accessed=4 * MIB, transcendentals=0),
+        cost_estimate=SMALL,
         name=f"pick{side}",
     )(picks, *pieces)
 
@@ -195,17 +209,43 @@
             pltpu.SemaphoreType.DMA,
         ],
         compiler_params=pltpu.CompilerParams(vmem_limit_bytes=16 * MIB),
-        cost_estimate=pl.CostEstimate(
-            flops=8 * 12 * BS**3, bytes_accessed=8 * MIB, transcendentals=0
-        ),
+        cost_estimate=SMALL,
         name=f"alpha{side}",
     )(plan, *in_hbm(*pieces, picked, own), *before)
 
 
+def send_kernel(where, sends, own, out, sem):
+    copies = []
+    for i in range(SLOTS // 2):
+        slot = sends[(where[0] & 1) * (SLOTS // 2) + i]
+        copies.append(
+            pltpu.make_async_copy(own.at[slot >> 3, slot & 7], out.at[i], sem.at[i])
+        )
+    for copy in copies:
+        copy.start()
+    for copy in copies:
+        copy.wait()
+
+
+def send_call(where, sends, own):
+    return pl.pallas_call(
+        send_kernel,
+        out_shape=jax.ShapeDtypeStruct((SLOTS // 2, BS, BS), jnp.float32),
+        in_specs=[SMEM] * 2 + [HBM],
+        out_specs=VMEM,
+        scratch_shapes=[pltpu.SemaphoreType.DMA((SLOTS // 2,))],
+        cost_estimate=SMALL,
+        name="send",
+    )(where, sends, *in_hbm(own))
+
+
+HOPS = ((0, 1, 2, 6, 7), (3, 4, 5))
+
+
 def beta_kernel(call, targets, where, plan, *refs):
-    ring, refs = refs[0], refs[1:]
-    own, refs = refs[0], refs[1:]
-    par, refs = refs[:2], refs[2:]
+    numbers = HOPS[call]
+    pieces, refs = refs[: len(numbers)], refs[len(numbers) :]
+    own, got, other, refs = refs[0], refs[1], refs[2], refs[3:]
     before, refs = (refs[: len(targets)], refs[len(targets) :]) if call else ((), refs)
     outs, (data, tiles, data_sem, tile_sem, out_sem) = refs[: len(targets)], refs[len(targets) :]
     core = where[0] & 1
@@ -229,12 +269,17 @@
         def fetch(j, _, target=target, row=row, base=base):
             word = plan[row, j + 1]
             k = base + j
-            slot = word & 31
-            columns_of(k, ring.at[word >> 6], (word >> 5) & 1).start()
+            tile = word & 15
+            for number, ref in zip(numbers, pieces):
+                pl.when((word >> 6) == number)(
+                    lambda ref=ref: columns_of(k, ref, (word >> 5) & 1).start()
+                )
             if target == 0:
-                tile_from(k, own.at[slot >> 3, slot & 7]).start()
+                tile_from(k, own.at[(word >> 4) & 1, tile]).start()
             else:
-                start_one_of(par, core ^ (slot >> 3), lambda ref: tile_from(k, ref.at[slot & 7]))
+                start_one_of(
+                    (got, other), core ^ (tile >> 2), lambda ref: tile_from(k, ref.at[tile & 3])
+                )
             return 0
 
         lax.fori_loop(0, plan[row, 0], fetch, 0)
@@ -250,10 +295,10 @@
 
         def product(j, _, out=out, row=row, base=base):
             k = base + j
-            slot = plan[row, j + 1] & 31
-            columns_of(k, ring.at[0], 0).wait()
+            block = (plan[row, j + 1] >> 4) & 1
+            columns_of(k, pieces[0], 0).wait()
             tile_from(k, own.at[0, 0]).wait()
-            columns = pl.multiple_of((slot >> 3) * BS, BS)
+            columns = pl.multiple_of(block * BS, BS)
             out[:, pl.ds(columns, BS)] += dot3(data[k], tiles[k])
             return 0
 
@@ -261,51 +306,26 @@
         base = base + plan[row, 0]
 
 
-def beta_call(call, targets, where, plan, ring, own, par, before=()):
-    _, rows, n = ring.shape
-    most = 2 * SLOTS * len(targets)
+def beta_call(call, targets, where, plan, held, own, got, other, before=()):
+    n = held[0].shape[0]
+    pieces = [held[d] for d in HOPS[call]]
+    most = len(HOPS[call]) * len(targets)
     return pl.pallas_call(
         functools.partial(beta_kernel, call, targets),
-        out_shape=[jax.ShapeDtypeStruct((rows, n), jnp.float32)] * len(targets),
-        in_specs=[SMEM] * 2 + [HBM] * (2 + len(par)) + [ANY] * len(before),
+        out_shape=[jax.ShapeDtypeStruct((n, n), jnp.float32)] * len(targets),
+        in_specs=[SMEM] * 2 + [HBM] * (len(pieces) + 3) + [ANY] * len(before),
         out_specs=[VMEM] * len(targets),
         scratch_shapes=[
-            pltpu.VMEM((most, rows, BS), jnp.float32),
+            pltpu.VMEM((most, n, BS), jnp.float32),
             pltpu.VMEM((most, BS, BS), jnp.float32),
             pltpu.SemaphoreType.DMA((most,)),
             pltpu.SemaphoreType.DMA((most,)),
             pltpu.SemaphoreType.DMA((2,)),
         ],
-        compiler_params=pltpu.CompilerParams(vmem_limit_bytes=24 * MIB),
-        cost_estimate=pl.CostEstimate(
-            flops=8 * 6 * BS**3 * len(targets), bytes_accessed=6 * MIB, transcendentals=0
-        ),
+        compiler_params=pltpu.CompilerParams(vmem_limit_bytes=16 * MIB),
+        cost_estimate=SMALL,
         name=f"beta{call}{len(targets)}",
-    )(where, plan, *in_hbm(ring, own, *par), *before)
-
-
-def join_kernel(where, x, da, db, alpha, beta, out):
-    ylo = where[1] >> 3
-    out[...] = (da[...] + db[...]) * x[...] + alpha[...]
-    rows = pl.ds(pl.multiple_of(ylo * BS, BS), BS)
-    out[rows, :] += beta[...]
-
-
-def last_kernel(where, joined, beta_other, out, total, part, sems):
-    first = pl.multiple_of((1 - (where[1] >> 3)) * BS, BS)
-    rows = out.at[pl.ds(first, BS)]
-    copies = [
-        pltpu.make_async_copy(joined.at[pl.ds(first, BS)], total, sems.at[0]),
-        pltpu.make_async_copy(beta_other, part, sems.at[1]),
-    ]
-    for copy in copies:
-        copy.start()
-    for copy in copies:
-        copy.wait()
-    total[...] += part[...]
-    back = pltpu.make_async_copy(total, rows, sems.at[2])
-    back.start()
-    back.wait()
+    )(where, plan, *in_hbm(*pieces, own, got, other), *before)
 
 
 def per_device(
@@ -319,74 +339,53 @@
     beta_source,
     beta_live,
 ):
-    n = coeffs.shape[0]
-    core = lax.axis_index("core")
-    ylo = lax.axis_index("ylo")
     where = jnp.stack([lax.axis_index(ALPHA), lax.axis_index(BETA)]).astype(jnp.int32)
-    keep = lax.dynamic_slice_in_dim(coeffs, ylo * BS, BS, 0)
-    give = lax.dynamic_slice_in_dim(coeffs, (1 - ylo) * BS, BS, 0)
-    near = lax.all_gather(keep, "z")
-    p = swap(give, "ylo")
-    far = lax.all_gather(p, "z")
-    mine = lax.dynamic_index_in_dim(beta_tiles, core, 0, keepdims=False)
+    f1, b1 = step(coeffs, "z"), step(coeffs, "z", -1)
     uf, ub = step(coeffs, "x"), step(coeffs, "x", -1)
-    v = swap(after(coeffs, p), "yhi")
-    alpha_plan, beta_plan, picks = pl.pallas_call(
+    v = swap(coeffs, "yhi")
+    alpha_plan, beta_plan, picks, sends = pl.pallas_call(
         plan_kernel,
         out_shape=[
             jax.ShapeDtypeStruct((2, 16), jnp.int32),
             jax.ShapeDtypeStruct((4, 32), jnp.int32),
             jax.ShapeDtypeStruct((2, 4), jnp.int32),
+            jax.ShapeDtypeStruct((SLOTS,), jnp.int32),
         ],
         in_specs=[SMEM] * 5,
-        out_specs=[SMEM] * 3,
+        out_specs=[SMEM] * 4,
         name="plan",
-    )(after(where, uf), alpha_source, alpha_live, beta_source, beta_live)
-    uf, ub = lax.optimization_barrier((uf, ub))
+    )(where, alpha_source, alpha_live, beta_source, beta_live)
+    tiles = send_call(where, sends, beta_tiles)
+    f1, b1, uf, ub, v, tiles, picks = lax.optimization_barrier((f1, b1, uf, ub, v, tiles, picks))
+    f2, b2 = step(f1, "z"), step(b1, "z", -1)
     u2 = step(uf, "x")
-    got = swap(after(mine, uf), "ylo")
-    u2, v, picks = lax.optimization_barrier((u2, v, picks))
+    got = swap(tiles, "ylo")
+    f2, b2, u2, got = lax.optimization_barrier((f2, b2, u2, got))
+    f3, b3 = step(f2, "z"), step(b2, "z", -1)
     vf, vb = step(v, "x"), step(v, "x", -1)
-    u_picked = swap(pick_call(0, picks, [coeffs, uf, u2, ub]), "core")
+    other = swap(got, "core")
+    picked = pick_call(0, after(picks, other), [coeffs, uf, u2, ub])
+    held = [coeffs, f1, f2, None, None, None, b2, b1]
+    beta_own, beta_par = beta_call(0, (0, 1), where, beta_plan, held, beta_tiles, got, other)
+    f3, b3, vf, vb, picked, beta_own, beta_par = lax.optimization_barrier(
+        (f3, b3, vf, vb, picked, beta_own, beta_par)
+    )
+    held[3], held[4], held[5] = f3, step(f3, "z"), b3
+    v2 = step(vf, "x")
+    u_picked = swap(picked, "core")
     alpha = alpha_call(0, alpha_plan, [coeffs, uf, u2, ub], u_picked, alpha_tiles)
-    vf, vb, alpha, near = lax.optimization_barrier((vf, vb, alpha, near))
-    v2 = step(vf, "x")
-    other = swap(after(got, vf), "core")
-    beta = beta_call(0, (0, 1), where, beta_plan, near, beta_tiles, [got, other])
-    v2, beta_own, beta_par = lax.optimization_barrier((v2, *beta))
-    v_picked = swap(pick_call(1, picks, [v, vf, v2, vb]), "core")
-    alpha = alpha_call(1, alpha_plan, [v, vf, v2, vb], v_picked, alpha_tiles, [alpha])
-    far = after(far, alpha)
+    alpha, beta_par = lax.optimization_barrier((alpha, beta_par))
     (beta_par,) = beta_call(
-        1, (1,), where, beta_plan, far, beta_tiles, [got, other], [beta_par]
+        1, (1,), where, beta_plan, held, beta_tiles, got, other, [beta_par]
     )
     beta_other = swap(beta_par, "ylo")
     (beta_own,) = beta_call(
-        1, (0,), where, beta_plan, far, after(beta_tiles, beta_par), [got, other], [beta_own]
+        1, (0,), where, beta_plan, held, after(beta_tiles, beta_par), got, other, [beta_own]
     )
-
-    joined = pl.pallas_call(
-        join_kernel,
-        out_shape=jax.ShapeDtypeStruct((n, n), jnp.float32),
-        in_specs=[SMEM] + [VMEM] * 5,
-        out_specs=VMEM,
-        cost_estimate=pl.CostEstimate(flops=4 * n * n, bytes_accessed=5 * MIB, transcendentals=0),
-        name="join",
-    )(where, coeffs, diag_alpha[:, None], diag_beta[None, :], alpha, beta_own)
-    return pl.pallas_call(
-        last_kernel,
-        out_shape=jax.ShapeDtypeStruct((n, n), jnp.float32),
-        in_specs=[SMEM, ANY, ANY],
-        out_specs=ANY,
-        scratch_shapes=[
-            pltpu.VMEM((BS, n), jnp.float32),
-            pltpu.VMEM((BS, n), jnp.float32),
-            pltpu.SemaphoreType.DMA((3,)),
-        ],
-        input_output_aliases={1: 0},
-        cost_estimate=pl.CostEstimate(flops=n * BS, bytes_accessed=2 * MIB, transcendentals=0),
-        name="last",
-    )(where, joined, beta_other)
+    v_picked = swap(pick_call(1, after(picks, beta_own), [v, vf, v2, vb]), "core")
+    alpha = alpha_call(1, alpha_plan, [v, vf, v2, vb], v_picked, alpha_tiles, [alpha])
+    joined = (diag_alpha[:, None] + diag_beta[None, :]) * coeffs + alpha + beta_own
+    return lax.optimization_barrier(joined) + beta_other
 
 
 def solution(mesh):

time: 167 us -> 147 us (0.88)
  between operations: 13.6 us -> 0.24 us
  starting transfers between devices: 18.4 us -> 31.1 us
  Pallas kernels: 32.7 us -> 25.4 us
  local copies, waits for them, and re-layouts: 16.4 us -> 9.14 us
  waiting for transfers between devices: 83.9 us -> 78.6 us
    ppermute x0 -> x7, waiting for transfers between devices: none -> 27.4 us  [step(): return lax.ppermute(value, ('core', axis), pairs)]
    ppermute x7 -> x6, waiting for transfers between devices: 44.4 us -> 22 us  [swap(): return lax.ppermute(value, axis, [(0, 1), (1, 0)])]
    ppermute x0 -> x7, starting transfers between devices: none -> 14.8 us  [step(): return lax.ppermute(value, ('core', axis), pairs)]
    ppermute x6, waiting for transfers between devices: 39.4 us -> 29.2 us  [step(): return lax.ppermute(value, (axis, 'core'), pairs)]
    pallas_call x3, Pallas kernels: 10.9 us -> 6.16 us  [beta_call(): pl.pallas_call(functools.partial(beta_kernel, call, targets), out_shape=[...]
    ppermute x7 -> x6, starting transfers between devices: 11.1 us -> 7.39 us  [swap(): return lax.ppermute(value, axis, [(0, 1), (1, 0)])]
    squeeze x1 -> x0, local copies, waits for them, and re-layouts: 3.21 us -> none  [per_device(): mine = lax.dynamic_index_in_dim(beta_tiles, core, 0, keepdims=False)]
    pallas_call x2 -> x1, Pallas kernels: 5.72 us -> 2.87 us  [send_call(): pl.pallas_call(send_kernel, out_shape=jax.ShapeDtypeStruct((SLOTS // 2, B...]
  transfers between devices with their start and end apart: 15 -> 19, of which waited for: 12 -> 12; matrix products, arithmetic and copies ran while one was open for 4% -> 4% of each run, Pallas kernels for 16% -> 13%
where the time goes in v6:
time: 147 us
  waiting for transfers between devices  78.6 us (53%)
  starting transfers between devices  31.1 us (21%)
  Pallas kernels  25.4 us (17%)
  local copies, waits for them, and re-layouts  9.14 us (6%)
  other arithmetic  2.07 us (1%)
    ppermute x6, waiting for transfers between devices, step(): return lax.ppermute(value, (axis, 'core'), pairs)  29.2 us
    ppermute x7, waiting for transfers between devices, step(): return lax.ppermute(value, ('core', axis), pairs)  27.4 us
    ppermute x6, waiting for transfers between devices, swap(): return lax.ppermute(value, axis, [(0, 1), (1, 0)])  22 us
    ppermute x7, starting transfers between devices, step(): return lax.ppermute(value, ('core', axis), pairs)  14.8 us
    unnamed x36, local copies, waits for them, and re-layouts  9.14 us
    ppermute x6, starting transfers between devices, step(): return lax.ppermute(value, (axis, 'core'), pairs)  8.93 us
    ppermute x6, starting transfers between devices, swap(): return lax.ppermute(value, axis, [(0, 1), (1, 0)])  7.39 us
    pallas_call x2, Pallas kernels, pick_call(): pl.pallas_call(functools.partial(pick_kernel, side), out_shape=jax.ShapeD...  7.16 us
  transfers between devices with their start and end apart: 19, of which 12 were waited for; matrix products, arithmetic and copies ran while one was open for 4% of the time, Pallas kernels for 13%

profile of v6, /device:TPU:1, one launch (start us, length us, event | category | flops | bytes accessed | tf_op | source)
XLA Modules:
  0.0 146.6 jit_solution(5076109757412519142)
XLA Ops:
  0.0 6.4 %collective-permute-start = (f32[512,512]{1,0:T(8,128)}, f32[512,512]{1,0:T(8,128)}, u32[]{:S(2)}, u32[]{:S(2)}) collective-permute-start(f32[512,512]{1,0:T(8,128)} %refs_0_.5), channel_id=1, source_target_pairs={{0,1},{1,2},{2,3},{3,4},{4,5},{5,6},{6,7},{7,0},{16,23},{17,16},{1... | collective-permute-start | bytes 3145736 | tf_op jit(solution)/shard_map/ppermute | solution.py:35
  6.4 2.5 %collective-permute-start.2 = (f32[512,512]{1,0:T(8,128)}, f32[512,512]{1,0:T(8,128)S(1)}, u32[]{:S(2)}, u32[]{:S(2)}) collective-permute-start(f32[512,512]{1,0:T(8,128)} %refs_0_.5), channel_id=1, source_target_pairs={{0,32},{32,64},{64,96},{96,0},{16,112},{48,16},{80,48},{112,80},{1... | collective-permute-start | bytes 3145736 | tf_op jit(solution)/shard_map/ppermute | solution.py:38
  8.9 2.9 %collective-permute-start.4 = (f32[512,512]{1,0:T(8,128)}, f32[512,512]{1,0:T(8,128)}, u32[]{:S(2)}, u32[]{:S(2)}) collective-permute-start(f32[512,512]{1,0:T(8,128)} %refs_0_.5), channel_id=1, source_target_pairs={{0,128},{128,0},{1,129},{129,1},{2,130},{130,2},{3,131},{131,3},{4... | collective-permute-start | bytes 3145736 | tf_op jit(solution)/shard_map/ppermute | solution.py:27
  11.8 1.4 copy.10.alpha_source
  13.2 1.4 copy.11.alpha_live
  14.5 1.4 copy.12.beta_source
  15.9 1.4 copy.13.beta_live
  17.9 3.5 %plan.1 = (s32[2,16]{1,0:T(2,128)}, s32[4,32]{1,0:T(4,128)}, s32[2,4]{1,0:T(2,128)}, s32[8]{0:T(128)}) custom-call(s32[2]{0:T(128)} %pad_add_fusion.where, s32[32,8]{1,0:T(8,128)} %copy.10.alpha_source, s32[32,8]{1,0:T(8,128)} %copy.11.alpha_live, s32[32,8]{1,0:T(8,128)} %copy.12.beta_source, s32[32,8]{1,0:T(8,128)} %copy.13.beta_live), custom_call_target="tpu_custom_call" | custom-call | tf_op jit(solution)/shard_map/plan/pallas_call | solution.py:346
  21.4 2.9 %send.1 = f32[4,256,256]{2,1,0:T(8,128)} custom-call(s32[2]{0:T(128)} %pad_add_fusion.where, s32[8]{0:T(128)} %get-tuple-element.35.sends, f32[2,8,256,256]{3,2,1,0:T(8,128)} %refs_3_.2), custom_call_target="tpu_custom_call" | custom-call | flops 1048576 | bytes 262144 | tf_op jit(solution)/shard_map/send/pallas_call | solution.py:231
  24.3 4.2 %collective-permute-done.refs_1_ = f32[512,512]{1,0:T(8,128)} collective-permute-done((f32[512,512]{1,0:T(8,128)}, f32[512,512]{1,0:T(8,128)}, u32[]{:S(2)}, u32[]{:S(2)}) %collective-permute-start) | collective-permute-done | bytes 1048608 | tf_op jit(solution)/shard_map/ppermute | solution.py:35
  28.5 2.7 %collective-permute-done.1.refs_4_ = f32[512,512]{1,0:T(8,128)} collective-permute-done((f32[512,512]{1,0:T(8,128)}, f32[512,512]{1,0:T(8,128)}, u32[]{:S(2)}, u32[]{:S(2)}) %collective-permute-start.1) | collective-permute-done | bytes 1048608 | tf_op jit(solution)/shard_map/ppermute | solution.py:35
  31.3 3.2 %collective-permute-done.3.refs_3_ = f32[512,512]{1,0:T(8,128)S(1)} collective-permute-done((f32[512,512]{1,0:T(8,128)}, f32[512,512]{1,0:T(8,128)S(1)}, u32[]{:S(2)}, u32[]{:S(2)}) %collective-permute-start.3) | collective-permute-done | bytes 1048608 | tf_op jit(solution)/shard_map/ppermute | solution.py:38
  34.5 3.3 %collective-permute-start.7 = (f32[512,512]{1,0:T(8,128)S(1)}, f32[512,512]{1,0:T(8,128)S(1)}, u32[]{:S(2)}, u32[]{:S(2)}) collective-permute-start(f32[512,512]{1,0:T(8,128)S(1)} %collective-permute-done.2.refs_1_), channel_id=1, source_target_pairs={{0,32},{32,64},{64,96},{96,0},{16,112},{48,16},{80,48},{112,80},{1... | collective-permute-start | bytes 3145736 | tf_op jit(solution)/shard_map/ppermute | solution.py:38
  37.9 3.0 %collective-permute-start.5 = (f32[512,512]{1,0:T(8,128)}, f32[512,512]{1,0:T(8,128)}, u32[]{:S(2)}, u32[]{:S(2)}) collective-permute-start(f32[512,512]{1,0:T(8,128)} %collective-permute-done.refs_1_), channel_id=1, source_target_pairs={{0,1},{1,2},{2,3},{3,4},{4,5},{5,6},{6,7},{7,0},{16,23},{17,16},{1... | collective-permute-start | bytes 3145736 | tf_op jit(solution)/shard_map/ppermute | solution.py:35
  42.2 7.4 %collective-permute-done.7.refs_2_ = f32[512,512]{1,0:T(8,128)S(1)} collective-permute-done((f32[512,512]{1,0:T(8,128)S(1)}, f32[512,512]{1,0:T(8,128)S(1)}, u32[]{:S(2)}, u32[]{:S(2)}) %collective-permute-start.7) | collective-permute-done | bytes 1048608 | tf_op jit(solution)/shard_map/ppermute | solution.py:38
  49.6 13.9 %collective-permute-done.5.refs_2_ = f32[512,512]{1,0:T(8,128)} collective-permute-done((f32[512,512]{1,0:T(8,128)}, f32[512,512]{1,0:T(8,128)}, u32[]{:S(2)}, u32[]{:S(2)}) %collective-permute-start.5) | collective-permute-done | bytes 1048608 | tf_op jit(solution)/shard_map/ppermute | solution.py:35
  63.7 1.9 %collective-permute-done.8.refs_6_.refs_4_ = f32[4,256,256]{2,1,0:T(8,128)S(1)} collective-permute-done((f32[4,256,256]{2,1,0:T(8,128)}, f32[4,256,256]{2,1,0:T(8,128)S(1)}, u32[]{:S(2)}, u32[]{:S(2)}) %collective-permute-start.8) | collective-permute-done | bytes 1048608 | tf_op jit(solution)/shard_map/ppermute | solution.py:27
  67.4 2.7 %collective-permute-start.9 = (f32[512,512]{1,0:T(8,128)}, f32[512,512]{1,0:T(8,128)}, u32[]{:S(2)}, u32[]{:S(2)}) collective-permute-start(f32[512,512]{1,0:T(8,128)} %collective-permute-done.5.refs_2_), channel_id=1, source_target_pairs={{0,1},{1,2},{2,3},{3,4},{4,5},{5,6},{6,7},{7,0},{16,23},{17,16},{1... | collective-permute-start | bytes 3145736 | tf_op jit(solution)/shard_map/ppermute | solution.py:35
  70.1 3.6 %pick0.1 = f32[4,256,512]{2,1,0:T(8,128)} custom-call(s32[2,4]{1,0:T(2,128)} %get-tuple-element.61.picks, f32[512,512]{1,0:T(8,128)} %refs_0_.5, f32[512,512]{1,0:T(8,128)} %copy-done.8, f32[512,512]{1,0:T(8,128)} %copy-done.10, f32[512,512]{1,0:T(8,128)} %copy-done.9), custom_call_target="tpu_custom_call" | custom-call | flops 1048576 | bytes 262144 | tf_op jit(solution)/shard_map/pick0/pallas_call | solution.py:145
  74.7 16.2 %collective-permute-done.11.refs_1_ = f32[512,512]{1,0:T(8,128)} collective-permute-done((f32[512,512]{1,0:T(8,128)}, f32[512,512]{1,0:T(8,128)}, u32[]{:S(2)}, u32[]{:S(2)}) %collective-permute-start.11) | collective-permute-done | bytes 1048608 | tf_op jit(solution)/shard_map/ppermute | solution.py:38
  90.9 2.4 %collective-permute-done.12.refs_3_ = f32[512,512]{1,0:T(8,128)} collective-permute-done((f32[512,512]{1,0:T(8,128)}, f32[512,512]{1,0:T(8,128)}, u32[]{:S(2)}, u32[]{:S(2)}) %collective-permute-start.12) | collective-permute-done | bytes 1048608 | tf_op jit(solution)/shard_map/ppermute | solution.py:38
  94.5 2.7 %collective-permute-start.15 = (f32[512,512]{1,0:T(8,128)}, f32[512,512]{1,0:T(8,128)S(1)}, u32[]{:S(2)}, u32[]{:S(2)}) collective-permute-start(f32[512,512]{1,0:T(8,128)} %collective-permute-done.9.refs_0_), channel_id=1, source_target_pairs={{0,1},{1,2},{2,3},{3,4},{4,5},{5,6},{6,7},{7,0},{16,23},{17,16},{1... | collective-permute-start | bytes 3145736 | tf_op jit(solution)/shard_map/ppermute | solution.py:35
  97.2 1.6 %collective-permute-start.14 = (f32[512,512]{1,0:T(8,128)}, f32[512,512]{1,0:T(8,128)}, u32[]{:S(2)}, u32[]{:S(2)}) collective-permute-start(f32[512,512]{1,0:T(8,128)} %collective-permute-done.11.refs_1_), channel_id=1, source_target_pairs={{0,32},{32,64},{64,96},{96,0},{16,112},{48,16},{80,48},{112,80},{1... | collective-permute-start | bytes 3145736 | tf_op jit(solution)/shard_map/ppermute | solution.py:38
  100.2 2.6 %alpha0.1.refs_6_ = f32[512,512]{1,0:T(8,128)S(1)} custom-call(s32[2,16]{1,0:T(2,128)S(1)} %copy-done.2, f32[512,512]{1,0:T(8,128)} %refs_0_.5, f32[512,512]{1,0:T(8,128)} %copy-done.8, f32[512,512]{1,0:T(8,128)} %copy-done.10, f32[512,512]{1,0:T(8,128)} %copy-done.9, f32[4,256,512]{2,1,0:T(8,128)} %copy-done.13, f32[2,8,256,256]{3,2,1,0:T(8,128)} %refs_5_.5), custom_call_target="tpu_custom_call" | custom-call | flops 1048576 | bytes 262144 | tf_op jit(solution)/shard_map/alpha0/pallas_call | solution.py:199
  102.8 6.4 %collective-permute-done.15.refs_1_ = f32[512,512]{1,0:T(8,128)S(1)} collective-permute-done((f32[512,512]{1,0:T(8,128)}, f32[512,512]{1,0:T(8,128)S(1)}, u32[]{:S(2)}, u32[]{:S(2)}) %collective-permute-start.15) | collective-permute-done | bytes 1048608 | tf_op jit(solution)/shard_map/ppermute | solution.py:35
  110.2 2.2 %beta11.2 = f32[512,512]{1,0:T(8,128)S(1)} custom-call(s32[2]{0:T(128)S(1)} %copy-done.1, s32[4,32]{1,0:T(4,128)S(1)} %copy-done, f32[512,512]{1,0:T(8,128)} %collective-permute-done.9.refs_0_, f32[512,512]{1,0:T(8,128)} %copy-done.7, f32[512,512]{1,0:T(8,128)} %copy-done.6, f32[2,8,256,256]{3,2,1,0:T(8,128)} %refs_3_.2, f32[4,256,256]{2,1,0:T(8,128)} %copy-done.4, ...), custom_call_target="tpu_custom_call" | custom-call | flops 1048576 | bytes 262144 | tf_op jit(solution)/shard_map/beta11/pallas_call | solution.py:313
  112.4 3.0 %beta11.3 = f32[512,512]{1,0:T(8,128)S(1)} custom-call(s32[2]{0:T(128)S(1)} %copy-done.1, s32[4,32]{1,0:T(4,128)S(1)} %copy-done, f32[512,512]{1,0:T(8,128)} %collective-permute-done.9.refs_0_, f32[512,512]{1,0:T(8,128)} %copy-done.7, f32[512,512]{1,0:T(8,128)} %copy-done.6, f32[2,8,256,256]{3,2,1,0:T(8,128)} %refs_3_.2, f32[4,256,256]{2,1,0:T(8,128)} %copy-done.4, ...), custom_call_target="tpu_custom_call" | custom-call | flops 1048576 | bytes 262144 | tf_op jit(solution)/shard_map/beta11/pallas_call | solution.py:313
  115.5 3.6 %pick1.1 = f32[4,256,512]{2,1,0:T(8,128)} custom-call(s32[2,4]{1,0:T(2,128)} %get-tuple-element.61.picks, f32[512,512]{1,0:T(8,128)} %collective-permute-done.4.refs_0_, f32[512,512]{1,0:T(8,128)} %collective-permute-done.11.refs_1_, f32[512,512]{1,0:T(8,128)} %collective-permute-done.14.refs_2_, f32[512,512]{1,0:T(8,128)} %collective-permute-done.12.refs_3_), custom_call_target="tpu_custom_call" | custom-call | flops 1048576 | bytes 262144 | tf_op jit(solution)/shard_map/pick1/pallas_call | solution.py:145
  119.1 1.6 %collective-permute-start.17 = (f32[4,256,512]{2,1,0:T(8,128)}, f32[4,256,512]{2,1,0:T(8,128)S(1)}, u32[]{:S(2)}, u32[]{:S(2)}) collective-permute-start(f32[4,256,512]{2,1,0:T(8,128)} %pick1.1), channel_id=1, source_target_pairs={{0,16},{16,0},{1,17},{17,1},{2,18},{18,2},{3,19},{19,3},{4,20},{20... | collective-permute-start | bytes 6291464 | tf_op jit(solution)/shard_map/ppermute | solution.py:27
  120.7 4.0 %collective-permute-done.17.refs_4_ = f32[4,256,512]{2,1,0:T(8,128)S(1)} collective-permute-done((f32[4,256,512]{2,1,0:T(8,128)}, f32[4,256,512]{2,1,0:T(8,128)S(1)}, u32[]{:S(2)}, u32[]{:S(2)}) %collective-permute-start.17) | collective-permute-done | bytes 2097184 | tf_op jit(solution)/shard_map/ppermute | solution.py:27
  126.0 3.0 %alpha1.1 = f32[512,512]{1,0:T(8,128)S(1)} custom-call(s32[2,16]{1,0:T(2,128)S(1)} %copy-done.2, f32[512,512]{1,0:T(8,128)} %collective-permute-done.4.refs_0_, f32[512,512]{1,0:T(8,128)} %collective-permute-done.11.refs_1_, f32[512,512]{1,0:T(8,128)} %collective-permute-done.14.refs_2_, f32[512,512]{1,0:T(8,128)} %collective-permute-done.12.refs_3_, ...), custom_call_target="tpu_custom_call" | custom-call | flops 1048576 | bytes 262144 | tf_op jit(solution)/shard_map/alpha1/pallas_call | solution.py:199
  129.3 16.0 %collective-permute-done.18 = f32[512,512]{1,0:T(8,128)S(1)} collective-permute-done((f32[512,512]{1,0:T(8,128)S(1)}, f32[512,512]{1,0:T(8,128)S(1)}, u32[]{:S(2)}, u32[]{:S(2)}) %collective-permute-start.18) | collective-permute-done | bytes 1048608 | tf_op jit(solution)/shard_map/ppermute | solution.py:27
  (54 shorter events, 11.3 us)
Async XLA Ops:
  0.0 28.5 %collective-permute-start = (f32[512,512]{1,0:T(8,128)}, f32[512,512]{1,0:T(8,128)}, u32[]{:S(2)}, u32[]{:S(2)}) collective-permute-start(f32[512,512]{1,0:T(8,128)} %refs_0_.5), channel_id=1, source_target_pairs={{0,1},{1,2},{2,3},{3,4},{4,5},{5,6},{6,7},{7,0},{16,23},{17,16},{1... | collective-permute-start | bytes 3145736 | tf_op jit(solution)/shard_map/ppermute | solution.py:35
  6.4 24.9 %collective-permute-start.1 = (f32[512,512]{1,0:T(8,128)}, f32[512,512]{1,0:T(8,128)}, u32[]{:S(2)}, u32[]{:S(2)}) collective-permute-start(f32[512,512]{1,0:T(8,128)} %refs_0_.5), channel_id=1, source_target_pairs={{0,7},{1,0},{2,1},{3,2},{4,3},{5,4},{6,5},{7,6},{16,17},{17,18},{1... | collective-permute-start | bytes 3145736 | tf_op jit(solution)/shard_map/ppermute | solution.py:35
  6.4 24.9 %collective-permute-start.2 = (f32[512,512]{1,0:T(8,128)}, f32[512,512]{1,0:T(8,128)S(1)}, u32[]{:S(2)}, u32[]{:S(2)}) collective-permute-start(f32[512,512]{1,0:T(8,128)} %refs_0_.5), channel_id=1, source_target_pairs={{0,32},{32,64},{64,96},{96,0},{16,112},{48,16},{80,48},{112,80},{1... | collective-permute-start | bytes 3145736 | tf_op jit(solution)/shard_map/ppermute | solution.py:38
  8.9 25.6 %collective-permute-start.3 = (f32[512,512]{1,0:T(8,128)}, f32[512,512]{1,0:T(8,128)S(1)}, u32[]{:S(2)}, u32[]{:S(2)}) collective-permute-start(f32[512,512]{1,0:T(8,128)} %refs_0_.5), channel_id=1, source_target_pairs={{0,96},{32,0},{64,32},{96,64},{16,48},{48,80},{80,112},{112,16},{1... | collective-permute-start | bytes 3145736 | tf_op jit(solution)/shard_map/ppermute | solution.py:38
  8.9 25.6 %collective-permute-start.4 = (f32[512,512]{1,0:T(8,128)}, f32[512,512]{1,0:T(8,128)}, u32[]{:S(2)}, u32[]{:S(2)}) collective-permute-start(f32[512,512]{1,0:T(8,128)} %refs_0_.5), channel_id=1, source_target_pairs={{0,128},{128,0},{1,129},{129,1},{2,130},{130,2},{3,131},{131,3},{4... | collective-permute-start | bytes 3145736 | tf_op jit(solution)/shard_map/ppermute | solution.py:27
  31.3 32.4 %copy-start.8 = (f32[512,512]{1,0:T(8,128)}, f32[512,512]{1,0:T(8,128)S(1)}, u32[]{:S(2)}) copy-start(f32[512,512]{1,0:T(8,128)S(1)} %collective-permute-done.2.refs_1_) | copy-start | bytes 3145732
  34.5 6.4 %copy-start.9 = (f32[512,512]{1,0:T(8,128)}, f32[512,512]{1,0:T(8,128)S(1)}, u32[]{:S(2)}) copy-start(f32[512,512]{1,0:T(8,128)S(1)} %collective-permute-done.3.refs_3_) | copy-start | bytes 3145732
  34.5 39.2 %copy-start = (s32[4,32]{1,0:T(4,128)S(1)}, s32[4,32]{1,0:T(4,128)}, u32[]{:S(2)}) copy-start(s32[4,32]{1,0:T(4,128)} %get-tuple-element.49.plan) | copy-start | bytes 1540
  34.5 39.2 %copy-start.1 = (s32[2]{0:T(128)S(1)}, s32[2]{0:T(128)}, u32[]{:S(2)}) copy-start(s32[2]{0:T(128)} %pad_add_fusion.where) | copy-start | bytes 28
  34.5 15.1 %collective-permute-start.7 = (f32[512,512]{1,0:T(8,128)S(1)}, f32[512,512]{1,0:T(8,128)S(1)}, u32[]{:S(2)}, u32[]{:S(2)}) collective-permute-start(f32[512,512]{1,0:T(8,128)S(1)} %collective-permute-done.2.refs_1_), channel_id=1, source_target_pairs={{0,32},{32,64},{64,96},{96,0},{16,112},{48,16},{80,48},{112,80},{1... | collective-permute-start | bytes 3145736 | tf_op jit(solution)/shard_map/ppermute | solution.py:38
  37.9 25.6 %collective-permute-start.5 = (f32[512,512]{1,0:T(8,128)}, f32[512,512]{1,0:T(8,128)}, u32[]{:S(2)}, u32[]{:S(2)}) collective-permute-start(f32[512,512]{1,0:T(8,128)} %collective-permute-done.refs_1_), channel_id=1, source_target_pairs={{0,1},{1,2},{2,3},{3,4},{4,5},{5,6},{6,7},{7,0},{16,23},{17,16},{1... | collective-permute-start | bytes 3145736 | tf_op jit(solution)/shard_map/ppermute | solution.py:35
  40.9 22.8 %collective-permute-start.6 = (f32[512,512]{1,0:T(8,128)}, f32[512,512]{1,0:T(8,128)}, u32[]{:S(2)}, u32[]{:S(2)}) collective-permute-start(f32[512,512]{1,0:T(8,128)} %collective-permute-done.1.refs_4_), channel_id=1, source_target_pairs={{0,7},{1,0},{2,1},{3,2},{4,3},{5,4},{6,5},{7,6},{16,17},{17,18},{1... | collective-permute-start | bytes 3145736 | tf_op jit(solution)/shard_map/ppermute | solution.py:35
  40.9 24.7 %collective-permute-start.8 = (f32[4,256,256]{2,1,0:T(8,128)}, f32[4,256,256]{2,1,0:T(8,128)S(1)}, u32[]{:S(2)}, u32[]{:S(2)}) collective-permute-start(f32[4,256,256]{2,1,0:T(8,128)} %send.1), channel_id=1, source_target_pairs={{0,8},{8,0},{1,9},{9,1},{2,10},{10,2},{3,11},{11,3},{4,12},{12,4},... | collective-permute-start | bytes 3145736 | tf_op jit(solution)/shard_map/ppermute | solution.py:27
  49.6 17.1 %copy-start.10 = (f32[512,512]{1,0:T(8,128)}, f32[512,512]{1,0:T(8,128)S(1)}, u32[]{:S(2)}) copy-start(f32[512,512]{1,0:T(8,128)S(1)} %collective-permute-done.7.refs_2_) | copy-start | bytes 3145732
  65.6 8.1 %copy-start.4 = (f32[4,256,256]{2,1,0:T(8,128)}, f32[4,256,256]{2,1,0:T(8,128)S(1)}, u32[]{:S(2)}) copy-start(f32[4,256,256]{2,1,0:T(8,128)S(1)} %collective-permute-done.8.refs_6_.refs_4_) | copy-start | bytes 3145732
  65.6 4.5 %collective-permute-start.13 = (f32[4,256,256]{2,1,0:T(8,128)S(1)}, f32[4,256,256]{2,1,0:T(8,128)S(1)}, u32[]{:S(2)}, u32[]{:S(2)}) collective-permute-start(f32[4,256,256]{2,1,0:T(8,128)S(1)} %collective-permute-done.8.refs_6_.refs_4_), channel_id=1, source_target_pairs={{0,16},{16,0},{1,17},{17,1},{2,18},{18,2},{3,19},{19,3},{4,20},{20... | collective-permute-start | bytes 3145736 | tf_op jit(solution)/shard_map/ppermute | solution.py:27
  65.9 24.9 %collective-permute-start.11 = (f32[512,512]{1,0:T(8,128)}, f32[512,512]{1,0:T(8,128)}, u32[]{:S(2)}, u32[]{:S(2)}) collective-permute-start(f32[512,512]{1,0:T(8,128)} %collective-permute-done.4.refs_0_), channel_id=1, source_target_pairs={{0,32},{32,64},{64,96},{96,0},{16,112},{48,16},{80,48},{112,80},{1... | collective-permute-start | bytes 3145736 | tf_op jit(solution)/shard_map/ppermute | solution.py:38
  66.8 26.5 %collective-permute-start.12 = (f32[512,512]{1,0:T(8,128)}, f32[512,512]{1,0:T(8,128)}, u32[]{:S(2)}, u32[]{:S(2)}) collective-permute-start(f32[512,512]{1,0:T(8,128)} %collective-permute-done.4.refs_0_), channel_id=1, source_target_pairs={{0,96},{32,0},{64,32},{96,64},{16,48},{48,80},{80,112},{112,16},{1... | collective-permute-start | bytes 3145736 | tf_op jit(solution)/shard_map/ppermute | solution.py:38
  67.4 25.9 %collective-permute-start.10 = (f32[512,512]{1,0:T(8,128)}, f32[512,512]{1,0:T(8,128)S(1)}, u32[]{:S(2)}, u32[]{:S(2)}) collective-permute-start(f32[512,512]{1,0:T(8,128)} %collective-permute-done.6.refs_3_), channel_id=1, source_target_pairs={{0,7},{1,0},{2,1},{3,2},{4,3},{5,4},{6,5},{7,6},{16,17},{17,18},{1... | collective-permute-start | bytes 3145736 | tf_op jit(solution)/shard_map/ppermute | solution.py:35
  67.4 25.9 %collective-permute-start.9 = (f32[512,512]{1,0:T(8,128)}, f32[512,512]{1,0:T(8,128)}, u32[]{:S(2)}, u32[]{:S(2)}) collective-permute-start(f32[512,512]{1,0:T(8,128)} %collective-permute-done.5.refs_2_), channel_id=1, source_target_pairs={{0,1},{1,2},{2,3},{3,4},{4,5},{5,6},{6,7},{7,0},{16,23},{17,16},{1... | collective-permute-start | bytes 3145736 | tf_op jit(solution)/shard_map/ppermute | solution.py:35
  70.1 3.6 %copy-start.5 = (f32[4,256,256]{2,1,0:T(8,128)}, f32[4,256,256]{2,1,0:T(8,128)S(1)}, u32[]{:S(2)}) copy-start(f32[4,256,256]{2,1,0:T(8,128)S(1)} %collective-permute-done.13.refs_7_.refs_5_) | copy-start | bytes 3145732
  73.7 19.6 %copy-start.12 = (f32[4,256,512]{2,1,0:T(8,128)S(1)}, f32[4,256,512]{2,1,0:T(8,128)}, u32[]{:S(2)}) copy-start(f32[4,256,512]{2,1,0:T(8,128)} %pick0.1) | copy-start | bytes 6291460
  73.7 26.4 %copy-start.2 = (s32[2,16]{1,0:T(2,128)S(1)}, s32[2,16]{1,0:T(2,128)}, u32[]{:S(2)}) copy-start(s32[2,16]{1,0:T(2,128)} %get-tuple-element.34.plan) | copy-start | bytes 388
  93.3 9.5 %copy-start.6 = (f32[512,512]{1,0:T(8,128)}, f32[512,512]{1,0:T(8,128)S(1)}, u32[]{:S(2)}) copy-start(f32[512,512]{1,0:T(8,128)S(1)} %collective-permute-done.10.refs_2_) | copy-start | bytes 3145732
  93.3 5.6 %collective-permute-start.16 = (f32[4,256,512]{2,1,0:T(8,128)S(1)}, f32[4,256,512]{2,1,0:T(8,128)S(1)}, u32[]{:S(2)}, u32[]{:S(2)}) collective-permute-start(f32[4,256,512]{2,1,0:T(8,128)S(1)} %copy-done.12), channel_id=1, source_target_pairs={{0,16},{16,0},{1,17},{17,1},{2,18},{18,2},{3,19},{19,3},{4,20},{20... | collective-permute-start | bytes 6291464 | tf_op jit(solution)/shard_map/ppermute | solution.py:27
  94.5 14.7 %collective-permute-start.15 = (f32[512,512]{1,0:T(8,128)}, f32[512,512]{1,0:T(8,128)S(1)}, u32[]{:S(2)}, u32[]{:S(2)}) collective-permute-start(f32[512,512]{1,0:T(8,128)} %collective-permute-done.9.refs_0_), channel_id=1, source_target_pairs={{0,1},{1,2},{2,3},{3,4},{4,5},{5,6},{6,7},{7,0},{16,23},{17,16},{1... | collective-permute-start | bytes 3145736 | tf_op jit(solution)/shard_map/ppermute | solution.py:35
  97.2 18.3 %collective-permute-start.14 = (f32[512,512]{1,0:T(8,128)}, f32[512,512]{1,0:T(8,128)}, u32[]{:S(2)}, u32[]{:S(2)}) collective-permute-start(f32[512,512]{1,0:T(8,128)} %collective-permute-done.11.refs_1_), channel_id=1, source_target_pairs={{0,32},{32,64},{64,96},{96,0},{16,112},{48,16},{80,48},{112,80},{1... | collective-permute-start | bytes 3145736 | tf_op jit(solution)/shard_map/ppermute | solution.py:38
  119.0 10.0 %copy-start.3 = (f32[512,512]{1,0:T(8,128)S(1)}, f32[512,512]{1,0:T(8,128)}, u32[]{:S(2)}) copy-start(f32[512,512]{1,0:T(8,128)} %refs_0_.5) | copy-start | bytes 3145732
  119.1 10.0 %copy-start.14 = (f32[512]{0:T(512)S(1)}, f32[512]{0:T(512)}, u32[]{:S(2)}) copy-start(f32[512]{0:T(512)} %param.11) | copy-start | bytes 6148
  119.1 10.0 %copy-start.15 = (f32[512]{0:T(512)S(1)}, f32[512]{0:T(512)}, u32[]{:S(2)}) copy-start(f32[512]{0:T(512)} %param.10) | copy-start | bytes 6148
  119.1 5.6 %collective-permute-start.17 = (f32[4,256,512]{2,1,0:T(8,128)}, f32[4,256,512]{2,1,0:T(8,128)S(1)}, u32[]{:S(2)}, u32[]{:S(2)}) collective-permute-start(f32[4,256,512]{2,1,0:T(8,128)} %pick1.1), channel_id=1, source_target_pairs={{0,16},{16,0},{1,17},{17,1},{2,18},{18,2},{3,19},{19,3},{4,20},{20... | collective-permute-start | bytes 6291464 | tf_op jit(solution)/shard_map/ppermute | solution.py:27
  120.7 24.7 %collective-permute-start.18 = (f32[512,512]{1,0:T(8,128)S(1)}, f32[512,512]{1,0:T(8,128)S(1)}, u32[]{:S(2)}, u32[]{:S(2)}) collective-permute-start(f32[512,512]{1,0:T(8,128)S(1)} %beta11.2), channel_id=1, source_target_pairs={{0,8},{8,0},{1,9},{9,1},{2,10},{10,2},{3,11},{11,3},{4,12},{12,4},... | collective-permute-start | bytes 3145736 | tf_op jit(solution)/shard_map/ppermute | solution.py:27
  (3 other events, 3.7 us)

commit v7 on v6

--- a/solution.py
+++ b/solution.py
@@ -60,9 +60,8 @@
 ):
     me, mb = where[0], where[1]
     up = (me & 1) == 0
-    for row in range(2):
-        alpha_plan[row, 0] = 0
-    for row in range(4):
+    alpha_plan[0, 0] = 0
+    for row in range(6):
         beta_plan[row, 0] = 0
 
     def put(plan, row, word):
@@ -79,8 +78,8 @@
             owner = src >> 1
             ahead = (me >> 1) - (owner >> 1)
             hops = jnp.where((owner & 1) == 0, ahead, -ahead) & 3
-            piece = hops + 4 * ((owner ^ me) & 1)
-            put(alpha_plan, (owner >> 3) ^ (me >> 3), piece * 64 + (src & 1) * 32 + slot)
+            piece = hops + 4 * ((owner >> 3) ^ (me >> 3)) + 8 * ((owner ^ me) & 1)
+            put(alpha_plan, 0, piece * 64 + (src & 1) * 32 + slot)
 
         src = alpha_source[2 * (me ^ 1) + (slot >> 3), c]
         owner = src >> 1
@@ -88,7 +87,7 @@
         @pl.when(((owner ^ me) & 1) == 0)
         def _():
             ahead = (me >> 1) - (owner >> 1)
-            picks[(owner >> 3) ^ (me >> 3), jnp.where(up, ahead, -ahead) & 3] = src & 1
+            picks[4 * ((owner >> 3) ^ (me >> 3)) + (jnp.where(up, ahead, -ahead) & 3)] = src & 1
 
         return 0
 
@@ -104,6 +103,8 @@
             ahead = mb - owner
             d = jnp.where(up, ahead, -ahead) & 7
             call = jnp.where((d <= 2) | (d >= 6), 0, 1)
+            if target:
+                call = jnp.where(d == 4, 2, call)
             tile = place if target else c
             word = d * 64 + (src & 1) * 32 + (slot >> 3) * 16 + tile
             put(beta_plan, 2 * call + target, word)
@@ -126,11 +127,11 @@
         pl.when(piece == i)(lambda ref=ref: make(ref).start())
 
 
-def pick_kernel(side, picks, *refs):
-    pieces, (out, sem) = refs[:4], refs[4:]
+def pick_kernel(picks, *refs):
+    pieces, (out, sem) = refs[:8], refs[8:]
     copies = [
         pltpu.make_async_copy(
-            piece.at[pl.ds(pl.multiple_of(picks[side, d] * BS, BS), BS)], out.at[d], sem.at[d]
+            piece.at[pl.ds(pl.multiple_of(picks[d] * BS, BS), BS)], out.at[d], sem.at[d]
         )
         for d, piece in enumerate(pieces)
     ]
@@ -140,27 +141,24 @@
         copy.wait()
 
 
-def pick_call(side, picks, pieces):
+def pick_call(picks, pieces):
     n = pieces[0].shape[1]
     return pl.pallas_call(
-        functools.partial(pick_kernel, side),
-        out_shape=jax.ShapeDtypeStruct((4, BS, n), jnp.float32),
-        in_specs=[SMEM] + [ANY] * 4,
+        pick_kernel,
+        out_shape=jax.ShapeDtypeStruct((8, BS, n), jnp.float32),
+        in_specs=[SMEM] + [ANY] * 8,
         out_specs=VMEM,
-        scratch_shapes=[pltpu.SemaphoreType.DMA((4,))],
+        scratch_shapes=[pltpu.SemaphoreType.DMA((8,))],
+        compiler_params=pltpu.CompilerParams(vmem_limit_bytes=12 * MIB),
         cost_estimate=SMALL,
-        name=f"pick{side}",
+        name="pick",
     )(picks, *pieces)
 
 
-def alpha_kernel(side, plan, *refs):
-    pieces, picked, own, refs = refs[:4], refs[4], refs[5], refs[6:]
-    before, refs = (refs[:1], refs[1:]) if side else ((), refs)
-    out, data, tiles, data_sem, tile_sem, out_sem = refs
-    count = plan[side, 0]
-    if side:
-        first = pltpu.make_async_copy(before[0], out, out_sem)
-        first.start()
+def alpha_kernel(plan, *refs):
+    pieces, picked, own, refs = refs[:8], refs[8], refs[9], refs[10:]
+    out, data, tiles, data_sem, tile_sem = refs
+    count = plan[0, 0]
 
     def tile_of(k, slot):
         return pltpu.make_async_copy(own.at[slot >> 3, slot & 7], tiles.at[k], tile_sem.at[k])
@@ -169,22 +167,19 @@
         return pltpu.make_async_copy(ref, data.at[k], data_sem.at[k])
 
     def fetch(k, _):
-        word = plan[side, k + 1]
+        word = plan[0, k + 1]
         piece = word >> 6
         tile_of(k, word & 31).start()
         rows = pl.ds(pl.multiple_of(((word >> 5) & 1) * BS, BS), BS)
         start_one_of(pieces, piece, lambda ref: rows_of(k, ref.at[rows]))
-        pl.when(piece >= 4)(lambda: rows_of(k, picked.at[piece & 3]).start())
+        pl.when(piece >= 8)(lambda: rows_of(k, picked.at[piece & 7]).start())
         return 0
 
     lax.fori_loop(0, count, fetch, 0)
-    if side:
-        first.wait()
-    else:
-        out[...] = jnp.zeros_like(out)
+    out[...] = jnp.zeros_like(out)
 
     def product(k, _):
-        slot = plan[side, k + 1] & 31
+        slot = plan[0, k + 1] & 31
         tile_of(k, slot).wait()
         rows_of(k, picked.at[0]).wait()
         rows = pl.multiple_of((slot >> 3) * BS, BS)
@@ -194,24 +189,23 @@
     lax.fori_loop(0, count, product, 0)
 
 
-def alpha_call(side, plan, pieces, picked, own, before=()):
+def alpha_call(plan, pieces, picked, own):
     n = own.shape[0] * BS
     return pl.pallas_call(
-        functools.partial(alpha_kernel, side),
+        alpha_kernel,
         out_shape=jax.ShapeDtypeStruct((n, n), jnp.float32),
-        in_specs=[SMEM] + [HBM] * 6 + [ANY] * len(before),
+        in_specs=[SMEM] + [HBM] * 10,
         out_specs=VMEM,
         scratch_shapes=[
-            pltpu.VMEM((SLOTS, BS, n), jnp.float32),
-            pltpu.VMEM((SLOTS, BS, BS), jnp.float32),
-            pltpu.SemaphoreType.DMA((SLOTS,)),
-            pltpu.SemaphoreType.DMA((SLOTS,)),
-            pltpu.SemaphoreType.DMA,
+            pltpu.VMEM((2 * SLOTS, BS, n), jnp.float32),
+            pltpu.VMEM((2 * SLOTS, BS, BS), jnp.float32),
+            pltpu.SemaphoreType.DMA((2 * SLOTS,)),
+            pltpu.SemaphoreType.DMA((2 * SLOTS,)),
         ],
-        compiler_params=pltpu.CompilerParams(vmem_limit_bytes=16 * MIB),
+        compiler_params=pltpu.CompilerParams(vmem_limit_bytes=18 * MIB),
         cost_estimate=SMALL,
-        name=f"alpha{side}",
-    )(plan, *in_hbm(*pieces, picked, own), *before)
+        name="alpha",
+    )(plan, *in_hbm(*pieces, picked, own))
 
 
 def send_kernel(where, sends, own, out, sem):
@@ -239,14 +233,14 @@
     )(where, sends, *in_hbm(own))
 
 
-HOPS = ((0, 1, 2, 6, 7), (3, 4, 5))
+HOPS = {(0, 0): (0, 1, 2, 6, 7), (0, 1): (0, 1, 2, 6, 7), (1, 0): (3, 4, 5), (1, 1): (3, 5), (2, 1): (4,)}
 
 
 def beta_kernel(call, targets, where, plan, *refs):
-    numbers = HOPS[call]
+    numbers = HOPS[call, targets[0]]
     pieces, refs = refs[: len(numbers)], refs[len(numbers) :]
     own, got, other, refs = refs[0], refs[1], refs[2], refs[3:]
-    before, refs = (refs[: len(targets)], refs[len(targets) :]) if call else ((), refs)
+    before, refs = (refs[: len(targets)], refs[len(targets) :]) if call == 1 else ((), refs)
     outs, (data, tiles, data_sem, tile_sem, out_sem) = refs[: len(targets)], refs[len(targets) :]
     core = where[0] & 1
     firsts = [
@@ -285,7 +279,7 @@
         lax.fori_loop(0, plan[row, 0], fetch, 0)
         base = base + plan[row, 0]
     for out in outs:
-        if not call:
+        if call != 1:
             out[...] = jnp.zeros_like(out)
     for first in firsts:
         first.wait()
@@ -298,7 +292,7 @@
             block = (plan[row, j + 1] >> 4) & 1
             columns_of(k, pieces[0], 0).wait()
             tile_from(k, own.at[0, 0]).wait()
-            columns = pl.multiple_of(block * BS, BS)
+            columns = 0 if call == 2 else pl.multiple_of(block * BS, BS)
             out[:, pl.ds(columns, BS)] += dot3(data[k], tiles[k])
             return 0
 
@@ -308,11 +302,12 @@
 
 def beta_call(call, targets, where, plan, held, own, got, other, before=()):
     n = held[0].shape[0]
-    pieces = [held[d] for d in HOPS[call]]
-    most = len(HOPS[call]) * len(targets)
+    pieces = [held[d] for d in HOPS[call, targets[0]]]
+    most = len(pieces) * len(targets)
+    width = BS if call == 2 else n
     return pl.pallas_call(
         functools.partial(beta_kernel, call, targets),
-        out_shape=[jax.ShapeDtypeStruct((n, n), jnp.float32)] * len(targets),
+        out_shape=[jax.ShapeDtypeStruct((n, width), jnp.float32)] * len(targets),
         in_specs=[SMEM] * 2 + [HBM] * (len(pieces) + 3) + [ANY] * len(before),
         out_specs=[VMEM] * len(targets),
         scratch_shapes=[
@@ -323,7 +318,7 @@
             pltpu.SemaphoreType.DMA((2,)),
         ],
         compiler_params=pltpu.CompilerParams(vmem_limit_bytes=16 * MIB),
-        cost_estimate=SMALL,
+        cost_estimate=(pl.CostEstimate(flops=1 << 34, bytes_accessed=1 << 25, transcendentals=0) if call else SMALL),
         name=f"beta{call}{len(targets)}",
     )(where, plan, *in_hbm(*pieces, own, got, other), *before)
 
@@ -346,9 +341,9 @@
     alpha_plan, beta_plan, picks, sends = pl.pallas_call(
         plan_kernel,
         out_shape=[
-            jax.ShapeDtypeStruct((2, 16), jnp.int32),
-            jax.ShapeDtypeStruct((4, 32), jnp.int32),
-            jax.ShapeDtypeStruct((2, 4), jnp.int32),
+            jax.ShapeDtypeStruct((1, 32), jnp.int32),
+            jax.ShapeDtypeStruct((6, 32), jnp.int32),
+            jax.ShapeDtypeStruct((8,), jnp.int32),
             jax.ShapeDtypeStruct((SLOTS,), jnp.int32),
         ],
         in_specs=[SMEM] * 5,
@@ -356,36 +351,40 @@
         name="plan",
     )(where, alpha_source, alpha_live, beta_source, beta_live)
     tiles = send_call(where, sends, beta_tiles)
-    f1, b1, uf, ub, v, tiles, picks = lax.optimization_barrier((f1, b1, uf, ub, v, tiles, picks))
+    f1, b1, tiles = lax.optimization_barrier((f1, b1, tiles))
     f2, b2 = step(f1, "z"), step(b1, "z", -1)
-    u2 = step(uf, "x")
-    got = swap(tiles, "ylo")
-    f2, b2, u2, got = lax.optimization_barrier((f2, b2, u2, got))
+    uf, ub, v = lax.optimization_barrier((uf, ub, v, f1))[:3]
+    vf, vb = step(v, "x"), step(v, "x", -1)
+    got = swap(after(tiles, v), "ylo")
+    f2, b2 = lax.optimization_barrier((f2, b2))
     f3, b3 = step(f2, "z"), step(b2, "z", -1)
-    vf, vb = step(v, "x"), step(v, "x", -1)
+    vf, vb, got, uf = lax.optimization_barrier((vf, vb, got, uf, f2))[:4]
+    u2, v2 = step(uf, "x"), step(vf, "x")
     other = swap(got, "core")
-    picked = pick_call(0, after(picks, other), [coeffs, uf, u2, ub])
     held = [coeffs, f1, f2, None, None, None, b2, b1]
     beta_own, beta_par = beta_call(0, (0, 1), where, beta_plan, held, beta_tiles, got, other)
-    f3, b3, vf, vb, picked, beta_own, beta_par = lax.optimization_barrier(
-        (f3, b3, vf, vb, picked, beta_own, beta_par)
-    )
+    f3, b3, beta_own, beta_par = lax.optimization_barrier((f3, b3, beta_own, beta_par))
     held[3], held[4], held[5] = f3, step(f3, "z"), b3
-    v2 = step(vf, "x")
-    u_picked = swap(picked, "core")
-    alpha = alpha_call(0, alpha_plan, [coeffs, uf, u2, ub], u_picked, alpha_tiles)
-    alpha, beta_par = lax.optimization_barrier((alpha, beta_par))
     (beta_par,) = beta_call(
         1, (1,), where, beta_plan, held, beta_tiles, got, other, [beta_par]
     )
     beta_other = swap(beta_par, "ylo")
+    pieces = [coeffs, uf, u2, ub, v, vf, v2, vb]
+    picked = swap(pick_call(after(picks, beta_par), pieces), "core")
+    (far,) = beta_call(2, (1,), where, beta_plan, held, beta_tiles, got, other)
+    far_other = swap(far, "ylo")
+    alpha = alpha_call(alpha_plan, pieces, picked, after(alpha_tiles, far))
     (beta_own,) = beta_call(
-        1, (0,), where, beta_plan, held, after(beta_tiles, beta_par), got, other, [beta_own]
+        1, (0,), where, beta_plan, held, after(beta_tiles, far), got, other, [beta_own]
     )
-    v_picked = swap(pick_call(1, after(picks, beta_own), [v, vf, v2, vb]), "core")
-    alpha = alpha_call(1, alpha_plan, [v, vf, v2, vb], v_picked, alpha_tiles, [alpha])
     joined = (diag_alpha[:, None] + diag_beta[None, :]) * coeffs + alpha + beta_own
-    return lax.optimization_barrier(joined) + beta_other
+    joined, place = lax.optimization_barrier((joined, (where[1] + 4) & 7))
+    joined = lax.optimization_barrier(joined + beta_other)
+    block = lax.dynamic_index_in_dim(sends, place, 0, keepdims=False) >> 3
+    zero = jnp.zeros_like(far_other)
+    low = jnp.where(block == 0, far_other, zero)
+    high = jnp.where(block == 0, zero, far_other)
+    return joined + jnp.concatenate([low, high], axis=1)
 
 
 def solution(mesh):

time: 147 us -> 134 us (0.912)
  waiting for transfers between devices: 78.6 us -> 70.1 us
  starting transfers between devices: 31.1 us -> 28.1 us
  Pallas kernels: 25.4 us -> 23.8 us
    ppermute x6, waiting for transfers between devices: 29.2 us -> 6.84 us  [step(): return lax.ppermute(value, (axis, 'core'), pairs)]
    ppermute x7, waiting for transfers between devices: 27.4 us -> 39.5 us  [step(): return lax.ppermute(value, ('core', axis), pairs)]
    pallas_call x5 -> x3, Pallas kernels: 16.4 us -> 11.5 us  [the longest x1 4.26 us: alpha_call(): pl.pallas_call(alpha_kernel, out_shape=jax.ShapeDtypeStruct((n, n), jnp.f...]
    pallas_call x3 -> x4, Pallas kernels: 6.16 us -> 9.41 us  [beta_call(): pl.pallas_call(functools.partial(beta_kernel, call, targets), out_shape=[...]
    ppermute x6, waiting for transfers between devices: 22 us -> 23.8 us  [swap(): return lax.ppermute(value, axis, [(0, 1), (1, 0)])]
    unnamed x36 -> x52, local copies, waits for them, and re-layouts: 9.14 us -> 7.9 us
  transfers between devices with their start and end apart: 19 -> 19, of which waited for: 12 -> 12; matrix products, arithmetic and copies ran while one was open for 4% -> 5% of each run, Pallas kernels for 13% -> 16%
where the time goes in v7:
time: 134 us
  waiting for transfers between devices  70.1 us (52%)
  starting transfers between devices  28.1 us (21%)
  Pallas kernels  23.8 us (18%)
  local copies, waits for them, and re-layouts  8.48 us (6%)
  other arithmetic  2.22 us (2%)
    ppermute x7, waiting for transfers between devices, step(): return lax.ppermute(value, ('core', axis), pairs)  39.5 us
    ppermute x6, waiting for transfers between devices, swap(): return lax.ppermute(value, axis, [(0, 1), (1, 0)])  23.8 us
    ppermute x7, starting transfers between devices, step(): return lax.ppermute(value, ('core', axis), pairs)  13.6 us
    pallas_call x4, Pallas kernels, beta_call(): pl.pallas_call(functools.partial(beta_kernel, call, targets), out_shape=[...  9.41 us
    ppermute x6, starting transfers between devices, step(): return lax.ppermute(value, (axis, 'core'), pairs)  8.15 us
    unnamed x52, local copies, waits for them, and re-layouts  7.9 us
    ppermute x6, waiting for transfers between devices, step(): return lax.ppermute(value, (axis, 'core'), pairs)  6.84 us
    ppermute x6, starting transfers between devices, swap(): return lax.ppermute(value, axis, [(0, 1), (1, 0)])  6.39 us
  transfers between devices with their start and end apart: 19, of which 12 were waited for; matrix products, arithmetic and copies ran while one was open for 5% of the time, Pallas kernels for 16%

profile of v7, /device:TPU:1, one launch (start us, length us, event | category | flops | bytes accessed | tf_op | source)
XLA Modules:
  0.0 133.7 jit_solution(7109856681828989635)
XLA Ops:
  0.0 2.5 %collective-permute-start.4 = (f32[512,512]{1,0:T(8,128)}, f32[512,512]{1,0:T(8,128)S(1)}, u32[]{:S(2)}, u32[]{:S(2)}) collective-permute-start(f32[512,512]{1,0:T(8,128)} %refs_0_.5), channel_id=1, source_target_pairs={{0,7},{1,0},{2,1},{3,2},{4,3},{5,4},{6,5},{7,6},{16,17},{17,18},{1... | collective-permute-start | bytes 3145736 | tf_op jit(solution)/shard_map/ppermute | solution.py:35
  2.5 3.9 %collective-permute-start.3 = (f32[512,512]{1,0:T(8,128)}, f32[512,512]{1,0:T(8,128)}, u32[]{:S(2)}, u32[]{:S(2)}) collective-permute-start(f32[512,512]{1,0:T(8,128)} %refs_0_.5), channel_id=1, source_target_pairs={{0,1},{1,2},{2,3},{3,4},{4,5},{5,6},{6,7},{7,0},{16,23},{17,16},{1... | collective-permute-start | bytes 3145736 | tf_op jit(solution)/shard_map/ppermute | solution.py:35
  6.4 2.9 %collective-permute-start.2 = (f32[512,512]{1,0:T(8,128)}, f32[512,512]{1,0:T(8,128)S(1)}, u32[]{:S(2)}, u32[]{:S(2)}) collective-permute-start(f32[512,512]{1,0:T(8,128)} %refs_0_.5), channel_id=1, source_target_pairs={{0,128},{128,0},{1,129},{129,1},{2,130},{130,2},{3,131},{131,3},{4... | collective-permute-start | bytes 3145736 | tf_op jit(solution)/shard_map/ppermute | solution.py:27
  9.3 1.2 collective-permute-start.1
  10.5 1.5 %collective-permute-start = (f32[512,512]{1,0:T(8,128)}, f32[512,512]{1,0:T(8,128)}, u32[]{:S(2)}, u32[]{:S(2)}) collective-permute-start(f32[512,512]{1,0:T(8,128)} %refs_0_.5), channel_id=1, source_target_pairs={{0,32},{32,64},{64,96},{96,0},{16,112},{48,16},{80,48},{112,80},{1... | collective-permute-start | bytes 3145736 | tf_op jit(solution)/shard_map/ppermute | solution.py:38
  12.0 1.4 %copy.10.alpha_source = s32[32,8]{1,0:T(8,128)} copy(s32[32,8]{0,1:T(8,128)} %param.14) | data formatting | bytes 2048 | tf_op args[5]
  13.4 1.4 %copy.11.alpha_live = s32[32,8]{1,0:T(8,128)} copy(s32[32,8]{0,1:T(8,128)} %param.15) | data formatting | bytes 2048 | tf_op args[6]
  14.7 1.4 %copy.12.beta_source = s32[32,8]{1,0:T(8,128)} copy(s32[32,8]{0,1:T(8,128)} %param.16) | data formatting | bytes 2048 | tf_op args[7]
  16.1 1.4 %copy.13.beta_live = s32[32,8]{1,0:T(8,128)} copy(s32[32,8]{0,1:T(8,128)} %param.17) | data formatting | bytes 2048 | tf_op args[8]
  18.0 3.5 %plan.1 = (s32[1,32]{1,0:T(1,128)}, s32[6,32]{1,0:T(8,128)}, s32[8]{0:T(128)}, s32[8]{0:T(128)}) custom-call(s32[2]{0:T(128)} %pad_add_fusion.where, s32[32,8]{1,0:T(8,128)} %copy.10.alpha_source, s32[32,8]{1,0:T(8,128)} %copy.11.alpha_live, s32[32,8]{1,0:T(8,128)} %copy.12.beta_source, s32[32,8]{1,0:T(8,128)} %copy.13.beta_live), custom_call_target="tpu_custom_call" | custom-call | tf_op jit(solution)/shard_map/plan/pallas_call | solution.py:341
  21.6 2.9 %send.1 = f32[4,256,256]{2,1,0:T(8,128)} custom-call(s32[2]{0:T(128)} %pad_add_fusion.where, s32[8]{0:T(128)} %get-tuple-element.34.sends, f32[2,8,256,256]{3,2,1,0:T(8,128)} %refs_3_), custom_call_target="tpu_custom_call" | custom-call | flops 1048576 | bytes 262144 | tf_op jit(solution)/shard_map/send/pallas_call | solution.py:225
  24.4 1.8 %collective-permute-done.4.refs_4_ = f32[512,512]{1,0:T(8,128)S(1)} collective-permute-done((f32[512,512]{1,0:T(8,128)}, f32[512,512]{1,0:T(8,128)S(1)}, u32[]{:S(2)}, u32[]{:S(2)}) %collective-permute-start.4) | collective-permute-done | bytes 1048608 | tf_op jit(solution)/shard_map/ppermute | solution.py:35
  26.3 2.3 %collective-permute-done.3.refs_1_ = f32[512,512]{1,0:T(8,128)} collective-permute-done((f32[512,512]{1,0:T(8,128)}, f32[512,512]{1,0:T(8,128)}, u32[]{:S(2)}, u32[]{:S(2)}) %collective-permute-start.3) | collective-permute-done | bytes 1048608 | tf_op jit(solution)/shard_map/ppermute | solution.py:35
  29.1 2.9 %collective-permute-start.8 = (f32[512,512]{1,0:T(8,128)}, f32[512,512]{1,0:T(8,128)S(1)}, u32[]{:S(2)}, u32[]{:S(2)}) collective-permute-start(f32[512,512]{1,0:T(8,128)} %collective-permute-done.3.refs_1_), channel_id=1, source_target_pairs={{0,1},{1,2},{2,3},{3,4},{4,5},{5,6},{6,7},{7,0},{16,23},{17,16},{1... | collective-permute-start | bytes 3145736 | tf_op jit(solution)/shard_map/ppermute | solution.py:35
  32.0 3.6 %collective-permute-done.refs_1_ = f32[512,512]{1,0:T(8,128)} collective-permute-done((f32[512,512]{1,0:T(8,128)}, f32[512,512]{1,0:T(8,128)}, u32[]{:S(2)}, u32[]{:S(2)}) %collective-permute-start) | collective-permute-done | bytes 1048608 | tf_op jit(solution)/shard_map/ppermute | solution.py:38
  37.1 1.6 %collective-permute-start.5 = (f32[512,512]{1,0:T(8,128)S(1)}, f32[512,512]{1,0:T(8,128)S(1)}, u32[]{:S(2)}, u32[]{:S(2)}) collective-permute-start(f32[512,512]{1,0:T(8,128)S(1)} %collective-permute-done.2.refs_4_), channel_id=1, source_target_pairs={{0,32},{32,64},{64,96},{96,0},{16,112},{48,16},{80,48},{112,80},{1... | collective-permute-start | bytes 3145736 | tf_op jit(solution)/shard_map/ppermute | solution.py:38
  38.7 11.8 %collective-permute-done.9.refs_3_ = f32[512,512]{1,0:T(8,128)S(1)} collective-permute-done((f32[512,512]{1,0:T(8,128)S(1)}, f32[512,512]{1,0:T(8,128)S(1)}, u32[]{:S(2)}, u32[]{:S(2)}) %collective-permute-start.9) | collective-permute-done | bytes 1048608 | tf_op jit(solution)/shard_map/ppermute | solution.py:35
  50.5 3.0 %collective-permute-done.8.refs_2_ = f32[512,512]{1,0:T(8,128)S(1)} collective-permute-done((f32[512,512]{1,0:T(8,128)}, f32[512,512]{1,0:T(8,128)S(1)}, u32[]{:S(2)}, u32[]{:S(2)}) %collective-permute-start.8) | collective-permute-done | bytes 1048608 | tf_op jit(solution)/shard_map/ppermute | solution.py:35
  53.5 6.2 %collective-permute-done.7.refs_6_.refs_3_.refs_2_.refs_4_ = f32[4,256,256]{2,1,0:T(8,128)S(1)} collective-permute-done((f32[4,256,256]{2,1,0:T(8,128)}, f32[4,256,256]{2,1,0:T(8,128)S(1)}, u32[]{:S(2)}, u32[]{:S(2)}) %collective-permute-start.7) | collective-permute-done | bytes 1048608 | tf_op jit(solution)/shard_map/ppermute | solution.py:27
  59.7 2.2 %collective-permute-done.5.refs_5_ = f32[512,512]{1,0:T(8,128)S(1)} collective-permute-done((f32[512,512]{1,0:T(8,128)S(1)}, f32[512,512]{1,0:T(8,128)S(1)}, u32[]{:S(2)}, u32[]{:S(2)}) %collective-permute-start.5) | collective-permute-done | bytes 1048608 | tf_op jit(solution)/shard_map/ppermute | solution.py:38
  62.8 2.7 %collective-permute-start.12 = (f32[512,512]{1,0:T(8,128)S(1)}, f32[512,512]{1,0:T(8,128)}, u32[]{:S(2)}, u32[]{:S(2)}) collective-permute-start(f32[512,512]{1,0:T(8,128)S(1)} %collective-permute-done.8.refs_2_), channel_id=1, source_target_pairs={{0,1},{1,2},{2,3},{3,4},{4,5},{5,6},{6,7},{7,0},{16,23},{17,16},{1... | collective-permute-start | bytes 3145736 | tf_op jit(solution)/shard_map/ppermute | solution.py:35
  65.5 2.8 %collective-permute-start.10 = (f32[512,512]{1,0:T(8,128)}, f32[512,512]{1,0:T(8,128)S(1)}, u32[]{:S(2)}, u32[]{:S(2)}) collective-permute-start(f32[512,512]{1,0:T(8,128)} %collective-permute-done.refs_1_), channel_id=1, source_target_pairs={{0,32},{32,64},{64,96},{96,0},{16,112},{48,16},{80,48},{112,80},{1... | collective-permute-start | bytes 3145736 | tf_op jit(solution)/shard_map/ppermute | solution.py:38
  69.3 3.5 %beta02.1 = (f32[512,512]{1,0:T(8,128)S(1)}, f32[512,512]{1,0:T(8,128)S(1)}) custom-call(s32[2]{0:T(128)S(1)} %copy-done.8, s32[6,32]{1,0:T(8,128)S(1)} %copy-done.9, f32[512,512]{1,0:T(8,128)} %refs_0_.5, f32[512,512]{1,0:T(8,128)} %collective-permute-done.3.refs_1_, f32[512,512]{1,0:T(8,128)} %copy-done.19, f32[512,512]{1,0:T(8,128)} %copy-done.18, ...), custom_call_target="tpu_custom_call" | custom-call | flops 1048576 | bytes 262144 | tf_op jit(solution)/shard_map/beta02/pallas_call | solution.py:308
  73.8 14.8 %collective-permute-done.13.refs_1_.refs_2_ = f32[512,512]{1,0:T(8,128)S(1)} collective-permute-done((f32[512,512]{1,0:T(8,128)S(1)}, f32[512,512]{1,0:T(8,128)S(1)}, u32[]{:S(2)}, u32[]{:S(2)}) %collective-permute-start.13) | collective-permute-done | bytes 1048608 | tf_op jit(solution)/shard_map/ppermute | solution.py:35
  91.5 3.7 %pick.1 = f32[8,256,512]{2,1,0:T(8,128)} custom-call(s32[8]{0:T(128)S(1)} %copy-done.11, f32[512,512]{1,0:T(8,128)S(1)} %copy-done, f32[512,512]{1,0:T(8,128)} %collective-permute-done.refs_1_, f32[512,512]{1,0:T(8,128)S(1)} %collective-permute-done.10.refs_2_, f32[512,512]{1,0:T(8,128)S(1)} %collective-permute-done.1.refs_3_, ...), custom_call_target="tpu_custom_call" | custom-call | flops 1048576 | bytes 262144 | tf_op jit(solution)/shard_map/pick/pallas_call | solution.py:146
  97.4 5.8 %collective-permute-done.16.refs_0_.refs_1_ = f32[512,512]{1,0:T(8,128)} collective-permute-done((f32[512,512]{1,0:T(8,128)}, f32[512,512]{1,0:T(8,128)}, u32[]{:S(2)}, u32[]{:S(2)}) %collective-permute-start.16) | collective-permute-done | bytes 1048608 | tf_op jit(solution)/shard_map/ppermute | solution.py:35
  103.1 2.2 %beta21.1 = f32[512,256]{1,0:T(8,128)S(1)} custom-call(s32[2]{0:T(128)S(1)} %copy-done.8, s32[6,32]{1,0:T(8,128)S(1)} %copy-done.9, f32[512,512]{1,0:T(8,128)} %collective-permute-done.16.refs_0_.refs_1_, f32[2,8,256,256]{3,2,1,0:T(8,128)} %refs_3_, f32[4,256,256]{2,1,0:T(8,128)} %copy-done.16, f32[4,256,256]{2,1,0:T(8,128)} %copy-done.17), custom_call_target="tpu_custom_call" | custom-call | flops 17179869184 | bytes 33554432 | tf_op jit(solution)/shard_map/beta21/pallas_call | solution.py:308
  105.4 3.0 %beta11.3 = f32[512,512]{1,0:T(8,128)S(1)} custom-call(s32[2]{0:T(128)S(1)} %copy-done.8, s32[6,32]{1,0:T(8,128)S(1)} %copy-done.9, f32[512,512]{1,0:T(8,128)} %collective-permute-done.12.refs_0_, f32[512,512]{1,0:T(8,128)} %collective-permute-done.16.refs_0_.refs_1_, f32[512,512]{1,0:T(8,128)} %copy-done.23, f32[2,8,256,256]{3,2,1,0:T(8,128)} %refs_3_, ...), custom_call_target="tpu_custom_call" | custom-call | flops 17179869184 | bytes 33554432 | tf_op jit(solution)/shard_map/beta11/pallas_call | solution.py:308
  108.5 4.3 %alpha.1 = f32[512,512]{1,0:T(8,128)S(1)} custom-call(s32[1,32]{1,0:T(1,128)S(1)} %copy-done.10, f32[512,512]{1,0:T(8,128)} %refs_0_.5, f32[512,512]{1,0:T(8,128)} %collective-permute-done.refs_1_, f32[512,512]{1,0:T(8,128)} %copy-done.6, f32[512,512]{1,0:T(8,128)} %copy-done.3, f32[512,512]{1,0:T(8,128)} %copy-done.2, f32[512,512]{1,0:T(8,128)} %copy-done.5, ...), custom_call_target="tpu_custom_call" | custom-call | flops 1048576 | bytes 262144 | tf_op jit(solution)/shard_map/alpha/pallas_call | solution.py:194
  114.0 7.2 %collective-permute-done.17 = f32[512,512]{1,0:T(8,128)S(1)} collective-permute-done((f32[512,512]{1,0:T(8,128)}, f32[512,512]{1,0:T(8,128)S(1)}, u32[]{:S(2)}, u32[]{:S(2)}) %collective-permute-start.17) | collective-permute-done | bytes 1048608 | tf_op jit(solution)/shard_map/ppermute | solution.py:27
  122.1 10.4 %collective-permute-done.18 = f32[512,256]{1,0:T(8,128)S(1)} collective-permute-done((f32[512,256]{1,0:T(8,128)S(1)}, f32[512,256]{1,0:T(8,128)S(1)}, u32[]{:S(2)}, u32[]{:S(2)}) %collective-permute-start.18) | collective-permute-done | bytes 524320 | tf_op jit(solution)/shard_map/ppermute | solution.py:27
  132.5 1.1 maximum_add_fusion
  (72 shorter events, 12.1 us)
Async XLA Ops:
  0.0 26.3 %collective-permute-start.4 = (f32[512,512]{1,0:T(8,128)}, f32[512,512]{1,0:T(8,128)S(1)}, u32[]{:S(2)}, u32[]{:S(2)}) collective-permute-start(f32[512,512]{1,0:T(8,128)} %refs_0_.5), channel_id=1, source_target_pairs={{0,7},{1,0},{2,1},{3,2},{4,3},{5,4},{6,5},{7,6},{16,17},{17,18},{1... | collective-permute-start | bytes 3145736 | tf_op jit(solution)/shard_map/ppermute | solution.py:35
  2.5 26.1 %collective-permute-start.3 = (f32[512,512]{1,0:T(8,128)}, f32[512,512]{1,0:T(8,128)}, u32[]{:S(2)}, u32[]{:S(2)}) collective-permute-start(f32[512,512]{1,0:T(8,128)} %refs_0_.5), channel_id=1, source_target_pairs={{0,1},{1,2},{2,3},{3,4},{4,5},{5,6},{6,7},{7,0},{16,23},{17,16},{1... | collective-permute-start | bytes 3145736 | tf_op jit(solution)/shard_map/ppermute | solution.py:35
  6.4 25.6 %collective-permute-start.2 = (f32[512,512]{1,0:T(8,128)}, f32[512,512]{1,0:T(8,128)S(1)}, u32[]{:S(2)}, u32[]{:S(2)}) collective-permute-start(f32[512,512]{1,0:T(8,128)} %refs_0_.5), channel_id=1, source_target_pairs={{0,128},{128,0},{1,129},{129,1},{2,130},{130,2},{3,131},{131,3},{4... | collective-permute-start | bytes 3145736 | tf_op jit(solution)/shard_map/ppermute | solution.py:27
  9.3 22.7 %collective-permute-start.1 = (f32[512,512]{1,0:T(8,128)}, f32[512,512]{1,0:T(8,128)S(1)}, u32[]{:S(2)}, u32[]{:S(2)}) collective-permute-start(f32[512,512]{1,0:T(8,128)} %refs_0_.5), channel_id=1, source_target_pairs={{0,96},{32,0},{64,32},{96,64},{16,48},{48,80},{80,112},{112,16},{1... | collective-permute-start | bytes 3145736 | tf_op jit(solution)/shard_map/ppermute | solution.py:38
  10.5 25.1 %collective-permute-start = (f32[512,512]{1,0:T(8,128)}, f32[512,512]{1,0:T(8,128)}, u32[]{:S(2)}, u32[]{:S(2)}) collective-permute-start(f32[512,512]{1,0:T(8,128)} %refs_0_.5), channel_id=1, source_target_pairs={{0,32},{32,64},{64,96},{96,0},{16,112},{48,16},{80,48},{112,80},{1... | collective-permute-start | bytes 3145736 | tf_op jit(solution)/shard_map/ppermute | solution.py:38
  18.0 51.2 %copy-start.8 = (s32[2]{0:T(128)S(1)}, s32[2]{0:T(128)}, u32[]{:S(2)}) copy-start(s32[2]{0:T(128)} %pad_add_fusion.where) | copy-start | bytes 28
  21.5 47.7 %copy-start.9 = (s32[6,32]{1,0:T(8,128)S(1)}, s32[6,32]{1,0:T(8,128)}, u32[]{:S(2)}) copy-start(s32[6,32]{1,0:T(8,128)} %get-tuple-element.47.plan) | copy-start | bytes 2308
  26.3 42.0 %copy-start.15 = (f32[512,512]{1,0:T(8,128)}, f32[512,512]{1,0:T(8,128)S(1)}, u32[]{:S(2)}) copy-start(f32[512,512]{1,0:T(8,128)S(1)} %collective-permute-done.4.refs_4_) | copy-start | bytes 3145732
  28.6 22.0 %collective-permute-start.9 = (f32[512,512]{1,0:T(8,128)S(1)}, f32[512,512]{1,0:T(8,128)S(1)}, u32[]{:S(2)}, u32[]{:S(2)}) collective-permute-start(f32[512,512]{1,0:T(8,128)S(1)} %collective-permute-done.4.refs_4_), channel_id=1, source_target_pairs={{0,7},{1,0},{2,1},{3,2},{4,3},{5,4},{6,5},{7,6},{16,17},{17,18},{1... | collective-permute-start | bytes 3145736 | tf_op jit(solution)/shard_map/ppermute | solution.py:35
  29.1 24.4 %collective-permute-start.8 = (f32[512,512]{1,0:T(8,128)}, f32[512,512]{1,0:T(8,128)S(1)}, u32[]{:S(2)}, u32[]{:S(2)}) collective-permute-start(f32[512,512]{1,0:T(8,128)} %collective-permute-done.3.refs_1_), channel_id=1, source_target_pairs={{0,1},{1,2},{2,3},{3,4},{4,5},{5,6},{6,7},{7,0},{16,23},{17,16},{1... | collective-permute-start | bytes 3145736 | tf_op jit(solution)/shard_map/ppermute | solution.py:35
  32.0 59.5 %copy-start.2 = (f32[512,512]{1,0:T(8,128)}, f32[512,512]{1,0:T(8,128)S(1)}, u32[]{:S(2)}) copy-start(f32[512,512]{1,0:T(8,128)S(1)} %collective-permute-done.2.refs_4_) | copy-start | bytes 3145732
  32.0 59.5 %copy-start.3 = (f32[512,512]{1,0:T(8,128)}, f32[512,512]{1,0:T(8,128)S(1)}, u32[]{:S(2)}) copy-start(f32[512,512]{1,0:T(8,128)S(1)} %collective-permute-done.1.refs_3_) | copy-start | bytes 3145732
  35.6 24.1 %collective-permute-start.7 = (f32[4,256,256]{2,1,0:T(8,128)}, f32[4,256,256]{2,1,0:T(8,128)S(1)}, u32[]{:S(2)}, u32[]{:S(2)}) collective-permute-start(f32[4,256,256]{2,1,0:T(8,128)} %send.1), channel_id=1, source_target_pairs={{0,8},{8,0},{1,9},{9,1},{2,10},{10,2},{3,11},{11,3},{4,12},{12,4},... | collective-permute-start | bytes 3145736 | tf_op jit(solution)/shard_map/ppermute | solution.py:27
  36.0 23.7 %collective-permute-start.6 = (f32[512,512]{1,0:T(8,128)S(1)}, f32[512,512]{1,0:T(8,128)S(1)}, u32[]{:S(2)}, u32[]{:S(2)}) collective-permute-start(f32[512,512]{1,0:T(8,128)S(1)} %collective-permute-done.2.refs_4_), channel_id=1, source_target_pairs={{0,96},{32,0},{64,32},{96,64},{16,48},{48,80},{80,112},{112,16},{1... | collective-permute-start | bytes 3145736 | tf_op jit(solution)/shard_map/ppermute | solution.py:38
  37.1 24.8 %collective-permute-start.5 = (f32[512,512]{1,0:T(8,128)S(1)}, f32[512,512]{1,0:T(8,128)S(1)}, u32[]{:S(2)}, u32[]{:S(2)}) collective-permute-start(f32[512,512]{1,0:T(8,128)S(1)} %collective-permute-done.2.refs_4_), channel_id=1, source_target_pairs={{0,32},{32,64},{64,96},{96,0},{16,112},{48,16},{80,48},{112,80},{1... | collective-permute-start | bytes 3145736 | tf_op jit(solution)/shard_map/ppermute | solution.py:38
  50.5 17.8 %copy-start.18 = (f32[512,512]{1,0:T(8,128)}, f32[512,512]{1,0:T(8,128)S(1)}, u32[]{:S(2)}) copy-start(f32[512,512]{1,0:T(8,128)S(1)} %collective-permute-done.9.refs_3_) | copy-start | bytes 3145732
  53.5 14.8 %copy-start.19 = (f32[512,512]{1,0:T(8,128)}, f32[512,512]{1,0:T(8,128)S(1)}, u32[]{:S(2)}) copy-start(f32[512,512]{1,0:T(8,128)S(1)} %collective-permute-done.8.refs_2_) | copy-start | bytes 3145732
  59.7 8.6 %copy-start.16 = (f32[4,256,256]{2,1,0:T(8,128)}, f32[4,256,256]{2,1,0:T(8,128)S(1)}, u32[]{:S(2)}) copy-start(f32[4,256,256]{2,1,0:T(8,128)S(1)} %collective-permute-done.7.refs_6_.refs_3_.refs_2_.refs_4_) | copy-start | bytes 3145732
  59.7 31.7 %copy-start.4 = (f32[512,512]{1,0:T(8,128)}, f32[512,512]{1,0:T(8,128)S(1)}, u32[]{:S(2)}) copy-start(f32[512,512]{1,0:T(8,128)S(1)} %collective-permute-done.6.refs_7_) | copy-start | bytes 3145732
  61.9 29.5 %copy-start.5 = (f32[512,512]{1,0:T(8,128)}, f32[512,512]{1,0:T(8,128)S(1)}, u32[]{:S(2)}) copy-start(f32[512,512]{1,0:T(8,128)S(1)} %collective-permute-done.5.refs_5_) | copy-start | bytes 3145732
  61.9 6.3 %collective-permute-start.14 = (f32[4,256,256]{2,1,0:T(8,128)S(1)}, f32[4,256,256]{2,1,0:T(8,128)S(1)}, u32[]{:S(2)}, u32[]{:S(2)}) collective-permute-start(f32[4,256,256]{2,1,0:T(8,128)S(1)} %collective-permute-done.7.refs_6_.refs_3_.refs_2_.refs_4_), channel_id=1, source_target_pairs={{0,16},{16,0},{1,17},{17,1},{2,18},{18,2},{3,19},{19,3},{4,20},{20... | collective-permute-start | bytes 3145736 | tf_op jit(solution)/shard_map/ppermute | solution.py:27
  62.8 25.8 %collective-permute-start.13 = (f32[512,512]{1,0:T(8,128)S(1)}, f32[512,512]{1,0:T(8,128)S(1)}, u32[]{:S(2)}, u32[]{:S(2)}) collective-permute-start(f32[512,512]{1,0:T(8,128)S(1)} %collective-permute-done.9.refs_3_), channel_id=1, source_target_pairs={{0,7},{1,0},{2,1},{3,2},{4,3},{5,4},{6,5},{7,6},{16,17},{17,18},{1... | collective-permute-start | bytes 3145736 | tf_op jit(solution)/shard_map/ppermute | solution.py:35
  62.8 25.8 %collective-permute-start.12 = (f32[512,512]{1,0:T(8,128)S(1)}, f32[512,512]{1,0:T(8,128)}, u32[]{:S(2)}, u32[]{:S(2)}) collective-permute-start(f32[512,512]{1,0:T(8,128)S(1)} %collective-permute-done.8.refs_2_), channel_id=1, source_target_pairs={{0,1},{1,2},{2,3},{3,4},{4,5},{5,6},{6,7},{7,0},{16,23},{17,16},{1... | collective-permute-start | bytes 3145736 | tf_op jit(solution)/shard_map/ppermute | solution.py:35
  65.5 25.0 %collective-permute-start.10 = (f32[512,512]{1,0:T(8,128)}, f32[512,512]{1,0:T(8,128)S(1)}, u32[]{:S(2)}, u32[]{:S(2)}) collective-permute-start(f32[512,512]{1,0:T(8,128)} %collective-permute-done.refs_1_), channel_id=1, source_target_pairs={{0,32},{32,64},{64,96},{96,0},{16,112},{48,16},{80,48},{112,80},{1... | collective-permute-start | bytes 3145736 | tf_op jit(solution)/shard_map/ppermute | solution.py:38
  68.2 23.2 %collective-permute-start.11 = (f32[512,512]{1,0:T(8,128)S(1)}, f32[512,512]{1,0:T(8,128)S(1)}, u32[]{:S(2)}, u32[]{:S(2)}) collective-permute-start(f32[512,512]{1,0:T(8,128)S(1)} %collective-permute-done.5.refs_5_), channel_id=1, source_target_pairs={{0,32},{32,64},{64,96},{96,0},{16,112},{48,16},{80,48},{112,80},{1... | collective-permute-start | bytes 3145736 | tf_op jit(solution)/shard_map/ppermute | solution.py:38
  88.6 14.5 %collective-permute-start.16 = (f32[512,512]{1,0:T(8,128)}, f32[512,512]{1,0:T(8,128)}, u32[]{:S(2)}, u32[]{:S(2)}) collective-permute-start(f32[512,512]{1,0:T(8,128)} %collective-permute-done.12.refs_0_), channel_id=1, source_target_pairs={{0,1},{1,2},{2,3},{3,4},{4,5},{5,6},{6,7},{7,0},{16,23},{17,16},{1... | collective-permute-start | bytes 3145736 | tf_op jit(solution)/shard_map/ppermute | solution.py:35
  90.4 4.8 %copy-start.12 = (f32[512,512]{1,0:T(8,128)}, f32[512,512]{1,0:T(8,128)S(1)}, u32[]{:S(2)}) copy-start(f32[512,512]{1,0:T(8,128)S(1)} %beta11.2) | copy-start | bytes 3145732
  90.4 4.8 %copy-start.6 = (f32[512,512]{1,0:T(8,128)}, f32[512,512]{1,0:T(8,128)S(1)}, u32[]{:S(2)}) copy-start(f32[512,512]{1,0:T(8,128)S(1)} %collective-permute-done.10.refs_2_) | copy-start | bytes 3145732
  95.2 13.2 %collective-permute-start.15 = (f32[8,256,512]{2,1,0:T(8,128)}, f32[8,256,512]{2,1,0:T(8,128)}, u32[]{:S(2)}, u32[]{:S(2)}) collective-permute-start(f32[8,256,512]{2,1,0:T(8,128)} %pick.1), channel_id=1, source_target_pairs={{0,16},{16,0},{1,17},{17,1},{2,18},{18,2},{3,19},{19,3},{4,20},{20... | collective-permute-start | bytes 12582920 | tf_op jit(solution)/shard_map/ppermute | solution.py:27
  96.3 9.1 %copy-start.14 = (f32[512,512]{1,0:T(8,128)S(1)}, f32[512,512]{1,0:T(8,128)}, u32[]{:S(2)}) copy-start(f32[512,512]{1,0:T(8,128)} %copy-done.13) | copy-start | bytes 3145732
  96.3 24.9 %collective-permute-start.17 = (f32[512,512]{1,0:T(8,128)}, f32[512,512]{1,0:T(8,128)S(1)}, u32[]{:S(2)}, u32[]{:S(2)}) collective-permute-start(f32[512,512]{1,0:T(8,128)} %copy-done.12), channel_id=1, source_target_pairs={{0,8},{8,0},{1,9},{9,1},{2,10},{10,2},{3,11},{11,3},{4,12},{12,4},... | collective-permute-start | bytes 3145736 | tf_op jit(solution)/shard_map/ppermute | solution.py:27
  105.3 27.1 %collective-permute-start.18 = (f32[512,256]{1,0:T(8,128)S(1)}, f32[512,256]{1,0:T(8,128)S(1)}, u32[]{:S(2)}, u32[]{:S(2)}) collective-permute-start(f32[512,256]{1,0:T(8,128)S(1)} %beta21.1), channel_id=1, source_target_pairs={{0,8},{8,0},{1,9},{9,1},{2,10},{10,2},{3,11},{11,3},{4,12},{12,4},... | collective-permute-start | bytes 1572872 | tf_op jit(solution)/shard_map/ppermute | solution.py:27
  (11 other events, 29.3 us)

commit v8 on v7

--- a/solution.py
+++ b/solution.py
@@ -15,6 +15,7 @@
 BS = 256
 SLOTS = 8
 MIB = 1 << 20
+LARGE = pl.CostEstimate(flops=1 << 34, bytes_accessed=1 << 25, transcendentals=0)
 SMALL = pl.CostEstimate(flops=1 << 20, bytes_accessed=1 << 18, transcendentals=0)
 
 SMEM = pl.BlockSpec(memory_space=pltpu.SMEM)
@@ -61,7 +62,7 @@
     me, mb = where[0], where[1]
     up = (me & 1) == 0
     alpha_plan[0, 0] = 0
-    for row in range(6):
+    for row in range(3):
         beta_plan[row, 0] = 0
 
     def put(plan, row, word):
@@ -102,12 +103,10 @@
         def _():
             ahead = mb - owner
             d = jnp.where(up, ahead, -ahead) & 7
-            call = jnp.where((d <= 2) | (d >= 6), 0, 1)
-            if target:
-                call = jnp.where(d == 4, 2, call)
+            call = jnp.where(d == 4, 2, 1) if target else 0
             tile = place if target else c
             word = d * 64 + (src & 1) * 32 + (slot >> 3) * 16 + tile
-            put(beta_plan, 2 * call + target, word)
+            put(beta_plan, call, word)
 
         if not target:
 
@@ -127,13 +126,16 @@
         pl.when(piece == i)(lambda ref=ref: make(ref).start())
 
 
+SOON = (0, 1, 3, 4, 5, 7)
+
+
 def pick_kernel(picks, *refs):
-    pieces, (out, sem) = refs[:8], refs[8:]
+    pieces, (out, sem) = refs[:6], refs[6:]
     copies = [
         pltpu.make_async_copy(
-            piece.at[pl.ds(pl.multiple_of(picks[d] * BS, BS), BS)], out.at[d], sem.at[d]
+            piece.at[pl.ds(pl.multiple_of(picks[d] * BS, BS), BS)], out.at[i], sem.at[i]
         )
-        for d, piece in enumerate(pieces)
+        for i, (d, piece) in enumerate(zip(SOON, pieces))
     ]
     for copy in copies:
         copy.start()
@@ -145,10 +147,10 @@
     n = pieces[0].shape[1]
     return pl.pallas_call(
         pick_kernel,
-        out_shape=jax.ShapeDtypeStruct((8, BS, n), jnp.float32),
-        in_specs=[SMEM] + [ANY] * 8,
+        out_shape=jax.ShapeDtypeStruct((6, BS, n), jnp.float32),
+        in_specs=[SMEM] + [ANY] * 6,
         out_specs=VMEM,
-        scratch_shapes=[pltpu.SemaphoreType.DMA((8,))],
+        scratch_shapes=[pltpu.SemaphoreType.DMA((6,))],
         compiler_params=pltpu.CompilerParams(vmem_limit_bytes=12 * MIB),
         cost_estimate=SMALL,
         name="pick",
@@ -156,7 +158,7 @@
 
 
 def alpha_kernel(plan, *refs):
-    pieces, picked, own, refs = refs[:8], refs[8], refs[9], refs[10:]
+    pieces, (us2, vs2, picked, own), refs = refs[:8], refs[8:12], refs[12:]
     out, data, tiles, data_sem, tile_sem = refs
     count = plan[0, 0]
 
@@ -172,7 +174,12 @@
         tile_of(k, word & 31).start()
         rows = pl.ds(pl.multiple_of(((word >> 5) & 1) * BS, BS), BS)
         start_one_of(pieces, piece, lambda ref: rows_of(k, ref.at[rows]))
-        pl.when(piece >= 8)(lambda: rows_of(k, picked.at[piece & 7]).start())
+        pl.when(piece == 10)(lambda: rows_of(k, us2.at[rows]).start())
+        pl.when(piece == 14)(lambda: rows_of(k, vs2.at[rows]).start())
+        place = (piece & 7) - (piece > 10).astype(jnp.int32) - (piece > 14).astype(jnp.int32)
+        pl.when((piece >= 8) & (piece != 10) & (piece != 14))(
+            lambda: rows_of(k, picked.at[place]).start()
+        )
         return 0
 
     lax.fori_loop(0, count, fetch, 0)
@@ -189,12 +196,12 @@
     lax.fori_loop(0, count, product, 0)
 
 
-def alpha_call(plan, pieces, picked, own):
+def alpha_call(plan, pieces, us2, vs2, picked, own):
     n = own.shape[0] * BS
     return pl.pallas_call(
         alpha_kernel,
         out_shape=jax.ShapeDtypeStruct((n, n), jnp.float32),
-        in_specs=[SMEM] + [HBM] * 10,
+        in_specs=[SMEM] + [HBM] * 12,
         out_specs=VMEM,
         scratch_shapes=[
             pltpu.VMEM((2 * SLOTS, BS, n), jnp.float32),
@@ -205,7 +212,7 @@
         compiler_params=pltpu.CompilerParams(vmem_limit_bytes=18 * MIB),
         cost_estimate=SMALL,
         name="alpha",
-    )(plan, *in_hbm(*pieces, picked, own))
+    )(plan, *in_hbm(*pieces, us2, vs2, picked, own))
 
 
 def send_kernel(where, sends, own, out, sem):
@@ -233,21 +240,15 @@
     )(where, sends, *in_hbm(own))
 
 
-HOPS = {(0, 0): (0, 1, 2, 6, 7), (0, 1): (0, 1, 2, 6, 7), (1, 0): (3, 4, 5), (1, 1): (3, 5), (2, 1): (4,)}
-
-
-def beta_kernel(call, targets, where, plan, *refs):
-    numbers = HOPS[call, targets[0]]
+HOPS = (tuple(range(8)), (0, 1, 2, 3, 5, 6, 7), (4,))
+
+
+def beta_kernel(call, where, plan, *refs):
+    numbers = HOPS[call]
     pieces, refs = refs[: len(numbers)], refs[len(numbers) :]
-    own, got, other, refs = refs[0], refs[1], refs[2], refs[3:]
-    before, refs = (refs[: len(targets)], refs[len(targets) :]) if call == 1 else ((), refs)
-    outs, (data, tiles, data_sem, tile_sem, out_sem) = refs[: len(targets)], refs[len(targets) :]
+    own, got, other, out, data, tiles, data_sem, tile_sem = refs
     core = where[0] & 1
-    firsts = [
-        pltpu.make_async_copy(b, out, out_sem.at[i]) for i, (b, out) in enumerate(zip(before, outs))
-    ]
-    for first in firsts:
-        first.start()
+    count = plan[call, 0]
 
     def columns_of(k, ref, block):
         first = pl.multiple_of(block * BS, BS)
@@ -256,71 +257,53 @@
     def tile_from(k, ref):
         return pltpu.make_async_copy(ref, tiles.at[k], tile_sem.at[k])
 
-    base = 0
-    for target in targets:
-        row = 2 * call + target
-
-        def fetch(j, _, target=target, row=row, base=base):
-            word = plan[row, j + 1]
-            k = base + j
-            tile = word & 15
-            for number, ref in zip(numbers, pieces):
-                pl.when((word >> 6) == number)(
-                    lambda ref=ref: columns_of(k, ref, (word >> 5) & 1).start()
-                )
-            if target == 0:
-                tile_from(k, own.at[(word >> 4) & 1, tile]).start()
-            else:
-                start_one_of(
-                    (got, other), core ^ (tile >> 2), lambda ref: tile_from(k, ref.at[tile & 3])
-                )
-            return 0
-
-        lax.fori_loop(0, plan[row, 0], fetch, 0)
-        base = base + plan[row, 0]
-    for out in outs:
-        if call != 1:
-            out[...] = jnp.zeros_like(out)
-    for first in firsts:
-        first.wait()
-    base = 0
-    for target, out in zip(targets, outs):
-        row = 2 * call + target
-
-        def product(j, _, out=out, row=row, base=base):
-            k = base + j
-            block = (plan[row, j + 1] >> 4) & 1
-            columns_of(k, pieces[0], 0).wait()
-            tile_from(k, own.at[0, 0]).wait()
-            columns = 0 if call == 2 else pl.multiple_of(block * BS, BS)
-            out[:, pl.ds(columns, BS)] += dot3(data[k], tiles[k])
-            return 0
-
-        lax.fori_loop(0, plan[row, 0], product, 0)
-        base = base + plan[row, 0]
-
-
-def beta_call(call, targets, where, plan, held, own, got, other, before=()):
+    def fetch(k, _):
+        word = plan[call, k + 1]
+        tile = word & 15
+        for number, ref in zip(numbers, pieces):
+            pl.when((word >> 6) == number)(
+                lambda ref=ref: columns_of(k, ref, (word >> 5) & 1).start()
+            )
+        if call == 0:
+            tile_from(k, own.at[(word >> 4) & 1, tile]).start()
+        else:
+            start_one_of(
+                (got, other), core ^ (tile >> 2), lambda ref: tile_from(k, ref.at[tile & 3])
+            )
+        return 0
+
+    lax.fori_loop(0, count, fetch, 0)
+    out[...] = jnp.zeros_like(out)
+
+    def product(k, _):
+        block = (plan[call, k + 1] >> 4) & 1
+        columns_of(k, pieces[0], 0).wait()
+        tile_from(k, own.at[0, 0]).wait()
+        columns = 0 if call == 2 else pl.multiple_of(block * BS, BS)
+        out[:, pl.ds(columns, BS)] += dot3(data[k], tiles[k])
+        return 0
+
+    lax.fori_loop(0, count, product, 0)
+
+
+def beta_call(call, where, plan, held, own, got, other):
     n = held[0].shape[0]
-    pieces = [held[d] for d in HOPS[call, targets[0]]]
-    most = len(pieces) * len(targets)
-    width = BS if call == 2 else n
+    pieces = [held[d] for d in HOPS[call]]
     return pl.pallas_call(
-        functools.partial(beta_kernel, call, targets),
-        out_shape=[jax.ShapeDtypeStruct((n, width), jnp.float32)] * len(targets),
-        in_specs=[SMEM] * 2 + [HBM] * (len(pieces) + 3) + [ANY] * len(before),
-        out_specs=[VMEM] * len(targets),
+        functools.partial(beta_kernel, call),
+        out_shape=jax.ShapeDtypeStruct((n, BS if call == 2 else n), jnp.float32),
+        in_specs=[SMEM] * 2 + [HBM] * (len(pieces) + 3),
+        out_specs=VMEM,
         scratch_shapes=[
-            pltpu.VMEM((most, n, BS), jnp.float32),
-            pltpu.VMEM((most, BS, BS), jnp.float32),
-            pltpu.SemaphoreType.DMA((most,)),
-            pltpu.SemaphoreType.DMA((most,)),
-            pltpu.SemaphoreType.DMA((2,)),
+            pltpu.VMEM((len(pieces), n, BS), jnp.float32),
+            pltpu.VMEM((len(pieces), BS, BS), jnp.float32),
+            pltpu.SemaphoreType.DMA((len(pieces),)),
+            pltpu.SemaphoreType.DMA((len(pieces),)),
         ],
-        compiler_params=pltpu.CompilerParams(vmem_limit_bytes=16 * MIB),
-        cost_estimate=(pl.CostEstimate(flops=1 << 34, bytes_accessed=1 << 25, transcendentals=0) if call else SMALL),
-        name=f"beta{call}{len(targets)}",
-    )(where, plan, *in_hbm(*pieces, own, got, other), *before)
+        compiler_params=pltpu.CompilerParams(vmem_limit_bytes=12 * MIB),
+        cost_estimate=LARGE,
+        name=f"beta{call}",
+    )(where, plan, *in_hbm(*pieces, own, got, other))
 
 
 def per_device(
@@ -342,7 +325,7 @@
         plan_kernel,
         out_shape=[
             jax.ShapeDtypeStruct((1, 32), jnp.int32),
-            jax.ShapeDtypeStruct((6, 32), jnp.int32),
+            jax.ShapeDtypeStruct((3, 32), jnp.int32),
             jax.ShapeDtypeStruct((8,), jnp.int32),
             jax.ShapeDtypeStruct((SLOTS,), jnp.int32),
         ],
@@ -361,22 +344,18 @@
     vf, vb, got, uf = lax.optimization_barrier((vf, vb, got, uf, f2))[:4]
     u2, v2 = step(uf, "x"), step(vf, "x")
     other = swap(got, "core")
-    held = [coeffs, f1, f2, None, None, None, b2, b1]
-    beta_own, beta_par = beta_call(0, (0, 1), where, beta_plan, held, beta_tiles, got, other)
-    f3, b3, beta_own, beta_par = lax.optimization_barrier((f3, b3, beta_own, beta_par))
-    held[3], held[4], held[5] = f3, step(f3, "z"), b3
-    (beta_par,) = beta_call(
-        1, (1,), where, beta_plan, held, beta_tiles, got, other, [beta_par]
-    )
+    picked = pick_call(picks, [coeffs, uf, ub, v, vf, vb])
+    f3, b3, picked = lax.optimization_barrier((f3, b3, picked))
+    picked = swap(picked, "core")
+    held = [coeffs, f1, f2, f3, step(f3, "z"), b3, b2, b1]
+    beta_par = beta_call(1, where, beta_plan, held, beta_tiles, got, other)
     beta_other = swap(beta_par, "ylo")
     pieces = [coeffs, uf, u2, ub, v, vf, v2, vb]
-    picked = swap(pick_call(after(picks, beta_par), pieces), "core")
-    (far,) = beta_call(2, (1,), where, beta_plan, held, beta_tiles, got, other)
+    us2, vs2 = swap(after(u2, beta_par), "core"), swap(after(v2, beta_par), "core")
+    far = beta_call(2, where, beta_plan, held, beta_tiles, got, other)
     far_other = swap(far, "ylo")
-    alpha = alpha_call(alpha_plan, pieces, picked, after(alpha_tiles, far))
-    (beta_own,) = beta_call(
-        1, (0,), where, beta_plan, held, after(beta_tiles, far), got, other, [beta_own]
-    )
+    alpha = alpha_call(alpha_plan, pieces, us2, vs2, picked, after(alpha_tiles, far))
+    beta_own = beta_call(0, where, beta_plan, held, after(beta_tiles, far), got, other)
     joined = (diag_alpha[:, None] + diag_beta[None, :]) * coeffs + alpha + beta_own
     joined, place = lax.optimization_barrier((joined, (where[1] + 4) & 7))
     joined = lax.optimization_barrier(joined + beta_other)

time: 134 us -> 125 us (0.933)
  waiting for transfers between devices: 70.1 us -> 63 us
  Pallas kernels: 23.8 us -> 19 us
  local copies, waits for them, and re-layouts: 8.48 us -> 11.8 us
  starting transfers between devices: 28.1 us -> 26.7 us
    ppermute x6 -> x8, waiting for transfers between devices: 23.8 us -> 9.66 us  [swap(): return lax.ppermute(value, axis, [(0, 1), (1, 0)])]
    ppermute x7, waiting for transfers between devices: 39.5 us -> 45.8 us  [step(): return lax.ppermute(value, ('core', axis), pairs)]
    pallas_call x5 -> x4, Pallas kernels: 13.1 us -> 8.51 us  [the longest x3 6.61 us: beta_call(): pl.pallas_call(functools.partial(beta_kernel, call), out_shape=jax.ShapeD...]
    ppermute x7, starting transfers between devices: 13.6 us -> 9.34 us  [step(): return lax.ppermute(value, ('core', axis), pairs)]
    ppermute x6 -> x8, starting transfers between devices: 6.39 us -> 9.91 us  [swap(): return lax.ppermute(value, axis, [(0, 1), (1, 0)])]
    unnamed x52 -> x42, local copies, waits for them, and re-layouts: 7.9 us -> 11.2 us
  transfers between devices with their start and end apart: 19 -> 21, of which waited for: 12 -> 11; matrix products, arithmetic and copies ran while one was open for 5% -> 6% of each run, Pallas kernels for 16% -> 13%
where the time goes in v8:
time: 125 us; the launch traced here: 124 us
  waiting for transfers between devices  63 us (50%)
  starting transfers between devices  26.7 us (21%)
  Pallas kernels  19 us (15%)
  local copies, waits for them, and re-layouts  11.8 us (9%)
  other arithmetic  2.24 us (2%)
    ppermute x7, waiting for transfers between devices, step(): return lax.ppermute(value, ('core', axis), pairs)  45.8 us
    unnamed x42, local copies, waits for them, and re-layouts  11.2 us
    ppermute x8, starting transfers between devices, swap(): return lax.ppermute(value, axis, [(0, 1), (1, 0)])  9.91 us
    ppermute x8, waiting for transfers between devices, swap(): return lax.ppermute(value, axis, [(0, 1), (1, 0)])  9.66 us
    ppermute x7, starting transfers between devices, step(): return lax.ppermute(value, ('core', axis), pairs)  9.34 us
    ppermute x6, waiting for transfers between devices, step(): return lax.ppermute(value, (axis, 'core'), pairs)  7.54 us
    ppermute x6, starting transfers between devices, step(): return lax.ppermute(value, (axis, 'core'), pairs)  7.49 us
    pallas_call x3, Pallas kernels, beta_call(): pl.pallas_call(functools.partial(beta_kernel, call), out_shape=jax.ShapeD...  6.61 us
  transfers between devices with their start and end apart: 21, of which 11 were waited for; matrix products, arithmetic and copies ran while one was open for 6% of the time, Pallas kernels for 13%

profile of v8, /device:TPU:1, one launch (start us, length us, event | category | flops | bytes accessed | tf_op | source)
XLA Modules:
  0.0 123.7 jit_solution(7376688057781486484)
XLA Ops:
  0.0 6.4 %collective-permute-start.3 = (f32[512,512]{1,0:T(8,128)}, f32[512,512]{1,0:T(8,128)}, u32[]{:S(2)}, u32[]{:S(2)}) collective-permute-start(f32[512,512]{1,0:T(8,128)} %refs_0_.7), channel_id=1, source_target_pairs={{0,1},{1,2},{2,3},{3,4},{4,5},{5,6},{6,7},{7,0},{16,23},{17,16},{1... | collective-permute-start | bytes 3145736 | tf_op jit(solution)/shard_map/ppermute | solution.py:36
  6.4 2.5 %collective-permute-start = (f32[512,512]{1,0:T(8,128)}, f32[512,512]{1,0:T(8,128)S(1)}, u32[]{:S(2)}, u32[]{:S(2)}) collective-permute-start(f32[512,512]{1,0:T(8,128)} %refs_0_.7), channel_id=1, source_target_pairs={{0,32},{32,64},{64,96},{96,0},{16,112},{48,16},{80,48},{112,80},{1... | collective-permute-start | bytes 3145736 | tf_op jit(solution)/shard_map/ppermute | solution.py:39
  8.9 2.9 %collective-permute-start.2 = (f32[512,512]{1,0:T(8,128)}, f32[512,512]{1,0:T(8,128)}, u32[]{:S(2)}, u32[]{:S(2)}) collective-permute-start(f32[512,512]{1,0:T(8,128)} %refs_0_.7), channel_id=1, source_target_pairs={{0,128},{128,0},{1,129},{129,1},{2,130},{130,2},{3,131},{131,3},{4... | collective-permute-start | bytes 3145736 | tf_op jit(solution)/shard_map/ppermute | solution.py:28
  11.8 1.4 %copy.10.alpha_source = s32[32,8]{1,0:T(8,128)} copy(s32[32,8]{0,1:T(8,128)} %param.14) | data formatting | bytes 2048 | tf_op args[5]
  13.2 1.4 %copy.11.alpha_live = s32[32,8]{1,0:T(8,128)} copy(s32[32,8]{0,1:T(8,128)} %param.15) | data formatting | bytes 2048 | tf_op args[6]
  14.5 1.4 %copy.12.beta_source = s32[32,8]{1,0:T(8,128)} copy(s32[32,8]{0,1:T(8,128)} %param.16) | data formatting | bytes 2048 | tf_op args[7]
  15.9 1.4 %copy.13.beta_live = s32[32,8]{1,0:T(8,128)} copy(s32[32,8]{0,1:T(8,128)} %param.17) | data formatting | bytes 2048 | tf_op args[8]
  17.9 3.4 %plan.1 = (s32[1,32]{1,0:T(1,128)}, s32[3,32]{1,0:T(4,128)}, s32[8]{0:T(128)}, s32[8]{0:T(128)}) custom-call(s32[2]{0:T(128)} %pad_add_fusion.where, s32[32,8]{1,0:T(8,128)} %copy.10.alpha_source, s32[32,8]{1,0:T(8,128)} %copy.11.alpha_live, s32[32,8]{1,0:T(8,128)} %copy.12.beta_source, s32[32,8]{1,0:T(8,128)} %copy.13.beta_live), custom_call_target="tpu_custom_call" | custom-call | tf_op jit(solution)/shard_map/plan/pallas_call | solution.py:324
  21.3 2.9 %send.1 = f32[4,256,256]{2,1,0:T(8,128)} custom-call(s32[2]{0:T(128)} %pad_add_fusion.where, s32[8]{0:T(128)} %get-tuple-element.32.sends, f32[2,8,256,256]{3,2,1,0:T(8,128)} %refs_8_), custom_call_target="tpu_custom_call" | custom-call | flops 1048576 | bytes 262144 | tf_op jit(solution)/shard_map/send/pallas_call | solution.py:232
  24.2 4.3 %collective-permute-done.3.refs_1_ = f32[512,512]{1,0:T(8,128)} collective-permute-done((f32[512,512]{1,0:T(8,128)}, f32[512,512]{1,0:T(8,128)}, u32[]{:S(2)}, u32[]{:S(2)}) %collective-permute-start.3) | collective-permute-done | bytes 1048608 | tf_op jit(solution)/shard_map/ppermute | solution.py:36
  28.5 2.9 %collective-permute-done.4.refs_6_.refs_7_ = f32[512,512]{1,0:T(8,128)} collective-permute-done((f32[512,512]{1,0:T(8,128)}, f32[512,512]{1,0:T(8,128)}, u32[]{:S(2)}, u32[]{:S(2)}) %collective-permute-start.4) | collective-permute-done | bytes 1048608 | tf_op jit(solution)/shard_map/ppermute | solution.py:36
  32.8 1.8 %collective-permute-done.1.refs_2_.refs_3_ = f32[512,512]{1,0:T(8,128)S(1)} collective-permute-done((f32[512,512]{1,0:T(8,128)}, f32[512,512]{1,0:T(8,128)S(1)}, u32[]{:S(2)}, u32[]{:S(2)}) %collective-permute-start.1) | collective-permute-done | bytes 1048608 | tf_op jit(solution)/shard_map/ppermute | solution.py:39
  34.6 3.2 %collective-permute-start.5 = (f32[512,512]{1,0:T(8,128)}, f32[512,512]{1,0:T(8,128)}, u32[]{:S(2)}, u32[]{:S(2)}) collective-permute-start(f32[512,512]{1,0:T(8,128)} %collective-permute-done.2.refs_3_.refs_4_), channel_id=1, source_target_pairs={{0,32},{32,64},{64,96},{96,0},{16,112},{48,16},{80,48},{112,80},{1... | collective-permute-start | bytes 3145736 | tf_op jit(solution)/shard_map/ppermute | solution.py:39
  37.8 1.3 %collective-permute-start.7 = (f32[4,256,256]{2,1,0:T(8,128)}, f32[4,256,256]{2,1,0:T(8,128)}, u32[]{:S(2)}, u32[]{:S(2)}) collective-permute-start(f32[4,256,256]{2,1,0:T(8,128)} %send.1), channel_id=1, source_target_pairs={{0,8},{8,0},{1,9},{9,1},{2,10},{10,2},{3,11},{11,3},{4,12},{12,4},... | collective-permute-start | bytes 3145736 | tf_op jit(solution)/shard_map/ppermute | solution.py:28
  39.1 17.0 %collective-permute-done.8.refs_2_ = f32[512,512]{1,0:T(8,128)} collective-permute-done((f32[512,512]{1,0:T(8,128)}, f32[512,512]{1,0:T(8,128)}, u32[]{:S(2)}, u32[]{:S(2)}) %collective-permute-start.8) | collective-permute-done | bytes 1048608 | tf_op jit(solution)/shard_map/ppermute | solution.py:36
  56.1 1.7 %collective-permute-done.9.refs_5_.refs_6_ = f32[512,512]{1,0:T(8,128)} collective-permute-done((f32[512,512]{1,0:T(8,128)}, f32[512,512]{1,0:T(8,128)}, u32[]{:S(2)}, u32[]{:S(2)}) %collective-permute-start.9) | collective-permute-done | bytes 1048608 | tf_op jit(solution)/shard_map/ppermute | solution.py:36
  57.7 1.5 %collective-permute-start.13 = (f32[512,512]{1,0:T(8,128)}, f32[512,512]{1,0:T(8,128)}, u32[]{:S(2)}, u32[]{:S(2)}) collective-permute-start(f32[512,512]{1,0:T(8,128)} %collective-permute-done.9.refs_5_.refs_6_), channel_id=1, source_target_pairs={{0,7},{1,0},{2,1},{3,2},{4,3},{5,4},{6,5},{7,6},{16,17},{17,18},{1... | collective-permute-start | bytes 3145736 | tf_op jit(solution)/shard_map/ppermute | solution.py:36
  59.2 4.3 %collective-permute-done.6.refs_5_.refs_7_ = f32[512,512]{1,0:T(8,128)S(1)} collective-permute-done((f32[512,512]{1,0:T(8,128)}, f32[512,512]{1,0:T(8,128)S(1)}, u32[]{:S(2)}, u32[]{:S(2)}) %collective-permute-start.6) | collective-permute-done | bytes 1048608 | tf_op jit(solution)/shard_map/ppermute | solution.py:39
  64.6 1.8 %collective-permute-start.10 = (f32[512,512]{1,0:T(8,128)S(1)}, f32[512,512]{1,0:T(8,128)S(1)}, u32[]{:S(2)}, u32[]{:S(2)}) collective-permute-start(f32[512,512]{1,0:T(8,128)S(1)} %collective-permute-done.refs_1_), channel_id=1, source_target_pairs={{0,32},{32,64},{64,96},{96,0},{16,112},{48,16},{80,48},{112,80},{1... | collective-permute-start | bytes 3145736 | tf_op jit(solution)/shard_map/ppermute | solution.py:39
  66.4 1.2 copy-done.5
  67.6 1.9 %pick.1 = f32[6,256,512]{2,1,0:T(8,128)S(1)} custom-call(s32[8]{0:T(128)S(1)} %copy-done.8, f32[512,512]{1,0:T(8,128)S(1)} %copy-done, f32[512,512]{1,0:T(8,128)S(1)} %collective-permute-done.refs_1_, f32[512,512]{1,0:T(8,128)S(1)} %collective-permute-done.1.refs_2_.refs_3_, f32[512,512]{1,0:T(8,128)} %collective-permute-done.2.refs_3_.refs_4_, ...), custom_call_target="tpu_custom_call" | custom-call | flops 1048576 | bytes 262144 | tf_op jit(solution)/shard_map/pick/pallas_call | solution.py:148
  69.6 13.2 %collective-permute-done.12.refs_3_ = f32[512,512]{1,0:T(8,128)} collective-permute-done((f32[512,512]{1,0:T(8,128)}, f32[512,512]{1,0:T(8,128)}, u32[]{:S(2)}, u32[]{:S(2)}) %collective-permute-start.12) | collective-permute-done | bytes 1048608 | tf_op jit(solution)/shard_map/ppermute | solution.py:36
  83.9 2.6 %beta1.1 = f32[512,512]{1,0:T(8,128)S(1)} custom-call(s32[2]{0:T(128)S(1)} %copy-done.6, s32[3,32]{1,0:T(4,128)S(1)} %copy-done.9, f32[512,512]{1,0:T(8,128)} %refs_0_.7, f32[512,512]{1,0:T(8,128)} %collective-permute-done.3.refs_1_, f32[512,512]{1,0:T(8,128)} %collective-permute-done.8.refs_2_, f32[512,512]{1,0:T(8,128)} %collective-permute-done.12.refs_3_, ...), custom_call_target="tpu_custom_call" | custom-call | flops 17179869184 | bytes 33554432 | tf_op jit(solution)/shard_map/beta1/pallas_call | solution.py:292
  86.5 1.4 %collective-permute-start.19 = (f32[512,512]{1,0:T(8,128)S(1)}, f32[512,512]{1,0:T(8,128)S(1)}, u32[]{:S(2)}, u32[]{:S(2)}) collective-permute-start(f32[512,512]{1,0:T(8,128)S(1)} %beta1.1), channel_id=1, source_target_pairs={{0,8},{8,0},{1,9},{9,1},{2,10},{10,2},{3,11},{11,3},{4,12},{12,4},... | collective-permute-start | bytes 3145736 | tf_op jit(solution)/shard_map/ppermute | solution.py:28
  88.3 1.5 %collective-permute-done.11.refs_6_ = f32[512,512]{1,0:T(8,128)S(1)} collective-permute-done((f32[512,512]{1,0:T(8,128)}, f32[512,512]{1,0:T(8,128)S(1)}, u32[]{:S(2)}, u32[]{:S(2)}) %collective-permute-start.11) | collective-permute-done | bytes 1048608 | tf_op jit(solution)/shard_map/ppermute | solution.py:39
  89.7 2.6 %collective-permute-start.16 = (f32[512,512]{1,0:T(8,128)S(1)}, f32[512,512]{1,0:T(8,128)S(1)}, u32[]{:S(2)}, u32[]{:S(2)}) collective-permute-start(f32[512,512]{1,0:T(8,128)S(1)} %collective-permute-done.11.refs_6_), channel_id=1, source_target_pairs={{0,16},{16,0},{1,17},{17,1},{2,18},{18,2},{3,19},{19,3},{4,20},{20... | collective-permute-start | bytes 3145736 | tf_op jit(solution)/shard_map/ppermute | solution.py:28
  92.3 5.7 %collective-permute-done.18.refs_0_.refs_4_ = f32[512,512]{1,0:T(8,128)S(1)} collective-permute-done((f32[512,512]{1,0:T(8,128)}, f32[512,512]{1,0:T(8,128)S(1)}, u32[]{:S(2)}, u32[]{:S(2)}) %collective-permute-start.18) | collective-permute-done | bytes 1048608 | tf_op jit(solution)/shard_map/ppermute | solution.py:36
  99.6 1.4 %collective-permute-start.20 = (f32[512,256]{1,0:T(8,128)S(1)}, f32[512,256]{1,0:T(8,128)S(1)}, u32[]{:S(2)}, u32[]{:S(2)}) collective-permute-start(f32[512,256]{1,0:T(8,128)S(1)} %beta2.1), channel_id=1, source_target_pairs={{0,8},{8,0},{1,9},{9,1},{2,10},{10,2},{3,11},{11,3},{4,12},{12,4},... | collective-permute-start | bytes 1572872 | tf_op jit(solution)/shard_map/ppermute | solution.py:28
  101.0 3.4 %beta0.1 = f32[512,512]{1,0:T(8,128)S(1)} custom-call(s32[2]{0:T(128)S(1)} %copy-done.6, s32[3,32]{1,0:T(4,128)S(1)} %copy-done.9, f32[512,512]{1,0:T(8,128)} %refs_0_.7, f32[512,512]{1,0:T(8,128)} %collective-permute-done.3.refs_1_, f32[512,512]{1,0:T(8,128)} %collective-permute-done.8.refs_2_, f32[512,512]{1,0:T(8,128)} %collective-permute-done.12.refs_3_, ...), custom_call_target="tpu_custom_call" | custom-call | flops 17179869184 | bytes 33554432 | tf_op jit(solution)/shard_map/beta0/pallas_call | solution.py:292
  106.8 4.3 %alpha.1 = f32[512,512]{1,0:T(8,128)S(1)} custom-call(s32[1,32]{1,0:T(1,128)S(1)} %copy-done.7, f32[512,512]{1,0:T(8,128)} %refs_0_.7, f32[512,512]{1,0:T(8,128)} %copy-done.2, f32[512,512]{1,0:T(8,128)} %copy-done.11, f32[512,512]{1,0:T(8,128)} %copy-done.3, f32[512,512]{1,0:T(8,128)} %collective-permute-done.2.refs_3_.refs_4_, ...), custom_call_target="tpu_custom_call" | custom-call | flops 1048576 | bytes 262144 | tf_op jit(solution)/shard_map/alpha/pallas_call | solution.py:201
  112.9 9.6 %collective-permute-done.20 = f32[512,256]{1,0:T(8,128)S(1)} collective-permute-done((f32[512,256]{1,0:T(8,128)S(1)}, f32[512,256]{1,0:T(8,128)S(1)}, u32[]{:S(2)}, u32[]{:S(2)}) %collective-permute-start.20) | collective-permute-done | bytes 524320 | tf_op jit(solution)/shard_map/ppermute | solution.py:28
  122.6 1.1 maximum_add_fusion
  (65 shorter events, 9.8 us)
Async XLA Ops:
  0.0 66.4 %copy-start = (f32[512,512]{1,0:T(8,128)S(1)}, f32[512,512]{1,0:T(8,128)}, u32[]{:S(2)}) copy-start(f32[512,512]{1,0:T(8,128)} %refs_0_.7) | copy-start | bytes 3145732
  0.0 28.5 %collective-permute-start.3 = (f32[512,512]{1,0:T(8,128)}, f32[512,512]{1,0:T(8,128)}, u32[]{:S(2)}, u32[]{:S(2)}) collective-permute-start(f32[512,512]{1,0:T(8,128)} %refs_0_.7), channel_id=1, source_target_pairs={{0,1},{1,2},{2,3},{3,4},{4,5},{5,6},{6,7},{7,0},{16,23},{17,16},{1... | collective-permute-start | bytes 3145736 | tf_op jit(solution)/shard_map/ppermute | solution.py:36
  6.4 25.0 %collective-permute-start.4 = (f32[512,512]{1,0:T(8,128)}, f32[512,512]{1,0:T(8,128)}, u32[]{:S(2)}, u32[]{:S(2)}) collective-permute-start(f32[512,512]{1,0:T(8,128)} %refs_0_.7), channel_id=1, source_target_pairs={{0,7},{1,0},{2,1},{3,2},{4,3},{5,4},{6,5},{7,6},{16,17},{17,18},{1... | collective-permute-start | bytes 3145736 | tf_op jit(solution)/shard_map/ppermute | solution.py:36
  6.4 26.4 %collective-permute-start = (f32[512,512]{1,0:T(8,128)}, f32[512,512]{1,0:T(8,128)S(1)}, u32[]{:S(2)}, u32[]{:S(2)}) collective-permute-start(f32[512,512]{1,0:T(8,128)} %refs_0_.7), channel_id=1, source_target_pairs={{0,32},{32,64},{64,96},{96,0},{16,112},{48,16},{80,48},{112,80},{1... | collective-permute-start | bytes 3145736 | tf_op jit(solution)/shard_map/ppermute | solution.py:39
  8.9 25.7 %collective-permute-start.1 = (f32[512,512]{1,0:T(8,128)}, f32[512,512]{1,0:T(8,128)S(1)}, u32[]{:S(2)}, u32[]{:S(2)}) collective-permute-start(f32[512,512]{1,0:T(8,128)} %refs_0_.7), channel_id=1, source_target_pairs={{0,96},{32,0},{64,32},{96,64},{16,48},{48,80},{80,112},{112,16},{1... | collective-permute-start | bytes 3145736 | tf_op jit(solution)/shard_map/ppermute | solution.py:39
  8.9 25.7 %collective-permute-start.2 = (f32[512,512]{1,0:T(8,128)}, f32[512,512]{1,0:T(8,128)}, u32[]{:S(2)}, u32[]{:S(2)}) collective-permute-start(f32[512,512]{1,0:T(8,128)} %refs_0_.7), channel_id=1, source_target_pairs={{0,128},{128,0},{1,129},{129,1},{2,130},{130,2},{3,131},{131,3},{4... | collective-permute-start | bytes 3145736 | tf_op jit(solution)/shard_map/ppermute | solution.py:28
  21.3 45.1 %copy-start.8 = (s32[8]{0:T(128)S(1)}, s32[8]{0:T(128)}, u32[]{:S(2)}) copy-start(s32[8]{0:T(128)} %get-tuple-element.46.picks) | copy-start | bytes 100
  31.4 24.7 %collective-permute-start.8 = (f32[512,512]{1,0:T(8,128)}, f32[512,512]{1,0:T(8,128)}, u32[]{:S(2)}, u32[]{:S(2)}) collective-permute-start(f32[512,512]{1,0:T(8,128)} %collective-permute-done.3.refs_1_), channel_id=1, source_target_pairs={{0,1},{1,2},{2,3},{3,4},{4,5},{5,6},{6,7},{7,0},{16,23},{17,16},{1... | collective-permute-start | bytes 3145736 | tf_op jit(solution)/shard_map/ppermute | solution.py:36
  32.3 25.4 %collective-permute-start.9 = (f32[512,512]{1,0:T(8,128)}, f32[512,512]{1,0:T(8,128)}, u32[]{:S(2)}, u32[]{:S(2)}) collective-permute-start(f32[512,512]{1,0:T(8,128)} %collective-permute-done.4.refs_6_.refs_7_), channel_id=1, source_target_pairs={{0,7},{1,0},{2,1},{3,2},{4,3},{5,4},{6,5},{7,6},{16,17},{17,18},{1... | collective-permute-start | bytes 3145736 | tf_op jit(solution)/shard_map/ppermute | solution.py:36
  32.8 36.7 %copy-start.2 = (f32[512,512]{1,0:T(8,128)}, f32[512,512]{1,0:T(8,128)S(1)}, u32[]{:S(2)}) copy-start(f32[512,512]{1,0:T(8,128)S(1)} %collective-permute-done.refs_1_) | copy-start | bytes 3145732
  34.6 35.0 %copy-start.3 = (f32[512,512]{1,0:T(8,128)}, f32[512,512]{1,0:T(8,128)S(1)}, u32[]{:S(2)}) copy-start(f32[512,512]{1,0:T(8,128)S(1)} %collective-permute-done.1.refs_2_.refs_3_) | copy-start | bytes 3145732
  34.6 24.6 %collective-permute-start.5 = (f32[512,512]{1,0:T(8,128)}, f32[512,512]{1,0:T(8,128)}, u32[]{:S(2)}, u32[]{:S(2)}) collective-permute-start(f32[512,512]{1,0:T(8,128)} %collective-permute-done.2.refs_3_.refs_4_), channel_id=1, source_target_pairs={{0,32},{32,64},{64,96},{96,0},{16,112},{48,16},{80,48},{112,80},{1... | collective-permute-start | bytes 3145736 | tf_op jit(solution)/shard_map/ppermute | solution.py:39
  37.8 25.7 %collective-permute-start.6 = (f32[512,512]{1,0:T(8,128)}, f32[512,512]{1,0:T(8,128)S(1)}, u32[]{:S(2)}, u32[]{:S(2)}) collective-permute-start(f32[512,512]{1,0:T(8,128)} %collective-permute-done.2.refs_3_.refs_4_), channel_id=1, source_target_pairs={{0,96},{32,0},{64,32},{96,64},{16,48},{48,80},{80,112},{112,16},{1... | collective-permute-start | bytes 3145736 | tf_op jit(solution)/shard_map/ppermute | solution.py:39
  37.8 26.8 %collective-permute-start.7 = (f32[4,256,256]{2,1,0:T(8,128)}, f32[4,256,256]{2,1,0:T(8,128)}, u32[]{:S(2)}, u32[]{:S(2)}) collective-permute-start(f32[4,256,256]{2,1,0:T(8,128)} %send.1), channel_id=1, source_target_pairs={{0,8},{8,0},{1,9},{9,1},{2,10},{10,2},{3,11},{11,3},{4,12},{12,4},... | collective-permute-start | bytes 3145736 | tf_op jit(solution)/shard_map/ppermute | solution.py:28
  57.7 25.0 %collective-permute-start.12 = (f32[512,512]{1,0:T(8,128)}, f32[512,512]{1,0:T(8,128)}, u32[]{:S(2)}, u32[]{:S(2)}) collective-permute-start(f32[512,512]{1,0:T(8,128)} %collective-permute-done.8.refs_2_), channel_id=1, source_target_pairs={{0,1},{1,2},{2,3},{3,4},{4,5},{5,6},{6,7},{7,0},{16,23},{17,16},{1... | collective-permute-start | bytes 3145736 | tf_op jit(solution)/shard_map/ppermute | solution.py:36
  57.7 26.1 %collective-permute-start.13 = (f32[512,512]{1,0:T(8,128)}, f32[512,512]{1,0:T(8,128)}, u32[]{:S(2)}, u32[]{:S(2)}) collective-permute-start(f32[512,512]{1,0:T(8,128)} %collective-permute-done.9.refs_5_.refs_6_), channel_id=1, source_target_pairs={{0,7},{1,0},{2,1},{3,2},{4,3},{5,4},{6,5},{7,6},{16,17},{17,18},{1... | collective-permute-start | bytes 3145736 | tf_op jit(solution)/shard_map/ppermute | solution.py:36
  64.6 19.3 %collective-permute-start.14 = (f32[4,256,256]{2,1,0:T(8,128)}, f32[4,256,256]{2,1,0:T(8,128)}, u32[]{:S(2)}, u32[]{:S(2)}) collective-permute-start(f32[4,256,256]{2,1,0:T(8,128)} %collective-permute-done.7.refs_8_.refs_2_.refs_9_), channel_id=1, source_target_pairs={{0,16},{16,0},{1,17},{17,1},{2,18},{18,2},{3,19},{19,3},{4,20},{20... | collective-permute-start | bytes 3145736 | tf_op jit(solution)/shard_map/ppermute | solution.py:28
  64.6 23.3 %collective-permute-start.10 = (f32[512,512]{1,0:T(8,128)S(1)}, f32[512,512]{1,0:T(8,128)S(1)}, u32[]{:S(2)}, u32[]{:S(2)}) collective-permute-start(f32[512,512]{1,0:T(8,128)S(1)} %collective-permute-done.refs_1_), channel_id=1, source_target_pairs={{0,32},{32,64},{64,96},{96,0},{16,112},{48,16},{80,48},{112,80},{1... | collective-permute-start | bytes 3145736 | tf_op jit(solution)/shard_map/ppermute | solution.py:39
  66.4 23.4 %collective-permute-start.11 = (f32[512,512]{1,0:T(8,128)}, f32[512,512]{1,0:T(8,128)S(1)}, u32[]{:S(2)}, u32[]{:S(2)}) collective-permute-start(f32[512,512]{1,0:T(8,128)} %collective-permute-done.5.refs_4_.refs_5_), channel_id=1, source_target_pairs={{0,32},{32,64},{64,96},{96,0},{16,112},{48,16},{80,48},{112,80},{1... | collective-permute-start | bytes 3145736 | tf_op jit(solution)/shard_map/ppermute | solution.py:39
  67.6 16.2 %copy-start.6 = (s32[2]{0:T(128)S(1)}, s32[2]{0:T(128)}, u32[]{:S(2)}) copy-start(s32[2]{0:T(128)} %pad_add_fusion.where) | copy-start | bytes 28
  67.6 16.2 %copy-start.9 = (s32[3,32]{1,0:T(4,128)S(1)}, s32[3,32]{1,0:T(4,128)}, u32[]{:S(2)}) copy-start(s32[3,32]{1,0:T(4,128)} %get-tuple-element.44.plan) | copy-start | bytes 1156
  83.8 14.2 %collective-permute-start.18 = (f32[512,512]{1,0:T(8,128)}, f32[512,512]{1,0:T(8,128)S(1)}, u32[]{:S(2)}, u32[]{:S(2)}) collective-permute-start(f32[512,512]{1,0:T(8,128)} %collective-permute-done.12.refs_3_), channel_id=1, source_target_pairs={{0,1},{1,2},{2,3},{3,4},{4,5},{5,6},{6,7},{7,0},{16,23},{17,16},{1... | collective-permute-start | bytes 3145736 | tf_op jit(solution)/shard_map/ppermute | solution.py:36
  86.5 24.8 %collective-permute-start.19 = (f32[512,512]{1,0:T(8,128)S(1)}, f32[512,512]{1,0:T(8,128)S(1)}, u32[]{:S(2)}, u32[]{:S(2)}) collective-permute-start(f32[512,512]{1,0:T(8,128)S(1)} %beta1.1), channel_id=1, source_target_pairs={{0,8},{8,0},{1,9},{9,1},{2,10},{10,2},{3,11},{11,3},{4,12},{12,4},... | collective-permute-start | bytes 3145736 | tf_op jit(solution)/shard_map/ppermute | solution.py:28
  87.9 11.7 %copy-start.11 = (f32[512,512]{1,0:T(8,128)}, f32[512,512]{1,0:T(8,128)S(1)}, u32[]{:S(2)}) copy-start(f32[512,512]{1,0:T(8,128)S(1)} %collective-permute-done.10.refs_2_) | copy-start | bytes 3145732
  87.9 16.5 %collective-permute-start.15 = (f32[512,512]{1,0:T(8,128)S(1)}, f32[512,512]{1,0:T(8,128)S(1)}, u32[]{:S(2)}, u32[]{:S(2)}) collective-permute-start(f32[512,512]{1,0:T(8,128)S(1)} %collective-permute-done.10.refs_2_), channel_id=1, source_target_pairs={{0,16},{16,0},{1,17},{17,1},{2,18},{18,2},{3,19},{19,3},{4,20},{20... | collective-permute-start | bytes 3145736 | tf_op jit(solution)/shard_map/ppermute | solution.py:28
  89.7 9.9 %copy-start.12 = (f32[512,512]{1,0:T(8,128)}, f32[512,512]{1,0:T(8,128)S(1)}, u32[]{:S(2)}) copy-start(f32[512,512]{1,0:T(8,128)S(1)} %collective-permute-done.11.refs_6_) | copy-start | bytes 3145732
  89.7 14.7 %collective-permute-start.16 = (f32[512,512]{1,0:T(8,128)S(1)}, f32[512,512]{1,0:T(8,128)S(1)}, u32[]{:S(2)}, u32[]{:S(2)}) collective-permute-start(f32[512,512]{1,0:T(8,128)S(1)} %collective-permute-done.11.refs_6_), channel_id=1, source_target_pairs={{0,16},{16,0},{1,17},{17,1},{2,18},{18,2},{3,19},{19,3},{4,20},{20... | collective-permute-start | bytes 3145736 | tf_op jit(solution)/shard_map/ppermute | solution.py:28
  92.3 12.1 %collective-permute-start.17 = (f32[6,256,512]{2,1,0:T(8,128)S(1)}, f32[6,256,512]{2,1,0:T(8,128)S(1)}, u32[]{:S(2)}, u32[]{:S(2)}) collective-permute-start(f32[6,256,512]{2,1,0:T(8,128)S(1)} %pick.1), channel_id=1, source_target_pairs={{0,16},{16,0},{1,17},{17,1},{2,18},{18,2},{3,19},{19,3},{4,20},{20... | collective-permute-start | bytes 9437192 | tf_op jit(solution)/shard_map/ppermute | solution.py:28
  99.6 7.1 %copy-start.7 = (s32[1,32]{1,0:T(1,128)S(1)}, s32[1,32]{1,0:T(1,128)}, u32[]{:S(2)}) copy-start(s32[1,32]{1,0:T(1,128)} %get-tuple-element.31.plan) | copy-start | bytes 388
  99.6 22.9 %collective-permute-start.20 = (f32[512,256]{1,0:T(8,128)S(1)}, f32[512,256]{1,0:T(8,128)S(1)}, u32[]{:S(2)}, u32[]{:S(2)}) collective-permute-start(f32[512,256]{1,0:T(8,128)S(1)} %beta2.1), channel_id=1, source_target_pairs={{0,8},{8,0},{1,9},{9,1},{2,10},{10,2},{3,11},{11,3},{4,12},{12,4},... | collective-permute-start | bytes 1572872 | tf_op jit(solution)/shard_map/ppermute | solution.py:28
  106.8 4.3 %copy-start.15 = (f32[512]{0:T(512)S(1)}, f32[512]{0:T(512)}, u32[]{:S(2)}) copy-start(f32[512]{0:T(512)} %param.11) | copy-start | bytes 6148
  106.8 4.3 %copy-start.16 = (f32[512]{0:T(512)S(1)}, f32[512]{0:T(512)}, u32[]{:S(2)}) copy-start(f32[512]{0:T(512)} %param.10) | copy-start | bytes 6148
  (8 other events, 12.7 us)

commit v9 on v8

--- a/solution.py
+++ b/solution.py
@@ -246,7 +246,13 @@
 def beta_kernel(call, where, plan, *refs):
     numbers = HOPS[call]
     pieces, refs = refs[: len(numbers)], refs[len(numbers) :]
-    own, got, other, out, data, tiles, data_sem, tile_sem = refs
+    own, got, other, refs = refs[0], refs[1], refs[2], refs[3:]
+    before, refs = (refs[0], refs[1:]) if call == 2 else (None, refs)
+    outs, (data, tiles, data_sem, tile_sem, out_sem) = refs[:-5], refs[-5:]
+    n, half = data.shape[1], data.shape[1] // 2
+    if call == 2:
+        first = pltpu.make_async_copy(before, outs[0].at[:, pl.ds(0, n)], out_sem)
+        first.start()
     core = where[0] & 1
     count = plan[call, 0]
 
@@ -273,37 +279,69 @@
         return 0
 
     lax.fori_loop(0, count, fetch, 0)
-    out[...] = jnp.zeros_like(out)
+    if call == 2:
+        outs[0][:, n:] = jnp.zeros((half, BS), jnp.float32)
+        first.wait()
+    else:
+        for out in outs:
+            out[...] = jnp.zeros_like(out)
 
     def product(k, _):
         block = (plan[call, k + 1] >> 4) & 1
         columns_of(k, pieces[0], 0).wait()
         tile_from(k, own.at[0, 0]).wait()
-        columns = 0 if call == 2 else pl.multiple_of(block * BS, BS)
-        out[:, pl.ds(columns, BS)] += dot3(data[k], tiles[k])
+        columns = pl.ds(pl.multiple_of(block * BS, BS), BS)
+        if call == 0:
+            outs[0][:, columns] += dot3(data[k], tiles[k])
+        elif call == 1:
+            outs[0][:, columns] += dot3(data[k, :half], tiles[k])
+            outs[1][:, columns] += dot3(data[k, half:], tiles[k])
+        else:
+            outs[0][:, n:] += dot3(data[k, :half], tiles[k])
+            outs[0][:, columns] += dot3(data[k, half:], tiles[k])
         return 0
 
     lax.fori_loop(0, count, product, 0)
 
 
-def beta_call(call, where, plan, held, own, got, other):
+def beta_call(call, where, plan, held, own, got, other, before=()):
     n = held[0].shape[0]
     pieces = [held[d] for d in HOPS[call]]
+    shapes = ([(n, n)], [(n // 2, n)] * 2, [(n // 2, n + BS)])[call]
+    fixed = in_hbm(own, got, other)
+    pieces = pieces if call == 2 else in_hbm(*pieces)
     return pl.pallas_call(
         functools.partial(beta_kernel, call),
-        out_shape=jax.ShapeDtypeStruct((n, BS if call == 2 else n), jnp.float32),
-        in_specs=[SMEM] * 2 + [HBM] * (len(pieces) + 3),
-        out_specs=VMEM,
+        out_shape=[jax.ShapeDtypeStruct(shape, jnp.float32) for shape in shapes],
+        in_specs=[SMEM] * 2 + [ANY] * (len(pieces) + 3 + len(before)),
+        out_specs=[VMEM] * len(shapes),
         scratch_shapes=[
             pltpu.VMEM((len(pieces), n, BS), jnp.float32),
             pltpu.VMEM((len(pieces), BS, BS), jnp.float32),
             pltpu.SemaphoreType.DMA((len(pieces),)),
             pltpu.SemaphoreType.DMA((len(pieces),)),
+            pltpu.SemaphoreType.DMA,
         ],
         compiler_params=pltpu.CompilerParams(vmem_limit_bytes=12 * MIB),
         cost_estimate=LARGE,
         name=f"beta{call}",
-    )(where, plan, *in_hbm(*pieces, own, got, other))
+    )(where, plan, *pieces, *fixed, *before)
+
+
+def last_kernel(where, sends, joined, top, rest, out, top_here, rest_here, sems):
+    half, n = top.shape
+    copies = [
+        pltpu.make_async_copy(source, target, sems.at[i])
+        for i, (source, target) in enumerate(((joined, out), (top, top_here), (rest, rest_here)))
+    ]
+    for copy in copies:
+        copy.start()
+    block = sends[(where[1] + 4) & 7] >> 3
+    for copy in copies:
+        copy.wait()
+    out[:half] += top_here[...]
+    out[half:] += rest_here[:, :n]
+    out[:half, pl.ds(pl.multiple_of(block * BS, BS), BS)] += rest_here[:, n:]
 
 
 def per_device(
@@ -317,6 +355,7 @@
     beta_source,
     beta_live,
 ):
+    n = coeffs.shape[0]
     where = jnp.stack([lax.axis_index(ALPHA), lax.axis_index(BETA)]).astype(jnp.int32)
     f1, b1 = step(coeffs, "z"), step(coeffs, "z", -1)
     uf, ub = step(coeffs, "x"), step(coeffs, "x", -1)
@@ -348,22 +387,29 @@
     f3, b3, picked = lax.optimization_barrier((f3, b3, picked))
     picked = swap(picked, "core")
     held = [coeffs, f1, f2, f3, step(f3, "z"), b3, b2, b1]
-    beta_par = beta_call(1, where, beta_plan, held, beta_tiles, got, other)
-    beta_other = swap(beta_par, "ylo")
+    top, bottom = beta_call(1, where, beta_plan, held, beta_tiles, got, other)
+    top_other = swap(top, "ylo")
     pieces = [coeffs, uf, u2, ub, v, vf, v2, vb]
-    us2, vs2 = swap(after(u2, beta_par), "core"), swap(after(v2, beta_par), "core")
-    far = beta_call(2, where, beta_plan, held, beta_tiles, got, other)
-    far_other = swap(far, "ylo")
-    alpha = alpha_call(alpha_plan, pieces, us2, vs2, picked, after(alpha_tiles, far))
-    beta_own = beta_call(0, where, beta_plan, held, after(beta_tiles, far), got, other)
+    us2, vs2 = swap(after(u2, top), "core"), swap(after(v2, top), "core")
+    (rest,) = beta_call(2, where, beta_plan, held, beta_tiles, got, other, [bottom])
+    rest_other = swap(rest, "ylo")
+    alpha = alpha_call(alpha_plan, pieces, us2, vs2, picked, after(alpha_tiles, rest))
+    (beta_own,) = beta_call(0, where, beta_plan, held, after(beta_tiles, rest), got, other)
     joined = (diag_alpha[:, None] + diag_beta[None, :]) * coeffs + alpha + beta_own
-    joined, place = lax.optimization_barrier((joined, (where[1] + 4) & 7))
-    joined = lax.optimization_barrier(joined + beta_other)
-    block = lax.dynamic_index_in_dim(sends, place, 0, keepdims=False) >> 3
-    zero = jnp.zeros_like(far_other)
-    low = jnp.where(block == 0, far_other, zero)
-    high = jnp.where(block == 0, zero, far_other)
-    return joined + jnp.concatenate([low, high], axis=1)
+    return pl.pallas_call(
+        last_kernel,
+        out_shape=jax.ShapeDtypeStruct((n, n), jnp.float32),
+        in_specs=[SMEM] * 2 + [ANY] * 3,
+        out_specs=VMEM,
+        scratch_shapes=[
+            pltpu.VMEM(top_other.shape, jnp.float32),
+            pltpu.VMEM(rest_other.shape, jnp.float32),
+            pltpu.SemaphoreType.DMA((3,)),
+        ],
+        compiler_params=pltpu.CompilerParams(vmem_limit_bytes=8 * MIB),
+        cost_estimate=SMALL,
+        name="last",
+    )(where, sends, lax.optimization_barrier(joined), top_other, rest_other)
 
 
 def solution(mesh):

time: 125 us -> 121 us (0.968)
  Pallas kernels: 19 us -> 27.1 us
  waiting for transfers between devices: 63 us -> 56.6 us
  local copies, waits for them, and re-layouts: 11.8 us -> 9.08 us
  starting transfers between devices: 26.7 us -> 24.9 us
  other arithmetic: 2.24 us -> 0.83 us
    ppermute x8, waiting for transfers between devices: 9.66 us -> 2.97 us  [swap(): return lax.ppermute(value, axis, [(0, 1), (1, 0)])]
    pallas_call x3 -> x4, Pallas kernels: 6.61 us -> 11 us  [the longest x3 9.17 us: beta_call(): pl.pallas_call(functools.partial(beta_kernel, call), out_shape=[jax.Shape...]
    pallas_call x1, Pallas kernels: 4.25 us -> 8.08 us  [alpha_call(): pl.pallas_call(alpha_kernel, out_shape=jax.ShapeDtypeStruct((n, n), jnp.f...]
    ppermute x8, starting transfers between devices: 9.91 us -> 7.14 us  [swap(): return lax.ppermute(value, axis, [(0, 1), (1, 0)])]
    unnamed x42 -> x54, local copies, waits for them, and re-layouts: 11.2 us -> 9.08 us
    ppermute x7, waiting for transfers between devices: 45.8 us -> 47.6 us  [step(): return lax.ppermute(value, ('core', axis), pairs)]
    ppermute x6, waiting for transfers between devices: 7.54 us -> 6.05 us  [step(): return lax.ppermute(value, (axis, 'core'), pairs)]
    add x2 -> x0, other arithmetic: 1.34 us -> none  [the longest x1 1.13 us: per_device(): return joined + jnp.concatenate([low, high], axis=1)]
  transfers between devices with their start and end apart: 21 -> 21, of which waited for: 11 -> 10; matrix products, arithmetic and copies ran while one was open for 6% -> 5% of each run, Pallas kernels for 13% -> 19%
where the time goes in v9:
time: 121 us; the launch traced here: 119 us
  waiting for transfers between devices  56.6 us (47%)
  Pallas kernels  27.1 us (22%)
  starting transfers between devices  24.9 us (21%)
  local copies, waits for them, and re-layouts  9.08 us (8%)
    ppermute x7, waiting for transfers between devices, step(): return lax.ppermute(value, ('core', axis), pairs)  47.6 us
    ppermute x7, starting transfers between devices, step(): return lax.ppermute(value, ('core', axis), pairs)  9.34 us
    pallas_call x3, Pallas kernels, beta_call(): pl.pallas_call(functools.partial(beta_kernel, call), out_shape=[jax.Shape...  9.17 us
    unnamed x54, local copies, waits for them, and re-layouts  9.08 us
    ppermute x6, starting transfers between devices, step(): return lax.ppermute(value, (axis, 'core'), pairs)  8.37 us
    pallas_call x1, Pallas kernels, alpha_call(): pl.pallas_call(alpha_kernel, out_shape=jax.ShapeDtypeStruct((n, n), jnp.f...  8.08 us
    ppermute x8, starting transfers between devices, swap(): return lax.ppermute(value, axis, [(0, 1), (1, 0)])  7.14 us
    ppermute x6, waiting for transfers between devices, step(): return lax.ppermute(value, (axis, 'core'), pairs)  6.05 us
  transfers between devices with their start and end apart: 21, of which 10 were waited for; matrix products, arithmetic and copies ran while one was open for 5% of the time, Pallas kernels for 19%

profile of v9, /device:TPU:1, one launch (start us, length us, event | category | flops | bytes accessed | tf_op | source)
XLA Modules:
  0.0 118.9 jit_solution(17370194906320602126)
XLA Ops:
  0.0 6.4 %collective-permute-start.3 = (f32[512,512]{1,0:T(8,128)}, f32[512,512]{1,0:T(8,128)}, u32[]{:S(2)}, u32[]{:S(2)}) collective-permute-start(f32[512,512]{1,0:T(8,128)} %refs_0_.7), channel_id=1, source_target_pairs={{0,1},{1,2},{2,3},{3,4},{4,5},{5,6},{6,7},{7,0},{16,23},{17,16},{1... | collective-permute-start | bytes 3145736 | tf_op jit(solution)/shard_map/ppermute | solution.py:36
  6.4 2.5 %collective-permute-start = (f32[512,512]{1,0:T(8,128)}, f32[512,512]{1,0:T(8,128)S(1)}, u32[]{:S(2)}, u32[]{:S(2)}) collective-permute-start(f32[512,512]{1,0:T(8,128)} %refs_0_.7), channel_id=1, source_target_pairs={{0,32},{32,64},{64,96},{96,0},{16,112},{48,16},{80,48},{112,80},{1... | collective-permute-start | bytes 3145736 | tf_op jit(solution)/shard_map/ppermute | solution.py:39
  8.9 2.9 %collective-permute-start.2 = (f32[512,512]{1,0:T(8,128)}, f32[512,512]{1,0:T(8,128)}, u32[]{:S(2)}, u32[]{:S(2)}) collective-permute-start(f32[512,512]{1,0:T(8,128)} %refs_0_.7), channel_id=1, source_target_pairs={{0,128},{128,0},{1,129},{129,1},{2,130},{130,2},{3,131},{131,3},{4... | collective-permute-start | bytes 3145736 | tf_op jit(solution)/shard_map/ppermute | solution.py:28
  11.8 1.4 %copy.10.alpha_source = s32[32,8]{1,0:T(8,128)} copy(s32[32,8]{0,1:T(8,128)} %param.14) | data formatting | bytes 2048 | tf_op args[5]
  13.2 1.4 %copy.11.alpha_live = s32[32,8]{1,0:T(8,128)} copy(s32[32,8]{0,1:T(8,128)} %param.15) | data formatting | bytes 2048 | tf_op args[6]
  14.5 1.4 %copy.12.beta_source = s32[32,8]{1,0:T(8,128)} copy(s32[32,8]{0,1:T(8,128)} %param.16) | data formatting | bytes 2048 | tf_op args[7]
  15.9 1.4 %copy.13.beta_live = s32[32,8]{1,0:T(8,128)} copy(s32[32,8]{0,1:T(8,128)} %param.17) | data formatting | bytes 2048 | tf_op args[8]
  17.9 3.4 %plan.1 = (s32[1,32]{1,0:T(1,128)}, s32[3,32]{1,0:T(4,128)}, s32[8]{0:T(128)}, s32[8]{0:T(128)}) custom-call(s32[2]{0:T(128)} %pad_add_fusion.where, s32[32,8]{1,0:T(8,128)} %copy.10.alpha_source, s32[32,8]{1,0:T(8,128)} %copy.11.alpha_live, s32[32,8]{1,0:T(8,128)} %copy.12.beta_source, s32[32,8]{1,0:T(8,128)} %copy.13.beta_live), custom_call_target="tpu_custom_call" | custom-call | tf_op jit(solution)/shard_map/plan/pallas_call | solution.py:363
  21.3 2.9 %send.1 = f32[4,256,256]{2,1,0:T(8,128)} custom-call(s32[2]{0:T(128)} %pad_add_fusion.where, s32[8]{0:T(128)} %get-tuple-element.31.sends, f32[2,8,256,256]{3,2,1,0:T(8,128)} %refs_8_), custom_call_target="tpu_custom_call" | custom-call | flops 1048576 | bytes 262144 | tf_op jit(solution)/shard_map/send/pallas_call | solution.py:232
  24.2 4.3 %collective-permute-done.3.refs_1_ = f32[512,512]{1,0:T(8,128)} collective-permute-done((f32[512,512]{1,0:T(8,128)}, f32[512,512]{1,0:T(8,128)}, u32[]{:S(2)}, u32[]{:S(2)}) %collective-permute-start.3) | collective-permute-done | bytes 1048608 | tf_op jit(solution)/shard_map/ppermute | solution.py:36
  28.5 2.9 %collective-permute-done.4.refs_6_.refs_7_ = f32[512,512]{1,0:T(8,128)} collective-permute-done((f32[512,512]{1,0:T(8,128)}, f32[512,512]{1,0:T(8,128)}, u32[]{:S(2)}, u32[]{:S(2)}) %collective-permute-start.4) | collective-permute-done | bytes 1048608 | tf_op jit(solution)/shard_map/ppermute | solution.py:36
  31.4 0.9 collective-permute-start.8
  32.8 1.8 %collective-permute-done.1.refs_2_.refs_3_ = f32[512,512]{1,0:T(8,128)S(1)} collective-permute-done((f32[512,512]{1,0:T(8,128)}, f32[512,512]{1,0:T(8,128)S(1)}, u32[]{:S(2)}, u32[]{:S(2)}) %collective-permute-start.1) | collective-permute-done | bytes 1048608 | tf_op jit(solution)/shard_map/ppermute | solution.py:39
  34.6 3.2 %collective-permute-start.5 = (f32[512,512]{1,0:T(8,128)}, f32[512,512]{1,0:T(8,128)S(1)}, u32[]{:S(2)}, u32[]{:S(2)}) collective-permute-start(f32[512,512]{1,0:T(8,128)} %collective-permute-done.2.refs_3_.refs_4_), channel_id=1, source_target_pairs={{0,32},{32,64},{64,96},{96,0},{16,112},{48,16},{80,48},{112,80},{1... | collective-permute-start | bytes 3145736 | tf_op jit(solution)/shard_map/ppermute | solution.py:39
  37.8 1.3 %collective-permute-start.7 = (f32[4,256,256]{2,1,0:T(8,128)}, f32[4,256,256]{2,1,0:T(8,128)S(1)}, u32[]{:S(2)}, u32[]{:S(2)}) collective-permute-start(f32[4,256,256]{2,1,0:T(8,128)} %send.1), channel_id=1, source_target_pairs={{0,8},{8,0},{1,9},{9,1},{2,10},{10,2},{3,11},{11,3},{4,12},{12,4},... | collective-permute-start | bytes 3145736 | tf_op jit(solution)/shard_map/ppermute | solution.py:28
  39.1 16.9 %collective-permute-done.8.refs_2_ = f32[512,512]{1,0:T(8,128)S(1)} collective-permute-done((f32[512,512]{1,0:T(8,128)}, f32[512,512]{1,0:T(8,128)S(1)}, u32[]{:S(2)}, u32[]{:S(2)}) %collective-permute-start.8) | collective-permute-done | bytes 1048608 | tf_op jit(solution)/shard_map/ppermute | solution.py:36
  56.0 1.7 %collective-permute-done.9.refs_5_.refs_6_ = f32[512,512]{1,0:T(8,128)S(1)} collective-permute-done((f32[512,512]{1,0:T(8,128)}, f32[512,512]{1,0:T(8,128)S(1)}, u32[]{:S(2)}, u32[]{:S(2)}) %collective-permute-start.9) | collective-permute-done | bytes 1048608 | tf_op jit(solution)/shard_map/ppermute | solution.py:36
  57.6 1.5 %collective-permute-start.13 = (f32[512,512]{1,0:T(8,128)S(1)}, f32[512,512]{1,0:T(8,128)S(1)}, u32[]{:S(2)}, u32[]{:S(2)}) collective-permute-start(f32[512,512]{1,0:T(8,128)S(1)} %collective-permute-done.9.refs_5_.refs_6_), channel_id=1, source_target_pairs={{0,7},{1,0},{2,1},{3,2},{4,3},{5,4},{6,5},{7,6},{16,17},{17,18},{1... | collective-permute-start | bytes 3145736 | tf_op jit(solution)/shard_map/ppermute | solution.py:36
  59.1 4.3 %collective-permute-done.6.refs_5_.refs_7_ = f32[512,512]{1,0:T(8,128)S(1)} collective-permute-done((f32[512,512]{1,0:T(8,128)}, f32[512,512]{1,0:T(8,128)S(1)}, u32[]{:S(2)}, u32[]{:S(2)}) %collective-permute-start.6) | collective-permute-done | bytes 1048608 | tf_op jit(solution)/shard_map/ppermute | solution.py:39
  63.6 2.7 %collective-permute-start.10 = (f32[512,512]{1,0:T(8,128)S(1)}, f32[512,512]{1,0:T(8,128)S(1)}, u32[]{:S(2)}, u32[]{:S(2)}) collective-permute-start(f32[512,512]{1,0:T(8,128)S(1)} %collective-permute-done.refs_1_), channel_id=1, source_target_pairs={{0,32},{32,64},{64,96},{96,0},{16,112},{48,16},{80,48},{112,80},{1... | collective-permute-start | bytes 3145736 | tf_op jit(solution)/shard_map/ppermute | solution.py:39
  66.3 1.8 %pick.1 = f32[6,256,512]{2,1,0:T(8,128)S(1)} custom-call(s32[8]{0:T(128)S(1)} %copy-done.9, f32[512,512]{1,0:T(8,128)S(1)} %copy-done, f32[512,512]{1,0:T(8,128)S(1)} %collective-permute-done.refs_1_, f32[512,512]{1,0:T(8,128)S(1)} %collective-permute-done.1.refs_2_.refs_3_, f32[512,512]{1,0:T(8,128)} %collective-permute-done.2.refs_3_.refs_4_, ...), custom_call_target="tpu_custom_call" | custom-call | flops 1048576 | bytes 262144 | tf_op jit(solution)/shard_map/pick/pallas_call | solution.py:148
  68.1 14.4 %collective-permute-done.12.refs_3_ = f32[512,512]{1,0:T(8,128)S(1)} collective-permute-done((f32[512,512]{1,0:T(8,128)S(1)}, f32[512,512]{1,0:T(8,128)S(1)}, u32[]{:S(2)}, u32[]{:S(2)}) %collective-permute-start.12) | collective-permute-done | bytes 1048608 | tf_op jit(solution)/shard_map/ppermute | solution.py:36
  82.5 1.1 collective-permute-done.13.refs_4_.refs_5_
  84.9 3.7 %beta1.1 = (f32[256,512]{1,0:T(8,128)S(1)}, f32[256,512]{1,0:T(8,128)S(1)}) custom-call(s32[2]{0:T(128)S(1)} %copy-done.6, s32[3,32]{1,0:T(4,128)S(1)} %copy-done.11, f32[512,512]{1,0:T(8,128)} %refs_0_.7, f32[512,512]{1,0:T(8,128)} %collective-permute-done.3.refs_1_, f32[512,512]{1,0:T(8,128)} %copy-done.19, f32[512,512]{1,0:T(8,128)} %copy-done.22, ...), custom_call_target="tpu_custom_call" | custom-call | flops 17179869184 | bytes 33554432 | tf_op jit(solution)/shard_map/beta1/pallas_call | solution.py:313
  89.6 1.6 %collective-permute-start.16 = (f32[512,512]{1,0:T(8,128)S(1)}, f32[512,512]{1,0:T(8,128)S(1)}, u32[]{:S(2)}, u32[]{:S(2)}) collective-permute-start(f32[512,512]{1,0:T(8,128)S(1)} %collective-permute-done.11.refs_6_), channel_id=1, source_target_pairs={{0,16},{16,0},{1,17},{17,1},{2,18},{18,2},{3,19},{19,3},{4,20},{20... | collective-permute-start | bytes 3145736 | tf_op jit(solution)/shard_map/ppermute | solution.py:28
  91.2 6.3 %collective-permute-done.18.refs_0_.refs_4_ = f32[512,512]{1,0:T(8,128)S(1)} collective-permute-done((f32[512,512]{1,0:T(8,128)S(1)}, f32[512,512]{1,0:T(8,128)S(1)}, u32[]{:S(2)}, u32[]{:S(2)}) %collective-permute-start.18) | collective-permute-done | bytes 1048608 | tf_op jit(solution)/shard_map/ppermute | solution.py:36
  97.6 2.1 %beta2.1 = f32[256,768]{1,0:T(8,128)S(1)} custom-call(s32[2]{0:T(128)S(1)} %copy-done.6, s32[3,32]{1,0:T(4,128)S(1)} %copy-done.11, f32[512,512]{1,0:T(8,128)S(1)} %collective-permute-done.18.refs_0_.refs_4_, f32[2,8,256,256]{3,2,1,0:T(8,128)} %refs_8_, f32[4,256,256]{2,1,0:T(8,128)} %copy-done.21, f32[4,256,256]{2,1,0:T(8,128)} %copy-done.24, ...), custom_call_target="tpu_custom_call" | custom-call | flops 17179869184 | bytes 33554432 | tf_op jit(solution)/shard_map/beta2/pallas_call | solution.py:313
  99.9 3.4 %beta0.1 = f32[512,512]{1,0:T(8,128)S(1)} custom-call(s32[2]{0:T(128)S(1)} %copy-done.6, s32[3,32]{1,0:T(4,128)S(1)} %copy-done.11, f32[512,512]{1,0:T(8,128)} %refs_0_.7, f32[512,512]{1,0:T(8,128)} %collective-permute-done.3.refs_1_, f32[512,512]{1,0:T(8,128)} %copy-done.19, f32[512,512]{1,0:T(8,128)} %copy-done.22, f32[512,512]{1,0:T(8,128)} %copy-done.10, ...), custom_call_target="tpu_custom_call" | custom-call | flops 17179869184 | bytes 33554432 | tf_op jit(solution)/shard_map/beta0/pallas_call | solution.py:313
  104.6 1.0 copy-done.12
  105.6 8.1 %alpha.1 = f32[512,512]{1,0:T(8,128)S(1)} custom-call(s32[1,32]{1,0:T(1,128)S(1)} %copy-done.8, f32[512,512]{1,0:T(8,128)} %refs_0_.7, f32[512,512]{1,0:T(8,128)} %copy-done.2, f32[512,512]{1,0:T(8,128)} %copy-done.13, f32[512,512]{1,0:T(8,128)} %copy-done.3, f32[512,512]{1,0:T(8,128)} %collective-permute-done.2.refs_3_.refs_4_, f32[512,512]{1,0:T(8,128)} %copy-done.4, ...), custom_call_target="tpu_custom_call" | custom-call | flops 1048576 | bytes 262144 | tf_op jit(solution)/shard_map/alpha/pallas_call | solution.py:201
  114.0 3.0 %collective-permute-done.20.rest = f32[256,768]{1,0:T(8,128)S(1)} collective-permute-done((f32[256,768]{1,0:T(8,128)S(1)}, f32[256,768]{1,0:T(8,128)S(1)}, u32[]{:S(2)}, u32[]{:S(2)}) %collective-permute-start.20) | collective-permute-done | bytes 786464 | tf_op jit(solution)/shard_map/ppermute | solution.py:28
  116.9 1.8 %last.1 = f32[512,512]{1,0:T(8,128)} custom-call(s32[2]{0:T(128)S(1)} %copy-done.6, s32[8]{0:T(128)S(1)} %copy-done.7, f32[512,512]{1,0:T(8,128)S(1)} %add_add_fusion.joined, f32[256,512]{1,0:T(8,128)S(1)} %collective-permute-done.19.top, f32[256,768]{1,0:T(8,128)S(1)} %collective-permute-done.20.rest), custom_call_target="tpu_custom_call" | custom-call | flops 1048576 | bytes 262144 | tf_op jit(solution)/shard_map/last/pallas_call | solution.py:399
  (74 shorter events, 5.4 us)
Async XLA Ops:
  0.0 66.3 %copy-start = (f32[512,512]{1,0:T(8,128)S(1)}, f32[512,512]{1,0:T(8,128)}, u32[]{:S(2)}) copy-start(f32[512,512]{1,0:T(8,128)} %refs_0_.7) | copy-start | bytes 3145732
  0.0 28.5 %collective-permute-start.3 = (f32[512,512]{1,0:T(8,128)}, f32[512,512]{1,0:T(8,128)}, u32[]{:S(2)}, u32[]{:S(2)}) collective-permute-start(f32[512,512]{1,0:T(8,128)} %refs_0_.7), channel_id=1, source_target_pairs={{0,1},{1,2},{2,3},{3,4},{4,5},{5,6},{6,7},{7,0},{16,23},{17,16},{1... | collective-permute-start | bytes 3145736 | tf_op jit(solution)/shard_map/ppermute | solution.py:36
  6.4 25.0 %collective-permute-start.4 = (f32[512,512]{1,0:T(8,128)}, f32[512,512]{1,0:T(8,128)}, u32[]{:S(2)}, u32[]{:S(2)}) collective-permute-start(f32[512,512]{1,0:T(8,128)} %refs_0_.7), channel_id=1, source_target_pairs={{0,7},{1,0},{2,1},{3,2},{4,3},{5,4},{6,5},{7,6},{16,17},{17,18},{1... | collective-permute-start | bytes 3145736 | tf_op jit(solution)/shard_map/ppermute | solution.py:36
  6.4 26.4 %collective-permute-start = (f32[512,512]{1,0:T(8,128)}, f32[512,512]{1,0:T(8,128)S(1)}, u32[]{:S(2)}, u32[]{:S(2)}) collective-permute-start(f32[512,512]{1,0:T(8,128)} %refs_0_.7), channel_id=1, source_target_pairs={{0,32},{32,64},{64,96},{96,0},{16,112},{48,16},{80,48},{112,80},{1... | collective-permute-start | bytes 3145736 | tf_op jit(solution)/shard_map/ppermute | solution.py:39
  8.9 25.7 %collective-permute-start.1 = (f32[512,512]{1,0:T(8,128)}, f32[512,512]{1,0:T(8,128)S(1)}, u32[]{:S(2)}, u32[]{:S(2)}) collective-permute-start(f32[512,512]{1,0:T(8,128)} %refs_0_.7), channel_id=1, source_target_pairs={{0,96},{32,0},{64,32},{96,64},{16,48},{48,80},{80,112},{112,16},{1... | collective-permute-start | bytes 3145736 | tf_op jit(solution)/shard_map/ppermute | solution.py:39
  8.9 25.7 %collective-permute-start.2 = (f32[512,512]{1,0:T(8,128)}, f32[512,512]{1,0:T(8,128)}, u32[]{:S(2)}, u32[]{:S(2)}) collective-permute-start(f32[512,512]{1,0:T(8,128)} %refs_0_.7), channel_id=1, source_target_pairs={{0,128},{128,0},{1,129},{129,1},{2,130},{130,2},{3,131},{131,3},{4... | collective-permute-start | bytes 3145736 | tf_op jit(solution)/shard_map/ppermute | solution.py:28
  21.3 45.0 %copy-start.9 = (s32[8]{0:T(128)S(1)}, s32[8]{0:T(128)}, u32[]{:S(2)}) copy-start(s32[8]{0:T(128)} %get-tuple-element.46.picks) | copy-start | bytes 100
  31.4 24.6 %collective-permute-start.8 = (f32[512,512]{1,0:T(8,128)}, f32[512,512]{1,0:T(8,128)S(1)}, u32[]{:S(2)}, u32[]{:S(2)}) collective-permute-start(f32[512,512]{1,0:T(8,128)} %collective-permute-done.3.refs_1_), channel_id=1, source_target_pairs={{0,1},{1,2},{2,3},{3,4},{4,5},{5,6},{6,7},{7,0},{16,23},{17,16},{1... | collective-permute-start | bytes 3145736 | tf_op jit(solution)/shard_map/ppermute | solution.py:36
  32.3 25.3 %collective-permute-start.9 = (f32[512,512]{1,0:T(8,128)}, f32[512,512]{1,0:T(8,128)S(1)}, u32[]{:S(2)}, u32[]{:S(2)}) collective-permute-start(f32[512,512]{1,0:T(8,128)} %collective-permute-done.4.refs_6_.refs_7_), channel_id=1, source_target_pairs={{0,7},{1,0},{2,1},{3,2},{4,3},{5,4},{6,5},{7,6},{16,17},{17,18},{1... | collective-permute-start | bytes 3145736 | tf_op jit(solution)/shard_map/ppermute | solution.py:36
  32.8 35.2 %copy-start.2 = (f32[512,512]{1,0:T(8,128)}, f32[512,512]{1,0:T(8,128)S(1)}, u32[]{:S(2)}) copy-start(f32[512,512]{1,0:T(8,128)S(1)} %collective-permute-done.refs_1_) | copy-start | bytes 3145732
  34.6 33.5 %copy-start.3 = (f32[512,512]{1,0:T(8,128)}, f32[512,512]{1,0:T(8,128)S(1)}, u32[]{:S(2)}) copy-start(f32[512,512]{1,0:T(8,128)S(1)} %collective-permute-done.1.refs_2_.refs_3_) | copy-start | bytes 3145732
  34.6 24.5 %collective-permute-start.5 = (f32[512,512]{1,0:T(8,128)}, f32[512,512]{1,0:T(8,128)S(1)}, u32[]{:S(2)}, u32[]{:S(2)}) collective-permute-start(f32[512,512]{1,0:T(8,128)} %collective-permute-done.2.refs_3_.refs_4_), channel_id=1, source_target_pairs={{0,32},{32,64},{64,96},{96,0},{16,112},{48,16},{80,48},{112,80},{1... | collective-permute-start | bytes 3145736 | tf_op jit(solution)/shard_map/ppermute | solution.py:39
  37.8 25.6 %collective-permute-start.6 = (f32[512,512]{1,0:T(8,128)}, f32[512,512]{1,0:T(8,128)S(1)}, u32[]{:S(2)}, u32[]{:S(2)}) collective-permute-start(f32[512,512]{1,0:T(8,128)} %collective-permute-done.2.refs_3_.refs_4_), channel_id=1, source_target_pairs={{0,96},{32,0},{64,32},{96,64},{16,48},{48,80},{80,112},{112,16},{1... | collective-permute-start | bytes 3145736 | tf_op jit(solution)/shard_map/ppermute | solution.py:39
  37.8 25.6 %collective-permute-start.7 = (f32[4,256,256]{2,1,0:T(8,128)}, f32[4,256,256]{2,1,0:T(8,128)S(1)}, u32[]{:S(2)}, u32[]{:S(2)}) collective-permute-start(f32[4,256,256]{2,1,0:T(8,128)} %send.1), channel_id=1, source_target_pairs={{0,8},{8,0},{1,9},{9,1},{2,10},{10,2},{3,11},{11,3},{4,12},{12,4},... | collective-permute-start | bytes 3145736 | tf_op jit(solution)/shard_map/ppermute | solution.py:28
  56.0 12.1 %copy-start.19 = (f32[512,512]{1,0:T(8,128)}, f32[512,512]{1,0:T(8,128)S(1)}, u32[]{:S(2)}) copy-start(f32[512,512]{1,0:T(8,128)S(1)} %collective-permute-done.8.refs_2_) | copy-start | bytes 3145732
  57.6 10.5 %copy-start.20 = (f32[512,512]{1,0:T(8,128)}, f32[512,512]{1,0:T(8,128)S(1)}, u32[]{:S(2)}) copy-start(f32[512,512]{1,0:T(8,128)S(1)} %collective-permute-done.9.refs_5_.refs_6_) | copy-start | bytes 3145732
  57.6 24.9 %collective-permute-start.12 = (f32[512,512]{1,0:T(8,128)S(1)}, f32[512,512]{1,0:T(8,128)S(1)}, u32[]{:S(2)}, u32[]{:S(2)}) collective-permute-start(f32[512,512]{1,0:T(8,128)S(1)} %collective-permute-done.8.refs_2_), channel_id=1, source_target_pairs={{0,1},{1,2},{2,3},{3,4},{4,5},{5,6},{6,7},{7,0},{16,23},{17,16},{1... | collective-permute-start | bytes 3145736 | tf_op jit(solution)/shard_map/ppermute | solution.py:36
  57.6 26.0 %collective-permute-start.13 = (f32[512,512]{1,0:T(8,128)S(1)}, f32[512,512]{1,0:T(8,128)S(1)}, u32[]{:S(2)}, u32[]{:S(2)}) collective-permute-start(f32[512,512]{1,0:T(8,128)S(1)} %collective-permute-done.9.refs_5_.refs_6_), channel_id=1, source_target_pairs={{0,7},{1,0},{2,1},{3,2},{4,3},{5,4},{6,5},{7,6},{16,17},{17,18},{1... | collective-permute-start | bytes 3145736 | tf_op jit(solution)/shard_map/ppermute | solution.py:36
  59.1 9.0 %copy-start.4 = (f32[512,512]{1,0:T(8,128)}, f32[512,512]{1,0:T(8,128)S(1)}, u32[]{:S(2)}) copy-start(f32[512,512]{1,0:T(8,128)S(1)} %collective-permute-done.5.refs_4_.refs_5_) | copy-start | bytes 3145732
  63.4 20.2 %collective-permute-start.14 = (f32[4,256,256]{2,1,0:T(8,128)S(1)}, f32[4,256,256]{2,1,0:T(8,128)S(1)}, u32[]{:S(2)}, u32[]{:S(2)}) collective-permute-start(f32[4,256,256]{2,1,0:T(8,128)S(1)} %collective-permute-done.7.refs_8_.refs_2_.refs_9_), channel_id=1, source_target_pairs={{0,16},{16,0},{1,17},{17,1},{2,18},{18,2},{3,19},{19,3},{4,20},{20... | collective-permute-start | bytes 3145736 | tf_op jit(solution)/shard_map/ppermute | solution.py:28
  63.6 25.3 %collective-permute-start.10 = (f32[512,512]{1,0:T(8,128)S(1)}, f32[512,512]{1,0:T(8,128)S(1)}, u32[]{:S(2)}, u32[]{:S(2)}) collective-permute-start(f32[512,512]{1,0:T(8,128)S(1)} %collective-permute-done.refs_1_), channel_id=1, source_target_pairs={{0,32},{32,64},{64,96},{96,0},{16,112},{48,16},{80,48},{112,80},{1... | collective-permute-start | bytes 3145736 | tf_op jit(solution)/shard_map/ppermute | solution.py:39
  66.3 23.4 %collective-permute-start.11 = (f32[512,512]{1,0:T(8,128)S(1)}, f32[512,512]{1,0:T(8,128)S(1)}, u32[]{:S(2)}, u32[]{:S(2)}) collective-permute-start(f32[512,512]{1,0:T(8,128)S(1)} %collective-permute-done.5.refs_4_.refs_5_), channel_id=1, source_target_pairs={{0,32},{32,64},{64,96},{96,0},{16,112},{48,16},{80,48},{112,80},{1... | collective-permute-start | bytes 3145736 | tf_op jit(solution)/shard_map/ppermute | solution.py:39
  66.3 18.6 %copy-start.6 = (s32[2]{0:T(128)S(1)}, s32[2]{0:T(128)}, u32[]{:S(2)}) copy-start(s32[2]{0:T(128)} %pad_add_fusion.where) | copy-start | bytes 28
  66.3 18.6 %copy-start.11 = (s32[3,32]{1,0:T(4,128)S(1)}, s32[3,32]{1,0:T(4,128)}, u32[]{:S(2)}) copy-start(s32[3,32]{1,0:T(4,128)} %get-tuple-element.44.plan) | copy-start | bytes 1156
  83.6 13.9 %collective-permute-start.18 = (f32[512,512]{1,0:T(8,128)S(1)}, f32[512,512]{1,0:T(8,128)S(1)}, u32[]{:S(2)}, u32[]{:S(2)}) collective-permute-start(f32[512,512]{1,0:T(8,128)S(1)} %collective-permute-done.12.refs_3_), channel_id=1, source_target_pairs={{0,1},{1,2},{2,3},{3,4},{4,5},{5,6},{6,7},{7,0},{16,23},{17,16},{1... | collective-permute-start | bytes 3145736 | tf_op jit(solution)/shard_map/ppermute | solution.py:36
  88.6 25.4 %collective-permute-start.19 = (f32[256,512]{1,0:T(8,128)S(1)}, f32[256,512]{1,0:T(8,128)S(1)}, u32[]{:S(2)}, u32[]{:S(2)}) collective-permute-start(f32[256,512]{1,0:T(8,128)S(1)} %get-tuple-element.50), channel_id=1, source_target_pairs={{0,8},{8,0},{1,9},{9,1},{2,10},{10,2},{3,11},{11,3},{4,12},{12,4},... | collective-permute-start | bytes 1572872 | tf_op jit(solution)/shard_map/ppermute | solution.py:28
  88.9 10.8 %copy-start.13 = (f32[512,512]{1,0:T(8,128)}, f32[512,512]{1,0:T(8,128)S(1)}, u32[]{:S(2)}) copy-start(f32[512,512]{1,0:T(8,128)S(1)} %collective-permute-done.10.refs_2_) | copy-start | bytes 3145732
  88.9 14.4 %collective-permute-start.15 = (f32[512,512]{1,0:T(8,128)S(1)}, f32[512,512]{1,0:T(8,128)S(1)}, u32[]{:S(2)}, u32[]{:S(2)}) collective-permute-start(f32[512,512]{1,0:T(8,128)S(1)} %collective-permute-done.10.refs_2_), channel_id=1, source_target_pairs={{0,16},{16,0},{1,17},{17,1},{2,18},{18,2},{3,19},{19,3},{4,20},{20... | collective-permute-start | bytes 3145736 | tf_op jit(solution)/shard_map/ppermute | solution.py:28
  89.6 10.0 %copy-start.14 = (f32[512,512]{1,0:T(8,128)}, f32[512,512]{1,0:T(8,128)S(1)}, u32[]{:S(2)}) copy-start(f32[512,512]{1,0:T(8,128)S(1)} %collective-permute-done.11.refs_6_) | copy-start | bytes 3145732
  89.6 13.7 %collective-permute-start.16 = (f32[512,512]{1,0:T(8,128)S(1)}, f32[512,512]{1,0:T(8,128)S(1)}, u32[]{:S(2)}, u32[]{:S(2)}) collective-permute-start(f32[512,512]{1,0:T(8,128)S(1)} %collective-permute-done.11.refs_6_), channel_id=1, source_target_pairs={{0,16},{16,0},{1,17},{17,1},{2,18},{18,2},{3,19},{19,3},{4,20},{20... | collective-permute-start | bytes 3145736 | tf_op jit(solution)/shard_map/ppermute | solution.py:28
  91.2 12.1 %collective-permute-start.17 = (f32[6,256,512]{2,1,0:T(8,128)S(1)}, f32[6,256,512]{2,1,0:T(8,128)S(1)}, u32[]{:S(2)}, u32[]{:S(2)}) collective-permute-start(f32[6,256,512]{2,1,0:T(8,128)S(1)} %pick.1), channel_id=1, source_target_pairs={{0,16},{16,0},{1,17},{17,1},{2,18},{18,2},{3,19},{19,3},{4,20},{20... | collective-permute-start | bytes 9437192 | tf_op jit(solution)/shard_map/ppermute | solution.py:28
  99.7 17.3 %collective-permute-start.20 = (f32[256,768]{1,0:T(8,128)S(1)}, f32[256,768]{1,0:T(8,128)S(1)}, u32[]{:S(2)}, u32[]{:S(2)}) collective-permute-start(f32[256,768]{1,0:T(8,128)S(1)} %beta2.1), channel_id=1, source_target_pairs={{0,8},{8,0},{1,9},{9,1},{2,10},{10,2},{3,11},{11,3},{4,12},{12,4},... | collective-permute-start | bytes 2359304 | tf_op jit(solution)/shard_map/ppermute | solution.py:28
  (14 other events, 53.0 us)

commit v10 on v9

--- a/solution.py
+++ b/solution.py
@@ -240,31 +240,35 @@
     )(where, sends, *in_hbm(own))
 
 
-HOPS = (tuple(range(8)), (0, 1, 2, 3, 5, 6, 7), (4,))
+NEAR = (0, 1, 2, 3, 5, 6, 7)
+HOPS = (tuple(range(8)), NEAR, NEAR, (4,))
 
 
 def beta_kernel(call, where, plan, *refs):
     numbers = HOPS[call]
     pieces, refs = refs[: len(numbers)], refs[len(numbers) :]
     own, got, other, refs = refs[0], refs[1], refs[2], refs[3:]
-    before, refs = (refs[0], refs[1:]) if call == 2 else (None, refs)
-    outs, (data, tiles, data_sem, tile_sem, out_sem) = refs[:-5], refs[-5:]
-    n, half = data.shape[1], data.shape[1] // 2
-    if call == 2:
-        first = pltpu.make_async_copy(before, outs[0].at[:, pl.ds(0, n)], out_sem)
+    before, refs = (refs[0], refs[1:]) if call == 3 else (None, refs)
+    out, data, tiles, data_sem, tile_sem, out_sem = refs
+    rows, half = data.shape[1], BS
+    n = 2 * half
+    if call == 3:
+        first = pltpu.make_async_copy(before, out.at[:, pl.ds(0, n)], out_sem)
         first.start()
+    at = half if call == 2 else 0
+    row = min(call, 1) if call < 3 else 2
     core = where[0] & 1
-    count = plan[call, 0]
+    count = plan[row, 0]
 
     def columns_of(k, ref, block):
-        first = pl.multiple_of(block * BS, BS)
-        return pltpu.make_async_copy(ref.at[:, pl.ds(first, BS)], data.at[k], data_sem.at[k])
+        block = ref.at[pl.ds(at, rows), pl.ds(pl.multiple_of(block * BS, BS), BS)]
+        return pltpu.make_async_copy(block, data.at[k], data_sem.at[k])
 
     def tile_from(k, ref):
         return pltpu.make_async_copy(ref, tiles.at[k], tile_sem.at[k])
 
     def fetch(k, _):
-        word = plan[call, k + 1]
+        word = plan[row, k + 1]
         tile = word & 15
         for number, ref in zip(numbers, pieces):
             pl.when((word >> 6) == number)(
@@ -279,26 +283,22 @@
         return 0
 
     lax.fori_loop(0, count, fetch, 0)
-    if call == 2:
-        outs[0][:, n:] = jnp.zeros((half, BS), jnp.float32)
+    if call == 3:
+        out[:, n:] = jnp.zeros((half, BS), jnp.float32)
         first.wait()
     else:
-        for out in outs:
-            out[...] = jnp.zeros_like(out)
+        out[...] = jnp.zeros_like(out)
 
     def product(k, _):
-        block = (plan[call, k + 1] >> 4) & 1
+        block = (plan[row, k + 1] >> 4) & 1
         columns_of(k, pieces[0], 0).wait()
         tile_from(k, own.at[0, 0]).wait()
         columns = pl.ds(pl.multiple_of(block * BS, BS), BS)
-        if call == 0:
-            outs[0][:, columns] += dot3(data[k], tiles[k])
-        elif call == 1:
-            outs[0][:, columns] += dot3(data[k, :half], tiles[k])
-            outs[1][:, columns] += dot3(data[k, half:], tiles[k])
+        if call == 3:
+            out[:, n:] += dot3(data[k, :half], tiles[k])
+            out[:, columns] += dot3(data[k, half:], tiles[k])
         else:
-            outs[0][:, n:] += dot3(data[k, :half], tiles[k])
-            outs[0][:, columns] += dot3(data[k, half:], tiles[k])
+            out[:, columns] += dot3(data[k], tiles[k])
         return 0
 
     lax.fori_loop(0, count, product, 0)
@@ -306,17 +306,19 @@
 
 def beta_call(call, where, plan, held, own, got, other, before=()):
     n = held[0].shape[0]
-    pieces = [held[d] for d in HOPS[call]]
-    shapes = ([(n, n)], [(n // 2, n)] * 2, [(n // 2, n + BS)])[call]
-    fixed = in_hbm(own, got, other)
-    pieces = pieces if call == 2 else in_hbm(*pieces)
+    half = n // 2
+    rows = half if call in (1, 2) else n
+    shape = ((n, n), (half, n), (half, n), (half, n + BS))[call]
+    fresh = {1: (3, 5), 3: (4,)}.get(call, ())
+    pieces = [held[d] if d in fresh else in_hbm(held[d])[0] for d in HOPS[call]]
+    fixed = [*in_hbm(own, got), other] if call == 1 else in_hbm(own, got, other)
     return pl.pallas_call(
         functools.partial(beta_kernel, call),
-        out_shape=[jax.ShapeDtypeStruct(shape, jnp.float32) for shape in shapes],
+        out_shape=jax.ShapeDtypeStruct(shape, jnp.float32),
         in_specs=[SMEM] * 2 + [ANY] * (len(pieces) + 3 + len(before)),
-        out_specs=[VMEM] * len(shapes),
+        out_specs=VMEM,
         scratch_shapes=[
-            pltpu.VMEM((len(pieces), n, BS), jnp.float32),
+            pltpu.VMEM((len(pieces), rows, BS), jnp.float32),
             pltpu.VMEM((len(pieces), BS, BS), jnp.float32),
             pltpu.SemaphoreType.DMA((len(pieces),)),
             pltpu.SemaphoreType.DMA((len(pieces),)),
@@ -387,14 +389,15 @@
     f3, b3, picked = lax.optimization_barrier((f3, b3, picked))
     picked = swap(picked, "core")
     held = [coeffs, f1, f2, f3, step(f3, "z"), b3, b2, b1]
-    top, bottom = beta_call(1, where, beta_plan, held, beta_tiles, got, other)
+    top = beta_call(1, where, beta_plan, held, beta_tiles, got, other)
     top_other = swap(top, "ylo")
+    bottom = beta_call(2, where, beta_plan, held, after(beta_tiles, top), got, other)
     pieces = [coeffs, uf, u2, ub, v, vf, v2, vb]
     us2, vs2 = swap(after(u2, top), "core"), swap(after(v2, top), "core")
-    (rest,) = beta_call(2, where, beta_plan, held, beta_tiles, got, other, [bottom])
+    rest = beta_call(3, where, beta_plan, held, beta_tiles, got, other, [bottom])
     rest_other = swap(rest, "ylo")
     alpha = alpha_call(alpha_plan, pieces, us2, vs2, picked, after(alpha_tiles, rest))
-    (beta_own,) = beta_call(0, where, beta_plan, held, after(beta_tiles, rest), got, other)
+    beta_own = beta_call(0, where, beta_plan, held, after(beta_tiles, rest), got, other)
     joined = (diag_alpha[:, None] + diag_beta[None, :]) * coeffs + alpha + beta_own
     return pl.pallas_call(
         last_kernel,

time: 121 us -> 121 us (level)
  starting transfers between devices: 24.9 us -> 27.9 us
  waiting for transfers between devices: 56.6 us -> 54.3 us
  local copies, waits for them, and re-layouts: 9.08 us -> 7.81 us
    pallas_call x3 -> x4, Pallas kernels: 9.17 us -> 12.7 us  [beta_call(): pl.pallas_call(functools.partial(beta_kernel, call), out_shape=jax.ShapeD...]
    pallas_call x1, Pallas kernels: 8.08 us -> 4.64 us  [alpha_call(): pl.pallas_call(alpha_kernel, out_shape=jax.ShapeDtypeStruct((n, n), jnp.f...]
    ppermute x7, waiting for transfers between devices: 47.6 us -> 44.3 us  [step(): return lax.ppermute(value, ('core', axis), pairs)]
    ppermute x8, starting transfers between devices: 7.14 us -> 10.2 us  [swap(): return lax.ppermute(value, axis, [(0, 1), (1, 0)])]
    unnamed x54, local copies, waits for them, and re-layouts: 9.08 us -> 7.81 us
  transfers between devices with their start and end apart: 21 -> 21, of which waited for: 10 -> 11; matrix products, arithmetic and copies ran while one was open for 5% -> 5% of each run, Pallas kernels for 19% -> 19%
where the time goes in v10:
time: 121 us; the launch traced here: 119 us
  waiting for transfers between devices  54.3 us (45%)
  starting transfers between devices  27.9 us (23%)
  Pallas kernels  27.2 us (22%)
  local copies, waits for them, and re-layouts  7.81 us (6%)
    ppermute x7, waiting for transfers between devices, step(): return lax.ppermute(value, ('core', axis), pairs)  44.3 us
    pallas_call x4, Pallas kernels, beta_call(): pl.pallas_call(functools.partial(beta_kernel, call), out_shape=jax.ShapeD...  12.7 us
    ppermute x8, starting transfers between devices, swap(): return lax.ppermute(value, axis, [(0, 1), (1, 0)])  10.2 us
    ppermute x7, starting transfers between devices, step(): return lax.ppermute(value, ('core', axis), pairs)  9.34 us
    ppermute x6, starting transfers between devices, step(): return lax.ppermute(value, (axis, 'core'), pairs)  8.37 us
    unnamed x54, local copies, waits for them, and re-layouts  7.81 us
    ppermute x6, waiting for transfers between devices, step(): return lax.ppermute(value, (axis, 'core'), pairs)  6.23 us
    pallas_call x1, Pallas kernels, alpha_call(): pl.pallas_call(alpha_kernel, out_shape=jax.ShapeDtypeStruct((n, n), jnp.f...  4.64 us
  transfers between devices with their start and end apart: 21, of which 11 were waited for; matrix products, arithmetic and copies ran while one was open for 5% of the time, Pallas kernels for 19%

profile of v10, /device:TPU:1, one launch (start us, length us, event | category | flops | bytes accessed | tf_op | source)
XLA Modules:
  0.0 118.6 jit_solution(6267890493675018948)
XLA Ops:
  0.0 6.4 %collective-permute-start.3 = (f32[512,512]{1,0:T(8,128)}, f32[512,512]{1,0:T(8,128)}, u32[]{:S(2)}, u32[]{:S(2)}) collective-permute-start(f32[512,512]{1,0:T(8,128)} %refs_0_.9), channel_id=1, source_target_pairs={{0,1},{1,2},{2,3},{3,4},{4,5},{5,6},{6,7},{7,0},{16,23},{17,16},{1... | collective-permute-start | bytes 3145736 | tf_op jit(solution)/shard_map/ppermute | solution.py:36
  6.4 2.5 %collective-permute-start = (f32[512,512]{1,0:T(8,128)}, f32[512,512]{1,0:T(8,128)S(1)}, u32[]{:S(2)}, u32[]{:S(2)}) collective-permute-start(f32[512,512]{1,0:T(8,128)} %refs_0_.9), channel_id=1, source_target_pairs={{0,32},{32,64},{64,96},{96,0},{16,112},{48,16},{80,48},{112,80},{1... | collective-permute-start | bytes 3145736 | tf_op jit(solution)/shard_map/ppermute | solution.py:39
  8.9 2.9 %collective-permute-start.2 = (f32[512,512]{1,0:T(8,128)}, f32[512,512]{1,0:T(8,128)}, u32[]{:S(2)}, u32[]{:S(2)}) collective-permute-start(f32[512,512]{1,0:T(8,128)} %refs_0_.9), channel_id=1, source_target_pairs={{0,128},{128,0},{1,129},{129,1},{2,130},{130,2},{3,131},{131,3},{4... | collective-permute-start | bytes 3145736 | tf_op jit(solution)/shard_map/ppermute | solution.py:28
  11.8 1.4 %copy.10.alpha_source = s32[32,8]{1,0:T(8,128)} copy(s32[32,8]{0,1:T(8,128)} %param.14) | data formatting | bytes 2048 | tf_op args[5]
  13.2 1.4 %copy.11.alpha_live = s32[32,8]{1,0:T(8,128)} copy(s32[32,8]{0,1:T(8,128)} %param.15) | data formatting | bytes 2048 | tf_op args[6]
  14.5 1.4 %copy.12.beta_source = s32[32,8]{1,0:T(8,128)} copy(s32[32,8]{0,1:T(8,128)} %param.16) | data formatting | bytes 2048 | tf_op args[7]
  15.9 1.4 %copy.13.beta_live = s32[32,8]{1,0:T(8,128)} copy(s32[32,8]{0,1:T(8,128)} %param.17) | data formatting | bytes 2048 | tf_op args[8]
  17.9 3.4 %plan.1 = (s32[1,32]{1,0:T(1,128)}, s32[3,32]{1,0:T(4,128)}, s32[8]{0:T(128)}, s32[8]{0:T(128)}) custom-call(s32[2]{0:T(128)} %pad_add_fusion.where, s32[32,8]{1,0:T(8,128)} %copy.10.alpha_source, s32[32,8]{1,0:T(8,128)} %copy.11.alpha_live, s32[32,8]{1,0:T(8,128)} %copy.12.beta_source, s32[32,8]{1,0:T(8,128)} %copy.13.beta_live), custom_call_target="tpu_custom_call" | custom-call | tf_op jit(solution)/shard_map/plan/pallas_call | solution.py:365
  21.3 2.9 %send.1 = f32[4,256,256]{2,1,0:T(8,128)} custom-call(s32[2]{0:T(128)} %pad_add_fusion.where, s32[8]{0:T(128)} %get-tuple-element.30.sends, f32[2,8,256,256]{3,2,1,0:T(8,128)} %refs_8_), custom_call_target="tpu_custom_call" | custom-call | flops 1048576 | bytes 262144 | tf_op jit(solution)/shard_map/send/pallas_call | solution.py:232
  24.2 4.3 %collective-permute-done.3.refs_1_ = f32[512,512]{1,0:T(8,128)} collective-permute-done((f32[512,512]{1,0:T(8,128)}, f32[512,512]{1,0:T(8,128)}, u32[]{:S(2)}, u32[]{:S(2)}) %collective-permute-start.3) | collective-permute-done | bytes 1048608 | tf_op jit(solution)/shard_map/ppermute | solution.py:36
  28.5 2.9 %collective-permute-done.4.refs_6_.refs_7_ = f32[512,512]{1,0:T(8,128)} collective-permute-done((f32[512,512]{1,0:T(8,128)}, f32[512,512]{1,0:T(8,128)}, u32[]{:S(2)}, u32[]{:S(2)}) %collective-permute-start.4) | collective-permute-done | bytes 1048608 | tf_op jit(solution)/shard_map/ppermute | solution.py:36
  32.8 1.8 %collective-permute-done.1.refs_2_.refs_3_ = f32[512,512]{1,0:T(8,128)S(1)} collective-permute-done((f32[512,512]{1,0:T(8,128)}, f32[512,512]{1,0:T(8,128)S(1)}, u32[]{:S(2)}, u32[]{:S(2)}) %collective-permute-start.1) | collective-permute-done | bytes 1048608 | tf_op jit(solution)/shard_map/ppermute | solution.py:39
  34.6 3.2 %collective-permute-start.5 = (f32[512,512]{1,0:T(8,128)}, f32[512,512]{1,0:T(8,128)S(1)}, u32[]{:S(2)}, u32[]{:S(2)}) collective-permute-start(f32[512,512]{1,0:T(8,128)} %collective-permute-done.2.refs_3_.refs_4_), channel_id=1, source_target_pairs={{0,32},{32,64},{64,96},{96,0},{16,112},{48,16},{80,48},{112,80},{1... | collective-permute-start | bytes 3145736 | tf_op jit(solution)/shard_map/ppermute | solution.py:39
  37.8 1.3 %collective-permute-start.7 = (f32[4,256,256]{2,1,0:T(8,128)}, f32[4,256,256]{2,1,0:T(8,128)S(1)}, u32[]{:S(2)}, u32[]{:S(2)}) collective-permute-start(f32[4,256,256]{2,1,0:T(8,128)} %send.1), channel_id=1, source_target_pairs={{0,8},{8,0},{1,9},{9,1},{2,10},{10,2},{3,11},{11,3},{4,12},{12,4},... | collective-permute-start | bytes 3145736 | tf_op jit(solution)/shard_map/ppermute | solution.py:28
  39.1 16.9 %collective-permute-done.8.refs_2_ = f32[512,512]{1,0:T(8,128)S(1)} collective-permute-done((f32[512,512]{1,0:T(8,128)}, f32[512,512]{1,0:T(8,128)S(1)}, u32[]{:S(2)}, u32[]{:S(2)}) %collective-permute-start.8) | collective-permute-done | bytes 1048608 | tf_op jit(solution)/shard_map/ppermute | solution.py:36
  56.0 1.7 %collective-permute-done.9.refs_5_.refs_6_ = f32[512,512]{1,0:T(8,128)S(1)} collective-permute-done((f32[512,512]{1,0:T(8,128)}, f32[512,512]{1,0:T(8,128)S(1)}, u32[]{:S(2)}, u32[]{:S(2)}) %collective-permute-start.9) | collective-permute-done | bytes 1048608 | tf_op jit(solution)/shard_map/ppermute | solution.py:36
  57.6 1.5 %collective-permute-start.13 = (f32[512,512]{1,0:T(8,128)S(1)}, f32[512,512]{1,0:T(8,128)S(1)}, u32[]{:S(2)}, u32[]{:S(2)}) collective-permute-start(f32[512,512]{1,0:T(8,128)S(1)} %collective-permute-done.9.refs_5_.refs_6_), channel_id=1, source_target_pairs={{0,7},{1,0},{2,1},{3,2},{4,3},{5,4},{6,5},{7,6},{16,17},{17,18},{1... | collective-permute-start | bytes 3145736 | tf_op jit(solution)/shard_map/ppermute | solution.py:36
  59.1 4.3 %collective-permute-done.6.refs_5_.refs_7_ = f32[512,512]{1,0:T(8,128)S(1)} collective-permute-done((f32[512,512]{1,0:T(8,128)}, f32[512,512]{1,0:T(8,128)S(1)}, u32[]{:S(2)}, u32[]{:S(2)}) %collective-permute-start.6) | collective-permute-done | bytes 1048608 | tf_op jit(solution)/shard_map/ppermute | solution.py:39
  63.6 2.7 %collective-permute-start.10 = (f32[512,512]{1,0:T(8,128)S(1)}, f32[512,512]{1,0:T(8,128)S(1)}, u32[]{:S(2)}, u32[]{:S(2)}) collective-permute-start(f32[512,512]{1,0:T(8,128)S(1)} %collective-permute-done.refs_1_), channel_id=1, source_target_pairs={{0,32},{32,64},{64,96},{96,0},{16,112},{48,16},{80,48},{112,80},{1... | collective-permute-start | bytes 3145736 | tf_op jit(solution)/shard_map/ppermute | solution.py:39
  66.3 1.8 %pick.1 = f32[6,256,512]{2,1,0:T(8,128)S(1)} custom-call(s32[8]{0:T(128)S(1)} %copy-done.9, f32[512,512]{1,0:T(8,128)S(1)} %copy-done, f32[512,512]{1,0:T(8,128)S(1)} %collective-permute-done.refs_1_, f32[512,512]{1,0:T(8,128)S(1)} %collective-permute-done.1.refs_2_.refs_3_, f32[512,512]{1,0:T(8,128)} %collective-permute-done.2.refs_3_.refs_4_, ...), custom_call_target="tpu_custom_call" | custom-call | flops 1048576 | bytes 262144 | tf_op jit(solution)/shard_map/pick/pallas_call | solution.py:148
  68.1 14.4 %collective-permute-done.12.refs_3_ = f32[512,512]{1,0:T(8,128)S(1)} collective-permute-done((f32[512,512]{1,0:T(8,128)S(1)}, f32[512,512]{1,0:T(8,128)S(1)}, u32[]{:S(2)}, u32[]{:S(2)}) %collective-permute-start.12) | collective-permute-done | bytes 1048608 | tf_op jit(solution)/shard_map/ppermute | solution.py:36
  83.7 2.9 %beta1.1 = f32[256,512]{1,0:T(8,128)S(1)} custom-call(s32[2]{0:T(128)S(1)} %copy-done.6, s32[3,32]{1,0:T(4,128)S(1)} %copy-done.14, f32[512,512]{1,0:T(8,128)} %refs_0_.9, f32[512,512]{1,0:T(8,128)} %collective-permute-done.3.refs_1_, f32[512,512]{1,0:T(8,128)} %copy-done.22, f32[512,512]{1,0:T(8,128)S(1)} %collective-permute-done.12.refs_3_, ...), custom_call_target="tpu_custom_call" | custom-call | flops 17179869184 | bytes 33554432 | tf_op jit(solution)/shard_map/beta1/pallas_call | solution.py:315
  86.6 1.7 %collective-permute-start.19 = (f32[256,512]{1,0:T(8,128)S(1)}, f32[256,512]{1,0:T(8,128)S(1)}, u32[]{:S(2)}, u32[]{:S(2)}) collective-permute-start(f32[256,512]{1,0:T(8,128)S(1)} %beta1.1), channel_id=1, source_target_pairs={{0,8},{8,0},{1,9},{9,1},{2,10},{10,2},{3,11},{11,3},{4,12},{12,4},... | collective-permute-start | bytes 1572872 | tf_op jit(solution)/shard_map/ppermute | solution.py:28
  89.2 2.0 %collective-permute-start.16 = (f32[512,512]{1,0:T(8,128)S(1)}, f32[512,512]{1,0:T(8,128)S(1)}, u32[]{:S(2)}, u32[]{:S(2)}) collective-permute-start(f32[512,512]{1,0:T(8,128)S(1)} %collective-permute-done.11.refs_6_), channel_id=1, source_target_pairs={{0,16},{16,0},{1,17},{17,1},{2,18},{18,2},{3,19},{19,3},{4,20},{20... | collective-permute-start | bytes 3145736 | tf_op jit(solution)/shard_map/ppermute | solution.py:28
  91.2 3.2 %beta2.1.refs_4_ = f32[256,512]{1,0:T(8,128)S(1)} custom-call(s32[2]{0:T(128)S(1)} %copy-done.6, s32[3,32]{1,0:T(4,128)S(1)} %copy-done.14, f32[512,512]{1,0:T(8,128)} %refs_0_.9, f32[512,512]{1,0:T(8,128)} %collective-permute-done.3.refs_1_, f32[512,512]{1,0:T(8,128)} %copy-done.22, f32[512,512]{1,0:T(8,128)} %copy-done.10, f32[512,512]{1,0:T(8,128)} %copy-done.11, ...), custom_call_target="tpu_custom_call" | custom-call | flops 17179869184 | bytes 33554432 | tf_op jit(solution)/shard_map/beta2/pallas_call | solution.py:315
  94.4 3.2 %collective-permute-done.18.refs_0_.refs_4_ = f32[512,512]{1,0:T(8,128)S(1)} collective-permute-done((f32[512,512]{1,0:T(8,128)S(1)}, f32[512,512]{1,0:T(8,128)S(1)}, u32[]{:S(2)}, u32[]{:S(2)}) %collective-permute-start.18) | collective-permute-done | bytes 1048608 | tf_op jit(solution)/shard_map/ppermute | solution.py:36
  97.6 2.1 %beta3.1 = f32[256,768]{1,0:T(8,128)S(1)} custom-call(s32[2]{0:T(128)S(1)} %copy-done.6, s32[3,32]{1,0:T(4,128)S(1)} %copy-done.14, f32[512,512]{1,0:T(8,128)S(1)} %collective-permute-done.18.refs_0_.refs_4_, f32[2,8,256,256]{3,2,1,0:T(8,128)} %refs_8_, f32[4,256,256]{2,1,0:T(8,128)} %copy-done.24, f32[4,256,256]{2,1,0:T(8,128)} %copy-done.12, ...), custom_call_target="tpu_custom_call" | custom-call | flops 17179869184 | bytes 33554432 | tf_op jit(solution)/shard_map/beta3/pallas_call | solution.py:315
  99.7 1.4 %collective-permute-start.20 = (f32[256,768]{1,0:T(8,128)S(1)}, f32[256,768]{1,0:T(8,128)S(1)}, u32[]{:S(2)}, u32[]{:S(2)}) collective-permute-start(f32[256,768]{1,0:T(8,128)S(1)} %beta3.1), channel_id=1, source_target_pairs={{0,8},{8,0},{1,9},{9,1},{2,10},{10,2},{3,11},{11,3},{4,12},{12,4},... | collective-permute-start | bytes 2359304 | tf_op jit(solution)/shard_map/ppermute | solution.py:28
  101.0 4.5 %beta0.1 = f32[512,512]{1,0:T(8,128)S(1)} custom-call(s32[2]{0:T(128)S(1)} %copy-done.6, s32[3,32]{1,0:T(4,128)S(1)} %copy-done.14, f32[512,512]{1,0:T(8,128)} %refs_0_.9, f32[512,512]{1,0:T(8,128)} %collective-permute-done.3.refs_1_, f32[512,512]{1,0:T(8,128)} %copy-done.22, f32[512,512]{1,0:T(8,128)} %copy-done.10, f32[512,512]{1,0:T(8,128)} %copy-done.13, ...), custom_call_target="tpu_custom_call" | custom-call | flops 17179869184 | bytes 33554432 | tf_op jit(solution)/shard_map/beta0/pallas_call | solution.py:315
  108.0 4.6 %alpha.1 = f32[512,512]{1,0:T(8,128)S(1)} custom-call(s32[1,32]{1,0:T(1,128)S(1)} %copy-done.8, f32[512,512]{1,0:T(8,128)} %refs_0_.9, f32[512,512]{1,0:T(8,128)} %copy-done.2, f32[512,512]{1,0:T(8,128)} %copy-done.16, f32[512,512]{1,0:T(8,128)} %copy-done.3, f32[512,512]{1,0:T(8,128)} %collective-permute-done.2.refs_3_.refs_4_, f32[512,512]{1,0:T(8,128)} %copy-done.4, ...), custom_call_target="tpu_custom_call" | custom-call | flops 1048576 | bytes 262144 | tf_op jit(solution)/shard_map/alpha/pallas_call | solution.py:201
  112.9 3.7 %collective-permute-done.20.rest = f32[256,768]{1,0:T(8,128)S(1)} collective-permute-done((f32[256,768]{1,0:T(8,128)S(1)}, f32[256,768]{1,0:T(8,128)S(1)}, u32[]{:S(2)}, u32[]{:S(2)}) %collective-permute-start.20) | collective-permute-done | bytes 786464 | tf_op jit(solution)/shard_map/ppermute | solution.py:28
  116.6 1.8 %last.1 = f32[512,512]{1,0:T(8,128)} custom-call(s32[2]{0:T(128)S(1)} %copy-done.6, s32[8]{0:T(128)S(1)} %copy-done.7, f32[512,512]{1,0:T(8,128)S(1)} %add_add_fusion.joined, f32[256,512]{1,0:T(8,128)S(1)} %collective-permute-done.19.top, f32[256,768]{1,0:T(8,128)S(1)} %collective-permute-done.20.rest), custom_call_target="tpu_custom_call" | custom-call | flops 1048576 | bytes 262144 | tf_op jit(solution)/shard_map/last/pallas_call | solution.py:402
  (75 shorter events, 7.1 us)
Async XLA Ops:
  0.0 66.3 %copy-start = (f32[512,512]{1,0:T(8,128)S(1)}, f32[512,512]{1,0:T(8,128)}, u32[]{:S(2)}) copy-start(f32[512,512]{1,0:T(8,128)} %refs_0_.9) | copy-start | bytes 3145732
  0.0 28.5 %collective-permute-start.3 = (f32[512,512]{1,0:T(8,128)}, f32[512,512]{1,0:T(8,128)}, u32[]{:S(2)}, u32[]{:S(2)}) collective-permute-start(f32[512,512]{1,0:T(8,128)} %refs_0_.9), channel_id=1, source_target_pairs={{0,1},{1,2},{2,3},{3,4},{4,5},{5,6},{6,7},{7,0},{16,23},{17,16},{1... | collective-permute-start | bytes 3145736 | tf_op jit(solution)/shard_map/ppermute | solution.py:36
  6.4 25.0 %collective-permute-start.4 = (f32[512,512]{1,0:T(8,128)}, f32[512,512]{1,0:T(8,128)}, u32[]{:S(2)}, u32[]{:S(2)}) collective-permute-start(f32[512,512]{1,0:T(8,128)} %refs_0_.9), channel_id=1, source_target_pairs={{0,7},{1,0},{2,1},{3,2},{4,3},{5,4},{6,5},{7,6},{16,17},{17,18},{1... | collective-permute-start | bytes 3145736 | tf_op jit(solution)/shard_map/ppermute | solution.py:36
  6.4 26.4 %collective-permute-start = (f32[512,512]{1,0:T(8,128)}, f32[512,512]{1,0:T(8,128)S(1)}, u32[]{:S(2)}, u32[]{:S(2)}) collective-permute-start(f32[512,512]{1,0:T(8,128)} %refs_0_.9), channel_id=1, source_target_pairs={{0,32},{32,64},{64,96},{96,0},{16,112},{48,16},{80,48},{112,80},{1... | collective-permute-start | bytes 3145736 | tf_op jit(solution)/shard_map/ppermute | solution.py:39
  8.9 25.7 %collective-permute-start.1 = (f32[512,512]{1,0:T(8,128)}, f32[512,512]{1,0:T(8,128)S(1)}, u32[]{:S(2)}, u32[]{:S(2)}) collective-permute-start(f32[512,512]{1,0:T(8,128)} %refs_0_.9), channel_id=1, source_target_pairs={{0,96},{32,0},{64,32},{96,64},{16,48},{48,80},{80,112},{112,16},{1... | collective-permute-start | bytes 3145736 | tf_op jit(solution)/shard_map/ppermute | solution.py:39
  8.9 25.7 %collective-permute-start.2 = (f32[512,512]{1,0:T(8,128)}, f32[512,512]{1,0:T(8,128)}, u32[]{:S(2)}, u32[]{:S(2)}) collective-permute-start(f32[512,512]{1,0:T(8,128)} %refs_0_.9), channel_id=1, source_target_pairs={{0,128},{128,0},{1,129},{129,1},{2,130},{130,2},{3,131},{131,3},{4... | collective-permute-start | bytes 3145736 | tf_op jit(solution)/shard_map/ppermute | solution.py:28
  21.3 45.0 %copy-start.9 = (s32[8]{0:T(128)S(1)}, s32[8]{0:T(128)}, u32[]{:S(2)}) copy-start(s32[8]{0:T(128)} %get-tuple-element.45.picks) | copy-start | bytes 100
  31.4 24.6 %collective-permute-start.8 = (f32[512,512]{1,0:T(8,128)}, f32[512,512]{1,0:T(8,128)S(1)}, u32[]{:S(2)}, u32[]{:S(2)}) collective-permute-start(f32[512,512]{1,0:T(8,128)} %collective-permute-done.3.refs_1_), channel_id=1, source_target_pairs={{0,1},{1,2},{2,3},{3,4},{4,5},{5,6},{6,7},{7,0},{16,23},{17,16},{1... | collective-permute-start | bytes 3145736 | tf_op jit(solution)/shard_map/ppermute | solution.py:36
  32.3 25.3 %collective-permute-start.9 = (f32[512,512]{1,0:T(8,128)}, f32[512,512]{1,0:T(8,128)S(1)}, u32[]{:S(2)}, u32[]{:S(2)}) collective-permute-start(f32[512,512]{1,0:T(8,128)} %collective-permute-done.4.refs_6_.refs_7_), channel_id=1, source_target_pairs={{0,7},{1,0},{2,1},{3,2},{4,3},{5,4},{6,5},{7,6},{16,17},{17,18},{1... | collective-permute-start | bytes 3145736 | tf_op jit(solution)/shard_map/ppermute | solution.py:36
  32.8 35.2 %copy-start.2 = (f32[512,512]{1,0:T(8,128)}, f32[512,512]{1,0:T(8,128)S(1)}, u32[]{:S(2)}) copy-start(f32[512,512]{1,0:T(8,128)S(1)} %collective-permute-done.refs_1_) | copy-start | bytes 3145732
  34.6 33.5 %copy-start.3 = (f32[512,512]{1,0:T(8,128)}, f32[512,512]{1,0:T(8,128)S(1)}, u32[]{:S(2)}) copy-start(f32[512,512]{1,0:T(8,128)S(1)} %collective-permute-done.1.refs_2_.refs_3_) | copy-start | bytes 3145732
  34.6 24.5 %collective-permute-start.5 = (f32[512,512]{1,0:T(8,128)}, f32[512,512]{1,0:T(8,128)S(1)}, u32[]{:S(2)}, u32[]{:S(2)}) collective-permute-start(f32[512,512]{1,0:T(8,128)} %collective-permute-done.2.refs_3_.refs_4_), channel_id=1, source_target_pairs={{0,32},{32,64},{64,96},{96,0},{16,112},{48,16},{80,48},{112,80},{1... | collective-permute-start | bytes 3145736 | tf_op jit(solution)/shard_map/ppermute | solution.py:39
  37.8 25.6 %collective-permute-start.6 = (f32[512,512]{1,0:T(8,128)}, f32[512,512]{1,0:T(8,128)S(1)}, u32[]{:S(2)}, u32[]{:S(2)}) collective-permute-start(f32[512,512]{1,0:T(8,128)} %collective-permute-done.2.refs_3_.refs_4_), channel_id=1, source_target_pairs={{0,96},{32,0},{64,32},{96,64},{16,48},{48,80},{80,112},{112,16},{1... | collective-permute-start | bytes 3145736 | tf_op jit(solution)/shard_map/ppermute | solution.py:39
  37.8 25.6 %collective-permute-start.7 = (f32[4,256,256]{2,1,0:T(8,128)}, f32[4,256,256]{2,1,0:T(8,128)S(1)}, u32[]{:S(2)}, u32[]{:S(2)}) collective-permute-start(f32[4,256,256]{2,1,0:T(8,128)} %send.1), channel_id=1, source_target_pairs={{0,8},{8,0},{1,9},{9,1},{2,10},{10,2},{3,11},{11,3},{4,12},{12,4},... | collective-permute-start | bytes 3145736 | tf_op jit(solution)/shard_map/ppermute | solution.py:28
  56.0 12.1 %copy-start.22 = (f32[512,512]{1,0:T(8,128)}, f32[512,512]{1,0:T(8,128)S(1)}, u32[]{:S(2)}) copy-start(f32[512,512]{1,0:T(8,128)S(1)} %collective-permute-done.8.refs_2_) | copy-start | bytes 3145732
  57.6 10.5 %copy-start.23 = (f32[512,512]{1,0:T(8,128)}, f32[512,512]{1,0:T(8,128)S(1)}, u32[]{:S(2)}) copy-start(f32[512,512]{1,0:T(8,128)S(1)} %collective-permute-done.9.refs_5_.refs_6_) | copy-start | bytes 3145732
  57.6 24.9 %collective-permute-start.12 = (f32[512,512]{1,0:T(8,128)S(1)}, f32[512,512]{1,0:T(8,128)S(1)}, u32[]{:S(2)}, u32[]{:S(2)}) collective-permute-start(f32[512,512]{1,0:T(8,128)S(1)} %collective-permute-done.8.refs_2_), channel_id=1, source_target_pairs={{0,1},{1,2},{2,3},{3,4},{4,5},{5,6},{6,7},{7,0},{16,23},{17,16},{1... | collective-permute-start | bytes 3145736 | tf_op jit(solution)/shard_map/ppermute | solution.py:36
  57.6 26.0 %collective-permute-start.13 = (f32[512,512]{1,0:T(8,128)S(1)}, f32[512,512]{1,0:T(8,128)S(1)}, u32[]{:S(2)}, u32[]{:S(2)}) collective-permute-start(f32[512,512]{1,0:T(8,128)S(1)} %collective-permute-done.9.refs_5_.refs_6_), channel_id=1, source_target_pairs={{0,7},{1,0},{2,1},{3,2},{4,3},{5,4},{6,5},{7,6},{16,17},{17,18},{1... | collective-permute-start | bytes 3145736 | tf_op jit(solution)/shard_map/ppermute | solution.py:36
  59.1 9.0 %copy-start.4 = (f32[512,512]{1,0:T(8,128)}, f32[512,512]{1,0:T(8,128)S(1)}, u32[]{:S(2)}) copy-start(f32[512,512]{1,0:T(8,128)S(1)} %collective-permute-done.5.refs_4_.refs_5_) | copy-start | bytes 3145732
  63.4 20.2 %collective-permute-start.14 = (f32[4,256,256]{2,1,0:T(8,128)S(1)}, f32[4,256,256]{2,1,0:T(8,128)S(1)}, u32[]{:S(2)}, u32[]{:S(2)}) collective-permute-start(f32[4,256,256]{2,1,0:T(8,128)S(1)} %collective-permute-done.7.refs_8_.refs_2_.refs_9_), channel_id=1, source_target_pairs={{0,16},{16,0},{1,17},{17,1},{2,18},{18,2},{3,19},{19,3},{4,20},{20... | collective-permute-start | bytes 3145736 | tf_op jit(solution)/shard_map/ppermute | solution.py:28
  63.6 24.7 %collective-permute-start.10 = (f32[512,512]{1,0:T(8,128)S(1)}, f32[512,512]{1,0:T(8,128)S(1)}, u32[]{:S(2)}, u32[]{:S(2)}) collective-permute-start(f32[512,512]{1,0:T(8,128)S(1)} %collective-permute-done.refs_1_), channel_id=1, source_target_pairs={{0,32},{32,64},{64,96},{96,0},{16,112},{48,16},{80,48},{112,80},{1... | collective-permute-start | bytes 3145736 | tf_op jit(solution)/shard_map/ppermute | solution.py:39
  66.3 23.0 %collective-permute-start.11 = (f32[512,512]{1,0:T(8,128)S(1)}, f32[512,512]{1,0:T(8,128)S(1)}, u32[]{:S(2)}, u32[]{:S(2)}) collective-permute-start(f32[512,512]{1,0:T(8,128)S(1)} %collective-permute-done.5.refs_4_.refs_5_), channel_id=1, source_target_pairs={{0,32},{32,64},{64,96},{96,0},{16,112},{48,16},{80,48},{112,80},{1... | collective-permute-start | bytes 3145736 | tf_op jit(solution)/shard_map/ppermute | solution.py:39
  66.3 17.3 %copy-start.6 = (s32[2]{0:T(128)S(1)}, s32[2]{0:T(128)}, u32[]{:S(2)}) copy-start(s32[2]{0:T(128)} %pad_add_fusion.where) | copy-start | bytes 28
  66.3 17.3 %copy-start.14 = (s32[3,32]{1,0:T(4,128)S(1)}, s32[3,32]{1,0:T(4,128)}, u32[]{:S(2)}) copy-start(s32[3,32]{1,0:T(4,128)} %get-tuple-element.43.plan) | copy-start | bytes 1156
  83.6 13.9 %collective-permute-start.18 = (f32[512,512]{1,0:T(8,128)S(1)}, f32[512,512]{1,0:T(8,128)S(1)}, u32[]{:S(2)}, u32[]{:S(2)}) collective-permute-start(f32[512,512]{1,0:T(8,128)S(1)} %collective-permute-done.12.refs_3_), channel_id=1, source_target_pairs={{0,1},{1,2},{2,3},{3,4},{4,5},{5,6},{6,7},{7,0},{16,23},{17,16},{1... | collective-permute-start | bytes 3145736 | tf_op jit(solution)/shard_map/ppermute | solution.py:36
  86.6 26.3 %collective-permute-start.19 = (f32[256,512]{1,0:T(8,128)S(1)}, f32[256,512]{1,0:T(8,128)S(1)}, u32[]{:S(2)}, u32[]{:S(2)}) collective-permute-start(f32[256,512]{1,0:T(8,128)S(1)} %beta1.1), channel_id=1, source_target_pairs={{0,8},{8,0},{1,9},{9,1},{2,10},{10,2},{3,11},{11,3},{4,12},{12,4},... | collective-permute-start | bytes 1572872 | tf_op jit(solution)/shard_map/ppermute | solution.py:28
  88.2 6.1 %copy-start.16 = (f32[512,512]{1,0:T(8,128)}, f32[512,512]{1,0:T(8,128)S(1)}, u32[]{:S(2)}) copy-start(f32[512,512]{1,0:T(8,128)S(1)} %collective-permute-done.10.refs_2_) | copy-start | bytes 3145732
  88.2 17.4 %collective-permute-start.15 = (f32[512,512]{1,0:T(8,128)S(1)}, f32[512,512]{1,0:T(8,128)S(1)}, u32[]{:S(2)}, u32[]{:S(2)}) collective-permute-start(f32[512,512]{1,0:T(8,128)S(1)} %collective-permute-done.10.refs_2_), channel_id=1, source_target_pairs={{0,16},{16,0},{1,17},{17,1},{2,18},{18,2},{3,19},{19,3},{4,20},{20... | collective-permute-start | bytes 3145736 | tf_op jit(solution)/shard_map/ppermute | solution.py:28
  89.2 16.4 %collective-permute-start.16 = (f32[512,512]{1,0:T(8,128)S(1)}, f32[512,512]{1,0:T(8,128)S(1)}, u32[]{:S(2)}, u32[]{:S(2)}) collective-permute-start(f32[512,512]{1,0:T(8,128)S(1)} %collective-permute-done.11.refs_6_), channel_id=1, source_target_pairs={{0,16},{16,0},{1,17},{17,1},{2,18},{18,2},{3,19},{19,3},{4,20},{20... | collective-permute-start | bytes 3145736 | tf_op jit(solution)/shard_map/ppermute | solution.py:28
  91.2 14.4 %collective-permute-start.17 = (f32[6,256,512]{2,1,0:T(8,128)S(1)}, f32[6,256,512]{2,1,0:T(8,128)S(1)}, u32[]{:S(2)}, u32[]{:S(2)}) collective-permute-start(f32[6,256,512]{2,1,0:T(8,128)S(1)} %pick.1), channel_id=1, source_target_pairs={{0,16},{16,0},{1,17},{17,1},{2,18},{18,2},{3,19},{19,3},{4,20},{20... | collective-permute-start | bytes 9437192 | tf_op jit(solution)/shard_map/ppermute | solution.py:28
  99.7 8.3 %copy-start.8 = (s32[1,32]{1,0:T(1,128)S(1)}, s32[1,32]{1,0:T(1,128)}, u32[]{:S(2)}) copy-start(s32[1,32]{1,0:T(1,128)} %get-tuple-element.31.plan) | copy-start | bytes 388
  99.7 16.9 %collective-permute-start.20 = (f32[256,768]{1,0:T(8,128)S(1)}, f32[256,768]{1,0:T(8,128)S(1)}, u32[]{:S(2)}, u32[]{:S(2)}) collective-permute-start(f32[256,768]{1,0:T(8,128)S(1)} %beta3.1), channel_id=1, source_target_pairs={{0,8},{8,0},{1,9},{9,1},{2,10},{10,2},{3,11},{11,3},{4,12},{12,4},... | collective-permute-start | bytes 2359304 | tf_op jit(solution)/shard_map/ppermute | solution.py:28
  (14 other events, 49.2 us)

commit v11 on v10

--- a/solution.py
+++ b/solution.py
@@ -375,9 +375,9 @@
         name="plan",
     )(where, alpha_source, alpha_live, beta_source, beta_live)
     tiles = send_call(where, sends, beta_tiles)
-    f1, b1, tiles = lax.optimization_barrier((f1, b1, tiles))
+    f1, tiles = lax.optimization_barrier((f1, tiles))
     f2, b2 = step(f1, "z"), step(b1, "z", -1)
-    uf, ub, v = lax.optimization_barrier((uf, ub, v, f1))[:3]
+    uf, ub, v = lax.optimization_barrier((uf, ub, v, f1, b1))[:3]
     vf, vb = step(v, "x"), step(v, "x", -1)
     got = swap(after(tiles, v), "ylo")
     f2, b2 = lax.optimization_barrier((f2, b2))

time: 121 us -> 120 us (level)
    ppermute x7, waiting for transfers between devices: 44.3 us -> 40.2 us  [step(): return lax.ppermute(value, ('core', axis), pairs)]
    ppermute x6, waiting for transfers between devices: 6.23 us -> 9.01 us  [step(): return lax.ppermute(value, (axis, 'core'), pairs)]
    ppermute x8, starting transfers between devices: 10.2 us -> 8.22 us  [swap(): return lax.ppermute(value, axis, [(0, 1), (1, 0)])]
    ppermute x7, starting transfers between devices: 9.34 us -> 11.3 us  [step(): return lax.ppermute(value, ('core', axis), pairs)]
    pallas_call x4, Pallas kernels: 12.7 us -> 11.2 us  [beta_call(): pl.pallas_call(functools.partial(beta_kernel, call), out_shape=jax.ShapeD...]
    ppermute x8, waiting for transfers between devices: 3.7 us -> 4.93 us  [swap(): return lax.ppermute(value, axis, [(0, 1), (1, 0)])]
where the time goes in v11:
time: 120 us; the launch traced here: 118 us
  waiting for transfers between devices  54.1 us (45%)
  starting transfers between devices  27.9 us (23%)
  Pallas kernels  26.9 us (22%)
  local copies, waits for them, and re-layouts  7.81 us (7%)
    ppermute x7, waiting for transfers between devices, step(): return lax.ppermute(value, ('core', axis), pairs)  40.2 us
    ppermute x7, starting transfers between devices, step(): return lax.ppermute(value, ('core', axis), pairs)  11.3 us
    pallas_call x4, Pallas kernels, beta_call(): pl.pallas_call(functools.partial(beta_kernel, call), out_shape=jax.ShapeD...  11.2 us
    ppermute x6, waiting for transfers between devices, step(): return lax.ppermute(value, (axis, 'core'), pairs)  9.01 us
    ppermute x6, starting transfers between devices, step(): return lax.ppermute(value, (axis, 'core'), pairs)  8.37 us
    ppermute x8, starting transfers between devices, swap(): return lax.ppermute(value, axis, [(0, 1), (1, 0)])  8.22 us
    unnamed x54, local copies, waits for them, and re-layouts  7.81 us
    pallas_call x1, Pallas kernels, alpha_call(): pl.pallas_call(alpha_kernel, out_shape=jax.ShapeDtypeStruct((n, n), jnp.f...  5.82 us
  transfers between devices with their start and end apart: 21, of which 11 were waited for; matrix products, arithmetic and copies ran while one was open for 5% of the time, Pallas kernels for 19%

profile of v11, /device:TPU:1, one launch (start us, length us, event | category | flops | bytes accessed | tf_op | source)
XLA Modules:
  0.0 118.1 jit_solution(1647961079648833849)
XLA Ops:
  0.0 6.4 %collective-permute-start.3 = (f32[512,512]{1,0:T(8,128)}, f32[512,512]{1,0:T(8,128)}, u32[]{:S(2)}, u32[]{:S(2)}) collective-permute-start(f32[512,512]{1,0:T(8,128)} %refs_0_.9), channel_id=1, source_target_pairs={{0,1},{1,2},{2,3},{3,4},{4,5},{5,6},{6,7},{7,0},{16,23},{17,16},{1... | collective-permute-start | bytes 3145736 | tf_op jit(solution)/shard_map/ppermute | solution.py:36
  6.4 2.5 %collective-permute-start = (f32[512,512]{1,0:T(8,128)}, f32[512,512]{1,0:T(8,128)S(1)}, u32[]{:S(2)}, u32[]{:S(2)}) collective-permute-start(f32[512,512]{1,0:T(8,128)} %refs_0_.9), channel_id=1, source_target_pairs={{0,32},{32,64},{64,96},{96,0},{16,112},{48,16},{80,48},{112,80},{1... | collective-permute-start | bytes 3145736 | tf_op jit(solution)/shard_map/ppermute | solution.py:39
  8.9 2.9 %collective-permute-start.2 = (f32[512,512]{1,0:T(8,128)}, f32[512,512]{1,0:T(8,128)}, u32[]{:S(2)}, u32[]{:S(2)}) collective-permute-start(f32[512,512]{1,0:T(8,128)} %refs_0_.9), channel_id=1, source_target_pairs={{0,128},{128,0},{1,129},{129,1},{2,130},{130,2},{3,131},{131,3},{4... | collective-permute-start | bytes 3145736 | tf_op jit(solution)/shard_map/ppermute | solution.py:28
  11.8 1.4 %copy.10.alpha_source = s32[32,8]{1,0:T(8,128)} copy(s32[32,8]{0,1:T(8,128)} %param.14) | data formatting | bytes 2048 | tf_op args[5]
  13.2 1.4 %copy.11.alpha_live = s32[32,8]{1,0:T(8,128)} copy(s32[32,8]{0,1:T(8,128)} %param.15) | data formatting | bytes 2048 | tf_op args[6]
  14.5 1.4 %copy.12.beta_source = s32[32,8]{1,0:T(8,128)} copy(s32[32,8]{0,1:T(8,128)} %param.16) | data formatting | bytes 2048 | tf_op args[7]
  15.9 1.4 %copy.13.beta_live = s32[32,8]{1,0:T(8,128)} copy(s32[32,8]{0,1:T(8,128)} %param.17) | data formatting | bytes 2048 | tf_op args[8]
  17.9 3.4 %plan.1 = (s32[1,32]{1,0:T(1,128)}, s32[3,32]{1,0:T(4,128)}, s32[8]{0:T(128)}, s32[8]{0:T(128)}) custom-call(s32[2]{0:T(128)} %pad_add_fusion.where, s32[32,8]{1,0:T(8,128)} %copy.10.alpha_source, s32[32,8]{1,0:T(8,128)} %copy.11.alpha_live, s32[32,8]{1,0:T(8,128)} %copy.12.beta_source, s32[32,8]{1,0:T(8,128)} %copy.13.beta_live), custom_call_target="tpu_custom_call" | custom-call | tf_op jit(solution)/shard_map/plan/pallas_call | solution.py:365
  21.3 2.9 %send.1 = f32[4,256,256]{2,1,0:T(8,128)} custom-call(s32[2]{0:T(128)} %pad_add_fusion.where, s32[8]{0:T(128)} %get-tuple-element.29.sends, f32[2,8,256,256]{3,2,1,0:T(8,128)} %refs_8_), custom_call_target="tpu_custom_call" | custom-call | flops 1048576 | bytes 262144 | tf_op jit(solution)/shard_map/send/pallas_call | solution.py:232
  24.2 4.3 %collective-permute-done.3.refs_1_ = f32[512,512]{1,0:T(8,128)} collective-permute-done((f32[512,512]{1,0:T(8,128)}, f32[512,512]{1,0:T(8,128)}, u32[]{:S(2)}, u32[]{:S(2)}) %collective-permute-start.3) | collective-permute-done | bytes 1048608 | tf_op jit(solution)/shard_map/ppermute | solution.py:36
  28.5 3.4 %collective-permute-start.8 = (f32[512,512]{1,0:T(8,128)}, f32[512,512]{1,0:T(8,128)S(1)}, u32[]{:S(2)}, u32[]{:S(2)}) collective-permute-start(f32[512,512]{1,0:T(8,128)} %collective-permute-done.3.refs_1_), channel_id=1, source_target_pairs={{0,1},{1,2},{2,3},{3,4},{4,5},{5,6},{6,7},{7,0},{16,23},{17,16},{1... | collective-permute-start | bytes 3145736 | tf_op jit(solution)/shard_map/ppermute | solution.py:36
  31.9 2.7 %collective-permute-done.1.refs_2_.refs_3_ = f32[512,512]{1,0:T(8,128)S(1)} collective-permute-done((f32[512,512]{1,0:T(8,128)}, f32[512,512]{1,0:T(8,128)S(1)}, u32[]{:S(2)}, u32[]{:S(2)}) %collective-permute-start.1) | collective-permute-done | bytes 1048608 | tf_op jit(solution)/shard_map/ppermute | solution.py:39
  34.6 3.2 %collective-permute-start.5 = (f32[512,512]{1,0:T(8,128)}, f32[512,512]{1,0:T(8,128)S(1)}, u32[]{:S(2)}, u32[]{:S(2)}) collective-permute-start(f32[512,512]{1,0:T(8,128)} %collective-permute-done.2.refs_3_.refs_4_), channel_id=1, source_target_pairs={{0,32},{32,64},{64,96},{96,0},{16,112},{48,16},{80,48},{112,80},{1... | collective-permute-start | bytes 3145736 | tf_op jit(solution)/shard_map/ppermute | solution.py:39
  37.8 1.3 %collective-permute-start.7 = (f32[4,256,256]{2,1,0:T(8,128)}, f32[4,256,256]{2,1,0:T(8,128)S(1)}, u32[]{:S(2)}, u32[]{:S(2)}) collective-permute-start(f32[4,256,256]{2,1,0:T(8,128)} %send.1), channel_id=1, source_target_pairs={{0,8},{8,0},{1,9},{9,1},{2,10},{10,2},{3,11},{11,3},{4,12},{12,4},... | collective-permute-start | bytes 3145736 | tf_op jit(solution)/shard_map/ppermute | solution.py:28
  39.1 14.0 %collective-permute-done.8.refs_2_ = f32[512,512]{1,0:T(8,128)S(1)} collective-permute-done((f32[512,512]{1,0:T(8,128)}, f32[512,512]{1,0:T(8,128)S(1)}, u32[]{:S(2)}, u32[]{:S(2)}) %collective-permute-start.8) | collective-permute-done | bytes 1048608 | tf_op jit(solution)/shard_map/ppermute | solution.py:36
  53.0 4.1 %collective-permute-done.9.refs_5_.refs_6_ = f32[512,512]{1,0:T(8,128)S(1)} collective-permute-done((f32[512,512]{1,0:T(8,128)}, f32[512,512]{1,0:T(8,128)S(1)}, u32[]{:S(2)}, u32[]{:S(2)}) %collective-permute-start.9) | collective-permute-done | bytes 1048608 | tf_op jit(solution)/shard_map/ppermute | solution.py:36
  57.1 1.5 %collective-permute-start.13 = (f32[512,512]{1,0:T(8,128)S(1)}, f32[512,512]{1,0:T(8,128)S(1)}, u32[]{:S(2)}, u32[]{:S(2)}) collective-permute-start(f32[512,512]{1,0:T(8,128)S(1)} %collective-permute-done.9.refs_5_.refs_6_), channel_id=1, source_target_pairs={{0,7},{1,0},{2,1},{3,2},{4,3},{5,4},{6,5},{7,6},{16,17},{17,18},{1... | collective-permute-start | bytes 3145736 | tf_op jit(solution)/shard_map/ppermute | solution.py:36
  59.1 4.3 %collective-permute-done.6.refs_5_.refs_7_ = f32[512,512]{1,0:T(8,128)S(1)} collective-permute-done((f32[512,512]{1,0:T(8,128)}, f32[512,512]{1,0:T(8,128)S(1)}, u32[]{:S(2)}, u32[]{:S(2)}) %collective-permute-start.6) | collective-permute-done | bytes 1048608 | tf_op jit(solution)/shard_map/ppermute | solution.py:39
  63.6 2.7 %collective-permute-start.10 = (f32[512,512]{1,0:T(8,128)S(1)}, f32[512,512]{1,0:T(8,128)S(1)}, u32[]{:S(2)}, u32[]{:S(2)}) collective-permute-start(f32[512,512]{1,0:T(8,128)S(1)} %collective-permute-done.refs_1_), channel_id=1, source_target_pairs={{0,32},{32,64},{64,96},{96,0},{16,112},{48,16},{80,48},{112,80},{1... | collective-permute-start | bytes 3145736 | tf_op jit(solution)/shard_map/ppermute | solution.py:39
  66.3 1.8 %pick.1 = f32[6,256,512]{2,1,0:T(8,128)S(1)} custom-call(s32[8]{0:T(128)S(1)} %copy-done.9, f32[512,512]{1,0:T(8,128)S(1)} %copy-done, f32[512,512]{1,0:T(8,128)S(1)} %collective-permute-done.refs_1_, f32[512,512]{1,0:T(8,128)S(1)} %collective-permute-done.1.refs_2_.refs_3_, f32[512,512]{1,0:T(8,128)} %collective-permute-done.2.refs_3_.refs_4_, ...), custom_call_target="tpu_custom_call" | custom-call | flops 1048576 | bytes 262144 | tf_op jit(solution)/shard_map/pick/pallas_call | solution.py:148
  68.1 13.8 %collective-permute-done.12.refs_3_ = f32[512,512]{1,0:T(8,128)S(1)} collective-permute-done((f32[512,512]{1,0:T(8,128)S(1)}, f32[512,512]{1,0:T(8,128)S(1)}, u32[]{:S(2)}, u32[]{:S(2)}) %collective-permute-start.12) | collective-permute-done | bytes 1048608 | tf_op jit(solution)/shard_map/ppermute | solution.py:36
  83.1 2.9 %beta1.1 = f32[256,512]{1,0:T(8,128)S(1)} custom-call(s32[2]{0:T(128)S(1)} %copy-done.6, s32[3,32]{1,0:T(4,128)S(1)} %copy-done.14, f32[512,512]{1,0:T(8,128)} %refs_0_.9, f32[512,512]{1,0:T(8,128)} %collective-permute-done.3.refs_1_, f32[512,512]{1,0:T(8,128)} %copy-done.22, f32[512,512]{1,0:T(8,128)S(1)} %collective-permute-done.12.refs_3_, ...), custom_call_target="tpu_custom_call" | custom-call | flops 17179869184 | bytes 33554432 | tf_op jit(solution)/shard_map/beta1/pallas_call | solution.py:315
  86.0 1.4 %collective-permute-start.19 = (f32[256,512]{1,0:T(8,128)S(1)}, f32[256,512]{1,0:T(8,128)S(1)}, u32[]{:S(2)}, u32[]{:S(2)}) collective-permute-start(f32[256,512]{1,0:T(8,128)S(1)} %beta1.1), channel_id=1, source_target_pairs={{0,8},{8,0},{1,9},{9,1},{2,10},{10,2},{3,11},{11,3},{4,12},{12,4},... | collective-permute-start | bytes 1572872 | tf_op jit(solution)/shard_map/ppermute | solution.py:28
  87.7 1.5 %collective-permute-done.11.refs_6_ = f32[512,512]{1,0:T(8,128)S(1)} collective-permute-done((f32[512,512]{1,0:T(8,128)S(1)}, f32[512,512]{1,0:T(8,128)S(1)}, u32[]{:S(2)}, u32[]{:S(2)}) %collective-permute-start.11) | collective-permute-done | bytes 1048608 | tf_op jit(solution)/shard_map/ppermute | solution.py:39
  89.2 2.0 %collective-permute-start.16 = (f32[512,512]{1,0:T(8,128)S(1)}, f32[512,512]{1,0:T(8,128)S(1)}, u32[]{:S(2)}, u32[]{:S(2)}) collective-permute-start(f32[512,512]{1,0:T(8,128)S(1)} %collective-permute-done.11.refs_6_), channel_id=1, source_target_pairs={{0,16},{16,0},{1,17},{17,1},{2,18},{18,2},{3,19},{19,3},{4,20},{20... | collective-permute-start | bytes 3145736 | tf_op jit(solution)/shard_map/ppermute | solution.py:28
  91.2 2.9 %beta2.1.refs_4_ = f32[256,512]{1,0:T(8,128)S(1)} custom-call(s32[2]{0:T(128)S(1)} %copy-done.6, s32[3,32]{1,0:T(4,128)S(1)} %copy-done.14, f32[512,512]{1,0:T(8,128)} %refs_0_.9, f32[512,512]{1,0:T(8,128)} %collective-permute-done.3.refs_1_, f32[512,512]{1,0:T(8,128)} %copy-done.22, f32[512,512]{1,0:T(8,128)} %copy-done.10, f32[512,512]{1,0:T(8,128)} %copy-done.11, ...), custom_call_target="tpu_custom_call" | custom-call | flops 17179869184 | bytes 33554432 | tf_op jit(solution)/shard_map/beta2/pallas_call | solution.py:315
  94.1 2.9 %collective-permute-done.18.refs_0_.refs_4_ = f32[512,512]{1,0:T(8,128)S(1)} collective-permute-done((f32[512,512]{1,0:T(8,128)S(1)}, f32[512,512]{1,0:T(8,128)S(1)}, u32[]{:S(2)}, u32[]{:S(2)}) %collective-permute-start.18) | collective-permute-done | bytes 1048608 | tf_op jit(solution)/shard_map/ppermute | solution.py:36
  97.0 2.1 %beta3.1 = f32[256,768]{1,0:T(8,128)S(1)} custom-call(s32[2]{0:T(128)S(1)} %copy-done.6, s32[3,32]{1,0:T(4,128)S(1)} %copy-done.14, f32[512,512]{1,0:T(8,128)S(1)} %collective-permute-done.18.refs_0_.refs_4_, f32[2,8,256,256]{3,2,1,0:T(8,128)} %refs_8_, f32[4,256,256]{2,1,0:T(8,128)} %copy-done.24, f32[4,256,256]{2,1,0:T(8,128)} %copy-done.12, ...), custom_call_target="tpu_custom_call" | custom-call | flops 17179869184 | bytes 33554432 | tf_op jit(solution)/shard_map/beta3/pallas_call | solution.py:315
  99.3 3.4 %beta0.1 = f32[512,512]{1,0:T(8,128)S(1)} custom-call(s32[2]{0:T(128)S(1)} %copy-done.6, s32[3,32]{1,0:T(4,128)S(1)} %copy-done.14, f32[512,512]{1,0:T(8,128)} %refs_0_.9, f32[512,512]{1,0:T(8,128)} %collective-permute-done.3.refs_1_, f32[512,512]{1,0:T(8,128)} %copy-done.22, f32[512,512]{1,0:T(8,128)} %copy-done.10, f32[512,512]{1,0:T(8,128)} %copy-done.13, ...), custom_call_target="tpu_custom_call" | custom-call | flops 17179869184 | bytes 33554432 | tf_op jit(solution)/shard_map/beta0/pallas_call | solution.py:315
  105.1 5.8 %alpha.1 = f32[512,512]{1,0:T(8,128)S(1)} custom-call(s32[1,32]{1,0:T(1,128)S(1)} %copy-done.8, f32[512,512]{1,0:T(8,128)} %refs_0_.9, f32[512,512]{1,0:T(8,128)} %copy-done.2, f32[512,512]{1,0:T(8,128)} %copy-done.16, f32[512,512]{1,0:T(8,128)} %copy-done.3, f32[512,512]{1,0:T(8,128)} %collective-permute-done.2.refs_3_.refs_4_, f32[512,512]{1,0:T(8,128)} %copy-done.4, ...), custom_call_target="tpu_custom_call" | custom-call | flops 1048576 | bytes 262144 | tf_op jit(solution)/shard_map/alpha/pallas_call | solution.py:201
  111.2 4.9 %collective-permute-done.20.rest = f32[256,768]{1,0:T(8,128)S(1)} collective-permute-done((f32[256,768]{1,0:T(8,128)S(1)}, f32[256,768]{1,0:T(8,128)S(1)}, u32[]{:S(2)}, u32[]{:S(2)}) %collective-permute-start.20) | collective-permute-done | bytes 786464 | tf_op jit(solution)/shard_map/ppermute | solution.py:28
  116.1 1.8 %last.1 = f32[512,512]{1,0:T(8,128)} custom-call(s32[2]{0:T(128)S(1)} %copy-done.6, s32[8]{0:T(128)S(1)} %copy-done.7, f32[512,512]{1,0:T(8,128)S(1)} %add_add_fusion.joined, f32[256,512]{1,0:T(8,128)S(1)} %collective-permute-done.19.top, f32[256,768]{1,0:T(8,128)S(1)} %collective-permute-done.20.rest), custom_call_target="tpu_custom_call" | custom-call | flops 1048576 | bytes 262144 | tf_op jit(solution)/shard_map/last/pallas_call | solution.py:402
  (75 shorter events, 5.6 us)
Async XLA Ops:
  0.0 66.3 %copy-start = (f32[512,512]{1,0:T(8,128)S(1)}, f32[512,512]{1,0:T(8,128)}, u32[]{:S(2)}) copy-start(f32[512,512]{1,0:T(8,128)} %refs_0_.9) | copy-start | bytes 3145732
  0.0 28.5 %collective-permute-start.3 = (f32[512,512]{1,0:T(8,128)}, f32[512,512]{1,0:T(8,128)}, u32[]{:S(2)}, u32[]{:S(2)}) collective-permute-start(f32[512,512]{1,0:T(8,128)} %refs_0_.9), channel_id=1, source_target_pairs={{0,1},{1,2},{2,3},{3,4},{4,5},{5,6},{6,7},{7,0},{16,23},{17,16},{1... | collective-permute-start | bytes 3145736 | tf_op jit(solution)/shard_map/ppermute | solution.py:36
  6.4 25.5 %collective-permute-start.4 = (f32[512,512]{1,0:T(8,128)}, f32[512,512]{1,0:T(8,128)}, u32[]{:S(2)}, u32[]{:S(2)}) collective-permute-start(f32[512,512]{1,0:T(8,128)} %refs_0_.9), channel_id=1, source_target_pairs={{0,7},{1,0},{2,1},{3,2},{4,3},{5,4},{6,5},{7,6},{16,17},{17,18},{1... | collective-permute-start | bytes 3145736 | tf_op jit(solution)/shard_map/ppermute | solution.py:36
  6.4 25.5 %collective-permute-start = (f32[512,512]{1,0:T(8,128)}, f32[512,512]{1,0:T(8,128)S(1)}, u32[]{:S(2)}, u32[]{:S(2)}) collective-permute-start(f32[512,512]{1,0:T(8,128)} %refs_0_.9), channel_id=1, source_target_pairs={{0,32},{32,64},{64,96},{96,0},{16,112},{48,16},{80,48},{112,80},{1... | collective-permute-start | bytes 3145736 | tf_op jit(solution)/shard_map/ppermute | solution.py:39
  8.9 25.7 %collective-permute-start.1 = (f32[512,512]{1,0:T(8,128)}, f32[512,512]{1,0:T(8,128)S(1)}, u32[]{:S(2)}, u32[]{:S(2)}) collective-permute-start(f32[512,512]{1,0:T(8,128)} %refs_0_.9), channel_id=1, source_target_pairs={{0,96},{32,0},{64,32},{96,64},{16,48},{48,80},{80,112},{112,16},{1... | collective-permute-start | bytes 3145736 | tf_op jit(solution)/shard_map/ppermute | solution.py:39
  8.9 25.7 %collective-permute-start.2 = (f32[512,512]{1,0:T(8,128)}, f32[512,512]{1,0:T(8,128)}, u32[]{:S(2)}, u32[]{:S(2)}) collective-permute-start(f32[512,512]{1,0:T(8,128)} %refs_0_.9), channel_id=1, source_target_pairs={{0,128},{128,0},{1,129},{129,1},{2,130},{130,2},{3,131},{131,3},{4... | collective-permute-start | bytes 3145736 | tf_op jit(solution)/shard_map/ppermute | solution.py:28
  21.3 45.0 %copy-start.9 = (s32[8]{0:T(128)S(1)}, s32[8]{0:T(128)}, u32[]{:S(2)}) copy-start(s32[8]{0:T(128)} %get-tuple-element.43.picks) | copy-start | bytes 100
  28.5 24.5 %collective-permute-start.8 = (f32[512,512]{1,0:T(8,128)}, f32[512,512]{1,0:T(8,128)S(1)}, u32[]{:S(2)}, u32[]{:S(2)}) collective-permute-start(f32[512,512]{1,0:T(8,128)} %collective-permute-done.3.refs_1_), channel_id=1, source_target_pairs={{0,1},{1,2},{2,3},{3,4},{4,5},{5,6},{6,7},{7,0},{16,23},{17,16},{1... | collective-permute-start | bytes 3145736 | tf_op jit(solution)/shard_map/ppermute | solution.py:36
  31.9 25.3 %collective-permute-start.9 = (f32[512,512]{1,0:T(8,128)}, f32[512,512]{1,0:T(8,128)S(1)}, u32[]{:S(2)}, u32[]{:S(2)}) collective-permute-start(f32[512,512]{1,0:T(8,128)} %collective-permute-done.4.refs_6_.refs_7_), channel_id=1, source_target_pairs={{0,7},{1,0},{2,1},{3,2},{4,3},{5,4},{6,5},{7,6},{16,17},{17,18},{1... | collective-permute-start | bytes 3145736 | tf_op jit(solution)/shard_map/ppermute | solution.py:36
  31.9 36.2 %copy-start.2 = (f32[512,512]{1,0:T(8,128)}, f32[512,512]{1,0:T(8,128)S(1)}, u32[]{:S(2)}) copy-start(f32[512,512]{1,0:T(8,128)S(1)} %collective-permute-done.refs_1_) | copy-start | bytes 3145732
  34.6 33.5 %copy-start.3 = (f32[512,512]{1,0:T(8,128)}, f32[512,512]{1,0:T(8,128)S(1)}, u32[]{:S(2)}) copy-start(f32[512,512]{1,0:T(8,128)S(1)} %collective-permute-done.1.refs_2_.refs_3_) | copy-start | bytes 3145732
  34.6 24.5 %collective-permute-start.5 = (f32[512,512]{1,0:T(8,128)}, f32[512,512]{1,0:T(8,128)S(1)}, u32[]{:S(2)}, u32[]{:S(2)}) collective-permute-start(f32[512,512]{1,0:T(8,128)} %collective-permute-done.2.refs_3_.refs_4_), channel_id=1, source_target_pairs={{0,32},{32,64},{64,96},{96,0},{16,112},{48,16},{80,48},{112,80},{1... | collective-permute-start | bytes 3145736 | tf_op jit(solution)/shard_map/ppermute | solution.py:39
  37.8 25.6 %collective-permute-start.6 = (f32[512,512]{1,0:T(8,128)}, f32[512,512]{1,0:T(8,128)S(1)}, u32[]{:S(2)}, u32[]{:S(2)}) collective-permute-start(f32[512,512]{1,0:T(8,128)} %collective-permute-done.2.refs_3_.refs_4_), channel_id=1, source_target_pairs={{0,96},{32,0},{64,32},{96,64},{16,48},{48,80},{80,112},{112,16},{1... | collective-permute-start | bytes 3145736 | tf_op jit(solution)/shard_map/ppermute | solution.py:39
  37.8 25.6 %collective-permute-start.7 = (f32[4,256,256]{2,1,0:T(8,128)}, f32[4,256,256]{2,1,0:T(8,128)S(1)}, u32[]{:S(2)}, u32[]{:S(2)}) collective-permute-start(f32[4,256,256]{2,1,0:T(8,128)} %send.1), channel_id=1, source_target_pairs={{0,8},{8,0},{1,9},{9,1},{2,10},{10,2},{3,11},{11,3},{4,12},{12,4},... | collective-permute-start | bytes 3145736 | tf_op jit(solution)/shard_map/ppermute | solution.py:28
  53.0 15.1 %copy-start.22 = (f32[512,512]{1,0:T(8,128)}, f32[512,512]{1,0:T(8,128)S(1)}, u32[]{:S(2)}) copy-start(f32[512,512]{1,0:T(8,128)S(1)} %collective-permute-done.8.refs_2_) | copy-start | bytes 3145732
  57.1 11.0 %copy-start.23 = (f32[512,512]{1,0:T(8,128)}, f32[512,512]{1,0:T(8,128)S(1)}, u32[]{:S(2)}) copy-start(f32[512,512]{1,0:T(8,128)S(1)} %collective-permute-done.9.refs_5_.refs_6_) | copy-start | bytes 3145732
  57.1 24.8 %collective-permute-start.12 = (f32[512,512]{1,0:T(8,128)S(1)}, f32[512,512]{1,0:T(8,128)S(1)}, u32[]{:S(2)}, u32[]{:S(2)}) collective-permute-start(f32[512,512]{1,0:T(8,128)S(1)} %collective-permute-done.8.refs_2_), channel_id=1, source_target_pairs={{0,1},{1,2},{2,3},{3,4},{4,5},{5,6},{6,7},{7,0},{16,23},{17,16},{1... | collective-permute-start | bytes 3145736 | tf_op jit(solution)/shard_map/ppermute | solution.py:36
  57.1 25.9 %collective-permute-start.13 = (f32[512,512]{1,0:T(8,128)S(1)}, f32[512,512]{1,0:T(8,128)S(1)}, u32[]{:S(2)}, u32[]{:S(2)}) collective-permute-start(f32[512,512]{1,0:T(8,128)S(1)} %collective-permute-done.9.refs_5_.refs_6_), channel_id=1, source_target_pairs={{0,7},{1,0},{2,1},{3,2},{4,3},{5,4},{6,5},{7,6},{16,17},{17,18},{1... | collective-permute-start | bytes 3145736 | tf_op jit(solution)/shard_map/ppermute | solution.py:36
  59.1 9.0 %copy-start.4 = (f32[512,512]{1,0:T(8,128)}, f32[512,512]{1,0:T(8,128)S(1)}, u32[]{:S(2)}) copy-start(f32[512,512]{1,0:T(8,128)S(1)} %collective-permute-done.5.refs_4_.refs_5_) | copy-start | bytes 3145732
  63.4 19.7 %collective-permute-start.14 = (f32[4,256,256]{2,1,0:T(8,128)S(1)}, f32[4,256,256]{2,1,0:T(8,128)S(1)}, u32[]{:S(2)}, u32[]{:S(2)}) collective-permute-start(f32[4,256,256]{2,1,0:T(8,128)S(1)} %collective-permute-done.7.refs_8_.refs_2_.refs_9_), channel_id=1, source_target_pairs={{0,16},{16,0},{1,17},{17,1},{2,18},{18,2},{3,19},{19,3},{4,20},{20... | collective-permute-start | bytes 3145736 | tf_op jit(solution)/shard_map/ppermute | solution.py:28
  63.6 23.8 %collective-permute-start.10 = (f32[512,512]{1,0:T(8,128)S(1)}, f32[512,512]{1,0:T(8,128)S(1)}, u32[]{:S(2)}, u32[]{:S(2)}) collective-permute-start(f32[512,512]{1,0:T(8,128)S(1)} %collective-permute-done.refs_1_), channel_id=1, source_target_pairs={{0,32},{32,64},{64,96},{96,0},{16,112},{48,16},{80,48},{112,80},{1... | collective-permute-start | bytes 3145736 | tf_op jit(solution)/shard_map/ppermute | solution.py:39
  66.3 23.0 %collective-permute-start.11 = (f32[512,512]{1,0:T(8,128)S(1)}, f32[512,512]{1,0:T(8,128)S(1)}, u32[]{:S(2)}, u32[]{:S(2)}) collective-permute-start(f32[512,512]{1,0:T(8,128)S(1)} %collective-permute-done.5.refs_4_.refs_5_), channel_id=1, source_target_pairs={{0,32},{32,64},{64,96},{96,0},{16,112},{48,16},{80,48},{112,80},{1... | collective-permute-start | bytes 3145736 | tf_op jit(solution)/shard_map/ppermute | solution.py:39
  66.3 16.8 %copy-start.6 = (s32[2]{0:T(128)S(1)}, s32[2]{0:T(128)}, u32[]{:S(2)}) copy-start(s32[2]{0:T(128)} %pad_add_fusion.where) | copy-start | bytes 28
  66.3 16.8 %copy-start.14 = (s32[3,32]{1,0:T(4,128)S(1)}, s32[3,32]{1,0:T(4,128)}, u32[]{:S(2)}) copy-start(s32[3,32]{1,0:T(4,128)} %get-tuple-element.41.plan) | copy-start | bytes 1156
  83.1 13.9 %collective-permute-start.18 = (f32[512,512]{1,0:T(8,128)S(1)}, f32[512,512]{1,0:T(8,128)S(1)}, u32[]{:S(2)}, u32[]{:S(2)}) collective-permute-start(f32[512,512]{1,0:T(8,128)S(1)} %collective-permute-done.12.refs_3_), channel_id=1, source_target_pairs={{0,1},{1,2},{2,3},{3,4},{4,5},{5,6},{6,7},{7,0},{16,23},{17,16},{1... | collective-permute-start | bytes 3145736 | tf_op jit(solution)/shard_map/ppermute | solution.py:36
  86.0 25.1 %collective-permute-start.19 = (f32[256,512]{1,0:T(8,128)S(1)}, f32[256,512]{1,0:T(8,128)S(1)}, u32[]{:S(2)}, u32[]{:S(2)}) collective-permute-start(f32[256,512]{1,0:T(8,128)S(1)} %beta1.1), channel_id=1, source_target_pairs={{0,8},{8,0},{1,9},{9,1},{2,10},{10,2},{3,11},{11,3},{4,12},{12,4},... | collective-permute-start | bytes 1572872 | tf_op jit(solution)/shard_map/ppermute | solution.py:28
  87.4 6.7 %copy-start.16 = (f32[512,512]{1,0:T(8,128)}, f32[512,512]{1,0:T(8,128)S(1)}, u32[]{:S(2)}) copy-start(f32[512,512]{1,0:T(8,128)S(1)} %collective-permute-done.10.refs_2_) | copy-start | bytes 3145732
  87.4 15.3 %collective-permute-start.15 = (f32[512,512]{1,0:T(8,128)S(1)}, f32[512,512]{1,0:T(8,128)S(1)}, u32[]{:S(2)}, u32[]{:S(2)}) collective-permute-start(f32[512,512]{1,0:T(8,128)S(1)} %collective-permute-done.10.refs_2_), channel_id=1, source_target_pairs={{0,16},{16,0},{1,17},{17,1},{2,18},{18,2},{3,19},{19,3},{4,20},{20... | collective-permute-start | bytes 3145736 | tf_op jit(solution)/shard_map/ppermute | solution.py:28
  89.2 13.5 %collective-permute-start.16 = (f32[512,512]{1,0:T(8,128)S(1)}, f32[512,512]{1,0:T(8,128)S(1)}, u32[]{:S(2)}, u32[]{:S(2)}) collective-permute-start(f32[512,512]{1,0:T(8,128)S(1)} %collective-permute-done.11.refs_6_), channel_id=1, source_target_pairs={{0,16},{16,0},{1,17},{17,1},{2,18},{18,2},{3,19},{19,3},{4,20},{20... | collective-permute-start | bytes 3145736 | tf_op jit(solution)/shard_map/ppermute | solution.py:28
  91.2 11.6 %collective-permute-start.17 = (f32[6,256,512]{2,1,0:T(8,128)S(1)}, f32[6,256,512]{2,1,0:T(8,128)S(1)}, u32[]{:S(2)}, u32[]{:S(2)}) collective-permute-start(f32[6,256,512]{2,1,0:T(8,128)S(1)} %pick.1), channel_id=1, source_target_pairs={{0,16},{16,0},{1,17},{17,1},{2,18},{18,2},{3,19},{19,3},{4,20},{20... | collective-permute-start | bytes 9437192 | tf_op jit(solution)/shard_map/ppermute | solution.py:28
  99.1 6.0 %copy-start.8 = (s32[1,32]{1,0:T(1,128)S(1)}, s32[1,32]{1,0:T(1,128)}, u32[]{:S(2)}) copy-start(s32[1,32]{1,0:T(1,128)} %get-tuple-element.30.plan) | copy-start | bytes 388
  99.1 17.0 %collective-permute-start.20 = (f32[256,768]{1,0:T(8,128)S(1)}, f32[256,768]{1,0:T(8,128)S(1)}, u32[]{:S(2)}, u32[]{:S(2)}) collective-permute-start(f32[256,768]{1,0:T(8,128)S(1)} %beta3.1), channel_id=1, source_target_pairs={{0,8},{8,0},{1,9},{9,1},{2,10},{10,2},{3,11},{11,3},{4,12},{12,4},... | collective-permute-start | bytes 2359304 | tf_op jit(solution)/shard_map/ppermute | solution.py:28
  (14 other events, 53.7 us)

commit v12 on v11

--- a/solution.py
+++ b/solution.py
@@ -330,20 +330,12 @@
     )(where, plan, *pieces, *fixed, *before)
 
 
-def last_kernel(where, sends, joined, top, rest, out, top_here, rest_here, sems):
+def last_kernel(where, sends, joined, top, rest, out):
     half, n = top.shape
-    copies = [
-        pltpu.make_async_copy(source, target, sems.at[i])
-        for i, (source, target) in enumerate(((joined, out), (top, top_here), (rest, rest_here)))
-    ]
-    for copy in copies:
-        copy.start()
     block = sends[(where[1] + 4) & 7] >> 3
-    for copy in copies:
-        copy.wait()
-    out[:half] += top_here[...]
-    out[half:] += rest_here[:, :n]
-    out[:half, pl.ds(pl.multiple_of(block * BS, BS), BS)] += rest_here[:, n:]
+    out[half:] = joined[half:] + rest[:, :n]
+    out[:half] = joined[:half] + top[...]
+    out[:half, pl.ds(pl.multiple_of(block * BS, BS), BS)] += rest[:, n:]
 
 
 def per_device(
@@ -399,20 +391,19 @@
     alpha = alpha_call(alpha_plan, pieces, us2, vs2, picked, after(alpha_tiles, rest))
     beta_own = beta_call(0, where, beta_plan, held, after(beta_tiles, rest), got, other)
     joined = (diag_alpha[:, None] + diag_beta[None, :]) * coeffs + alpha + beta_own
+    parts = [
+        pltpu.with_memory_space_constraint(part, pltpu.VMEM)
+        for part in (lax.optimization_barrier(joined), top_other, rest_other)
+    ]
     return pl.pallas_call(
         last_kernel,
         out_shape=jax.ShapeDtypeStruct((n, n), jnp.float32),
-        in_specs=[SMEM] * 2 + [ANY] * 3,
+        in_specs=[SMEM] * 2 + [VMEM] * 3,
         out_specs=VMEM,
-        scratch_shapes=[
-            pltpu.VMEM(top_other.shape, jnp.float32),
-            pltpu.VMEM(rest_other.shape, jnp.float32),
-            pltpu.SemaphoreType.DMA((3,)),
-        ],
         compiler_params=pltpu.CompilerParams(vmem_limit_bytes=8 * MIB),
         cost_estimate=SMALL,
         name="last",
-    )(where, sends, lax.optimization_barrier(joined), top_other, rest_other)
+    )(where, sends, *parts)
 
 
 def solution(mesh):

time: 120 us -> 119 us (level)
  starting transfers between devices: 27.9 us -> 31.1 us
  Pallas kernels: 26.9 us -> 24 us
    ppermute x8, starting transfers between devices: 8.22 us -> 11.4 us  [swap(): return lax.ppermute(value, axis, [(0, 1), (1, 0)])]
    pallas_call x4, Pallas kernels: 11.2 us -> 8.08 us  [beta_call(): pl.pallas_call(functools.partial(beta_kernel, call), out_shape=jax.ShapeD...]
  transfers between devices with their start and end apart: 21 -> 21, of which waited for: 11 -> 11; matrix products, arithmetic and copies ran while one was open for 5% -> 5% of each run, Pallas kernels for 19% -> 16%
where the time goes in v12:
time: 119 us; the launch traced here: 118 us
  waiting for transfers between devices  53.4 us (45%)
  starting transfers between devices  31.1 us (26%)
  Pallas kernels  24 us (20%)
  local copies, waits for them, and re-layouts  8.15 us (7%)
    ppermute x7, waiting for transfers between devices, step(): return lax.ppermute(value, ('core', axis), pairs)  40.7 us
    ppermute x8, starting transfers between devices, swap(): return lax.ppermute(value, axis, [(0, 1), (1, 0)])  11.4 us
    ppermute x7, starting transfers between devices, step(): return lax.ppermute(value, ('core', axis), pairs)  11.3 us
    ppermute x6, waiting for transfers between devices, step(): return lax.ppermute(value, (axis, 'core'), pairs)  8.83 us
    ppermute x6, starting transfers between devices, step(): return lax.ppermute(value, (axis, 'core'), pairs)  8.37 us
    unnamed x54, local copies, waits for them, and re-layouts  8.15 us
    pallas_call x4, Pallas kernels, beta_call(): pl.pallas_call(functools.partial(beta_kernel, call), out_shape=jax.ShapeD...  8.08 us
    pallas_call x1, Pallas kernels, alpha_call(): pl.pallas_call(alpha_kernel, out_shape=jax.ShapeDtypeStruct((n, n), jnp.f...  6.19 us
  transfers between devices with their start and end apart: 21, of which 11 were waited for; matrix products, arithmetic and copies ran while one was open for 5% of the time, Pallas kernels for 16%

profile of v12, /device:TPU:1, one launch (start us, length us, event | category | flops | bytes accessed | tf_op | source)
XLA Modules:
  0.0 117.9 jit_solution(6772768648541753091)
XLA Ops:
  0.0 6.4 %collective-permute-start.3 = (f32[512,512]{1,0:T(8,128)}, f32[512,512]{1,0:T(8,128)}, u32[]{:S(2)}, u32[]{:S(2)}) collective-permute-start(f32[512,512]{1,0:T(8,128)} %refs_0_.9), channel_id=1, source_target_pairs={{0,1},{1,2},{2,3},{3,4},{4,5},{5,6},{6,7},{7,0},{16,23},{17,16},{1... | collective-permute-start | bytes 3145736 | tf_op jit(solution)/shard_map/ppermute | solution.py:36
  6.4 2.5 %collective-permute-start = (f32[512,512]{1,0:T(8,128)}, f32[512,512]{1,0:T(8,128)S(1)}, u32[]{:S(2)}, u32[]{:S(2)}) collective-permute-start(f32[512,512]{1,0:T(8,128)} %refs_0_.9), channel_id=1, source_target_pairs={{0,32},{32,64},{64,96},{96,0},{16,112},{48,16},{80,48},{112,80},{1... | collective-permute-start | bytes 3145736 | tf_op jit(solution)/shard_map/ppermute | solution.py:39
  8.9 2.9 %collective-permute-start.2 = (f32[512,512]{1,0:T(8,128)}, f32[512,512]{1,0:T(8,128)}, u32[]{:S(2)}, u32[]{:S(2)}) collective-permute-start(f32[512,512]{1,0:T(8,128)} %refs_0_.9), channel_id=1, source_target_pairs={{0,128},{128,0},{1,129},{129,1},{2,130},{130,2},{3,131},{131,3},{4... | collective-permute-start | bytes 3145736 | tf_op jit(solution)/shard_map/ppermute | solution.py:28
  11.8 1.4 %copy.10.alpha_source = s32[32,8]{1,0:T(8,128)} copy(s32[32,8]{0,1:T(8,128)} %param.14) | data formatting | bytes 2048 | tf_op args[5]
  13.2 1.4 %copy.11.alpha_live = s32[32,8]{1,0:T(8,128)} copy(s32[32,8]{0,1:T(8,128)} %param.15) | data formatting | bytes 2048 | tf_op args[6]
  14.5 1.4 %copy.12.beta_source = s32[32,8]{1,0:T(8,128)} copy(s32[32,8]{0,1:T(8,128)} %param.16) | data formatting | bytes 2048 | tf_op args[7]
  15.9 1.4 %copy.13.beta_live = s32[32,8]{1,0:T(8,128)} copy(s32[32,8]{0,1:T(8,128)} %param.17) | data formatting | bytes 2048 | tf_op args[8]
  17.9 3.4 %plan.1 = (s32[1,32]{1,0:T(1,128)}, s32[3,32]{1,0:T(4,128)}, s32[8]{0:T(128)}, s32[8]{0:T(128)}) custom-call(s32[2]{0:T(128)} %pad_add_fusion.where, s32[32,8]{1,0:T(8,128)} %copy.10.alpha_source, s32[32,8]{1,0:T(8,128)} %copy.11.alpha_live, s32[32,8]{1,0:T(8,128)} %copy.12.beta_source, s32[32,8]{1,0:T(8,128)} %copy.13.beta_live), custom_call_target="tpu_custom_call" | custom-call | tf_op jit(solution)/shard_map/plan/pallas_call | solution.py:357
  21.3 2.9 %send.1 = f32[4,256,256]{2,1,0:T(8,128)} custom-call(s32[2]{0:T(128)} %pad_add_fusion.where, s32[8]{0:T(128)} %get-tuple-element.29.sends, f32[2,8,256,256]{3,2,1,0:T(8,128)} %refs_8_), custom_call_target="tpu_custom_call" | custom-call | flops 1048576 | bytes 262144 | tf_op jit(solution)/shard_map/send/pallas_call | solution.py:232
  24.2 4.3 %collective-permute-done.3.refs_1_ = f32[512,512]{1,0:T(8,128)} collective-permute-done((f32[512,512]{1,0:T(8,128)}, f32[512,512]{1,0:T(8,128)}, u32[]{:S(2)}, u32[]{:S(2)}) %collective-permute-start.3) | collective-permute-done | bytes 1048608 | tf_op jit(solution)/shard_map/ppermute | solution.py:36
  28.5 3.4 %collective-permute-start.8 = (f32[512,512]{1,0:T(8,128)}, f32[512,512]{1,0:T(8,128)S(1)}, u32[]{:S(2)}, u32[]{:S(2)}) collective-permute-start(f32[512,512]{1,0:T(8,128)} %collective-permute-done.3.refs_1_), channel_id=1, source_target_pairs={{0,1},{1,2},{2,3},{3,4},{4,5},{5,6},{6,7},{7,0},{16,23},{17,16},{1... | collective-permute-start | bytes 3145736 | tf_op jit(solution)/shard_map/ppermute | solution.py:36
  31.9 2.7 %collective-permute-done.1.refs_2_.refs_3_ = f32[512,512]{1,0:T(8,128)S(1)} collective-permute-done((f32[512,512]{1,0:T(8,128)}, f32[512,512]{1,0:T(8,128)S(1)}, u32[]{:S(2)}, u32[]{:S(2)}) %collective-permute-start.1) | collective-permute-done | bytes 1048608 | tf_op jit(solution)/shard_map/ppermute | solution.py:39
  34.6 3.2 %collective-permute-start.5 = (f32[512,512]{1,0:T(8,128)}, f32[512,512]{1,0:T(8,128)S(1)}, u32[]{:S(2)}, u32[]{:S(2)}) collective-permute-start(f32[512,512]{1,0:T(8,128)} %collective-permute-done.2.refs_3_.refs_4_), channel_id=1, source_target_pairs={{0,32},{32,64},{64,96},{96,0},{16,112},{48,16},{80,48},{112,80},{1... | collective-permute-start | bytes 3145736 | tf_op jit(solution)/shard_map/ppermute | solution.py:39
  37.8 1.3 %collective-permute-start.7 = (f32[4,256,256]{2,1,0:T(8,128)}, f32[4,256,256]{2,1,0:T(8,128)S(1)}, u32[]{:S(2)}, u32[]{:S(2)}) collective-permute-start(f32[4,256,256]{2,1,0:T(8,128)} %send.1), channel_id=1, source_target_pairs={{0,8},{8,0},{1,9},{9,1},{2,10},{10,2},{3,11},{11,3},{4,12},{12,4},... | collective-permute-start | bytes 3145736 | tf_op jit(solution)/shard_map/ppermute | solution.py:28
  39.1 14.0 %collective-permute-done.8.refs_2_ = f32[512,512]{1,0:T(8,128)S(1)} collective-permute-done((f32[512,512]{1,0:T(8,128)}, f32[512,512]{1,0:T(8,128)S(1)}, u32[]{:S(2)}, u32[]{:S(2)}) %collective-permute-start.8) | collective-permute-done | bytes 1048608 | tf_op jit(solution)/shard_map/ppermute | solution.py:36
  53.0 4.1 %collective-permute-done.9.refs_5_.refs_6_ = f32[512,512]{1,0:T(8,128)S(1)} collective-permute-done((f32[512,512]{1,0:T(8,128)}, f32[512,512]{1,0:T(8,128)S(1)}, u32[]{:S(2)}, u32[]{:S(2)}) %collective-permute-start.9) | collective-permute-done | bytes 1048608 | tf_op jit(solution)/shard_map/ppermute | solution.py:36
  57.1 1.5 %collective-permute-start.13 = (f32[512,512]{1,0:T(8,128)S(1)}, f32[512,512]{1,0:T(8,128)S(1)}, u32[]{:S(2)}, u32[]{:S(2)}) collective-permute-start(f32[512,512]{1,0:T(8,128)S(1)} %collective-permute-done.9.refs_5_.refs_6_), channel_id=1, source_target_pairs={{0,7},{1,0},{2,1},{3,2},{4,3},{5,4},{6,5},{7,6},{16,17},{17,18},{1... | collective-permute-start | bytes 3145736 | tf_op jit(solution)/shard_map/ppermute | solution.py:36
  59.1 4.3 %collective-permute-done.6.refs_5_.refs_7_ = f32[512,512]{1,0:T(8,128)S(1)} collective-permute-done((f32[512,512]{1,0:T(8,128)}, f32[512,512]{1,0:T(8,128)S(1)}, u32[]{:S(2)}, u32[]{:S(2)}) %collective-permute-start.6) | collective-permute-done | bytes 1048608 | tf_op jit(solution)/shard_map/ppermute | solution.py:39
  63.6 2.7 %collective-permute-start.10 = (f32[512,512]{1,0:T(8,128)S(1)}, f32[512,512]{1,0:T(8,128)S(1)}, u32[]{:S(2)}, u32[]{:S(2)}) collective-permute-start(f32[512,512]{1,0:T(8,128)S(1)} %collective-permute-done.refs_1_), channel_id=1, source_target_pairs={{0,32},{32,64},{64,96},{96,0},{16,112},{48,16},{80,48},{112,80},{1... | collective-permute-start | bytes 3145736 | tf_op jit(solution)/shard_map/ppermute | solution.py:39
  66.3 1.8 %pick.1 = f32[6,256,512]{2,1,0:T(8,128)S(1)} custom-call(s32[8]{0:T(128)S(1)} %copy-done.9, f32[512,512]{1,0:T(8,128)S(1)} %copy-done, f32[512,512]{1,0:T(8,128)S(1)} %collective-permute-done.refs_1_, f32[512,512]{1,0:T(8,128)S(1)} %collective-permute-done.1.refs_2_.refs_3_, f32[512,512]{1,0:T(8,128)} %collective-permute-done.2.refs_3_.refs_4_, ...), custom_call_target="tpu_custom_call" | custom-call | flops 1048576 | bytes 262144 | tf_op jit(solution)/shard_map/pick/pallas_call | solution.py:148
  68.1 13.8 %collective-permute-done.12.refs_3_ = f32[512,512]{1,0:T(8,128)S(1)} collective-permute-done((f32[512,512]{1,0:T(8,128)S(1)}, f32[512,512]{1,0:T(8,128)S(1)}, u32[]{:S(2)}, u32[]{:S(2)}) %collective-permute-start.12) | collective-permute-done | bytes 1048608 | tf_op jit(solution)/shard_map/ppermute | solution.py:36
  83.1 2.1 %beta1.1 = f32[256,512]{1,0:T(8,128)S(1)} custom-call(s32[2]{0:T(128)S(1)} %copy-done.6, s32[3,32]{1,0:T(4,128)S(1)} %copy-done.14, f32[512,512]{1,0:T(8,128)} %refs_0_.9, f32[512,512]{1,0:T(8,128)} %collective-permute-done.3.refs_1_, f32[512,512]{1,0:T(8,128)} %copy-done.22, f32[512,512]{1,0:T(8,128)S(1)} %collective-permute-done.12.refs_3_, ...), custom_call_target="tpu_custom_call" | custom-call | flops 17179869184 | bytes 33554432 | tf_op jit(solution)/shard_map/beta1/pallas_call | solution.py:315
  85.3 1.9 %collective-permute-start.19 = (f32[256,512]{1,0:T(8,128)S(1)}, f32[256,512]{1,0:T(8,128)S(1)}, u32[]{:S(2)}, u32[]{:S(2)}) collective-permute-start(f32[256,512]{1,0:T(8,128)S(1)} %beta1.1), channel_id=1, source_target_pairs={{0,8},{8,0},{1,9},{9,1},{2,10},{10,2},{3,11},{11,3},{4,12},{12,4},... | collective-permute-start | bytes 1572872 | tf_op jit(solution)/shard_map/ppermute | solution.py:28
  87.9 1.4 %collective-permute-done.11.refs_6_ = f32[512,512]{1,0:T(8,128)S(1)} collective-permute-done((f32[512,512]{1,0:T(8,128)S(1)}, f32[512,512]{1,0:T(8,128)S(1)}, u32[]{:S(2)}, u32[]{:S(2)}) %collective-permute-start.11) | collective-permute-done | bytes 1048608 | tf_op jit(solution)/shard_map/ppermute | solution.py:39
  89.2 2.0 %collective-permute-start.16 = (f32[512,512]{1,0:T(8,128)S(1)}, f32[512,512]{1,0:T(8,128)S(1)}, u32[]{:S(2)}, u32[]{:S(2)}) collective-permute-start(f32[512,512]{1,0:T(8,128)S(1)} %collective-permute-done.11.refs_6_), channel_id=1, source_target_pairs={{0,16},{16,0},{1,17},{17,1},{2,18},{18,2},{3,19},{19,3},{4,20},{20... | collective-permute-start | bytes 3145736 | tf_op jit(solution)/shard_map/ppermute | solution.py:28
  91.2 2.3 %beta2.1.refs_4_ = f32[256,512]{1,0:T(8,128)S(1)} custom-call(s32[2]{0:T(128)S(1)} %copy-done.6, s32[3,32]{1,0:T(4,128)S(1)} %copy-done.14, f32[512,512]{1,0:T(8,128)} %refs_0_.9, f32[512,512]{1,0:T(8,128)} %collective-permute-done.3.refs_1_, f32[512,512]{1,0:T(8,128)} %copy-done.22, f32[512,512]{1,0:T(8,128)} %copy-done.10, f32[512,512]{1,0:T(8,128)} %copy-done.11, ...), custom_call_target="tpu_custom_call" | custom-call | flops 17179869184 | bytes 33554432 | tf_op jit(solution)/shard_map/beta2/pallas_call | solution.py:315
  93.5 3.5 %collective-permute-done.18.refs_0_.refs_4_ = f32[512,512]{1,0:T(8,128)S(1)} collective-permute-done((f32[512,512]{1,0:T(8,128)S(1)}, f32[512,512]{1,0:T(8,128)S(1)}, u32[]{:S(2)}, u32[]{:S(2)}) %collective-permute-start.18) | collective-permute-done | bytes 1048608 | tf_op jit(solution)/shard_map/ppermute | solution.py:36
  98.0 2.5 %collective-permute-start.20 = (f32[256,768]{1,0:T(8,128)S(1)}, f32[256,768]{1,0:T(8,128)S(1)}, u32[]{:S(2)}, u32[]{:S(2)}) collective-permute-start(f32[256,768]{1,0:T(8,128)S(1)} %beta3.1), channel_id=1, source_target_pairs={{0,8},{8,0},{1,9},{9,1},{2,10},{10,2},{3,11},{11,3},{4,12},{12,4},... | collective-permute-start | bytes 2359304 | tf_op jit(solution)/shard_map/ppermute | solution.py:28
  100.5 3.0 %beta0.1 = f32[512,512]{1,0:T(8,128)S(1)} custom-call(s32[2]{0:T(128)S(1)} %copy-done.6, s32[3,32]{1,0:T(4,128)S(1)} %copy-done.14, f32[512,512]{1,0:T(8,128)} %refs_0_.9, f32[512,512]{1,0:T(8,128)} %collective-permute-done.3.refs_1_, f32[512,512]{1,0:T(8,128)} %copy-done.22, f32[512,512]{1,0:T(8,128)} %copy-done.10, f32[512,512]{1,0:T(8,128)} %copy-done.13, ...), custom_call_target="tpu_custom_call" | custom-call | flops 17179869184 | bytes 33554432 | tf_op jit(solution)/shard_map/beta0/pallas_call | solution.py:315
  105.9 6.2 %alpha.1 = f32[512,512]{1,0:T(8,128)S(1)} custom-call(s32[1,32]{1,0:T(1,128)S(1)} %copy-done.8, f32[512,512]{1,0:T(8,128)} %refs_0_.9, f32[512,512]{1,0:T(8,128)} %copy-done.2, f32[512,512]{1,0:T(8,128)} %copy-done.16, f32[512,512]{1,0:T(8,128)} %copy-done.3, f32[512,512]{1,0:T(8,128)} %collective-permute-done.2.refs_3_.refs_4_, f32[512,512]{1,0:T(8,128)} %copy-done.4, ...), custom_call_target="tpu_custom_call" | custom-call | flops 1048576 | bytes 262144 | tf_op jit(solution)/shard_map/alpha/pallas_call | solution.py:201
  112.3 3.9 %collective-permute-done.20.rest = f32[256,768]{1,0:T(8,128)S(1)} collective-permute-done((f32[256,768]{1,0:T(8,128)S(1)}, f32[256,768]{1,0:T(8,128)S(1)}, u32[]{:S(2)}, u32[]{:S(2)}) %collective-permute-start.20) | collective-permute-done | bytes 786464 | tf_op jit(solution)/shard_map/ppermute | solution.py:28
  116.2 1.6 %last.1 = f32[512,512]{1,0:T(8,128)} custom-call(s32[2]{0:T(128)S(1)} %copy-done.6, s32[8]{0:T(128)S(1)} %copy-done.7, f32[512,512]{1,0:T(8,128)S(1)} %add_add_fusion.joined, f32[256,512]{1,0:T(8,128)S(1)} %collective-permute-done.19.top, f32[256,768]{1,0:T(8,128)S(1)} %collective-permute-done.20.rest), custom_call_target="tpu_custom_call" | custom-call | flops 1048576 | bytes 262144 | tf_op jit(solution)/shard_map/last/pallas_call | solution.py:398
  (75 shorter events, 6.9 us)
Async XLA Ops:
  0.0 66.3 %copy-start = (f32[512,512]{1,0:T(8,128)S(1)}, f32[512,512]{1,0:T(8,128)}, u32[]{:S(2)}) copy-start(f32[512,512]{1,0:T(8,128)} %refs_0_.9) | copy-start | bytes 3145732
  0.0 28.5 %collective-permute-start.3 = (f32[512,512]{1,0:T(8,128)}, f32[512,512]{1,0:T(8,128)}, u32[]{:S(2)}, u32[]{:S(2)}) collective-permute-start(f32[512,512]{1,0:T(8,128)} %refs_0_.9), channel_id=1, source_target_pairs={{0,1},{1,2},{2,3},{3,4},{4,5},{5,6},{6,7},{7,0},{16,23},{17,16},{1... | collective-permute-start | bytes 3145736 | tf_op jit(solution)/shard_map/ppermute | solution.py:36
  6.4 25.5 %collective-permute-start.4 = (f32[512,512]{1,0:T(8,128)}, f32[512,512]{1,0:T(8,128)}, u32[]{:S(2)}, u32[]{:S(2)}) collective-permute-start(f32[512,512]{1,0:T(8,128)} %refs_0_.9), channel_id=1, source_target_pairs={{0,7},{1,0},{2,1},{3,2},{4,3},{5,4},{6,5},{7,6},{16,17},{17,18},{1... | collective-permute-start | bytes 3145736 | tf_op jit(solution)/shard_map/ppermute | solution.py:36
  6.4 25.5 %collective-permute-start = (f32[512,512]{1,0:T(8,128)}, f32[512,512]{1,0:T(8,128)S(1)}, u32[]{:S(2)}, u32[]{:S(2)}) collective-permute-start(f32[512,512]{1,0:T(8,128)} %refs_0_.9), channel_id=1, source_target_pairs={{0,32},{32,64},{64,96},{96,0},{16,112},{48,16},{80,48},{112,80},{1... | collective-permute-start | bytes 3145736 | tf_op jit(solution)/shard_map/ppermute | solution.py:39
  8.9 25.7 %collective-permute-start.1 = (f32[512,512]{1,0:T(8,128)}, f32[512,512]{1,0:T(8,128)S(1)}, u32[]{:S(2)}, u32[]{:S(2)}) collective-permute-start(f32[512,512]{1,0:T(8,128)} %refs_0_.9), channel_id=1, source_target_pairs={{0,96},{32,0},{64,32},{96,64},{16,48},{48,80},{80,112},{112,16},{1... | collective-permute-start | bytes 3145736 | tf_op jit(solution)/shard_map/ppermute | solution.py:39
  8.9 25.7 %collective-permute-start.2 = (f32[512,512]{1,0:T(8,128)}, f32[512,512]{1,0:T(8,128)}, u32[]{:S(2)}, u32[]{:S(2)}) collective-permute-start(f32[512,512]{1,0:T(8,128)} %refs_0_.9), channel_id=1, source_target_pairs={{0,128},{128,0},{1,129},{129,1},{2,130},{130,2},{3,131},{131,3},{4... | collective-permute-start | bytes 3145736 | tf_op jit(solution)/shard_map/ppermute | solution.py:28
  21.3 45.0 %copy-start.9 = (s32[8]{0:T(128)S(1)}, s32[8]{0:T(128)}, u32[]{:S(2)}) copy-start(s32[8]{0:T(128)} %get-tuple-element.43.picks) | copy-start | bytes 100
  28.5 24.5 %collective-permute-start.8 = (f32[512,512]{1,0:T(8,128)}, f32[512,512]{1,0:T(8,128)S(1)}, u32[]{:S(2)}, u32[]{:S(2)}) collective-permute-start(f32[512,512]{1,0:T(8,128)} %collective-permute-done.3.refs_1_), channel_id=1, source_target_pairs={{0,1},{1,2},{2,3},{3,4},{4,5},{5,6},{6,7},{7,0},{16,23},{17,16},{1... | collective-permute-start | bytes 3145736 | tf_op jit(solution)/shard_map/ppermute | solution.py:36
  31.9 25.3 %collective-permute-start.9 = (f32[512,512]{1,0:T(8,128)}, f32[512,512]{1,0:T(8,128)S(1)}, u32[]{:S(2)}, u32[]{:S(2)}) collective-permute-start(f32[512,512]{1,0:T(8,128)} %collective-permute-done.4.refs_6_.refs_7_), channel_id=1, source_target_pairs={{0,7},{1,0},{2,1},{3,2},{4,3},{5,4},{6,5},{7,6},{16,17},{17,18},{1... | collective-permute-start | bytes 3145736 | tf_op jit(solution)/shard_map/ppermute | solution.py:36
  31.9 36.2 %copy-start.2 = (f32[512,512]{1,0:T(8,128)}, f32[512,512]{1,0:T(8,128)S(1)}, u32[]{:S(2)}) copy-start(f32[512,512]{1,0:T(8,128)S(1)} %collective-permute-done.refs_1_) | copy-start | bytes 3145732
  34.6 33.5 %copy-start.3 = (f32[512,512]{1,0:T(8,128)}, f32[512,512]{1,0:T(8,128)S(1)}, u32[]{:S(2)}) copy-start(f32[512,512]{1,0:T(8,128)S(1)} %collective-permute-done.1.refs_2_.refs_3_) | copy-start | bytes 3145732
  34.6 24.5 %collective-permute-start.5 = (f32[512,512]{1,0:T(8,128)}, f32[512,512]{1,0:T(8,128)S(1)}, u32[]{:S(2)}, u32[]{:S(2)}) collective-permute-start(f32[512,512]{1,0:T(8,128)} %collective-permute-done.2.refs_3_.refs_4_), channel_id=1, source_target_pairs={{0,32},{32,64},{64,96},{96,0},{16,112},{48,16},{80,48},{112,80},{1... | collective-permute-start | bytes 3145736 | tf_op jit(solution)/shard_map/ppermute | solution.py:39
  37.8 25.6 %collective-permute-start.6 = (f32[512,512]{1,0:T(8,128)}, f32[512,512]{1,0:T(8,128)S(1)}, u32[]{:S(2)}, u32[]{:S(2)}) collective-permute-start(f32[512,512]{1,0:T(8,128)} %collective-permute-done.2.refs_3_.refs_4_), channel_id=1, source_target_pairs={{0,96},{32,0},{64,32},{96,64},{16,48},{48,80},{80,112},{112,16},{1... | collective-permute-start | bytes 3145736 | tf_op jit(solution)/shard_map/ppermute | solution.py:39
  37.8 25.6 %collective-permute-start.7 = (f32[4,256,256]{2,1,0:T(8,128)}, f32[4,256,256]{2,1,0:T(8,128)S(1)}, u32[]{:S(2)}, u32[]{:S(2)}) collective-permute-start(f32[4,256,256]{2,1,0:T(8,128)} %send.1), channel_id=1, source_target_pairs={{0,8},{8,0},{1,9},{9,1},{2,10},{10,2},{3,11},{11,3},{4,12},{12,4},... | collective-permute-start | bytes 3145736 | tf_op jit(solution)/shard_map/ppermute | solution.py:28
  53.0 15.1 %copy-start.22 = (f32[512,512]{1,0:T(8,128)}, f32[512,512]{1,0:T(8,128)S(1)}, u32[]{:S(2)}) copy-start(f32[512,512]{1,0:T(8,128)S(1)} %collective-permute-done.8.refs_2_) | copy-start | bytes 3145732
  57.1 11.0 %copy-start.23 = (f32[512,512]{1,0:T(8,128)}, f32[512,512]{1,0:T(8,128)S(1)}, u32[]{:S(2)}) copy-start(f32[512,512]{1,0:T(8,128)S(1)} %collective-permute-done.9.refs_5_.refs_6_) | copy-start | bytes 3145732
  57.1 24.8 %collective-permute-start.12 = (f32[512,512]{1,0:T(8,128)S(1)}, f32[512,512]{1,0:T(8,128)S(1)}, u32[]{:S(2)}, u32[]{:S(2)}) collective-permute-start(f32[512,512]{1,0:T(8,128)S(1)} %collective-permute-done.8.refs_2_), channel_id=1, source_target_pairs={{0,1},{1,2},{2,3},{3,4},{4,5},{5,6},{6,7},{7,0},{16,23},{17,16},{1... | collective-permute-start | bytes 3145736 | tf_op jit(solution)/shard_map/ppermute | solution.py:36
  57.1 25.9 %collective-permute-start.13 = (f32[512,512]{1,0:T(8,128)S(1)}, f32[512,512]{1,0:T(8,128)S(1)}, u32[]{:S(2)}, u32[]{:S(2)}) collective-permute-start(f32[512,512]{1,0:T(8,128)S(1)} %collective-permute-done.9.refs_5_.refs_6_), channel_id=1, source_target_pairs={{0,7},{1,0},{2,1},{3,2},{4,3},{5,4},{6,5},{7,6},{16,17},{17,18},{1... | collective-permute-start | bytes 3145736 | tf_op jit(solution)/shard_map/ppermute | solution.py:36
  59.1 9.0 %copy-start.4 = (f32[512,512]{1,0:T(8,128)}, f32[512,512]{1,0:T(8,128)S(1)}, u32[]{:S(2)}) copy-start(f32[512,512]{1,0:T(8,128)S(1)} %collective-permute-done.5.refs_4_.refs_5_) | copy-start | bytes 3145732
  63.4 19.7 %collective-permute-start.14 = (f32[4,256,256]{2,1,0:T(8,128)S(1)}, f32[4,256,256]{2,1,0:T(8,128)S(1)}, u32[]{:S(2)}, u32[]{:S(2)}) collective-permute-start(f32[4,256,256]{2,1,0:T(8,128)S(1)} %collective-permute-done.7.refs_8_.refs_2_.refs_9_), channel_id=1, source_target_pairs={{0,16},{16,0},{1,17},{17,1},{2,18},{18,2},{3,19},{19,3},{4,20},{20... | collective-permute-start | bytes 3145736 | tf_op jit(solution)/shard_map/ppermute | solution.py:28
  63.6 23.6 %collective-permute-start.10 = (f32[512,512]{1,0:T(8,128)S(1)}, f32[512,512]{1,0:T(8,128)S(1)}, u32[]{:S(2)}, u32[]{:S(2)}) collective-permute-start(f32[512,512]{1,0:T(8,128)S(1)} %collective-permute-done.refs_1_), channel_id=1, source_target_pairs={{0,32},{32,64},{64,96},{96,0},{16,112},{48,16},{80,48},{112,80},{1... | collective-permute-start | bytes 3145736 | tf_op jit(solution)/shard_map/ppermute | solution.py:39
  66.3 23.0 %collective-permute-start.11 = (f32[512,512]{1,0:T(8,128)S(1)}, f32[512,512]{1,0:T(8,128)S(1)}, u32[]{:S(2)}, u32[]{:S(2)}) collective-permute-start(f32[512,512]{1,0:T(8,128)S(1)} %collective-permute-done.5.refs_4_.refs_5_), channel_id=1, source_target_pairs={{0,32},{32,64},{64,96},{96,0},{16,112},{48,16},{80,48},{112,80},{1... | collective-permute-start | bytes 3145736 | tf_op jit(solution)/shard_map/ppermute | solution.py:39
  66.3 16.8 %copy-start.6 = (s32[2]{0:T(128)S(1)}, s32[2]{0:T(128)}, u32[]{:S(2)}) copy-start(s32[2]{0:T(128)} %pad_add_fusion.where) | copy-start | bytes 28
  66.3 16.8 %copy-start.14 = (s32[3,32]{1,0:T(4,128)S(1)}, s32[3,32]{1,0:T(4,128)}, u32[]{:S(2)}) copy-start(s32[3,32]{1,0:T(4,128)} %get-tuple-element.41.plan) | copy-start | bytes 1156
  83.1 13.9 %collective-permute-start.18 = (f32[512,512]{1,0:T(8,128)S(1)}, f32[512,512]{1,0:T(8,128)S(1)}, u32[]{:S(2)}, u32[]{:S(2)}) collective-permute-start(f32[512,512]{1,0:T(8,128)S(1)} %collective-permute-done.12.refs_3_), channel_id=1, source_target_pairs={{0,1},{1,2},{2,3},{3,4},{4,5},{5,6},{6,7},{7,0},{16,23},{17,16},{1... | collective-permute-start | bytes 3145736 | tf_op jit(solution)/shard_map/ppermute | solution.py:36
  85.3 27.1 %collective-permute-start.19 = (f32[256,512]{1,0:T(8,128)S(1)}, f32[256,512]{1,0:T(8,128)S(1)}, u32[]{:S(2)}, u32[]{:S(2)}) collective-permute-start(f32[256,512]{1,0:T(8,128)S(1)} %beta1.1), channel_id=1, source_target_pairs={{0,8},{8,0},{1,9},{9,1},{2,10},{10,2},{3,11},{11,3},{4,12},{12,4},... | collective-permute-start | bytes 1572872 | tf_op jit(solution)/shard_map/ppermute | solution.py:28
  87.1 6.4 %copy-start.16 = (f32[512,512]{1,0:T(8,128)}, f32[512,512]{1,0:T(8,128)S(1)}, u32[]{:S(2)}) copy-start(f32[512,512]{1,0:T(8,128)S(1)} %collective-permute-done.10.refs_2_) | copy-start | bytes 3145732
  87.1 16.4 %collective-permute-start.15 = (f32[512,512]{1,0:T(8,128)S(1)}, f32[512,512]{1,0:T(8,128)S(1)}, u32[]{:S(2)}, u32[]{:S(2)}) collective-permute-start(f32[512,512]{1,0:T(8,128)S(1)} %collective-permute-done.10.refs_2_), channel_id=1, source_target_pairs={{0,16},{16,0},{1,17},{17,1},{2,18},{18,2},{3,19},{19,3},{4,20},{20... | collective-permute-start | bytes 3145736 | tf_op jit(solution)/shard_map/ppermute | solution.py:28
  89.2 14.3 %collective-permute-start.16 = (f32[512,512]{1,0:T(8,128)S(1)}, f32[512,512]{1,0:T(8,128)S(1)}, u32[]{:S(2)}, u32[]{:S(2)}) collective-permute-start(f32[512,512]{1,0:T(8,128)S(1)} %collective-permute-done.11.refs_6_), channel_id=1, source_target_pairs={{0,16},{16,0},{1,17},{17,1},{2,18},{18,2},{3,19},{19,3},{4,20},{20... | collective-permute-start | bytes 3145736 | tf_op jit(solution)/shard_map/ppermute | solution.py:28
  91.2 12.3 %collective-permute-start.17 = (f32[6,256,512]{2,1,0:T(8,128)S(1)}, f32[6,256,512]{2,1,0:T(8,128)S(1)}, u32[]{:S(2)}, u32[]{:S(2)}) collective-permute-start(f32[6,256,512]{2,1,0:T(8,128)S(1)} %pick.1), channel_id=1, source_target_pairs={{0,16},{16,0},{1,17},{17,1},{2,18},{18,2},{3,19},{19,3},{4,20},{20... | collective-permute-start | bytes 9437192 | tf_op jit(solution)/shard_map/ppermute | solution.py:28
  98.0 7.8 %copy-start.8 = (s32[1,32]{1,0:T(1,128)S(1)}, s32[1,32]{1,0:T(1,128)}, u32[]{:S(2)}) copy-start(s32[1,32]{1,0:T(1,128)} %get-tuple-element.30.plan) | copy-start | bytes 388
  98.0 18.2 %collective-permute-start.20 = (f32[256,768]{1,0:T(8,128)S(1)}, f32[256,768]{1,0:T(8,128)S(1)}, u32[]{:S(2)}, u32[]{:S(2)}) collective-permute-start(f32[256,768]{1,0:T(8,128)S(1)} %beta3.1), channel_id=1, source_target_pairs={{0,8},{8,0},{1,9},{9,1},{2,10},{10,2},{3,11},{11,3},{4,12},{12,4},... | collective-permute-start | bytes 2359304 | tf_op jit(solution)/shard_map/ppermute | solution.py:28
  (14 other events, 49.8 us)

commit v13 on v11

--- a/solution.py
+++ b/solution.py
@@ -380,9 +380,8 @@
     uf, ub, v = lax.optimization_barrier((uf, ub, v, f1, b1))[:3]
     vf, vb = step(v, "x"), step(v, "x", -1)
     got = swap(after(tiles, v), "ylo")
-    f2, b2 = lax.optimization_barrier((f2, b2))
     f3, b3 = step(f2, "z"), step(b2, "z", -1)
-    vf, vb, got, uf = lax.optimization_barrier((vf, vb, got, uf, f2))[:4]
+    vf, vb, got, uf = lax.optimization_barrier((vf, vb, got, uf, b2))[:4]
     u2, v2 = step(uf, "x"), step(vf, "x")
     other = swap(got, "core")
     picked = pick_call(picks, [coeffs, uf, ub, v, vf, vb])

time: 120 us -> 120 us (level)
  starting transfers between devices: 27.9 us -> 33.2 us
  Pallas kernels: 26.9 us -> 24 us
  waiting for transfers between devices: 54.1 us -> 52.2 us
    ppermute x7, waiting for transfers between devices: 40.2 us -> 32.4 us  [step(): return lax.ppermute(value, ('core', axis), pairs)]
    ppermute x7, starting transfers between devices: 11.3 us -> 14.9 us  [step(): return lax.ppermute(value, ('core', axis), pairs)]
    ppermute x8, starting transfers between devices: 8.22 us -> 11.5 us  [swap(): return lax.ppermute(value, axis, [(0, 1), (1, 0)])]
    ppermute x6, waiting for transfers between devices: 9.01 us -> 12 us  [step(): return lax.ppermute(value, (axis, 'core'), pairs)]
    ppermute x8, waiting for transfers between devices: 4.93 us -> 7.79 us  [swap(): return lax.ppermute(value, axis, [(0, 1), (1, 0)])]
    ppermute x6, starting transfers between devices: 8.37 us -> 6.79 us  [step(): return lax.ppermute(value, (axis, 'core'), pairs)]
    pallas_call x1, Pallas kernels: 5.82 us -> 4.27 us  [alpha_call(): pl.pallas_call(alpha_kernel, out_shape=jax.ShapeDtypeStruct((n, n), jnp.f...]
    pallas_call x4, Pallas kernels: 11.2 us -> 9.86 us  [beta_call(): pl.pallas_call(functools.partial(beta_kernel, call), out_shape=jax.ShapeD...]
  transfers between devices with their start and end apart: 21 -> 21, of which waited for: 11 -> 8; matrix products, arithmetic and copies ran while one was open for 5% -> 5% of each run, Pallas kernels for 19% -> 16%
where the time goes in v13:
time: 120 us; the launch traced here: 119 us
  waiting for transfers between devices  52.2 us (44%)
  starting transfers between devices  33.2 us (28%)
  Pallas kernels  24 us (20%)
  local copies, waits for them, and re-layouts  8.14 us (7%)
    ppermute x7, waiting for transfers between devices, step(): return lax.ppermute(value, ('core', axis), pairs)  32.4 us
    ppermute x7, starting transfers between devices, step(): return lax.ppermute(value, ('core', axis), pairs)  14.9 us
    ppermute x6, waiting for transfers between devices, step(): return lax.ppermute(value, (axis, 'core'), pairs)  12 us
    ppermute x8, starting transfers between devices, swap(): return lax.ppermute(value, axis, [(0, 1), (1, 0)])  11.5 us
    pallas_call x4, Pallas kernels, beta_call(): pl.pallas_call(functools.partial(beta_kernel, call), out_shape=jax.ShapeD...  9.86 us
    unnamed x54, local copies, waits for them, and re-layouts  8.14 us
    ppermute x8, waiting for transfers between devices, swap(): return lax.ppermute(value, axis, [(0, 1), (1, 0)])  7.79 us
    ppermute x6, starting transfers between devices, step(): return lax.ppermute(value, (axis, 'core'), pairs)  6.79 us
  transfers between devices with their start and end apart: 21, of which 8 were waited for; matrix products, arithmetic and copies ran while one was open for 5% of the time, Pallas kernels for 16%

profile of v13, /device:TPU:1, one launch (start us, length us, event | category | flops | bytes accessed | tf_op | source)
XLA Modules:
  0.0 118.9 jit_solution(2498507585773670378)
XLA Ops:
  0.0 6.4 %collective-permute-start.3 = (f32[512,512]{1,0:T(8,128)}, f32[512,512]{1,0:T(8,128)}, u32[]{:S(2)}, u32[]{:S(2)}) collective-permute-start(f32[512,512]{1,0:T(8,128)} %refs_0_.9), channel_id=1, source_target_pairs={{0,1},{1,2},{2,3},{3,4},{4,5},{5,6},{6,7},{7,0},{16,23},{17,16},{1... | collective-permute-start | bytes 3145736 | tf_op jit(solution)/shard_map/ppermute | solution.py:36
  6.4 2.5 %collective-permute-start = (f32[512,512]{1,0:T(8,128)}, f32[512,512]{1,0:T(8,128)S(1)}, u32[]{:S(2)}, u32[]{:S(2)}) collective-permute-start(f32[512,512]{1,0:T(8,128)} %refs_0_.9), channel_id=1, source_target_pairs={{0,32},{32,64},{64,96},{96,0},{16,112},{48,16},{80,48},{112,80},{1... | collective-permute-start | bytes 3145736 | tf_op jit(solution)/shard_map/ppermute | solution.py:39
  8.9 2.9 %collective-permute-start.2 = (f32[512,512]{1,0:T(8,128)}, f32[512,512]{1,0:T(8,128)}, u32[]{:S(2)}, u32[]{:S(2)}) collective-permute-start(f32[512,512]{1,0:T(8,128)} %refs_0_.9), channel_id=1, source_target_pairs={{0,128},{128,0},{1,129},{129,1},{2,130},{130,2},{3,131},{131,3},{4... | collective-permute-start | bytes 3145736 | tf_op jit(solution)/shard_map/ppermute | solution.py:28
  11.8 1.4 %copy.10.alpha_source = s32[32,8]{1,0:T(8,128)} copy(s32[32,8]{0,1:T(8,128)} %param.14) | data formatting | bytes 2048 | tf_op args[5]
  13.2 1.4 %copy.11.alpha_live = s32[32,8]{1,0:T(8,128)} copy(s32[32,8]{0,1:T(8,128)} %param.15) | data formatting | bytes 2048 | tf_op args[6]
  14.5 1.4 %copy.12.beta_source = s32[32,8]{1,0:T(8,128)} copy(s32[32,8]{0,1:T(8,128)} %param.16) | data formatting | bytes 2048 | tf_op args[7]
  15.9 1.4 %copy.13.beta_live = s32[32,8]{1,0:T(8,128)} copy(s32[32,8]{0,1:T(8,128)} %param.17) | data formatting | bytes 2048 | tf_op args[8]
  17.9 3.4 %plan.1 = (s32[1,32]{1,0:T(1,128)}, s32[3,32]{1,0:T(4,128)}, s32[8]{0:T(128)}, s32[8]{0:T(128)}) custom-call(s32[2]{0:T(128)} %pad_add_fusion.where, s32[32,8]{1,0:T(8,128)} %copy.10.alpha_source, s32[32,8]{1,0:T(8,128)} %copy.11.alpha_live, s32[32,8]{1,0:T(8,128)} %copy.12.beta_source, s32[32,8]{1,0:T(8,128)} %copy.13.beta_live), custom_call_target="tpu_custom_call" | custom-call | tf_op jit(solution)/shard_map/plan/pallas_call | solution.py:365
  21.3 2.9 %send.1 = f32[4,256,256]{2,1,0:T(8,128)} custom-call(s32[2]{0:T(128)} %pad_add_fusion.where, s32[8]{0:T(128)} %get-tuple-element.27.sends, f32[2,8,256,256]{3,2,1,0:T(8,128)} %refs_8_), custom_call_target="tpu_custom_call" | custom-call | flops 1048576 | bytes 262144 | tf_op jit(solution)/shard_map/send/pallas_call | solution.py:232
  24.2 4.3 %collective-permute-done.3.refs_1_ = f32[512,512]{1,0:T(8,128)} collective-permute-done((f32[512,512]{1,0:T(8,128)}, f32[512,512]{1,0:T(8,128)}, u32[]{:S(2)}, u32[]{:S(2)}) %collective-permute-start.3) | collective-permute-done | bytes 1048608 | tf_op jit(solution)/shard_map/ppermute | solution.py:36
  28.5 3.4 %collective-permute-start.11 = (f32[512,512]{1,0:T(8,128)}, f32[512,512]{1,0:T(8,128)S(1)}, u32[]{:S(2)}, u32[]{:S(2)}) collective-permute-start(f32[512,512]{1,0:T(8,128)} %collective-permute-done.3.refs_1_), channel_id=1, source_target_pairs={{0,1},{1,2},{2,3},{3,4},{4,5},{5,6},{6,7},{7,0},{16,23},{17,16},{1... | collective-permute-start | bytes 3145736 | tf_op jit(solution)/shard_map/ppermute | solution.py:36
  31.9 2.7 %collective-permute-done.1.refs_2_.refs_3_ = f32[512,512]{1,0:T(8,128)S(1)} collective-permute-done((f32[512,512]{1,0:T(8,128)}, f32[512,512]{1,0:T(8,128)S(1)}, u32[]{:S(2)}, u32[]{:S(2)}) %collective-permute-start.1) | collective-permute-done | bytes 1048608 | tf_op jit(solution)/shard_map/ppermute | solution.py:39
  34.6 3.2 %collective-permute-start.5 = (f32[512,512]{1,0:T(8,128)}, f32[512,512]{1,0:T(8,128)S(1)}, u32[]{:S(2)}, u32[]{:S(2)}) collective-permute-start(f32[512,512]{1,0:T(8,128)} %collective-permute-done.2.refs_3_.refs_4_), channel_id=1, source_target_pairs={{0,32},{32,64},{64,96},{96,0},{16,112},{48,16},{80,48},{112,80},{1... | collective-permute-start | bytes 3145736 | tf_op jit(solution)/shard_map/ppermute | solution.py:39
  37.8 1.3 %collective-permute-start.7 = (f32[4,256,256]{2,1,0:T(8,128)}, f32[4,256,256]{2,1,0:T(8,128)S(1)}, u32[]{:S(2)}, u32[]{:S(2)}) collective-permute-start(f32[4,256,256]{2,1,0:T(8,128)} %send.1), channel_id=1, source_target_pairs={{0,8},{8,0},{1,9},{9,1},{2,10},{10,2},{3,11},{11,3},{4,12},{12,4},... | collective-permute-start | bytes 3145736 | tf_op jit(solution)/shard_map/ppermute | solution.py:28
  39.1 5.2 %collective-permute-done.11.refs_2_ = f32[512,512]{1,0:T(8,128)S(1)} collective-permute-done((f32[512,512]{1,0:T(8,128)}, f32[512,512]{1,0:T(8,128)S(1)}, u32[]{:S(2)}, u32[]{:S(2)}) %collective-permute-start.11) | collective-permute-done | bytes 1048608 | tf_op jit(solution)/shard_map/ppermute | solution.py:36
  44.3 3.3 %collective-permute-start.12 = (f32[512,512]{1,0:T(8,128)S(1)}, f32[512,512]{1,0:T(8,128)S(1)}, u32[]{:S(2)}, u32[]{:S(2)}) collective-permute-start(f32[512,512]{1,0:T(8,128)S(1)} %collective-permute-done.11.refs_2_), channel_id=1, source_target_pairs={{0,1},{1,2},{2,3},{3,4},{4,5},{5,6},{6,7},{7,0},{16,23},{17,16},{1... | collective-permute-start | bytes 3145736 | tf_op jit(solution)/shard_map/ppermute | solution.py:36
  47.6 12.4 %collective-permute-done.8.refs_5_.refs_6_ = f32[512,512]{1,0:T(8,128)S(1)} collective-permute-done((f32[512,512]{1,0:T(8,128)}, f32[512,512]{1,0:T(8,128)S(1)}, u32[]{:S(2)}, u32[]{:S(2)}) %collective-permute-start.8) | collective-permute-done | bytes 1048608 | tf_op jit(solution)/shard_map/ppermute | solution.py:36
  60.1 3.3 %collective-permute-done.6.refs_5_.refs_7_ = f32[512,512]{1,0:T(8,128)S(1)} collective-permute-done((f32[512,512]{1,0:T(8,128)}, f32[512,512]{1,0:T(8,128)S(1)}, u32[]{:S(2)}, u32[]{:S(2)}) %collective-permute-start.6) | collective-permute-done | bytes 1048608 | tf_op jit(solution)/shard_map/ppermute | solution.py:39
  63.4 2.8 %collective-permute-start.14 = (f32[4,256,256]{2,1,0:T(8,128)S(1)}, f32[4,256,256]{2,1,0:T(8,128)S(1)}, u32[]{:S(2)}, u32[]{:S(2)}) collective-permute-start(f32[4,256,256]{2,1,0:T(8,128)S(1)} %collective-permute-done.7.refs_8_.refs_2_.refs_9_), channel_id=1, source_target_pairs={{0,16},{16,0},{1,17},{17,1},{2,18},{18,2},{3,19},{19,3},{4,20},{20... | collective-permute-start | bytes 3145736 | tf_op jit(solution)/shard_map/ppermute | solution.py:28
  66.2 1.1 collective-permute-start.9
  67.3 1.8 %pick.1 = f32[6,256,512]{2,1,0:T(8,128)S(1)} custom-call(s32[8]{0:T(128)S(1)} %copy-done.9, f32[512,512]{1,0:T(8,128)S(1)} %copy-done, f32[512,512]{1,0:T(8,128)S(1)} %collective-permute-done.refs_1_, f32[512,512]{1,0:T(8,128)S(1)} %collective-permute-done.1.refs_2_.refs_3_, f32[512,512]{1,0:T(8,128)} %collective-permute-done.2.refs_3_.refs_4_, ...), custom_call_target="tpu_custom_call" | custom-call | flops 1048576 | bytes 262144 | tf_op jit(solution)/shard_map/pick/pallas_call | solution.py:148
  69.2 10.4 %collective-permute-done.13.refs_4_.refs_5_ = f32[512,512]{1,0:T(8,128)S(1)} collective-permute-done((f32[512,512]{1,0:T(8,128)S(1)}, f32[512,512]{1,0:T(8,128)S(1)}, u32[]{:S(2)}, u32[]{:S(2)}) %collective-permute-start.13) | collective-permute-done | bytes 1048608 | tf_op jit(solution)/shard_map/ppermute | solution.py:36
  79.6 1.7 %collective-permute-start.18 = (f32[512,512]{1,0:T(8,128)S(1)}, f32[512,512]{1,0:T(8,128)S(1)}, u32[]{:S(2)}, u32[]{:S(2)}) collective-permute-start(f32[512,512]{1,0:T(8,128)S(1)} %collective-permute-done.12.refs_3_), channel_id=1, source_target_pairs={{0,1},{1,2},{2,3},{3,4},{4,5},{5,6},{6,7},{7,0},{16,23},{17,16},{1... | collective-permute-start | bytes 3145736 | tf_op jit(solution)/shard_map/ppermute | solution.py:36
  81.4 3.1 %beta1.1 = f32[256,512]{1,0:T(8,128)S(1)} custom-call(s32[2]{0:T(128)S(1)} %copy-done.6, s32[3,32]{1,0:T(4,128)S(1)} %copy-done.14, f32[512,512]{1,0:T(8,128)} %refs_0_.9, f32[512,512]{1,0:T(8,128)} %collective-permute-done.3.refs_1_, f32[512,512]{1,0:T(8,128)} %copy-done.22, f32[512,512]{1,0:T(8,128)S(1)} %collective-permute-done.12.refs_3_, ...), custom_call_target="tpu_custom_call" | custom-call | flops 17179869184 | bytes 33554432 | tf_op jit(solution)/shard_map/beta1/pallas_call | solution.py:315
  85.3 6.0 %collective-permute-done.10.refs_6_ = f32[512,512]{1,0:T(8,128)S(1)} collective-permute-done((f32[512,512]{1,0:T(8,128)S(1)}, f32[512,512]{1,0:T(8,128)S(1)}, u32[]{:S(2)}, u32[]{:S(2)}) %collective-permute-start.10) | collective-permute-done | bytes 1048608 | tf_op jit(solution)/shard_map/ppermute | solution.py:39
  91.3 2.2 %collective-permute-start.16 = (f32[512,512]{1,0:T(8,128)S(1)}, f32[512,512]{1,0:T(8,128)S(1)}, u32[]{:S(2)}, u32[]{:S(2)}) collective-permute-start(f32[512,512]{1,0:T(8,128)S(1)} %collective-permute-done.10.refs_6_), channel_id=1, source_target_pairs={{0,16},{16,0},{1,17},{17,1},{2,18},{18,2},{3,19},{19,3},{4,20},{20... | collective-permute-start | bytes 3145736 | tf_op jit(solution)/shard_map/ppermute | solution.py:28
  93.5 3.4 %beta2.1.refs_4_ = f32[256,512]{1,0:T(8,128)S(1)} custom-call(s32[2]{0:T(128)S(1)} %copy-done.6, s32[3,32]{1,0:T(4,128)S(1)} %copy-done.14, f32[512,512]{1,0:T(8,128)} %refs_0_.9, f32[512,512]{1,0:T(8,128)} %collective-permute-done.3.refs_1_, f32[512,512]{1,0:T(8,128)} %copy-done.22, f32[512,512]{1,0:T(8,128)} %copy-done.10, f32[512,512]{1,0:T(8,128)} %copy-done.11, ...), custom_call_target="tpu_custom_call" | custom-call | flops 17179869184 | bytes 33554432 | tf_op jit(solution)/shard_map/beta2/pallas_call | solution.py:315
  98.0 1.6 %collective-permute-start.20 = (f32[256,768]{1,0:T(8,128)S(1)}, f32[256,768]{1,0:T(8,128)S(1)}, u32[]{:S(2)}, u32[]{:S(2)}) collective-permute-start(f32[256,768]{1,0:T(8,128)S(1)} %beta3.1), channel_id=1, source_target_pairs={{0,8},{8,0},{1,9},{9,1},{2,10},{10,2},{3,11},{11,3},{4,12},{12,4},... | collective-permute-start | bytes 2359304 | tf_op jit(solution)/shard_map/ppermute | solution.py:28
  99.6 2.6 %beta0.1 = f32[512,512]{1,0:T(8,128)S(1)} custom-call(s32[2]{0:T(128)S(1)} %copy-done.6, s32[3,32]{1,0:T(4,128)S(1)} %copy-done.14, f32[512,512]{1,0:T(8,128)} %refs_0_.9, f32[512,512]{1,0:T(8,128)} %collective-permute-done.3.refs_1_, f32[512,512]{1,0:T(8,128)} %copy-done.22, f32[512,512]{1,0:T(8,128)} %copy-done.10, f32[512,512]{1,0:T(8,128)} %copy-done.13, ...), custom_call_target="tpu_custom_call" | custom-call | flops 17179869184 | bytes 33554432 | tf_op jit(solution)/shard_map/beta0/pallas_call | solution.py:315
  104.6 4.3 %alpha.1 = f32[512,512]{1,0:T(8,128)S(1)} custom-call(s32[1,32]{1,0:T(1,128)S(1)} %copy-done.8, f32[512,512]{1,0:T(8,128)} %refs_0_.9, f32[512,512]{1,0:T(8,128)} %copy-done.2, f32[512,512]{1,0:T(8,128)} %copy-done.16, f32[512,512]{1,0:T(8,128)} %copy-done.3, f32[512,512]{1,0:T(8,128)} %collective-permute-done.2.refs_3_.refs_4_, f32[512,512]{1,0:T(8,128)} %copy-done.4, ...), custom_call_target="tpu_custom_call" | custom-call | flops 1048576 | bytes 262144 | tf_op jit(solution)/shard_map/alpha/pallas_call | solution.py:201
  109.2 7.8 %collective-permute-done.20.rest = f32[256,768]{1,0:T(8,128)S(1)} collective-permute-done((f32[256,768]{1,0:T(8,128)S(1)}, f32[256,768]{1,0:T(8,128)S(1)}, u32[]{:S(2)}, u32[]{:S(2)}) %collective-permute-start.20) | collective-permute-done | bytes 786464 | tf_op jit(solution)/shard_map/ppermute | solution.py:28
  116.9 1.8 %last.1 = f32[512,512]{1,0:T(8,128)} custom-call(s32[2]{0:T(128)S(1)} %copy-done.6, s32[8]{0:T(128)S(1)} %copy-done.7, f32[512,512]{1,0:T(8,128)S(1)} %add_add_fusion.joined, f32[256,512]{1,0:T(8,128)S(1)} %collective-permute-done.19.top, f32[256,768]{1,0:T(8,128)S(1)} %collective-permute-done.20.rest), custom_call_target="tpu_custom_call" | custom-call | flops 1048576 | bytes 262144 | tf_op jit(solution)/shard_map/last/pallas_call | solution.py:401
  (75 shorter events, 5.1 us)
Async XLA Ops:
  0.0 67.3 %copy-start = (f32[512,512]{1,0:T(8,128)S(1)}, f32[512,512]{1,0:T(8,128)}, u32[]{:S(2)}) copy-start(f32[512,512]{1,0:T(8,128)} %refs_0_.9) | copy-start | bytes 3145732
  0.0 28.5 %collective-permute-start.3 = (f32[512,512]{1,0:T(8,128)}, f32[512,512]{1,0:T(8,128)}, u32[]{:S(2)}, u32[]{:S(2)}) collective-permute-start(f32[512,512]{1,0:T(8,128)} %refs_0_.9), channel_id=1, source_target_pairs={{0,1},{1,2},{2,3},{3,4},{4,5},{5,6},{6,7},{7,0},{16,23},{17,16},{1... | collective-permute-start | bytes 3145736 | tf_op jit(solution)/shard_map/ppermute | solution.py:36
  6.4 25.5 %collective-permute-start.4 = (f32[512,512]{1,0:T(8,128)}, f32[512,512]{1,0:T(8,128)}, u32[]{:S(2)}, u32[]{:S(2)}) collective-permute-start(f32[512,512]{1,0:T(8,128)} %refs_0_.9), channel_id=1, source_target_pairs={{0,7},{1,0},{2,1},{3,2},{4,3},{5,4},{6,5},{7,6},{16,17},{17,18},{1... | collective-permute-start | bytes 3145736 | tf_op jit(solution)/shard_map/ppermute | solution.py:36
  6.4 25.5 %collective-permute-start = (f32[512,512]{1,0:T(8,128)}, f32[512,512]{1,0:T(8,128)S(1)}, u32[]{:S(2)}, u32[]{:S(2)}) collective-permute-start(f32[512,512]{1,0:T(8,128)} %refs_0_.9), channel_id=1, source_target_pairs={{0,32},{32,64},{64,96},{96,0},{16,112},{48,16},{80,48},{112,80},{1... | collective-permute-start | bytes 3145736 | tf_op jit(solution)/shard_map/ppermute | solution.py:39
  8.9 25.7 %collective-permute-start.1 = (f32[512,512]{1,0:T(8,128)}, f32[512,512]{1,0:T(8,128)S(1)}, u32[]{:S(2)}, u32[]{:S(2)}) collective-permute-start(f32[512,512]{1,0:T(8,128)} %refs_0_.9), channel_id=1, source_target_pairs={{0,96},{32,0},{64,32},{96,64},{16,48},{48,80},{80,112},{112,16},{1... | collective-permute-start | bytes 3145736 | tf_op jit(solution)/shard_map/ppermute | solution.py:39
  8.9 25.7 %collective-permute-start.2 = (f32[512,512]{1,0:T(8,128)}, f32[512,512]{1,0:T(8,128)}, u32[]{:S(2)}, u32[]{:S(2)}) collective-permute-start(f32[512,512]{1,0:T(8,128)} %refs_0_.9), channel_id=1, source_target_pairs={{0,128},{128,0},{1,129},{129,1},{2,130},{130,2},{3,131},{131,3},{4... | collective-permute-start | bytes 3145736 | tf_op jit(solution)/shard_map/ppermute | solution.py:28
  21.3 46.0 %copy-start.9 = (s32[8]{0:T(128)S(1)}, s32[8]{0:T(128)}, u32[]{:S(2)}) copy-start(s32[8]{0:T(128)} %get-tuple-element.39.picks) | copy-start | bytes 100
  28.5 15.8 %collective-permute-start.11 = (f32[512,512]{1,0:T(8,128)}, f32[512,512]{1,0:T(8,128)S(1)}, u32[]{:S(2)}, u32[]{:S(2)}) collective-permute-start(f32[512,512]{1,0:T(8,128)} %collective-permute-done.3.refs_1_), channel_id=1, source_target_pairs={{0,1},{1,2},{2,3},{3,4},{4,5},{5,6},{6,7},{7,0},{16,23},{17,16},{1... | collective-permute-start | bytes 3145736 | tf_op jit(solution)/shard_map/ppermute | solution.py:36
  31.9 37.2 %copy-start.2 = (f32[512,512]{1,0:T(8,128)}, f32[512,512]{1,0:T(8,128)S(1)}, u32[]{:S(2)}) copy-start(f32[512,512]{1,0:T(8,128)S(1)} %collective-permute-done.refs_1_) | copy-start | bytes 3145732
  34.6 34.5 %copy-start.3 = (f32[512,512]{1,0:T(8,128)}, f32[512,512]{1,0:T(8,128)S(1)}, u32[]{:S(2)}) copy-start(f32[512,512]{1,0:T(8,128)S(1)} %collective-permute-done.1.refs_2_.refs_3_) | copy-start | bytes 3145732
  34.6 25.4 %collective-permute-start.5 = (f32[512,512]{1,0:T(8,128)}, f32[512,512]{1,0:T(8,128)S(1)}, u32[]{:S(2)}, u32[]{:S(2)}) collective-permute-start(f32[512,512]{1,0:T(8,128)} %collective-permute-done.2.refs_3_.refs_4_), channel_id=1, source_target_pairs={{0,32},{32,64},{64,96},{96,0},{16,112},{48,16},{80,48},{112,80},{1... | collective-permute-start | bytes 3145736 | tf_op jit(solution)/shard_map/ppermute | solution.py:39
  37.8 25.6 %collective-permute-start.6 = (f32[512,512]{1,0:T(8,128)}, f32[512,512]{1,0:T(8,128)S(1)}, u32[]{:S(2)}, u32[]{:S(2)}) collective-permute-start(f32[512,512]{1,0:T(8,128)} %collective-permute-done.2.refs_3_.refs_4_), channel_id=1, source_target_pairs={{0,96},{32,0},{64,32},{96,64},{16,48},{48,80},{80,112},{112,16},{1... | collective-permute-start | bytes 3145736 | tf_op jit(solution)/shard_map/ppermute | solution.py:39
  37.8 22.3 %collective-permute-start.8 = (f32[512,512]{1,0:T(8,128)}, f32[512,512]{1,0:T(8,128)S(1)}, u32[]{:S(2)}, u32[]{:S(2)}) collective-permute-start(f32[512,512]{1,0:T(8,128)} %collective-permute-done.4.refs_6_.refs_7_), channel_id=1, source_target_pairs={{0,7},{1,0},{2,1},{3,2},{4,3},{5,4},{6,5},{7,6},{16,17},{17,18},{1... | collective-permute-start | bytes 3145736 | tf_op jit(solution)/shard_map/ppermute | solution.py:36
  37.8 25.6 %collective-permute-start.7 = (f32[4,256,256]{2,1,0:T(8,128)}, f32[4,256,256]{2,1,0:T(8,128)S(1)}, u32[]{:S(2)}, u32[]{:S(2)}) collective-permute-start(f32[4,256,256]{2,1,0:T(8,128)} %send.1), channel_id=1, source_target_pairs={{0,8},{8,0},{1,9},{9,1},{2,10},{10,2},{3,11},{11,3},{4,12},{12,4},... | collective-permute-start | bytes 3145736 | tf_op jit(solution)/shard_map/ppermute | solution.py:28
  44.3 24.8 %copy-start.22 = (f32[512,512]{1,0:T(8,128)}, f32[512,512]{1,0:T(8,128)S(1)}, u32[]{:S(2)}) copy-start(f32[512,512]{1,0:T(8,128)S(1)} %collective-permute-done.11.refs_2_) | copy-start | bytes 3145732
  44.3 24.8 %collective-permute-start.12 = (f32[512,512]{1,0:T(8,128)S(1)}, f32[512,512]{1,0:T(8,128)S(1)}, u32[]{:S(2)}, u32[]{:S(2)}) collective-permute-start(f32[512,512]{1,0:T(8,128)S(1)} %collective-permute-done.11.refs_2_), channel_id=1, source_target_pairs={{0,1},{1,2},{2,3},{3,4},{4,5},{5,6},{6,7},{7,0},{16,23},{17,16},{1... | collective-permute-start | bytes 3145736 | tf_op jit(solution)/shard_map/ppermute | solution.py:36
  60.0 9.1 %copy-start.23 = (f32[512,512]{1,0:T(8,128)}, f32[512,512]{1,0:T(8,128)S(1)}, u32[]{:S(2)}) copy-start(f32[512,512]{1,0:T(8,128)S(1)} %collective-permute-done.8.refs_5_.refs_6_) | copy-start | bytes 3145732
  60.0 19.6 %collective-permute-start.13 = (f32[512,512]{1,0:T(8,128)S(1)}, f32[512,512]{1,0:T(8,128)S(1)}, u32[]{:S(2)}, u32[]{:S(2)}) collective-permute-start(f32[512,512]{1,0:T(8,128)S(1)} %collective-permute-done.8.refs_5_.refs_6_), channel_id=1, source_target_pairs={{0,7},{1,0},{2,1},{3,2},{4,3},{5,4},{6,5},{7,6},{16,17},{17,18},{1... | collective-permute-start | bytes 3145736 | tf_op jit(solution)/shard_map/ppermute | solution.py:36
  60.1 9.1 %copy-start.4 = (f32[512,512]{1,0:T(8,128)}, f32[512,512]{1,0:T(8,128)S(1)}, u32[]{:S(2)}) copy-start(f32[512,512]{1,0:T(8,128)S(1)} %collective-permute-done.5.refs_4_.refs_5_) | copy-start | bytes 3145732
  63.4 18.0 %collective-permute-start.14 = (f32[4,256,256]{2,1,0:T(8,128)S(1)}, f32[4,256,256]{2,1,0:T(8,128)S(1)}, u32[]{:S(2)}, u32[]{:S(2)}) collective-permute-start(f32[4,256,256]{2,1,0:T(8,128)S(1)} %collective-permute-done.7.refs_8_.refs_2_.refs_9_), channel_id=1, source_target_pairs={{0,16},{16,0},{1,17},{17,1},{2,18},{18,2},{3,19},{19,3},{4,20},{20... | collective-permute-start | bytes 3145736 | tf_op jit(solution)/shard_map/ppermute | solution.py:28
  66.2 19.1 %collective-permute-start.9 = (f32[512,512]{1,0:T(8,128)S(1)}, f32[512,512]{1,0:T(8,128)S(1)}, u32[]{:S(2)}, u32[]{:S(2)}) collective-permute-start(f32[512,512]{1,0:T(8,128)S(1)} %collective-permute-done.refs_1_), channel_id=1, source_target_pairs={{0,32},{32,64},{64,96},{96,0},{16,112},{48,16},{80,48},{112,80},{1... | collective-permute-start | bytes 3145736 | tf_op jit(solution)/shard_map/ppermute | solution.py:39
  67.3 24.1 %collective-permute-start.10 = (f32[512,512]{1,0:T(8,128)S(1)}, f32[512,512]{1,0:T(8,128)S(1)}, u32[]{:S(2)}, u32[]{:S(2)}) collective-permute-start(f32[512,512]{1,0:T(8,128)S(1)} %collective-permute-done.5.refs_4_.refs_5_), channel_id=1, source_target_pairs={{0,32},{32,64},{64,96},{96,0},{16,112},{48,16},{80,48},{112,80},{1... | collective-permute-start | bytes 3145736 | tf_op jit(solution)/shard_map/ppermute | solution.py:39
  67.3 14.1 %copy-start.6 = (s32[2]{0:T(128)S(1)}, s32[2]{0:T(128)}, u32[]{:S(2)}) copy-start(s32[2]{0:T(128)} %pad_add_fusion.where) | copy-start | bytes 28
  67.3 14.1 %copy-start.14 = (s32[3,32]{1,0:T(4,128)S(1)}, s32[3,32]{1,0:T(4,128)}, u32[]{:S(2)}) copy-start(s32[3,32]{1,0:T(4,128)} %get-tuple-element.38.plan) | copy-start | bytes 1156
  69.1 15.4 %copy-start.10 = (f32[512,512]{1,0:T(8,128)}, f32[512,512]{1,0:T(8,128)S(1)}, u32[]{:S(2)}) copy-start(f32[512,512]{1,0:T(8,128)S(1)} %collective-permute-done.12.refs_3_) | copy-start | bytes 3145732
  79.6 17.4 %collective-permute-start.18 = (f32[512,512]{1,0:T(8,128)S(1)}, f32[512,512]{1,0:T(8,128)S(1)}, u32[]{:S(2)}, u32[]{:S(2)}) collective-permute-start(f32[512,512]{1,0:T(8,128)S(1)} %collective-permute-done.12.refs_3_), channel_id=1, source_target_pairs={{0,1},{1,2},{2,3},{3,4},{4,5},{5,6},{6,7},{7,0},{16,23},{17,16},{1... | collective-permute-start | bytes 3145736 | tf_op jit(solution)/shard_map/ppermute | solution.py:36
  84.5 24.6 %collective-permute-start.19 = (f32[256,512]{1,0:T(8,128)S(1)}, f32[256,512]{1,0:T(8,128)S(1)}, u32[]{:S(2)}, u32[]{:S(2)}) collective-permute-start(f32[256,512]{1,0:T(8,128)S(1)} %beta1.1), channel_id=1, source_target_pairs={{0,8},{8,0},{1,9},{9,1},{2,10},{10,2},{3,11},{11,3},{4,12},{12,4},... | collective-permute-start | bytes 1572872 | tf_op jit(solution)/shard_map/ppermute | solution.py:28
  85.3 11.6 %copy-start.16 = (f32[512,512]{1,0:T(8,128)}, f32[512,512]{1,0:T(8,128)S(1)}, u32[]{:S(2)}) copy-start(f32[512,512]{1,0:T(8,128)S(1)} %collective-permute-done.9.refs_2_) | copy-start | bytes 3145732
  85.3 16.9 %collective-permute-start.15 = (f32[512,512]{1,0:T(8,128)S(1)}, f32[512,512]{1,0:T(8,128)S(1)}, u32[]{:S(2)}, u32[]{:S(2)}) collective-permute-start(f32[512,512]{1,0:T(8,128)S(1)} %collective-permute-done.9.refs_2_), channel_id=1, source_target_pairs={{0,16},{16,0},{1,17},{17,1},{2,18},{18,2},{3,19},{19,3},{4,20},{20... | collective-permute-start | bytes 3145736 | tf_op jit(solution)/shard_map/ppermute | solution.py:28
  91.3 10.9 %collective-permute-start.16 = (f32[512,512]{1,0:T(8,128)S(1)}, f32[512,512]{1,0:T(8,128)S(1)}, u32[]{:S(2)}, u32[]{:S(2)}) collective-permute-start(f32[512,512]{1,0:T(8,128)S(1)} %collective-permute-done.10.refs_6_), channel_id=1, source_target_pairs={{0,16},{16,0},{1,17},{17,1},{2,18},{18,2},{3,19},{19,3},{4,20},{20... | collective-permute-start | bytes 3145736 | tf_op jit(solution)/shard_map/ppermute | solution.py:28
  93.5 8.8 %collective-permute-start.17 = (f32[6,256,512]{2,1,0:T(8,128)S(1)}, f32[6,256,512]{2,1,0:T(8,128)S(1)}, u32[]{:S(2)}, u32[]{:S(2)}) collective-permute-start(f32[6,256,512]{2,1,0:T(8,128)S(1)} %pick.1), channel_id=1, source_target_pairs={{0,16},{16,0},{1,17},{17,1},{2,18},{18,2},{3,19},{19,3},{4,20},{20... | collective-permute-start | bytes 9437192 | tf_op jit(solution)/shard_map/ppermute | solution.py:28
  98.0 18.9 %collective-permute-start.20 = (f32[256,768]{1,0:T(8,128)S(1)}, f32[256,768]{1,0:T(8,128)S(1)}, u32[]{:S(2)}, u32[]{:S(2)}) collective-permute-start(f32[256,768]{1,0:T(8,128)S(1)} %beta3.1), channel_id=1, source_target_pairs={{0,8},{8,0},{1,9},{9,1},{2,10},{10,2},{3,11},{11,3},{4,12},{12,4},... | collective-permute-start | bytes 2359304 | tf_op jit(solution)/shard_map/ppermute | solution.py:28
  (14 other events, 58.3 us)
